TPU v7x, 128 devices: a whole 4x4x4 slice. The times are simulated.
128 devices in a mesh: row: 8 (over y, core), col: 16 (over x, z).
Axes of the slice: x: 4, y: 4, z: 4, core: 2. Of those that a mesh axis runs over, the one named last changes fastest.
Arguments:
- descriptors: bfloat16 [16384, 1024], P(('row', 'col'))
- gradients: bfloat16 [3, 4, 16384, 1024], P(None, None, ('row', 'col'))
- sparse_panel: bfloat16 [512, 1024], P('col')
- sparse_trail: bfloat16 [2048, 1024], P('col')
- atom_counts: int32 [128, 8], P(('row', 'col')), may hold values from 1 to 16, 64 in all within a row
- owner_rows: int32 [128, 8], P(('row', 'col')), may hold values from 0 to 7, each once within a row
- neighbor_ids: int32 [1024, 16, 4], P(('row', 'col')), may hold values from 0 to 65519
Outputs:
- panel_factor: float32 [512, 512], replicated
- cross_factor: float32 [2048, 512], P('col')
- trail_residual: float32 [2048, 65536], P('col', 'row')
Inputs may be any that keep to these rules, and one draw needn't show every extreme that they name: `atom_counts`: the structures of one device's line hold 64 atoms together, and every line has a structure of 16 atoms. `owner_rows`: every device gives exactly one structure to each row group.
All inputs are finite; a program needn't handle non-finite values.
Results may differ from a plain program's by a relative error of at most 0.0043.
Values may be sent and summed in bfloat16 or wider, within the bound.
No kernel may reach another device: no remote copies, remote signals or barrier semaphores. Data moves between devices by JAX's collectives and lax.ppermute only.
A program may use at most 128 MiB of HBM per device.

v0:
```python
import jax
import jax.numpy as jnp
from jax import lax
from jax.sharding import PartitionSpec as P

ridge_value = 0.1


def slot_rows(environments, desc_here, slope_here, count_here, neighbor_here, owner_here):
    struct_count = count_here.shape[0]
    atom_slots = neighbor_here.shape[1]
    neighbor_count = neighbor_here.shape[2]
    env_count = environments.shape[0]
    correlation = lax.dot_general(
        environments, desc_here, (((1,), (1,)), ((), ())), preferred_element_type=jnp.float32
    )
    slope_dots = lax.dot_general(
        environments, slope_here, (((1,), (1,)), ((), ())), preferred_element_type=jnp.float32
    )
    slope_dots = slope_dots.reshape(env_count, 3, neighbor_count, struct_count, atom_slots)
    slot_index = jnp.arange(atom_slots, dtype=jnp.int32)
    live_mask = (slot_index[None, :] < count_here[:, None]).astype(jnp.float32)
    squares = (correlation * correlation).reshape(env_count, struct_count, atom_slots)
    energy = jnp.sum(squares * live_mask[None], axis=2) / count_here.astype(jnp.float32)[None, :]
    partner = neighbor_here % count_here[:, None, None]
    struct_index = jnp.arange(struct_count, dtype=jnp.int32)
    flat_index = (struct_index[:, None, None] * atom_slots + partner).reshape(-1)
    picked = jnp.take(correlation, flat_index, axis=1).reshape(
        env_count, struct_count, atom_slots, neighbor_count
    )
    picked = jnp.transpose(picked, (0, 3, 1, 2))
    forces = -2.0 * jnp.sum(picked[:, None] * slope_dots, axis=2) * live_mask[None, None]
    forces = jnp.transpose(forces, (0, 2, 3, 1)).reshape(env_count, struct_count, 3 * atom_slots)
    padding = jnp.zeros((env_count, struct_count, atom_slots - 1), jnp.float32)
    slot_values = jnp.concatenate([energy[:, :, None], forces, padding], axis=2).astype(
        jnp.bfloat16
    )
    chosen = (owner_here[None, :] == struct_index[:, None]).astype(jnp.int32)
    owner_order = jnp.sum(struct_index[None, :] * chosen, axis=1)
    return jnp.take(slot_values, owner_order, axis=1)


def factor_panel(gram_sum, cross_sum, total_rows):
    gram_matrix = gram_sum / total_rows + ridge_value * jnp.eye(
        gram_sum.shape[0], dtype=jnp.float32
    )
    lower_factor = jnp.linalg.cholesky(gram_matrix)
    coupling = lax.linalg.triangular_solve(
        lower_factor, cross_sum / total_rows, left_side=True, lower=True
    )
    weights = lax.linalg.triangular_solve(
        lower_factor, coupling, left_side=True, lower=True, transpose_a=True
    )
    return (lower_factor.T, coupling, weights)


def split_weights(weights):
    weight_high = weights.astype(jnp.bfloat16)
    held_high = lax.optimization_barrier(weight_high)
    weight_low = (weights - held_high.astype(jnp.float32)).astype(jnp.bfloat16)
    return (weight_high, weight_low)


def reduce_products(gram_part, cross_part):
    return lax.psum((gram_part, cross_part), ("row", "col"))


def contract_rows(left_side, right_side):
    return lax.dot_general(
        left_side, right_side, (((1,), (1,)), ((), ())), preferred_element_type=jnp.float32
    )


def contract_cols(left_side, right_side):
    return lax.dot_general(
        left_side, right_side, (((0,), (0,)), ((), ())), preferred_element_type=jnp.float32
    )


def arrange_direct(block_rows, row_count, col_count):
    env_width = block_rows.shape[0] // col_count
    slot_count = block_rows.shape[2]
    shaped = block_rows.reshape(col_count, env_width, row_count, slot_count)
    return jnp.transpose(shaped, (2, 0, 1, 3)).reshape(row_count * col_count, env_width, slot_count)


def restore_direct(block_rows, row_count, col_count):
    env_width = block_rows.shape[1]
    slot_count = block_rows.shape[2]
    shaped = block_rows.reshape(row_count, col_count, env_width, slot_count)
    return jnp.transpose(shaped, (2, 1, 0, 3)).reshape(
        env_width, row_count * col_count * slot_count
    )


def per_device(
    descriptors, gradients, sparse_panel, sparse_trail, atom_counts, owner_rows, neighbor_ids
):
    row_count = lax.axis_size("row")
    col_count = lax.axis_size("col")
    col_index = lax.axis_index("col")
    count_here = atom_counts[0]
    owner_here = owner_rows[0]
    slope_here = gradients.reshape(-1, gradients.shape[3])
    panel_width = sparse_panel.shape[0]
    trail_width = sparse_trail.shape[0]
    panel_total = panel_width * col_count
    trail_total = trail_width * col_count
    slot_count = 4 * neighbor_ids.shape[1]
    total_rows = row_count * row_count * col_count * slot_count
    own_envs = jnp.concatenate([sparse_panel, sparse_trail], axis=0)
    kernel_rows = slot_rows(
        lax.all_gather(own_envs, "col", axis=0, tiled=True),
        descriptors,
        slope_here,
        count_here,
        neighbor_ids,
        owner_here,
    )
    blocks = kernel_rows.reshape(col_count, panel_width + trail_width, row_count, slot_count)
    panel_rows = blocks[:, :panel_width].reshape(panel_total, row_count, slot_count)
    trail_rows = blocks[:, panel_width:].reshape(trail_total, row_count, slot_count)
    received = (
        lax.all_to_all(
            arrange_direct(panel_rows, row_count, col_count),
            ("row", "col"),
            split_axis=0,
            concat_axis=0,
            tiled=True,
        ),
        lax.all_to_all(
            arrange_direct(trail_rows, row_count, col_count),
            ("row", "col"),
            split_axis=0,
            concat_axis=0,
            tiled=True,
        ),
    )
    panel_own = restore_direct(received[0], row_count, col_count)
    trail_own = restore_direct(received[1], row_count, col_count)
    segment = lax.all_gather(panel_own, "col", axis=0, tiled=True)
    columns = jnp.concatenate(
        [contract_rows(segment, panel_own), contract_rows(segment, trail_own)], axis=1
    )
    gram_part = lax.dynamic_update_slice(
        jnp.zeros((panel_total, panel_total), jnp.float32),
        columns[:, :panel_width],
        (0, col_index * panel_width),
    )
    cross_part = lax.dynamic_update_slice(
        jnp.zeros((panel_total, trail_total), jnp.float32),
        columns[:, panel_width:],
        (0, col_index * trail_width),
    )
    gram_sum, cross_sum = reduce_products(gram_part, cross_part)
    panel_factor, coupling, weights = factor_panel(gram_sum, cross_sum, total_rows)
    coupling_own = lax.dynamic_slice_in_dim(coupling, col_index * trail_width, trail_width, 1)
    weights_own = lax.dynamic_slice_in_dim(weights, col_index * trail_width, trail_width, 1)
    weight_high, weight_low = split_weights(weights_own)
    segment = lax.all_gather(panel_own, "col", axis=0, tiled=True)
    trail_residual = (
        trail_own.astype(jnp.float32)
        - contract_cols(weight_high, segment)
        - contract_cols(weight_low, segment)
    )
    cross_factor = coupling_own.T
    return (panel_factor, cross_factor, trail_residual)


def solution(mesh):
    return jax.shard_map(
        per_device,
        mesh=mesh,
        in_specs=(
            P(("row", "col"), None),
            P(None, None, ("row", "col"), None),
            P("col", None),
            P("col", None),
            P(("row", "col"), None),
            P(("row", "col"), None),
            P(("row", "col"), None, None),
        ),
        out_specs=(P(), P("col", None), P("col", "row")),
        check_vma=False,
    )
```

profile of v0, /device:TPU:1, one launch (start us, length us, event | category | flops | bytes accessed | tf_op | source)
XLA Modules:
  0.0 593.4 jit_solution(4389010923176962485)
XLA Ops:
  14.9 55.6 %all-gather.3.cloned.1.call-done = bf16[2560,1024]{1,0:T(8,128)(2,1)} async-done(((bf16[160,1024]{1,0:T(8,128)(2,1)}), bf16[2560,1024]{1,0:T(8,128)(2,1)}) %all-gather.3.cloned.1.call-update) | async-done | bytes 5242896 | tf_op jit(solution)/shard_map/all_gather | solution.py:113
  70.5 5.4 multiply_reduce_fusion.1
  75.9 7.7 %gather_fusion = f32[512,2560]{1,0:T(8,128)} fusion(f32[2560,128]{0,1:T(8,128)} %get-tuple-element.64, s32[1024]{0:T(1024)S(1)} %pad_clamp_fusion.1), kind=kCustom, calls=%fused_computation | custom fusion | bytes 10487808 | tf_op jit(solution)/shard_map/jit(_take)/gather | solution.py:28
  83.6 7.1 %gather.17 = f32[2560,8,16,4]{0,3,2,1:T(4,128)} reshape(f32[2560,512]{0,1:T(8,128)} %bitcast.121) | data formatting | bytes 10485760 | tf_op jit(solution)/shard_map/jit(_take)/gather | solution.py:28
  90.7 4.6 fusion.1
  95.4 12.1 %multiply_reduce_fusion = f32[2560,3,8,16]{0,3,2,1:T(8,128)S(1)} fusion(f32[2560,4,8,16]{0,3,2,1:T(8,128)S(1)} %fusion.1, bf16[3,4,8,16,1024]{4,3,2,1,0:T(8,128)(2,1)S(1)} %bitcast.117, bf16[2560,1024]{1,0:T(8,128)(2,1)} %all-gather.3.cloned.1.call-done), kind=kOutput, calls=%fused_computation.4 | convolution fusion | flops 8059944960 | bytes 17563648 | tf_op jit(solution)/shard_map/dot_general | solution.py:17
  112.8 8.6 %gather.19 = bf16[16,160,8,64]{1,0,3,2:T(8,128)(2,1)} reshape(bf16[2560,8,64]{0,2,1:T(8,128)(2,1)} %bitcast.120) | data formatting | bytes 5242880 | tf_op jit(solution)/shard_map/jit(_take)/gather | solution.py:40
  121.4 3.6 copy_select_fusion.1
  129.1 21.1 %all_to_all.10 = bf16[128,2,1024]{2,1,0:T(2,128)(2,1)S(1)} all-to-all(bf16[128,2,1024]{2,1,0:T(2,128)(2,1)S(1)} %reshape.290), channel_id=1, replica_groups=mesh['row'=8,'col'=16] {'row','col'}, dimensions={0} | all-to-all | bytes 1048576 | tf_op jit(solution)/shard_map/all_to_all | solution.py:124
  153.1 4.3 slice.149
  157.4 4.8 all-to-all-start.1
  162.3 36.1 %all-to-all-done.1 = bf16[128,128,64]{1,2,0:T(8,128)(2,1)S(1)} async-done(((bf16[128,128,64]{1,2,0:T(8,128)(2,1)}), bf16[128,128,64]{1,2,0:T(8,128)(2,1)S(1)}, u32[]{:S(2)}, u32[]{:S(2)}) %all-to-all-start.1) | async-done | bytes 2097184 | tf_op jit(solution)/shard_map/all_to_all | solution.py:131
  200.1 40.1 %all-gather.5.cloned.1.call-done = bf16[512,8192]{1,0:T(8,128)(2,1)} async-done(((bf16[32,8192]{1,0:T(8,128)(2,1)}), bf16[512,8192]{1,0:T(8,128)(2,1)}) %all-gather.5.cloned.1.call-update) | async-done | bytes 8388624 | tf_op jit(solution)/shard_map/all_gather | solution.py:141
  240.3 6.1 %convolution_dynamic-update-slice_fusion.3 = f32[512,512]{0,1:T(8,128)S(1)} fusion(f32[512,512]{0,1:T(8,128)S(1)} %broadcast_in_dim.40, s32[]{:T(128)S(6)} %select_n.80, bf16[512,8192]{1,0:T(8,128)(2,1)} %all-gather.5.cloned.1.call-done, bf16[32,8192]{1,0:T(8,128)(2,1)S(1)} %copy-done.8), kind=kOutput, calls=%fused_computation.54 | convolution fusion | flops 268435456 | bytes 8978436 | tf_op jit(solution)/shard_map/dot_general | solution.py:69
  247.4 2.5 broadcast_in_dim.46
  249.9 3.1 convolution_dynamic-update-slice_fusion
  253.0 3.1 copy.81
  256.2 153.1 %all-reduce.4.cloned.1.call-done = (f32[512,512]{0,1:T(8,128)}, f32[512,2048]{1,0:T(8,128)}) async-done(((f32[512,512]{0,1:T(8,128)}, f32[512,2048]{1,0:T(8,128)}), (f32[512,512]{0,1:T(8,128)}, f32[512,2048]{1,0:T(8,128)})) %all-reduce.4.cloned.1.call-update) | async-done | bytes 5242896 | tf_op jit(solution)/shard_map/psum | solution.py:65
  411.3 11.7 %cholesky.103 = f32[128,128]{1,0:T(8,128)S(1)} custom-call(f32[128,128]{1,0:T(8,128)S(1)} %cholesky.263), custom_call_target="Cholesky" | custom-call | tf_op jit(solution)/shard_map/jit(cholesky)/cholesky | solution.py:47
  423.2 9.8 %custom-call.32 = f32[1,128,128]{1,2,0:T(8,128)S(1)} custom-call(f32[1,128,128]{2,1,0:T(8,128)S(1)} %get-tuple-element.62), custom_call_target="InvertDiagBlocksLowerTriangular" | custom-call | tf_op jit(solution)/shard_map/jit(cholesky)/cholesky | solution.py:47
  433.8 11.7 %cholesky.215 = f32[128,128]{1,0:T(8,128)S(1)} custom-call(f32[128,128]{1,0:T(8,128)S(1)} %cholesky.267), custom_call_target="Cholesky" | custom-call | tf_op jit(solution)/shard_map/jit(cholesky)/cholesky | solution.py:47
  445.8 10.2 %custom-call.33 = f32[1,128,128]{1,2,0:T(8,128)S(1)} custom-call(f32[1,128,128]{2,1,0:T(8,128)S(1)} %get-tuple-element.60), custom_call_target="InvertDiagBlocksLowerTriangular" | custom-call | tf_op jit(solution)/shard_map/jit(cholesky)/cholesky | solution.py:47
  456.9 11.7 %cholesky.236 = f32[128,128]{1,0:T(8,128)S(1)} custom-call(f32[128,128]{1,0:T(8,128)S(1)} %cholesky.272), custom_call_target="Cholesky" | custom-call | tf_op jit(solution)/shard_map/jit(cholesky)/cholesky | solution.py:47
  468.8 9.8 %custom-call.34 = f32[1,128,128]{1,2,0:T(8,128)S(1)} custom-call(f32[1,128,128]{2,1,0:T(8,128)S(1)} %get-tuple-element.58), custom_call_target="InvertDiagBlocksLowerTriangular" | custom-call | tf_op jit(solution)/shard_map/jit(cholesky)/cholesky | solution.py:47
  479.4 11.9 %cholesky.253 = f32[128,128]{1,0:T(8,128)S(1)} custom-call(f32[128,128]{1,0:T(8,128)S(1)} %convolution_subtract_fusion.8), custom_call_target="Cholesky" | custom-call | tf_op jit(solution)/shard_map/jit(cholesky)/cholesky | solution.py:47
  494.1 4.8 broadcast_multiply_fusion
  502.7 11.1 %while.1 = (s32[]{:T(128)}, f32[512,512]{0,1:T(8,128)S(1)}, s32[4,2]{0,1:T(2,128)S(1)}, f32[4,128,128]{2,1,0:T(8,128)}, s32[]{:T(128)}) while((s32[]{:T(128)}, f32[512,512]{0,1:T(8,128)S(1)}, s32[4,2]{0,1:T(2,128)S(1)}, f32[4,128,128]{2,1,0:T(8,128)}, s32[]{:T(128)}) %tuple.40), condition=%wide.while_cond, body=%wide.while_body.sunk | while | flops 2 | bytes 393329 | solution.py:48
  513.9 40.2 %custom-call.35 = f32[4,128,128]{1,2,0:T(8,128)S(1)} custom-call(f32[4,128,128]{2,1,0:T(8,128)} %get-tuple-element.10), custom_call_target="InvertDiagBlocksLowerTriangular" | custom-call | tf_op jit(solution)/shard_map/triangular_solve | solution.py:48
  562.2 3.2 fusion.17
  573.3 2.5 convolution_subtract_fusion.2
  576.9 3.1 fusion.14
  583.0 3.6 convolution_subtract_fusion
  (135 shorter events, 62.8 us)
Async XLA Ops:
  7.2 88.2 %copy-start = (bf16[3,4,128,1024]{3,2,1,0:T(8,128)(2,1)S(1)}, bf16[3,4,128,1024]{3,2,1,0:T(8,128)(2,1)}, u32[]{:S(2)}) copy-start(bf16[3,4,128,1024]{3,2,1,0:T(8,128)(2,1)} %param.8) | copy-start | bytes 9437188
  7.2 63.3 %all-gather.3.cloned.1.call-start = ((), (), s32[]{:S(2)}) async-start(), calls=%async_computation.2 | async-start | bytes 5570560 | tf_op jit(solution)/shard_map/all_gather | solution.py:113
  9.1 231.0 %all-gather.5.cloned.1.call-start = ((), (), s32[]{:S(2)}) async-start(), calls=%async_computation.3 | async-start | bytes 8912896 | tf_op jit(solution)/shard_map/all_gather | solution.py:141
  125.0 2.0 copy-start.5
  157.4 82.8 %copy-start.8 = (bf16[32,8192]{1,0:T(8,128)(2,1)S(1)}, bf16[32,8192]{1,0:T(8,128)(2,1)}, u32[]{:S(2)}) copy-start(bf16[32,8192]{1,0:T(8,128)(2,1)} %reshape.250) | copy-start | bytes 1572868
  157.4 41.0 %all-to-all-start.1 = ((bf16[128,128,64]{1,2,0:T(8,128)(2,1)}), bf16[128,128,64]{1,2,0:T(8,128)(2,1)S(1)}, u32[]{:S(2)}, u32[]{:S(2)}) async-start(bf16[128,128,64]{1,2,0:T(8,128)(2,1)} %bitcast.123), calls=%async_computation.1 | async-start | bytes 4194304 | tf_op jit(solution)/shard_map/all_to_all | solution.py:131
  162.3 247.0 %all-reduce.4.cloned.1.call-start = ((), (), s32[]{:S(2)}) async-start(), calls=%async_computation.4 | async-start | bytes 10485760 | tf_op jit(solution)/shard_map/psum | solution.py:65
  240.3 9.7 %copy-start.2 = (bf16[512,8192]{1,0:T(8,128)(2,1)S(1)}, bf16[512,8192]{1,0:T(8,128)(2,1)}, u32[]{:S(2)}) copy-start(bf16[512,8192]{1,0:T(8,128)(2,1)} %all-gather.5.cloned.1.call-done) | copy-start | bytes 25165828
  246.4 1.0 copy-start.11
  247.4 2.5 copy-start.7
  409.2 1.8 copy-start.10
  513.9 45.9 %copy-start.9 = (f32[512,512]{0,1:T(8,128)}, f32[512,512]{0,1:T(8,128)S(1)}, u32[]{:S(2)}) copy-start(f32[512,512]{0,1:T(8,128)S(1)} %get-tuple-element.126) | copy-start | bytes 3145732
  554.1 5.8 copy-start.4
  562.2 4.3 copy-start.3
  573.3 7.8 %slice-start = ((s8[8388608]{0:T(1024)(128)(4,1)}), s8[4194304]{0:T(1024)(128)(4,1)S(1)}, s32[]{:S(2)}) async-start(s8[8388608]{0:T(1024)(128)(4,1)} %bitcast.118), calls=%async_computation.5 | async-start | bytes 8388608
  576.9 4.2 slice-start.1
  580.0 1.6 copy-start.6
  583.0 3.6 copy-start.1
Sparse Core Ops, SparseCore 0:
  10.8 59.6 all-gather.2
  153.2 86.8 all-gather.4
  253.1 156.0 all-reduce.3
where the time goes:
time: 604 us; the launch traced here: 593 us
  waiting for transfers between devices  285 us (47%)
  other arithmetic  145 us (24%)
  local copies, waits for them, and re-layouts  61.6 us (10%)
  matrix products  58.4 us (10%)
  blocking collectives  21.1 us (3%)
  between operations  17.2 us (3%)
    psum x1, waiting for transfers between devices, reduce_products(): return lax.psum((gram_part, cross_part), ('row', 'col'))  153 us
    another operation x15, other arithmetic, factor_panel(): lower_factor = jnp.linalg.cholesky(gram_matrix)  79.7 us
    all_gather x1, waiting for transfers between devices, per_device(): lax.all_gather(own_envs, 'col', axis=0, tiled=True)  55.6 us
    another operation x3, other arithmetic, factor_panel(): lax.linalg.triangular_solve(lower_factor, cross_sum / total_rows, left_si...  41.4 us
    all_gather x1, waiting for transfers between devices, per_device(): segment = lax.all_gather(panel_own, 'col', axis=0, tiled=True)  40.1 us
    all_to_all x1, waiting for transfers between devices, per_device(): lax.all_to_all(arrange_direct(trail_rows, row_count, col_count), ('row',...  36.1 us
    all_to_all x1, blocking collectives, per_device(): lax.all_to_all(arrange_direct(panel_rows, row_count, col_count), ('row',...  21.1 us
    gather x2, local copies, waits for them, and re-layouts, slot_rows(): jnp.take(correlation, flat_index, axis=1)  14.8 us
  transfers between devices with their start and end apart: 4, of which 4 were waited for; matrix products, arithmetic and copies ran while one was open for 2% of the time, Pallas kernels for 0%

commit v1 on v0

v1 whole, which is shorter than its diff:
```python
import functools

import jax
import jax.numpy as jnp
from jax import lax
from jax.experimental import pallas as pl
from jax.experimental.pallas import tpu as pltpu
from jax.sharding import PartitionSpec as P

ridge_value = 0.1
HIGHEST = lax.Precision.HIGHEST
F32 = jnp.float32
BF16 = jnp.bfloat16
NT = (((1,), (1,)), ((), ()))
NN = (((1,), (0,)), ((), ()))
TN = (((0,), (0,)), ((), ()))

CORE_SWAP = [(i, i ^ 1) for i in range(8)]


def y_shift(s):
    return [(2 * y + c, 2 * ((y + s) % 4) + c) for y in range(4) for c in range(2)]


def z_shift(s):
    return [(x * 4 + z, x * 4 + (z + s) % 4) for x in range(4) for z in range(4)]


def x_shift(s):
    return [(x * 4 + z, ((x + s) % 4) * 4 + z) for x in range(4) for z in range(4)]


def dot(a, b, dims, precision=None):
    return lax.dot_general(a, b, dims, precision=precision, preferred_element_type=F32)


def in_order(pieces, index):
    return jnp.concatenate(
        [lax.select_n((index - j) % 4, *pieces) for j in range(4)], axis=0
    )


def gather4(v, axis, shift, index):
    pieces = [v] + [lax.ppermute(v, axis, shift(s)) for s in (1, 2, 3)]
    return in_order(pieces, index)


def ring4(v, axis, shift, index):
    h = v.shape[0] // 2
    a = lax.ppermute(v, axis, shift(1))
    b = lax.ppermute(v, axis, shift(3))
    c = lax.ppermute(a[:h], axis, shift(1))
    d = lax.ppermute(b[h:], axis, shift(3))
    return in_order([v, a, jnp.concatenate([c, d], axis=0), b], index)


def scatter4(v, axis, shift, index):
    n = v.shape[0] // 4
    total = lax.dynamic_slice_in_dim(v, index * n, n, 0)
    got = [
        lax.ppermute(
            lax.dynamic_slice_in_dim(v, ((index + s) % 4) * n, n, 0), axis, shift(s)
        )
        for s in (1, 2, 3)
    ]
    return total + got[0] + got[1] + got[2]


def swap_add(v, core):
    n = v.shape[0] // 2
    mine = lax.dynamic_slice_in_dim(v, core * n, n, 0)
    other = lax.dynamic_slice_in_dim(v, (1 - core) * n, n, 0)
    return mine + lax.ppermute(other, "row", CORE_SWAP)


def swap_gather(v, core):
    other = lax.ppermute(v, "row", CORE_SWAP)
    first = core == 0
    return jnp.where(first, v, other), jnp.where(first, other, v)


def spread4(v, axis, shift):
    got = [lax.ppermute(v, axis, shift(s)) for s in (1, 2, 3)]
    return v + got[0] + got[1] + got[2]


def tables(count, owner, neighbors):
    structs = jnp.arange(8, dtype=jnp.int32)
    offset = jnp.sum(jnp.where(structs[None, :] < structs[:, None], count[None, :], 0), axis=1)
    atoms = jnp.arange(64, dtype=jnp.int32)
    inside = (atoms[:, None] >= offset[None, :]) & (
        atoms[:, None] < (offset + count)[None, :]
    )
    slot = jnp.sum(jnp.where(inside, 16 * structs + atoms[:, None] - offset, 0), axis=1)
    slots = jnp.arange(128, dtype=jnp.int32)
    live = slot[:, None] == slots[None, :]
    partner = (16 * structs[:, None, None] + neighbors % count[:, None, None]).reshape(128, 4)
    picked = jnp.sum(jnp.where(live[:, :, None], partner[None], 0), axis=1)
    rows = jnp.concatenate([slot, picked.T.reshape(256)])
    pick_atoms = (rows[:, None] == slots[None, :]).astype(BF16)
    mean = (inside.astype(F32) / count.astype(F32)[None, :]).T
    of_group = owner[None, :] == structs[:, None]
    struct_g = jnp.sum(jnp.where(of_group, structs[None, :], 0), axis=1)
    count_g = jnp.sum(jnp.where(of_group, count[None, :], 0), axis=1)
    offset_g = jnp.sum(jnp.where(of_group, offset[None, :], 0), axis=1)
    place = jnp.arange(64, dtype=jnp.int32)[None, :]
    atom, part = (place - 1) // 3, (place - 1) % 3
    is_force = (place >= 1) & (atom < count_g[:, None])
    column = jnp.where(is_force, part * 64 + offset_g[:, None] + atom, -1)
    column = jnp.where(place == 0, 192 + struct_g[:, None], column).reshape(512)
    order = (column[:, None] == jnp.arange(256, dtype=jnp.int32)[None, :]).astype(BF16)
    return pick_atoms, mean, order


def compact_rows(env, atoms, grads, mean):
    near = dot(atoms, env, NT)
    slope = dot(grads, env, NT)
    inner = near[:64]
    parts = []
    for k in range(3):
        total = near[64:128] * slope[k * 256 : k * 256 + 64]
        for j in range(1, 4):
            total = total + near[64 + j * 64 : 128 + j * 64] * slope[
                k * 256 + j * 64 : k * 256 + j * 64 + 64
            ]
        parts.append((-2.0 * total).astype(BF16))
    energy = dot(mean, inner * inner, NN, HIGHEST)
    pad = jnp.zeros((56, env.shape[0]), F32)
    parts.append(jnp.concatenate([energy, pad], axis=0).astype(BF16))
    return jnp.concatenate(parts, axis=0)


def panel_kernel(env_ref, atoms_ref, grads_ref, mean_ref, order_ref, out_ref, gram_ref):
    rows = compact_rows(env_ref[...], atoms_ref[...], grads_ref[...], mean_ref[...])
    out_ref[...] = dot(order_ref[...], rows, NN).astype(BF16).reshape(out_ref.shape)
    gram_ref[...] = dot(rows, rows, TN)


def trail_kernel(env_ref, atoms_ref, grads_ref, mean_ref, order_ref, out_ref):
    rows = compact_rows(env_ref[...], atoms_ref[...], grads_ref[...], mean_ref[...])
    full = dot(order_ref[...], rows, NN).astype(BF16)
    for c in range(out_ref.shape[1]):
        out_ref[:, c] = full[:, c * 128 : c * 128 + 128].reshape(8, 64, 128)


def params():
    return pltpu.CompilerParams(vmem_limit_bytes=40 << 20)


def panel_rows(env, atoms, grads, mean, order):
    m = env.shape[0]
    return pl.pallas_call(
        panel_kernel,
        out_shape=(
            jax.ShapeDtypeStruct((8, 64, m), BF16),
            jax.ShapeDtypeStruct((m, m), F32),
        ),
        compiler_params=params(),
        cost_estimate=pl.CostEstimate(
            flops=2 * m * 1024 * 1088, bytes_accessed=5 << 20, transcendentals=0
        ),
    )(env, atoms, grads, mean, order)


def trail_rows(env, atoms, grads, mean, order):
    m = env.shape[0]
    tile = 512
    whole = lambda shape: pl.BlockSpec(shape, lambda i: (0, 0))
    return pl.pallas_call(
        trail_kernel,
        out_shape=jax.ShapeDtypeStruct((8, m // 128, 64, 128), BF16),
        grid=(m // tile,),
        in_specs=[
            pl.BlockSpec((tile, 1024), lambda i: (i, 0)),
            whole(atoms.shape),
            whole(grads.shape),
            whole(mean.shape),
            whole(order.shape),
        ],
        out_specs=pl.BlockSpec((8, tile // 128, 64, 128), lambda i: (0, i, 0, 0)),
        compiler_params=params(),
        cost_estimate=pl.CostEstimate(
            flops=2 * m * 1024 * 1088, bytes_accessed=9 << 20, transcendentals=0
        ),
    )(env, atoms, grads, mean, order)


def eliminate(a):
    lanes = lax.broadcasted_iota(jnp.int32, (8, 128), 1)
    subs = lax.broadcasted_iota(jnp.int32, (8, 128), 0)
    left = [a[8 * g : 8 * g + 8] for g in range(16)]
    right = [(lanes == subs + 8 * g).astype(F32) for g in range(16)]
    done = []
    for p in range(16):
        count = 16 - p
        cols = [
            [
                jnp.broadcast_to(left[g][:, 8 * p + q : 8 * p + q + 1], (8, 128))
                for g in range(count)
            ]
            for q in range(8)
        ]
        pivots = jnp.ones((8, 128), F32)
        for q in range(8):
            pivot = cols[q][0][q : q + 1]
            inverse = 1.0 / pivot
            pivots = jnp.where(subs == q, pivot, pivots)
            ratio = [c * inverse for c in cols[q]]
            ratio[0] = jnp.where(subs > q, ratio[0], 0.0)
            for t in range(q + 1, 8):
                here = cols[t][0][q : q + 1]
                for g in range(count):
                    cols[t][g] = cols[t][g] - ratio[g] * here
            row_left = left[0][q : q + 1]
            row_right = right[0][q : q + 1]
            for g in range(count):
                left[g] = left[g] - ratio[g] * row_left
                right[g] = right[g] - ratio[g] * row_right
        done.append(right[0] * lax.rsqrt(pivots))
        left, right = left[1:], right[1:]
    return jnp.concatenate(done, axis=0)


def factor_kernel(rows_total, gram_ref, factor_ref, inverse_ref, work):
    n = gram_ref.shape[0]
    r = lax.broadcasted_iota(jnp.int32, (n, n), 0)
    c = lax.broadcasted_iota(jnp.int32, (n, n), 1)
    work[:, :n] = gram_ref[...] / rows_total + jnp.where(r == c, ridge_value, 0.0)
    work[:, n:] = jnp.where(r == c, 1.0, 0.0)

    def step(b, carry):
        at = pl.multiple_of(b * 128, 128)
        low = eliminate(work[pl.ds(at, 128), pl.ds(at, 128)])
        row = dot(low, work[pl.ds(at, 128), :], NN, HIGHEST)
        lane = lax.broadcasted_iota(jnp.int32, (128, n), 1)
        later = jnp.where(lane >= at + 128, row[:, :n], 0.0)
        work[...] = work[...] - dot(later, row, TN, HIGHEST)
        work[pl.ds(at, 128), :] = row
        return carry

    lax.fori_loop(0, n // 128, step, 0)
    factor_ref[...] = jnp.where(c >= r, work[:, :n], 0.0)
    inverse_ref[...] = jnp.where(c <= r, work[:, n:], 0.0)


def factor_panel(gram, rows_total):
    n = gram.shape[0]
    return pl.pallas_call(
        functools.partial(factor_kernel, float(rows_total)),
        out_shape=(jax.ShapeDtypeStruct((n, n), F32), jax.ShapeDtypeStruct((n, n), F32)),
        scratch_shapes=[pltpu.VMEM((n, 2 * n), F32)],
        compiler_params=params(),
        cost_estimate=pl.CostEstimate(
            flops=20 * n * n * n, bytes_accessed=4 << 20, transcendentals=n
        ),
    )(gram)


def cross_kernel(panel_ref, trail_ref, out_ref):
    @pl.when(pl.program_id(0) == 0)
    def _():
        out_ref[...] = jnp.zeros_like(out_ref)

    trail = trail_ref[...].reshape(512, 128)
    out_ref[...] += dot(trail, panel_ref[0], TN)


def cross_part(segment, trail):
    n = segment.shape[2]
    return pl.pallas_call(
        cross_kernel,
        out_shape=jax.ShapeDtypeStruct((128, n), F32),
        grid=(segment.shape[0],),
        in_specs=[
            pl.BlockSpec((1, 512, n), lambda i: (i, 0, 0)),
            pl.BlockSpec((8, 1, 64, 128), lambda i: (0, i, 0, 0)),
        ],
        out_specs=pl.BlockSpec((128, n), lambda i: (0, 0)),
        compiler_params=params(),
        cost_estimate=pl.CostEstimate(
            flops=2 * 128 * n * 8192, bytes_accessed=11 << 20, transcendentals=0
        ),
    )(segment, trail)


def residual_kernel(
    rows_total, cross_ref, inverse_ref, panel_ref, trail_ref, coupling_ref, out_ref, weights
):
    @pl.when(pl.program_id(0) == 0)
    def _():
        coupling = dot(cross_ref[...] / rows_total, inverse_ref[...], NT, HIGHEST)
        coupling_ref[...] = coupling
        solved = dot(coupling, inverse_ref[...], NN, HIGHEST)
        high = solved.astype(BF16)
        weights[:128] = high
        weights[128:] = (solved - high.astype(F32)).astype(BF16)

    r = lax.broadcasted_iota(jnp.int32, (128, 128), 0)
    c = lax.broadcasted_iota(jnp.int32, (128, 128), 1)
    same = (r == c).astype(BF16)
    both = dot(weights[...], panel_ref[0], NT)
    own = dot(same, trail_ref[...].reshape(512, 128), NT)
    out_ref[...] = own - both[:128] - both[128:]


def residual(cross, inverse, segment, trail, rows_total):
    n = inverse.shape[0]
    chunks = segment.shape[0]
    whole = lambda shape: pl.BlockSpec(shape, lambda i: (0, 0))
    return pl.pallas_call(
        functools.partial(residual_kernel, float(rows_total)),
        out_shape=(
            jax.ShapeDtypeStruct((128, n), F32),
            jax.ShapeDtypeStruct((128, 512 * chunks), F32),
        ),
        grid=(chunks,),
        in_specs=[
            whole((128, n)),
            whole((n, n)),
            pl.BlockSpec((1, 512, n), lambda i: (i, 0, 0)),
            pl.BlockSpec((8, 1, 64, 128), lambda i: (0, i, 0, 0)),
        ],
        out_specs=(whole((128, n)), pl.BlockSpec((128, 512), lambda i: (0, i))),
        scratch_shapes=[pltpu.VMEM((256, n), BF16)],
        compiler_params=params(),
        cost_estimate=pl.CostEstimate(
            flops=4 * 128 * n * 8192, bytes_accessed=16 << 20, transcendentals=0
        ),
    )(cross, inverse, segment, trail)


def sum_all(v, core, y):
    v = scatter4(swap_add(v, core), "row", y_shift, y)
    v = spread4(spread4(v, "col", z_shift), "col", x_shift)
    v = gather4(v, "row", y_shift, y)
    return jnp.concatenate(swap_gather(v, core), axis=0)


def sum_row(v, core, y):
    v = scatter4(swap_add(v, core), "row", y_shift, y)
    v = gather4(v, "row", y_shift, y)
    return jnp.concatenate(swap_gather(v, core), axis=0)


def per_device(
    descriptors, gradients, sparse_panel, sparse_trail, atom_counts, owner_rows, neighbor_ids
):
    row = lax.axis_index("row")
    col = lax.axis_index("col")
    core, y = row % 2, row // 2
    x, z = col // 4, col % 4
    rows_total = 65536

    own = lax.dynamic_slice_in_dim(sparse_panel, core * 16, 16, 0)
    own = gather4(gather4(own, "col", z_shift, z), "col", x_shift, x)
    low, high = swap_gather(own, core)
    env_panel = jnp.stack(
        [low.reshape(16, 16, 1024), high.reshape(16, 16, 1024)], axis=1
    ).reshape(512, 1024)

    pick_atoms, mean, order = tables(atom_counts[0], owner_rows[0], neighbor_ids)
    atoms = dot(pick_atoms, descriptors, NN).astype(BF16)
    grads = lax.dot_general(
        gradients.reshape(12, 128, 1024),
        pick_atoms[:64],
        (((1,), (1,)), ((), ())),
        preferred_element_type=F32,
    )
    grads = jnp.transpose(grads, (0, 2, 1)).astype(BF16).reshape(768, 1024)

    panel, gram = panel_rows(env_panel, atoms, grads, mean, order)
    panel = lax.all_to_all(panel, "row", 0, 0, tiled=True).reshape(512, 512)
    segment = lax.all_gather(panel, "col", axis=0, tiled=False)

    own = lax.dynamic_slice_in_dim(sparse_trail, row * 16, 16, 0)
    own = gather4(gather4(own, "col", z_shift, z), "col", x_shift, x)
    own = ring4(own, "row", y_shift, y)
    low, high = swap_gather(own, core)
    env_trail = jnp.stack(
        [low.reshape(4, 16, 16, 1024), high.reshape(4, 16, 16, 1024)], axis=1
    )
    env_trail = jnp.transpose(env_trail, (2, 0, 1, 3, 4)).reshape(2048, 1024)
    trail = trail_rows(env_trail, atoms, grads, mean, order).reshape(128, 64, 128)
    trail = lax.all_to_all(trail, ("row", "col"), 0, 0, tiled=True).reshape(8, 16, 64, 128)

    gram = sum_all(gram, core, y)
    factor, inverse = factor_panel(gram, rows_total)

    cross = sum_row(cross_part(segment, trail), core, y)
    coupling, result = residual(cross, inverse, segment, trail, rows_total)
    return factor, coupling, result


def solution(mesh):
    return jax.shard_map(
        per_device,
        mesh=mesh,
        in_specs=(
            P(("row", "col"), None),
            P(None, None, ("row", "col"), None),
            P("col", None),
            P("col", None),
            P(("row", "col"), None),
            P(("row", "col"), None),
            P(("row", "col"), None, None),
        ),
        out_specs=(P(), P("col", None), P("col", "row")),
        check_vma=False,
    )
```

time: 604 us -> 280 us (0.46); the launches traced: 593 us -> 279 us
  waiting for transfers between devices: 285 us -> 69 us
  other arithmetic: 145 us -> 22.3 us
  starting transfers between devices: 4.96 us -> 75.3 us
  Pallas kernels: 0 us -> 59.2 us
  matrix products: 58.4 us -> 2.75 us
  local copies, waits for them, and re-layouts: 61.6 us -> 21.2 us
  blocking collectives: 21.1 us -> 13.8 us
    psum x1 -> x0, waiting for transfers between devices: 153 us -> none  [reduce_products(): return lax.psum((gram_part, cross_part), ('row', 'col'))]
    another operation x19 -> x2, other arithmetic: 121 us -> 0.49 us  [the longest x1 0.39 us: per_device(): jnp.stack([low.reshape(4, 16, 16, 1024), high.reshape(4, 16, 16, 1024)],...]
    all_gather x2 -> x1, waiting for transfers between devices: 95.7 us -> 0.01 us  [per_device(): segment = lax.all_gather(panel, 'col', axis=0, tiled=False)]
    ppermute x0 -> x40, waiting for transfers between devices: none -> 69 us  [the longest x6 24.8 us: scatter4(): lax.ppermute(lax.dynamic_slice_in_dim(v, (index + s) % 4 * n, n, 0), axis...]
    ppermute x0 -> x40, starting transfers between devices: none -> 65.6 us  [the longest x18 26 us: gather4(): pieces = [v] + [lax.ppermute(v, axis, shift(s)) for s in (1, 2, 3)]]
    pallas_call x0 -> x5, Pallas kernels: none -> 59.2 us  [the longest x1 26.7 us: factor_panel(): pl.pallas_call(functools.partial(factor_kernel, float(rows_total)), out_s...]
    all_to_all x1, waiting for transfers between devices: 36.1 us -> 0.01 us  [per_device(): lax.all_to_all(trail, ('row', 'col'), 0, 0, tiled=True)]
    dot_general x6 -> x2, matrix products: 31.8 us -> 2.75 us  [the longest x1 2.17 us: dot(): lax.dot_general(a, b, dims, precision=precision, preferred_element_type=F32)]
  transfers between devices with their start and end apart: 4 -> 42, of which waited for: 4 -> 27; matrix products, arithmetic and copies ran while one was open for 2% -> 12% of each run, Pallas kernels for 0% -> 16%
where the time goes in v1:
time: 280 us; the launch traced here: 279 us
  starting transfers between devices  75.3 us (27%)
  waiting for transfers between devices  69 us (25%)
  Pallas kernels  59.2 us (21%)
  other arithmetic  22.3 us (8%)
  local copies, waits for them, and re-layouts  21.2 us (8%)
  between operations  15 us (5%)
  blocking collectives  13.8 us (5%)
    pallas_call x1, Pallas kernels, factor_panel(): pl.pallas_call(functools.partial(factor_kernel, float(rows_total)), out_s...  26.7 us
    ppermute x18, starting transfers between devices, gather4(): pieces = [v] + [lax.ppermute(v, axis, shift(s)) for s in (1, 2, 3)]  26 us
    ppermute x6, waiting for transfers between devices, scatter4(): lax.ppermute(lax.dynamic_slice_in_dim(v, (index + s) % 4 * n, n, 0), axis...  24.8 us
    ppermute x18, waiting for transfers between devices, gather4(): pieces = [v] + [lax.ppermute(v, axis, shift(s)) for s in (1, 2, 3)]  20.6 us
    ppermute x4, starting transfers between devices, swap_gather(): other = lax.ppermute(v, 'row', CORE_SWAP)  15.1 us
    pallas_call x1, Pallas kernels, residual(): pl.pallas_call(functools.partial(residual_kernel, float(rows_total)), out...  14.1 us
    all_to_all x1, blocking collectives, per_device(): panel = lax.all_to_all(panel, 'row', 0, 0, tiled=True).reshape(512, 512)  13.8 us
    unnamed x65, local copies, waits for them, and re-layouts  12.8 us
  transfers between devices with their start and end apart: 42, of which 27 were waited for; matrix products, arithmetic and copies ran while one was open for 12% of the time, Pallas kernels for 16%

profile of v1, /device:TPU:1, one launch (start us, length us, event | category | flops | bytes accessed | tf_op | source)
XLA Modules:
  0.0 278.7 jit_solution(684057860236477457)
XLA Ops:
  8.2 2.5 collective-permute-start
  10.6 3.3 %collective-permute-start.1 = (bf16[16,1024]{1,0:T(8,128)(2,1)S(1)}, bf16[16,1024]{1,0:T(8,128)(2,1)S(1)}, u32[]{:S(2)}, u32[]{:S(2)}) collective-permute-start(bf16[16,1024]{1,0:T(8,128)(2,1)S(1)} %constant_dynamic-slice_fusion.9), channel_id=1, source_target_pairs={{0,2},{1,3},{2,0},{3,1},{4,6},{5,7},{6,4},{7,5},{8,10},{9,11},{10,... | collective-permute-start | bytes 98312 | tf_op jit(solution)/shard_map/ppermute | solution.py:44
  25.4 2.5 collective-permute-start.4
  29.2 3.2 %collective-permute-done.4 = bf16[64,1024]{1,0:T(8,128)(2,1)S(1)} collective-permute-done((bf16[64,1024]{1,0:T(8,128)(2,1)S(1)}, bf16[64,1024]{1,0:T(8,128)(2,1)S(1)}, u32[]{:S(2)}, u32[]{:S(2)}) %collective-permute-start.4) | collective-permute-done | bytes 131104 | tf_op jit(solution)/shard_map/ppermute | solution.py:44
  33.1 2.4 collective-permute-start.6
  40.5 13.8 %all_to_all.10 = bf16[8,64,512]{2,1,0:T(8,128)(2,1)} all-to-all(bf16[8,64,512]{2,1,0:T(8,128)(2,1)S(1)} %get-tuple-element.11), channel_id=1, replica_groups=mesh['row'=8,'col'=16] {'row'}, dimensions={0} | all-to-all | bytes 1048576 | tf_op jit(solution)/shard_map/all_to_all | solution.py:372
  62.2 2.6 collective-permute-start.25
  67.6 7.9 %collective-permute-done.25 = bf16[64,1024]{1,0:T(8,128)(2,1)S(1)} collective-permute-done((bf16[64,1024]{1,0:T(8,128)(2,1)S(1)}, bf16[64,1024]{1,0:T(8,128)(2,1)S(1)}, u32[]{:S(2)}, u32[]{:S(2)}) %collective-permute-start.25) | collective-permute-done | bytes 131104 | tf_op jit(solution)/shard_map/ppermute | solution.py:44
  75.9 2.7 collective-permute-start.29
  78.5 8.2 %collective-permute-done.27 = bf16[256,1024]{1,0:T(8,128)(2,1)S(1)} collective-permute-done((bf16[256,1024]{1,0:T(8,128)(2,1)S(1)}, bf16[256,1024]{1,0:T(8,128)(2,1)S(1)}, u32[]{:S(2)}, u32[]{:S(2)}) %collective-permute-start.27) | collective-permute-done | bytes 524320 | tf_op jit(solution)/shard_map/ppermute | solution.py:50
  89.7 2.9 %collective-permute-start.30 = (bf16[128,1024]{1,0:T(8,128)(2,1)}, bf16[128,1024]{1,0:T(8,128)(2,1)}, u32[]{:S(2)}, u32[]{:S(2)}) collective-permute-start(bf16[128,1024]{1,0:T(8,128)(2,1)} %slice.14), channel_id=1, source_target_pairs={{0,96},{16,112},{32,0},{48,16},{64,32},{80,48},{96,64},{112,80},{1... | collective-permute-start | bytes 786440 | tf_op jit(solution)/shard_map/ppermute | solution.py:53
  92.7 2.6 collective-permute-done.28
  102.0 5.9 %collective-permute-start.31 = (bf16[1024,1024]{1,0:T(8,128)(2,1)}, bf16[1024,1024]{1,0:T(8,128)(2,1)}, u32[]{:S(2)}, u32[]{:S(2)}) collective-permute-start(bf16[1024,1024]{1,0:T(8,128)(2,1)} %pad_maximum_fusion.1), channel_id=1, source_target_pairs={{0,16},{16,0},{32,48},{48,32},{64,80},{80,64},{96,112},{112,96},{1... | collective-permute-start | bytes 6291464 | tf_op jit(solution)/shard_map/ppermute | solution.py:77
  112.0 2.7 broadcast_select_fusion.1
  116.6 6.8 %shard_map.96 = bf16[8,16,64,128]{3,2,1,0:T(8,128)(2,1)S(1)} custom-call(bf16[2048,1024]{1,0:T(8,128)(2,1)S(1)} %bitcast.43, bf16[320,1024]{1,0:T(8,128)(2,1)S(1)} %copy-done.7, bf16[768,1024]{1,0:T(8,128)(2,1)S(1)} %bitcast.46, f32[8,64]{1,0:T(8,128)S(1)} %convert_divide_fusion.mean_ref, bf16[512,256]{1,0:T(8,128)(2,1)S(1)} %fusion.order_ref), custom_call_target="tpu_custom_call" | custom-call | flops 4563402752 | bytes 9437184 | tf_op jit(solution)/shard_map/pallas_call | solution.py:169
  124.8 9.7 %all-to-all-start.1 = ((bf16[128,64,128]{2,1,0:T(8,128)(2,1)}), bf16[128,64,128]{2,1,0:T(8,128)(2,1)}, u32[]{:S(2)}, u32[]{:S(2)}) async-start(bf16[128,64,128]{2,1,0:T(8,128)(2,1)} %bitcast.44), calls=%async_computation.1 | async-start | bytes 4194304 | tf_op jit(solution)/shard_map/all_to_all | solution.py:384
  137.3 2.6 collective-permute-start.10
  141.7 19.2 %collective-permute-done.10 = f32[64,512]{1,0:T(8,128)S(1)} collective-permute-done((f32[64,512]{1,0:T(8,128)}, f32[64,512]{1,0:T(8,128)S(1)}, u32[]{:S(2)}, u32[]{:S(2)}) %collective-permute-start.10) | collective-permute-done | bytes 131104 | tf_op jit(solution)/shard_map/ppermute | solution.py:61
  161.9 3.3 %collective-permute-done.9 = f32[64,512]{1,0:T(8,128)} collective-permute-done((f32[64,512]{1,0:T(8,128)S(1)}, f32[64,512]{1,0:T(8,128)}, u32[]{:S(2)}, u32[]{:S(2)}) %collective-permute-start.9) | collective-permute-done | bytes 131104 | tf_op jit(solution)/shard_map/ppermute | solution.py:61
  167.8 2.9 %collective-permute-start.12 = (f32[64,512]{1,0:T(8,128)S(1)}, f32[64,512]{1,0:T(8,128)S(1)}, u32[]{:S(2)}, u32[]{:S(2)}) collective-permute-start(f32[64,512]{1,0:T(8,128)S(1)} %add_add_fusion.2), channel_id=1, source_target_pairs={{0,2},{1,3},{2,0},{3,1},{4,6},{5,7},{6,4},{7,5},{8,10},{9,11},{10,... | collective-permute-start | bytes 393224 | tf_op jit(solution)/shard_map/ppermute | solution.py:83
  172.5 3.7 %collective-permute-done.12 = f32[64,512]{1,0:T(8,128)S(1)} collective-permute-done((f32[64,512]{1,0:T(8,128)S(1)}, f32[64,512]{1,0:T(8,128)S(1)}, u32[]{:S(2)}, u32[]{:S(2)}) %collective-permute-start.12) | collective-permute-done | bytes 131104 | tf_op jit(solution)/shard_map/ppermute | solution.py:83
  178.0 2.4 collective-permute-start.15
  182.0 2.9 %collective-permute-done.15 = f32[64,512]{1,0:T(8,128)S(1)} collective-permute-done((f32[64,512]{1,0:T(8,128)S(1)}, f32[64,512]{1,0:T(8,128)S(1)}, u32[]{:S(2)}, u32[]{:S(2)}) %collective-permute-start.15) | collective-permute-done | bytes 131104 | tf_op jit(solution)/shard_map/ppermute | solution.py:83
  188.6 3.3 %collective-permute-done.17 = f32[64,512]{1,0:T(8,128)S(1)} collective-permute-done((f32[64,512]{1,0:T(8,128)S(1)}, f32[64,512]{1,0:T(8,128)S(1)}, u32[]{:S(2)}, u32[]{:S(2)}) %collective-permute-start.17) | collective-permute-done | bytes 131104 | tf_op jit(solution)/shard_map/ppermute | solution.py:44
  195.9 3.5 %collective-permute-start.20 = (f32[256,512]{1,0:T(8,128)}, f32[256,512]{1,0:T(8,128)}, u32[]{:S(2)}, u32[]{:S(2)}) collective-permute-start(f32[256,512]{1,0:T(8,128)} %pad_maximum_fusion.5), channel_id=1, source_target_pairs={{0,16},{16,0},{32,48},{48,32},{64,80},{80,64},{96,112},{112,96},{1... | collective-permute-start | bytes 1572872 | tf_op jit(solution)/shard_map/ppermute | solution.py:77
  199.4 3.4 %copy-done.1 = bf16[16,512,512]{2,1,0:T(8,128)(2,1)S(1)} copy-done((bf16[16,512,512]{2,1,0:T(8,128)(2,1)S(1)}, bf16[16,512,512]{2,1,0:T(8,128)(2,1)}, u32[]{:S(2)}) %copy-start.1) | copy-done | bytes 8388632
  202.8 9.8 %shard_map.97 = f32[128,512]{1,0:T(8,128)S(1)} custom-call(bf16[16,512,512]{2,1,0:T(8,128)(2,1)S(1)} %copy-done.1, bf16[8,16,64,128]{3,2,1,0:T(8,128)(2,1)} %bitcast.22.trail_ref), custom_call_target="tpu_custom_call" | custom-call | flops 1073741824 | bytes 11534336 | tf_op jit(solution)/shard_map/pallas_call | solution.py:270
  215.9 3.2 %collective-permute-start.34 = (f32[16,512]{1,0:T(8,128)S(1)}, f32[16,512]{1,0:T(8,128)S(1)}, u32[]{:S(2)}, u32[]{:S(2)}) collective-permute-start(f32[16,512]{1,0:T(8,128)S(1)} %get-tuple-element.51), channel_id=1, source_target_pairs={{0,64},{16,80},{32,96},{48,112},{64,0},{80,16},{96,32},{112,48},{1... | collective-permute-start | bytes 98312 | tf_op jit(solution)/shard_map/ppermute | solution.py:61
  222.4 2.3 collective-permute-start.37
  227.5 3.4 %collective-permute-start.39 = (f32[64,512]{1,0:T(8,128)S(1)}, f32[64,512]{1,0:T(8,128)S(1)}, u32[]{:S(2)}, u32[]{:S(2)}) collective-permute-start(f32[64,512]{1,0:T(8,128)S(1)} %pad_maximum_fusion.10), channel_id=1, source_target_pairs={{0,16},{16,0},{32,48},{48,32},{64,80},{80,64},{96,112},{112,96},{1... | collective-permute-start | bytes 393224 | tf_op jit(solution)/shard_map/ppermute | solution.py:77
  230.9 26.7 %shard_map.95 = (f32[512,512]{1,0:T(8,128)}, f32[512,512]{1,0:T(8,128)S(1)}) custom-call(f32[512,512]{1,0:T(8,128)S(1)} %pad_maximum_fusion.3.gram_ref), custom_call_target="tpu_custom_call" | custom-call | flops 2684354560 | bytes 4194304 | tf_op jit(solution)/shard_map/pallas_call | solution.py:248
  257.7 14.1 %shard_map.98 = (f32[128,512]{1,0:T(8,128)}, f32[128,8192]{1,0:T(8,128)}) custom-call(f32[128,512]{1,0:T(8,128)S(1)} %pad_maximum_fusion.7.cross_ref, f32[512,512]{1,0:T(8,128)S(1)} %get-tuple-element.12.inverse_ref, bf16[16,512,512]{2,1,0:T(8,128)(2,1)S(1)} %bitcast.42, bf16[8,16,64,128]{3,2,1,0:T(8,128)(2,1)} %bitcast.22.trail_ref), custom_call_target="tpu_custom_call" | custom-call | flops 2147483648 | bytes 16777216 | tf_op jit(solution)/shard_map/pallas_call | solution.py:310
  (189 shorter events, 77.5 us)
Async XLA Ops:
  7.2 192.2 %all-gather.2.cloned.1.call-start = ((), (), s32[]{:S(2)}) async-start(), calls=%async_computation.2 | async-start | bytes 8912896 | tf_op jit(solution)/shard_map/all_gather | solution.py:373
  8.2 15.1 %collective-permute-start = (bf16[16,1024]{1,0:T(8,128)(2,1)S(1)}, bf16[16,1024]{1,0:T(8,128)(2,1)S(1)}, u32[]{:S(2)}, u32[]{:S(2)}) collective-permute-start(bf16[16,1024]{1,0:T(8,128)(2,1)S(1)} %constant_dynamic-slice_fusion.9), channel_id=1, source_target_pairs={{0,1},{1,2},{2,3},{3,0},{4,5},{5,6},{6,7},{7,4},{8,9},{9,10},{10,1... | collective-permute-start | bytes 98312 | tf_op jit(solution)/shard_map/ppermute | solution.py:44
  10.6 12.6 %collective-permute-start.1 = (bf16[16,1024]{1,0:T(8,128)(2,1)S(1)}, bf16[16,1024]{1,0:T(8,128)(2,1)S(1)}, u32[]{:S(2)}, u32[]{:S(2)}) collective-permute-start(bf16[16,1024]{1,0:T(8,128)(2,1)S(1)} %constant_dynamic-slice_fusion.9), channel_id=1, source_target_pairs={{0,2},{1,3},{2,0},{3,1},{4,6},{5,7},{6,4},{7,5},{8,10},{9,11},{10,... | collective-permute-start | bytes 98312 | tf_op jit(solution)/shard_map/ppermute | solution.py:44
  13.9 9.3 %collective-permute-start.2 = (bf16[16,1024]{1,0:T(8,128)(2,1)S(1)}, bf16[16,1024]{1,0:T(8,128)(2,1)S(1)}, u32[]{:S(2)}, u32[]{:S(2)}) collective-permute-start(bf16[16,1024]{1,0:T(8,128)(2,1)S(1)} %constant_dynamic-slice_fusion.9), channel_id=1, source_target_pairs={{0,3},{1,0},{2,1},{3,2},{4,7},{5,4},{6,5},{7,6},{8,11},{9,8},{10,9... | collective-permute-start | bytes 98312 | tf_op jit(solution)/shard_map/ppermute | solution.py:44
  24.1 5.1 %collective-permute-start.3 = (bf16[64,1024]{1,0:T(8,128)(2,1)S(1)}, bf16[64,1024]{1,0:T(8,128)(2,1)S(1)}, u32[]{:S(2)}, u32[]{:S(2)}) collective-permute-start(bf16[64,1024]{1,0:T(8,128)(2,1)S(1)} %pad_maximum_fusion.8), channel_id=1, source_target_pairs={{0,4},{1,5},{2,6},{3,7},{4,8},{5,9},{6,10},{7,11},{8,12},{9,13},{1... | collective-permute-start | bytes 393224 | tf_op jit(solution)/shard_map/ppermute | solution.py:44
  25.4 7.0 %collective-permute-start.4 = (bf16[64,1024]{1,0:T(8,128)(2,1)S(1)}, bf16[64,1024]{1,0:T(8,128)(2,1)S(1)}, u32[]{:S(2)}, u32[]{:S(2)}) collective-permute-start(bf16[64,1024]{1,0:T(8,128)(2,1)S(1)} %pad_maximum_fusion.8), channel_id=1, source_target_pairs={{0,8},{1,9},{2,10},{3,11},{4,12},{5,13},{6,14},{7,15},{8,0},{9,1},... | collective-permute-start | bytes 393224 | tf_op jit(solution)/shard_map/ppermute | solution.py:44
  27.8 5.0 %collective-permute-start.5 = (bf16[64,1024]{1,0:T(8,128)(2,1)S(1)}, bf16[64,1024]{1,0:T(8,128)(2,1)S(1)}, u32[]{:S(2)}, u32[]{:S(2)}) collective-permute-start(bf16[64,1024]{1,0:T(8,128)(2,1)S(1)} %pad_maximum_fusion.8), channel_id=1, source_target_pairs={{0,12},{1,13},{2,14},{3,15},{4,0},{5,1},{6,2},{7,3},{8,4},{9,5},{1... | collective-permute-start | bytes 393224 | tf_op jit(solution)/shard_map/ppermute | solution.py:44
  61.2 6.4 %collective-permute-start.24 = (bf16[64,1024]{1,0:T(8,128)(2,1)S(1)}, bf16[64,1024]{1,0:T(8,128)(2,1)S(1)}, u32[]{:S(2)}, u32[]{:S(2)}) collective-permute-start(bf16[64,1024]{1,0:T(8,128)(2,1)S(1)} %pad_maximum_fusion.9), channel_id=1, source_target_pairs={{0,4},{1,5},{2,6},{3,7},{4,8},{5,9},{6,10},{7,11},{8,12},{9,13},{1... | collective-permute-start | bytes 393224 | tf_op jit(solution)/shard_map/ppermute | solution.py:44
  62.2 13.3 %collective-permute-start.25 = (bf16[64,1024]{1,0:T(8,128)(2,1)S(1)}, bf16[64,1024]{1,0:T(8,128)(2,1)S(1)}, u32[]{:S(2)}, u32[]{:S(2)}) collective-permute-start(bf16[64,1024]{1,0:T(8,128)(2,1)S(1)} %pad_maximum_fusion.9), channel_id=1, source_target_pairs={{0,8},{1,9},{2,10},{3,11},{4,12},{5,13},{6,14},{7,15},{8,0},{9,1},... | collective-permute-start | bytes 393224 | tf_op jit(solution)/shard_map/ppermute | solution.py:44
  64.8 10.7 %collective-permute-start.26 = (bf16[64,1024]{1,0:T(8,128)(2,1)S(1)}, bf16[64,1024]{1,0:T(8,128)(2,1)S(1)}, u32[]{:S(2)}, u32[]{:S(2)}) collective-permute-start(bf16[64,1024]{1,0:T(8,128)(2,1)S(1)} %pad_maximum_fusion.9), channel_id=1, source_target_pairs={{0,12},{1,13},{2,14},{3,15},{4,0},{5,1},{6,2},{7,3},{8,4},{9,5},{1... | collective-permute-start | bytes 393224 | tf_op jit(solution)/shard_map/ppermute | solution.py:44
  75.8 10.9 %collective-permute-start.27 = (bf16[256,1024]{1,0:T(8,128)(2,1)S(1)}, bf16[256,1024]{1,0:T(8,128)(2,1)S(1)}, u32[]{:S(2)}, u32[]{:S(2)}) collective-permute-start(bf16[256,1024]{1,0:T(8,128)(2,1)S(1)} %pad_maximum_fusion.6), channel_id=1, source_target_pairs={{0,32},{16,48},{32,64},{48,80},{64,96},{80,112},{96,0},{112,16},{1... | collective-permute-start | bytes 1572872 | tf_op jit(solution)/shard_map/ppermute | solution.py:50
  75.9 12.4 %collective-permute-start.29 = (bf16[256,1024]{1,0:T(8,128)(2,1)S(1)}, bf16[256,1024]{1,0:T(8,128)(2,1)S(1)}, u32[]{:S(2)}, u32[]{:S(2)}) collective-permute-start(bf16[256,1024]{1,0:T(8,128)(2,1)S(1)} %pad_maximum_fusion.6), channel_id=1, source_target_pairs={{0,96},{16,112},{32,0},{48,16},{64,32},{80,48},{96,64},{112,80},{1... | collective-permute-start | bytes 1572872 | tf_op jit(solution)/shard_map/ppermute | solution.py:51
  88.2 7.0 %collective-permute-start.28 = (bf16[128,1024]{1,0:T(8,128)(2,1)}, bf16[128,1024]{1,0:T(8,128)(2,1)}, u32[]{:S(2)}, u32[]{:S(2)}) collective-permute-start(bf16[128,1024]{1,0:T(8,128)(2,1)} %slice.13), channel_id=1, source_target_pairs={{0,32},{16,48},{32,64},{48,80},{64,96},{80,112},{96,0},{112,16},{1... | collective-permute-start | bytes 786440 | tf_op jit(solution)/shard_map/ppermute | solution.py:52
  89.7 6.6 %collective-permute-start.30 = (bf16[128,1024]{1,0:T(8,128)(2,1)}, bf16[128,1024]{1,0:T(8,128)(2,1)}, u32[]{:S(2)}, u32[]{:S(2)}) collective-permute-start(bf16[128,1024]{1,0:T(8,128)(2,1)} %slice.14), channel_id=1, source_target_pairs={{0,96},{16,112},{32,0},{48,16},{64,32},{80,48},{96,64},{112,80},{1... | collective-permute-start | bytes 786440 | tf_op jit(solution)/shard_map/ppermute | solution.py:53
  102.0 10.0 %collective-permute-start.31 = (bf16[1024,1024]{1,0:T(8,128)(2,1)}, bf16[1024,1024]{1,0:T(8,128)(2,1)}, u32[]{:S(2)}, u32[]{:S(2)}) collective-permute-start(bf16[1024,1024]{1,0:T(8,128)(2,1)} %pad_maximum_fusion.1), channel_id=1, source_target_pairs={{0,16},{16,0},{32,48},{48,32},{64,80},{80,64},{96,112},{112,96},{1... | collective-permute-start | bytes 6291464 | tf_op jit(solution)/shard_map/ppermute | solution.py:77
  109.8 24.8 %collective-permute-start.7 = (f32[256,512]{1,0:T(8,128)}, f32[256,512]{1,0:T(8,128)}, u32[]{:S(2)}, u32[]{:S(2)}) collective-permute-start(f32[256,512]{1,0:T(8,128)} %constant_dynamic-slice_fusion.8), channel_id=1, source_target_pairs={{0,16},{16,0},{32,48},{48,32},{64,80},{80,64},{96,112},{112,96},{1... | collective-permute-start | bytes 1572872 | tf_op jit(solution)/shard_map/ppermute | solution.py:73
  124.8 74.6 %all-to-all-start.1 = ((bf16[128,64,128]{2,1,0:T(8,128)(2,1)}), bf16[128,64,128]{2,1,0:T(8,128)(2,1)}, u32[]{:S(2)}, u32[]{:S(2)}) async-start(bf16[128,64,128]{2,1,0:T(8,128)(2,1)} %bitcast.44), calls=%async_computation.1 | async-start | bytes 4194304 | tf_op jit(solution)/shard_map/all_to_all | solution.py:384
  137.3 23.6 %collective-permute-start.10 = (f32[64,512]{1,0:T(8,128)}, f32[64,512]{1,0:T(8,128)S(1)}, u32[]{:S(2)}, u32[]{:S(2)}) collective-permute-start(f32[64,512]{1,0:T(8,128)} %get-tuple-element.37), channel_id=1, source_target_pairs={{0,96},{16,112},{32,0},{48,16},{64,32},{80,48},{96,64},{112,80},{1... | collective-permute-start | bytes 393224 | tf_op jit(solution)/shard_map/ppermute | solution.py:61
  140.0 21.9 %collective-permute-start.8 = (f32[64,512]{1,0:T(8,128)S(1)}, f32[64,512]{1,0:T(8,128)}, u32[]{:S(2)}, u32[]{:S(2)}) collective-permute-start(f32[64,512]{1,0:T(8,128)S(1)} %get-tuple-element.36), channel_id=1, source_target_pairs={{0,32},{16,48},{32,64},{48,80},{64,96},{80,112},{96,0},{112,16},{1... | collective-permute-start | bytes 393224 | tf_op jit(solution)/shard_map/ppermute | solution.py:61
  140.0 25.2 %collective-permute-start.9 = (f32[64,512]{1,0:T(8,128)S(1)}, f32[64,512]{1,0:T(8,128)}, u32[]{:S(2)}, u32[]{:S(2)}) collective-permute-start(f32[64,512]{1,0:T(8,128)S(1)} %get-tuple-element.38), channel_id=1, source_target_pairs={{0,64},{16,80},{32,96},{48,112},{64,0},{80,16},{96,32},{112,48},{1... | collective-permute-start | bytes 393224 | tf_op jit(solution)/shard_map/ppermute | solution.py:61
  166.3 6.3 %collective-permute-start.11 = (f32[64,512]{1,0:T(8,128)S(1)}, f32[64,512]{1,0:T(8,128)S(1)}, u32[]{:S(2)}, u32[]{:S(2)}) collective-permute-start(f32[64,512]{1,0:T(8,128)S(1)} %add_add_fusion.2), channel_id=1, source_target_pairs={{0,1},{1,2},{2,3},{3,0},{4,5},{5,6},{6,7},{7,4},{8,9},{9,10},{10,1... | collective-permute-start | bytes 393224 | tf_op jit(solution)/shard_map/ppermute | solution.py:83
  167.8 8.4 %collective-permute-start.12 = (f32[64,512]{1,0:T(8,128)S(1)}, f32[64,512]{1,0:T(8,128)S(1)}, u32[]{:S(2)}, u32[]{:S(2)}) collective-permute-start(f32[64,512]{1,0:T(8,128)S(1)} %add_add_fusion.2), channel_id=1, source_target_pairs={{0,2},{1,3},{2,0},{3,1},{4,6},{5,7},{6,4},{7,5},{8,10},{9,11},{10,... | collective-permute-start | bytes 393224 | tf_op jit(solution)/shard_map/ppermute | solution.py:83
  170.7 5.5 %collective-permute-start.13 = (f32[64,512]{1,0:T(8,128)S(1)}, f32[64,512]{1,0:T(8,128)S(1)}, u32[]{:S(2)}, u32[]{:S(2)}) collective-permute-start(f32[64,512]{1,0:T(8,128)S(1)} %add_add_fusion.2), channel_id=1, source_target_pairs={{0,3},{1,0},{2,1},{3,2},{4,7},{5,4},{6,5},{7,6},{8,11},{9,8},{10,9... | collective-permute-start | bytes 393224 | tf_op jit(solution)/shard_map/ppermute | solution.py:83
  176.3 5.7 %collective-permute-start.14 = (f32[64,512]{1,0:T(8,128)S(1)}, f32[64,512]{1,0:T(8,128)S(1)}, u32[]{:S(2)}, u32[]{:S(2)}) collective-permute-start(f32[64,512]{1,0:T(8,128)S(1)} %add_add_fusion.1), channel_id=1, source_target_pairs={{0,4},{1,5},{2,6},{3,7},{4,8},{5,9},{6,10},{7,11},{8,12},{9,13},{1... | collective-permute-start | bytes 393224 | tf_op jit(solution)/shard_map/ppermute | solution.py:83
  178.0 6.9 %collective-permute-start.15 = (f32[64,512]{1,0:T(8,128)S(1)}, f32[64,512]{1,0:T(8,128)S(1)}, u32[]{:S(2)}, u32[]{:S(2)}) collective-permute-start(f32[64,512]{1,0:T(8,128)S(1)} %add_add_fusion.1), channel_id=1, source_target_pairs={{0,8},{1,9},{2,10},{3,11},{4,12},{5,13},{6,14},{7,15},{8,0},{9,1},... | collective-permute-start | bytes 393224 | tf_op jit(solution)/shard_map/ppermute | solution.py:83
  180.4 5.0 %collective-permute-start.16 = (f32[64,512]{1,0:T(8,128)S(1)}, f32[64,512]{1,0:T(8,128)S(1)}, u32[]{:S(2)}, u32[]{:S(2)}) collective-permute-start(f32[64,512]{1,0:T(8,128)S(1)} %add_add_fusion.1), channel_id=1, source_target_pairs={{0,12},{1,13},{2,14},{3,15},{4,0},{5,1},{6,2},{7,3},{8,4},{9,5},{1... | collective-permute-start | bytes 393224 | tf_op jit(solution)/shard_map/ppermute | solution.py:83
  185.4 6.5 %collective-permute-start.17 = (f32[64,512]{1,0:T(8,128)S(1)}, f32[64,512]{1,0:T(8,128)S(1)}, u32[]{:S(2)}, u32[]{:S(2)}) collective-permute-start(f32[64,512]{1,0:T(8,128)S(1)} %add_add_fusion), channel_id=1, source_target_pairs={{0,32},{16,48},{32,64},{48,80},{64,96},{80,112},{96,0},{112,16},{1... | collective-permute-start | bytes 393224 | tf_op jit(solution)/shard_map/ppermute | solution.py:44
  186.1 5.8 %collective-permute-start.18 = (f32[64,512]{1,0:T(8,128)S(1)}, f32[64,512]{1,0:T(8,128)S(1)}, u32[]{:S(2)}, u32[]{:S(2)}) collective-permute-start(f32[64,512]{1,0:T(8,128)S(1)} %add_add_fusion), channel_id=1, source_target_pairs={{0,64},{16,80},{32,96},{48,112},{64,0},{80,16},{96,32},{112,48},{1... | collective-permute-start | bytes 393224 | tf_op jit(solution)/shard_map/ppermute | solution.py:44
  187.7 5.5 %collective-permute-start.19 = (f32[64,512]{1,0:T(8,128)S(1)}, f32[64,512]{1,0:T(8,128)}, u32[]{:S(2)}, u32[]{:S(2)}) collective-permute-start(f32[64,512]{1,0:T(8,128)S(1)} %add_add_fusion), channel_id=1, source_target_pairs={{0,96},{16,112},{32,0},{48,16},{64,32},{80,48},{96,64},{112,80},{1... | collective-permute-start | bytes 393224 | tf_op jit(solution)/shard_map/ppermute | solution.py:44
  195.9 23.3 %collective-permute-start.20 = (f32[256,512]{1,0:T(8,128)}, f32[256,512]{1,0:T(8,128)}, u32[]{:S(2)}, u32[]{:S(2)}) collective-permute-start(f32[256,512]{1,0:T(8,128)} %pad_maximum_fusion.5), channel_id=1, source_target_pairs={{0,16},{16,0},{32,48},{48,32},{64,80},{80,64},{96,112},{112,96},{1... | collective-permute-start | bytes 1572872 | tf_op jit(solution)/shard_map/ppermute | solution.py:77
  215.9 5.0 %collective-permute-start.34 = (f32[16,512]{1,0:T(8,128)S(1)}, f32[16,512]{1,0:T(8,128)S(1)}, u32[]{:S(2)}, u32[]{:S(2)}) collective-permute-start(f32[16,512]{1,0:T(8,128)S(1)} %get-tuple-element.51), channel_id=1, source_target_pairs={{0,64},{16,80},{32,96},{48,112},{64,0},{80,16},{96,32},{112,48},{1... | collective-permute-start | bytes 98312 | tf_op jit(solution)/shard_map/ppermute | solution.py:61
  227.5 30.1 %collective-permute-start.39 = (f32[64,512]{1,0:T(8,128)S(1)}, f32[64,512]{1,0:T(8,128)S(1)}, u32[]{:S(2)}, u32[]{:S(2)}) collective-permute-start(f32[64,512]{1,0:T(8,128)S(1)} %pad_maximum_fusion.10), channel_id=1, source_target_pairs={{0,16},{16,0},{32,48},{48,32},{64,80},{80,64},{96,112},{112,96},{1... | collective-permute-start | bytes 393224 | tf_op jit(solution)/shard_map/ppermute | solution.py:77
  (42 other events, 263.7 us)
Sparse Core Ops, SparseCore 0:
  54.5 70.2 all-gather.1

commit v2 on v1

--- a/solution.py
+++ b/solution.py
@@ -84,32 +84,87 @@
     return v + got[0] + got[1] + got[2]
 
 
-def tables(count, owner, neighbors):
-    structs = jnp.arange(8, dtype=jnp.int32)
-    offset = jnp.sum(jnp.where(structs[None, :] < structs[:, None], count[None, :], 0), axis=1)
-    atoms = jnp.arange(64, dtype=jnp.int32)
-    inside = (atoms[:, None] >= offset[None, :]) & (
-        atoms[:, None] < (offset + count)[None, :]
-    )
-    slot = jnp.sum(jnp.where(inside, 16 * structs + atoms[:, None] - offset, 0), axis=1)
-    slots = jnp.arange(128, dtype=jnp.int32)
-    live = slot[:, None] == slots[None, :]
-    partner = (16 * structs[:, None, None] + neighbors % count[:, None, None]).reshape(128, 4)
-    picked = jnp.sum(jnp.where(live[:, :, None], partner[None], 0), axis=1)
-    rows = jnp.concatenate([slot, picked.T.reshape(256)])
-    pick_atoms = (rows[:, None] == slots[None, :]).astype(BF16)
-    mean = (inside.astype(F32) / count.astype(F32)[None, :]).T
-    of_group = owner[None, :] == structs[:, None]
-    struct_g = jnp.sum(jnp.where(of_group, structs[None, :], 0), axis=1)
-    count_g = jnp.sum(jnp.where(of_group, count[None, :], 0), axis=1)
-    offset_g = jnp.sum(jnp.where(of_group, offset[None, :], 0), axis=1)
-    place = jnp.arange(64, dtype=jnp.int32)[None, :]
-    atom, part = (place - 1) // 3, (place - 1) % 3
-    is_force = (place >= 1) & (atom < count_g[:, None])
-    column = jnp.where(is_force, part * 64 + offset_g[:, None] + atom, -1)
-    column = jnp.where(place == 0, 192 + struct_g[:, None], column).reshape(512)
-    order = (column[:, None] == jnp.arange(256, dtype=jnp.int32)[None, :]).astype(BF16)
-    return pick_atoms, mean, order
+def prep_kernel(
+    count_ref, owner_ref, neighbor_ref, desc_ref, grad_ref, atoms_ref, grads_ref, mean_ref, order_ref
+):
+    counts = [count_ref[0, s] for s in range(8)]
+    owners = [owner_ref[0, s] for s in range(8)]
+    offsets = [jnp.int32(0)]
+    for s in range(7):
+        offsets.append(offsets[s] + counts[s])
+
+    lane = lax.broadcasted_iota(jnp.int32, (8, 128), 1)
+    struct, atom = lane >> 4, lane & 15
+    count_l, offset_l = jnp.ones((8, 128), jnp.int32), jnp.zeros((8, 128), jnp.int32)
+    for s in range(8):
+        count_l = jnp.where(struct == s, counts[s], count_l)
+        offset_l = jnp.where(struct == s, offsets[s], offset_l)
+    place = jnp.where(atom < count_l, offset_l + atom, -1)
+    rows = lax.broadcasted_iota(jnp.int32, (64, 128), 0)
+    lanes = lax.broadcasted_iota(jnp.int32, (64, 128), 1)
+    live = place[:1] == rows
+    live_f = live.astype(F32)
+
+    value = neighbor_ref[...].astype(F32)
+    size = count_l.astype(F32)[:4]
+    rest = value - size * jnp.floor(value / size)
+    rest = jnp.where(rest < 0.0, rest + size, rest)
+    rest = jnp.where(rest >= size, rest - size, rest)
+    partner = rest + (16 * struct).astype(F32)[:4]
+
+    picks = [live_f.astype(BF16)]
+    for j in range(4):
+        slot = jnp.sum(live_f * partner[j : j + 1], axis=1, keepdims=True)
+        picks.append((slot == lanes.astype(F32)).astype(F32).astype(BF16))
+    desc = desc_ref[...]
+    for j in range(5):
+        atoms_ref[64 * j : 64 * j + 64] = dot(picks[j], desc, NN).astype(BF16)
+    for i in range(12):
+        grads_ref[64 * i : 64 * i + 64] = dot(picks[0], grad_ref[i], NN).astype(BF16)
+
+    sub8 = lax.broadcasted_iota(jnp.int32, (8, 64), 0)
+    atom8 = lax.broadcasted_iota(jnp.int32, (8, 64), 1)
+    low, size8 = jnp.zeros((8, 64), jnp.int32), jnp.ones((8, 64), jnp.int32)
+    for s in range(8):
+        low = jnp.where(sub8 == s, offsets[s], low)
+        size8 = jnp.where(sub8 == s, counts[s], size8)
+    inside = (atom8 >= low) & (atom8 < low + size8)
+    mean_ref[...] = jnp.where(inside, 1.0 / size8.astype(F32), 0.0)
+
+    r = lax.broadcasted_iota(jnp.int32, (64, 256), 0)
+    wanted = lax.broadcasted_iota(jnp.int32, (64, 256), 1)
+    third = ((r - 1) * 43) >> 7
+    part = (r - 1) - 3 * third
+    for g in range(8):
+        struct_g, count_g, offset_g = jnp.int32(0), jnp.int32(0), jnp.int32(0)
+        for s in range(8):
+            mine = owners[s] == g
+            struct_g = jnp.where(mine, s, struct_g)
+            count_g = jnp.where(mine, counts[s], count_g)
+            offset_g = jnp.where(mine, offsets[s], offset_g)
+        column = jnp.where(third < count_g, part * 64 + offset_g + third, -1)
+        column = jnp.where(r == 0, 192 + struct_g, column)
+        order_ref[64 * g : 64 * g + 64] = (column == wanted).astype(F32).astype(BF16)
+
+
+def prepare(count, owner, neighbors, descriptors, gradients):
+    smem = pl.BlockSpec(memory_space=pltpu.SMEM)
+    vmem = pl.BlockSpec(memory_space=pltpu.VMEM)
+    return pl.pallas_call(
+        prep_kernel,
+        out_shape=(
+            jax.ShapeDtypeStruct((320, 1024), BF16),
+            jax.ShapeDtypeStruct((768, 1024), BF16),
+            jax.ShapeDtypeStruct((8, 64), F32),
+            jax.ShapeDtypeStruct((512, 256), BF16),
+        ),
+        in_specs=[smem, smem, vmem, vmem, vmem],
+        out_specs=(vmem, vmem, vmem, vmem),
+        compiler_params=params(),
+        cost_estimate=pl.CostEstimate(
+            flops=2 * 64 * 128 * 1024 * 17, bytes_accessed=6 << 20, transcendentals=0
+        ),
+    )(count, owner, neighbors, descriptors, gradients)
 
 
 def compact_rows(env, atoms, grads, mean):
@@ -136,8 +191,14 @@
     gram_ref[...] = dot(rows, rows, TN)
 
 
-def trail_kernel(env_ref, atoms_ref, grads_ref, mean_ref, order_ref, out_ref):
-    rows = compact_rows(env_ref[...], atoms_ref[...], grads_ref[...], mean_ref[...])
+def trail_kernel(
+    core_ref, own_ref, other_ref, atoms_ref, grads_ref, mean_ref, order_ref, out_ref
+):
+    first = core_ref[0] == 0
+    own, other = own_ref[...], other_ref[...]
+    low, high = jnp.where(first, own, other), jnp.where(first, other, own)
+    env = jnp.concatenate([low, high], axis=1).reshape(-1, 1024)
+    rows = compact_rows(env, atoms_ref[...], grads_ref[...], mean_ref[...])
     full = dot(order_ref[...], rows, NN).astype(BF16)
     for c in range(out_ref.shape[1]):
         out_ref[:, c] = full[:, c * 128 : c * 128 + 128].reshape(8, 64, 128)
@@ -162,27 +223,32 @@
     )(env, atoms, grads, mean, order)
 
 
-def trail_rows(env, atoms, grads, mean, order):
-    m = env.shape[0]
-    tile = 512
-    whole = lambda shape: pl.BlockSpec(shape, lambda i: (0, 0))
+def trail_rows(core, own, other, atoms, grads, mean, order):
+    blocks = own.shape[0]
+    step = 4
+    half = pl.BlockSpec((step, 64, 1024), lambda i, core: (i, 0, 0))
+    whole = lambda shape: pl.BlockSpec(shape, lambda i, core: (0, 0))
     return pl.pallas_call(
         trail_kernel,
-        out_shape=jax.ShapeDtypeStruct((8, m // 128, 64, 128), BF16),
-        grid=(m // tile,),
-        in_specs=[
-            pl.BlockSpec((tile, 1024), lambda i: (i, 0)),
-            whole(atoms.shape),
-            whole(grads.shape),
-            whole(mean.shape),
-            whole(order.shape),
-        ],
-        out_specs=pl.BlockSpec((8, tile // 128, 64, 128), lambda i: (0, i, 0, 0)),
-        compiler_params=params(),
-        cost_estimate=pl.CostEstimate(
-            flops=2 * m * 1024 * 1088, bytes_accessed=9 << 20, transcendentals=0
-        ),
-    )(env, atoms, grads, mean, order)
+        out_shape=jax.ShapeDtypeStruct((8, blocks, 64, 128), BF16),
+        grid_spec=pltpu.PrefetchScalarGridSpec(
+            num_scalar_prefetch=1,
+            grid=(blocks // step,),
+            in_specs=[
+                half,
+                half,
+                whole(atoms.shape),
+                whole(grads.shape),
+                whole(mean.shape),
+                whole(order.shape),
+            ],
+            out_specs=pl.BlockSpec((8, step, 64, 128), lambda i, core: (0, i, 0, 0)),
+        ),
+        compiler_params=params(),
+        cost_estimate=pl.CostEstimate(
+            flops=2 * 2048 * 1024 * 1088, bytes_accessed=9 << 20, transcendentals=0
+        ),
+    )(core.reshape(1).astype(jnp.int32), own, other, atoms, grads, mean, order)
 
 
 def eliminate(a):
@@ -261,8 +327,11 @@
     def _():
         out_ref[...] = jnp.zeros_like(out_ref)
 
-    trail = trail_ref[...].reshape(512, 128)
-    out_ref[...] += dot(trail, panel_ref[0], TN)
+    n = panel_ref.shape[2]
+    trail = jnp.concatenate(
+        [trail_ref[:, i].reshape(512, 128) for i in range(panel_ref.shape[0])], axis=0
+    )
+    out_ref[...] += dot(trail, panel_ref[...].reshape(-1, n), TN)
 
 
 def cross_part(segment, trail):
@@ -270,10 +339,10 @@
     return pl.pallas_call(
         cross_kernel,
         out_shape=jax.ShapeDtypeStruct((128, n), F32),
-        grid=(segment.shape[0],),
+        grid=(segment.shape[0] // 4,),
         in_specs=[
-            pl.BlockSpec((1, 512, n), lambda i: (i, 0, 0)),
-            pl.BlockSpec((8, 1, 64, 128), lambda i: (0, i, 0, 0)),
+            pl.BlockSpec((4, 512, n), lambda i: (i, 0, 0)),
+            pl.BlockSpec((8, 4, 64, 128), lambda i: (0, i, 0, 0)),
         ],
         out_specs=pl.BlockSpec((128, n), lambda i: (0, 0)),
         compiler_params=params(),
@@ -298,9 +367,10 @@
     r = lax.broadcasted_iota(jnp.int32, (128, 128), 0)
     c = lax.broadcasted_iota(jnp.int32, (128, 128), 1)
     same = (r == c).astype(BF16)
-    both = dot(weights[...], panel_ref[0], NT)
-    own = dot(same, trail_ref[...].reshape(512, 128), NT)
-    out_ref[...] = own - both[:128] - both[128:]
+    for i in range(panel_ref.shape[0]):
+        both = dot(weights[...], panel_ref[i], NT)
+        own = dot(same, trail_ref[:, i].reshape(512, 128), NT)
+        out_ref[:, i * 512 : i * 512 + 512] = own - both[:128] - both[128:]
 
 
 def residual(cross, inverse, segment, trail, rows_total):
@@ -313,14 +383,14 @@
             jax.ShapeDtypeStruct((128, n), F32),
             jax.ShapeDtypeStruct((128, 512 * chunks), F32),
         ),
-        grid=(chunks,),
+        grid=(chunks // 4,),
         in_specs=[
             whole((128, n)),
             whole((n, n)),
-            pl.BlockSpec((1, 512, n), lambda i: (i, 0, 0)),
-            pl.BlockSpec((8, 1, 64, 128), lambda i: (0, i, 0, 0)),
+            pl.BlockSpec((4, 512, n), lambda i: (i, 0, 0)),
+            pl.BlockSpec((8, 4, 64, 128), lambda i: (0, i, 0, 0)),
         ],
-        out_specs=(whole((128, n)), pl.BlockSpec((128, 512), lambda i: (0, i))),
+        out_specs=(whole((128, n)), pl.BlockSpec((128, 2048), lambda i: (0, i))),
         scratch_shapes=[pltpu.VMEM((256, n), BF16)],
         compiler_params=params(),
         cost_estimate=pl.CostEstimate(
@@ -336,9 +406,8 @@
     return jnp.concatenate(swap_gather(v, core), axis=0)
 
 
-def sum_row(v, core, y):
-    v = scatter4(swap_add(v, core), "row", y_shift, y)
-    v = gather4(v, "row", y_shift, y)
+def sum_row(v, core):
+    v = spread4(swap_add(v, core), "row", y_shift)
     return jnp.concatenate(swap_gather(v, core), axis=0)
 
 
@@ -351,6 +420,8 @@
     x, z = col // 4, col % 4
     rows_total = 65536
 
+    trail_half = lax.dynamic_slice_in_dim(sparse_trail, core * 64, 64, 0)
+    trail_half = lax.all_gather(trail_half, "col", axis=0, tiled=False)
     own = lax.dynamic_slice_in_dim(sparse_panel, core * 16, 16, 0)
     own = gather4(gather4(own, "col", z_shift, z), "col", x_shift, x)
     low, high = swap_gather(own, core)
@@ -358,35 +429,31 @@
         [low.reshape(16, 16, 1024), high.reshape(16, 16, 1024)], axis=1
     ).reshape(512, 1024)
 
-    pick_atoms, mean, order = tables(atom_counts[0], owner_rows[0], neighbor_ids)
-    atoms = dot(pick_atoms, descriptors, NN).astype(BF16)
-    grads = lax.dot_general(
+    atoms, grads, mean, order = prepare(
+        atom_counts,
+        owner_rows,
+        neighbor_ids.reshape(128, 4).T,
+        descriptors,
         gradients.reshape(12, 128, 1024),
-        pick_atoms[:64],
-        (((1,), (1,)), ((), ())),
-        preferred_element_type=F32,
     )
-    grads = jnp.transpose(grads, (0, 2, 1)).astype(BF16).reshape(768, 1024)
 
     panel, gram = panel_rows(env_panel, atoms, grads, mean, order)
     panel = lax.all_to_all(panel, "row", 0, 0, tiled=True).reshape(512, 512)
+    panel, gram = lax.optimization_barrier((panel, gram))
     segment = lax.all_gather(panel, "col", axis=0, tiled=False)
-
-    own = lax.dynamic_slice_in_dim(sparse_trail, row * 16, 16, 0)
-    own = gather4(gather4(own, "col", z_shift, z), "col", x_shift, x)
-    own = ring4(own, "row", y_shift, y)
-    low, high = swap_gather(own, core)
-    env_trail = jnp.stack(
-        [low.reshape(4, 16, 16, 1024), high.reshape(4, 16, 16, 1024)], axis=1
-    )
-    env_trail = jnp.transpose(env_trail, (2, 0, 1, 3, 4)).reshape(2048, 1024)
-    trail = trail_rows(env_trail, atoms, grads, mean, order).reshape(128, 64, 128)
-    trail = lax.all_to_all(trail, ("row", "col"), 0, 0, tiled=True).reshape(8, 16, 64, 128)
-
     gram = sum_all(gram, core, y)
+
+    trail_half, gram = lax.optimization_barrier((trail_half, gram))
+    other_half = lax.ppermute(trail_half, "row", CORE_SWAP)
+    trail = trail_rows(core, trail_half, other_half, atoms, grads, mean, order)
+    trail, gram = lax.optimization_barrier((trail, gram))
+    trail = lax.all_to_all(
+        trail.reshape(128, 64, 128), ("row", "col"), 0, 0, tiled=True
+    ).reshape(8, 16, 64, 128)
     factor, inverse = factor_panel(gram, rows_total)
 
-    cross = sum_row(cross_part(segment, trail), core, y)
+    segment, inverse = lax.optimization_barrier((segment, inverse))
+    cross = sum_row(cross_part(segment, trail), core)
     coupling, result = residual(cross, inverse, segment, trail, rows_total)
     return factor, coupling, result
 

time: 280 us -> 197 us (0.70)
  starting transfers between devices: 75.3 us -> 34 us
  other arithmetic: 22.3 us -> 7.97 us
  Pallas kernels: 59.2 us -> 46.1 us
  local copies, waits for them, and re-layouts: 21.2 us -> 13.7 us
  waiting for transfers between devices: 69 us -> 65.8 us
    ppermute x6 -> x9, waiting for transfers between devices: 7.92 us -> 28.1 us  [spread4(): got = [lax.ppermute(v, axis, shift(s)) for s in (1, 2, 3)]]
    ppermute x6 -> x3, waiting for transfers between devices: 24.8 us -> 8.34 us  [scatter4(): lax.ppermute(lax.dynamic_slice_in_dim(v, (index + s) % 4 * n, n, 0), axis...]
    ppermute x18 -> x9, starting transfers between devices: 26 us -> 13.6 us  [gather4(): pieces = [v] + [lax.ppermute(v, axis, shift(s)) for s in (1, 2, 3)]]
    ppermute x4 -> x3, starting transfers between devices: 15.1 us -> 5.09 us  [swap_gather(): other = lax.ppermute(v, 'row', CORE_SWAP)]
    pallas_call x1, Pallas kernels: 9.76 us -> 2.09 us  [cross_part(): pl.pallas_call(cross_kernel, out_shape=jax.ShapeDtypeStruct((128, n), F32...]
    pallas_call x1, Pallas kernels: 14.1 us -> 7.21 us  [residual(): pl.pallas_call(functools.partial(residual_kernel, float(rows_total)), out...]
    ppermute x4 -> x1, waiting for transfers between devices: 10.8 us -> 4 us  [per_device(): other_half = lax.ppermute(trail_half, 'row', CORE_SWAP)]
    ppermute x18 -> x9, waiting for transfers between devices: 20.6 us -> 15.1 us  [gather4(): pieces = [v] + [lax.ppermute(v, axis, shift(s)) for s in (1, 2, 3)]]
  transfers between devices with their start and end apart: 42 -> 30, of which waited for: 27 -> 26; matrix products, arithmetic and copies ran while one was open for 12% -> 6% of each run, Pallas kernels for 16% -> 19%
where the time goes in v2:
time: 197 us; the launch traced here: 196 us
  waiting for transfers between devices  65.8 us (33%)
  Pallas kernels  46.1 us (23%)
  starting transfers between devices  34 us (17%)
  between operations  14.5 us (7%)
  blocking collectives  13.8 us (7%)
  local copies, waits for them, and re-layouts  13.7 us (7%)
  other arithmetic  7.97 us (4%)
    ppermute x9, waiting for transfers between devices, spread4(): got = [lax.ppermute(v, axis, shift(s)) for s in (1, 2, 3)]  28.1 us
    pallas_call x1, Pallas kernels, factor_panel(): pl.pallas_call(functools.partial(factor_kernel, float(rows_total)), out_s...  26.7 us
    ppermute x9, waiting for transfers between devices, gather4(): pieces = [v] + [lax.ppermute(v, axis, shift(s)) for s in (1, 2, 3)]  15.1 us
    all_to_all x1, blocking collectives, per_device(): panel = lax.all_to_all(panel, 'row', 0, 0, tiled=True).reshape(512, 512)  13.8 us
    ppermute x9, starting transfers between devices, gather4(): pieces = [v] + [lax.ppermute(v, axis, shift(s)) for s in (1, 2, 3)]  13.6 us
    unnamed x55, local copies, waits for them, and re-layouts  11.4 us
    ppermute x3, waiting for transfers between devices, scatter4(): lax.ppermute(lax.dynamic_slice_in_dim(v, (index + s) % 4 * n, n, 0), axis...  8.34 us
    pallas_call x1, Pallas kernels, residual(): pl.pallas_call(functools.partial(residual_kernel, float(rows_total)), out...  7.21 us
  transfers between devices with their start and end apart: 30, of which 26 were waited for; matrix products, arithmetic and copies ran while one was open for 6% of the time, Pallas kernels for 19%

profile of v2, /device:TPU:1, one launch (start us, length us, event | category | flops | bytes accessed | tf_op | source)
XLA Modules:
  0.0 195.9 jit_solution(12372844301263351424)
XLA Ops:
  9.6 4.4 %collective-permute-start.1 = (bf16[16,1024]{1,0:T(8,128)(2,1)S(1)}, bf16[16,1024]{1,0:T(8,128)(2,1)S(1)}, u32[]{:S(2)}, u32[]{:S(2)}) collective-permute-start(bf16[16,1024]{1,0:T(8,128)(2,1)S(1)} %constant_dynamic-slice_fusion.5), channel_id=1, source_target_pairs={{0,2},{1,3},{2,0},{3,1},{4,6},{5,7},{6,4},{7,5},{8,10},{9,11},{10,... | collective-permute-start | bytes 98312 | tf_op jit(solution)/shard_map/ppermute | solution.py:44
  20.5 2.7 %collective-permute-start.4 = (bf16[64,1024]{1,0:T(8,128)(2,1)}, bf16[64,1024]{1,0:T(8,128)(2,1)S(1)}, u32[]{:S(2)}, u32[]{:S(2)}) collective-permute-start(bf16[64,1024]{1,0:T(8,128)(2,1)} %pad_maximum_fusion.5), channel_id=1, source_target_pairs={{0,8},{1,9},{2,10},{3,11},{4,12},{5,13},{6,14},{7,15},{8,0},{9,1},... | collective-permute-start | bytes 393224 | tf_op jit(solution)/shard_map/ppermute | solution.py:44
  26.2 2.9 %collective-permute-done.5 = bf16[64,1024]{1,0:T(8,128)(2,1)} collective-permute-done((bf16[64,1024]{1,0:T(8,128)(2,1)}, bf16[64,1024]{1,0:T(8,128)(2,1)}, u32[]{:S(2)}, u32[]{:S(2)}) %collective-permute-start.5) | collective-permute-done | bytes 131104 | tf_op jit(solution)/shard_map/ppermute | solution.py:44
  29.2 1.8 collective-permute-done.3
  34.2 3.2 %collective-permute-start.6 = (bf16[256,1024]{1,0:T(8,128)(2,1)}, bf16[256,1024]{1,0:T(8,128)(2,1)}, u32[]{:S(2)}, u32[]{:S(2)}) collective-permute-start(bf16[256,1024]{1,0:T(8,128)(2,1)} %pad_maximum_fusion.2), channel_id=1, source_target_pairs={{0,16},{16,0},{32,48},{48,32},{64,80},{80,64},{96,112},{112,96},{1... | collective-permute-start | bytes 1572872 | tf_op jit(solution)/shard_map/ppermute | solution.py:77
  42.0 1.7 broadcast_select_fusion.1
  43.8 1.8 shard_map.95
  45.7 13.8 %all_to_all.10 = bf16[8,64,512]{2,1,0:T(8,128)(2,1)} all-to-all(bf16[8,64,512]{2,1,0:T(8,128)(2,1)S(1)} %get-tuple-element.25), channel_id=1, replica_groups=mesh['row'=8,'col'=16] {'row'}, dimensions={0} | all-to-all | bytes 1048576 | tf_op jit(solution)/shard_map/all_to_all | solution.py:441
  64.5 2.6 %collective-permute-done.10 = f32[64,512]{1,0:T(8,128)S(1)} collective-permute-done((f32[64,512]{1,0:T(8,128)S(1)}, f32[64,512]{1,0:T(8,128)S(1)}, u32[]{:S(2)}, u32[]{:S(2)}) %collective-permute-start.10) | collective-permute-done | bytes 131104 | tf_op jit(solution)/shard_map/ppermute | solution.py:61
  67.1 2.1 %collective-permute-done.9 = f32[64,512]{1,0:T(8,128)S(1)} collective-permute-done((f32[64,512]{1,0:T(8,128)S(1)}, f32[64,512]{1,0:T(8,128)S(1)}, u32[]{:S(2)}, u32[]{:S(2)}) %collective-permute-start.9) | collective-permute-done | bytes 131104 | tf_op jit(solution)/shard_map/ppermute | solution.py:61
  69.2 3.6 %collective-permute-done.8 = f32[64,512]{1,0:T(8,128)S(1)} collective-permute-done((f32[64,512]{1,0:T(8,128)S(1)}, f32[64,512]{1,0:T(8,128)S(1)}, u32[]{:S(2)}, u32[]{:S(2)}) %collective-permute-start.8) | collective-permute-done | bytes 131104 | tf_op jit(solution)/shard_map/ppermute | solution.py:61
  72.9 1.7 collective-permute-start.12
  74.9 5.2 %collective-permute-done.13 = f32[64,512]{1,0:T(8,128)S(1)} collective-permute-done((f32[64,512]{1,0:T(8,128)S(1)}, f32[64,512]{1,0:T(8,128)S(1)}, u32[]{:S(2)}, u32[]{:S(2)}) %collective-permute-start.13) | collective-permute-done | bytes 131104 | tf_op jit(solution)/shard_map/ppermute | solution.py:83
  80.1 1.7 collective-permute-done.12
  81.8 4.4 %collective-permute-done.11 = f32[64,512]{1,0:T(8,128)S(1)} collective-permute-done((f32[64,512]{1,0:T(8,128)S(1)}, f32[64,512]{1,0:T(8,128)S(1)}, u32[]{:S(2)}, u32[]{:S(2)}) %collective-permute-start.11) | collective-permute-done | bytes 131104 | tf_op jit(solution)/shard_map/ppermute | solution.py:83
  87.8 4.4 %collective-permute-done.16 = f32[64,512]{1,0:T(8,128)S(1)} collective-permute-done((f32[64,512]{1,0:T(8,128)S(1)}, f32[64,512]{1,0:T(8,128)S(1)}, u32[]{:S(2)}, u32[]{:S(2)}) %collective-permute-start.16) | collective-permute-done | bytes 131104 | tf_op jit(solution)/shard_map/ppermute | solution.py:83
  92.5 3.4 %collective-permute-done.14 = f32[64,512]{1,0:T(8,128)S(1)} collective-permute-done((f32[64,512]{1,0:T(8,128)S(1)}, f32[64,512]{1,0:T(8,128)S(1)}, u32[]{:S(2)}, u32[]{:S(2)}) %collective-permute-start.14) | collective-permute-done | bytes 131104 | tf_op jit(solution)/shard_map/ppermute | solution.py:83
  96.0 2.0 %collective-permute-start.18 = (f32[64,512]{1,0:T(8,128)S(1)}, f32[64,512]{1,0:T(8,128)S(1)}, u32[]{:S(2)}, u32[]{:S(2)}) collective-permute-start(f32[64,512]{1,0:T(8,128)S(1)} %add_add_fusion.1), channel_id=1, source_target_pairs={{0,64},{16,80},{32,96},{48,112},{64,0},{80,16},{96,32},{112,48},{1... | collective-permute-start | bytes 393224 | tf_op jit(solution)/shard_map/ppermute | solution.py:44
  99.5 1.9 collective-permute-done.18
  102.2 3.1 %collective-permute-done.17 = f32[64,512]{1,0:T(8,128)S(1)} collective-permute-done((f32[64,512]{1,0:T(8,128)S(1)}, f32[64,512]{1,0:T(8,128)S(1)}, u32[]{:S(2)}, u32[]{:S(2)}) %collective-permute-start.17) | collective-permute-done | bytes 131104 | tf_op jit(solution)/shard_map/ppermute | solution.py:44
  109.8 4.0 %collective-permute-done.21.other_ref = bf16[16,64,1024]{2,1,0:T(8,128)(2,1)S(1)} collective-permute-done((bf16[16,64,1024]{2,1,0:T(8,128)(2,1)}, bf16[16,64,1024]{2,1,0:T(8,128)(2,1)S(1)}, u32[]{:S(2)}, u32[]{:S(2)}) %collective-permute-start.21) | collective-permute-done | bytes 2097184 | tf_op jit(solution)/shard_map/ppermute | solution.py:447
  113.9 1.7 copy-done.9
  115.5 6.8 %shard_map.96 = bf16[8,16,64,128]{3,2,1,0:T(8,128)(2,1)S(1)} custom-call(s32[1]{0:T(128)} %bitcast.core_ref, bf16[16,64,1024]{2,1,0:T(8,128)(2,1)S(1)} %bitcast.26, bf16[16,64,1024]{2,1,0:T(8,128)(2,1)S(1)} %collective-permute-done.21.other_ref, bf16[320,1024]{1,0:T(8,128)(2,1)S(1)} %copy-done.13, bf16[768,1024]{1,0:T(8,128)(2,1)S(1)} %copy-done.11, ...), custom_call_target="tpu_custom_call" | custom-call | flops 4563402752 | bytes 9437184 | tf_op jit(solution)/shard_map/pallas_call | solution.py:231
  123.7 4.8 %all-to-all-start.1 = ((bf16[128,64,128]{2,1,0:T(8,128)(2,1)}), bf16[128,64,128]{2,1,0:T(8,128)(2,1)S(1)}, u32[]{:S(2)}, u32[]{:S(2)}) async-start(bf16[128,64,128]{2,1,0:T(8,128)(2,1)} %bitcast.22), calls=%async_computation.1 | async-start | bytes 4194304 | tf_op jit(solution)/shard_map/all_to_all | solution.py:450
  129.8 26.7 %shard_map.97 = (f32[512,512]{1,0:T(8,128)}, f32[512,512]{1,0:T(8,128)S(1)}) custom-call(f32[512,512]{1,0:T(8,128)S(1)} %copy-done.5), custom_call_target="tpu_custom_call" | custom-call | flops 2684354560 | bytes 4194304 | tf_op jit(solution)/shard_map/pallas_call | solution.py:314
  156.5 5.2 %all-to-all-done.1 = bf16[128,64,128]{2,1,0:T(8,128)(2,1)S(1)} async-done(((bf16[128,64,128]{2,1,0:T(8,128)(2,1)}), bf16[128,64,128]{2,1,0:T(8,128)(2,1)S(1)}, u32[]{:S(2)}, u32[]{:S(2)}) %all-to-all-start.1) | async-done | bytes 2097184 | tf_op jit(solution)/shard_map/all_to_all | solution.py:450
  161.7 3.4 %copy-done.1 = bf16[8192,512]{1,0:T(8,128)(2,1)S(1)} copy-done((bf16[8192,512]{1,0:T(8,128)(2,1)S(1)}, bf16[8192,512]{1,0:T(8,128)(2,1)}, u32[]{:S(2)}) %copy-start.1) | copy-done | bytes 8388632
  165.1 2.1 %shard_map.98 = f32[128,512]{1,0:T(8,128)S(1)} custom-call(bf16[16,512,512]{2,1,0:T(8,128)(2,1)S(1)} %bitcast.17, bf16[8,16,64,128]{3,2,1,0:T(8,128)(2,1)S(1)} %bitcast.19), custom_call_target="tpu_custom_call" | custom-call | flops 1073741824 | bytes 11534336 | tf_op jit(solution)/shard_map/pallas_call | solution.py:339
  171.4 2.7 %collective-permute-done.25 = f32[64,512]{1,0:T(8,128)S(1)} collective-permute-done((f32[64,512]{1,0:T(8,128)S(1)}, f32[64,512]{1,0:T(8,128)S(1)}, u32[]{:S(2)}, u32[]{:S(2)}) %collective-permute-start.25) | collective-permute-done | bytes 131104 | tf_op jit(solution)/shard_map/ppermute | solution.py:83
  174.1 2.3 %collective-permute-done.24 = f32[64,512]{1,0:T(8,128)S(1)} collective-permute-done((f32[64,512]{1,0:T(8,128)S(1)}, f32[64,512]{1,0:T(8,128)S(1)}, u32[]{:S(2)}, u32[]{:S(2)}) %collective-permute-start.24) | collective-permute-done | bytes 131104 | tf_op jit(solution)/shard_map/ppermute | solution.py:83
  176.3 3.8 %collective-permute-done.23 = f32[64,512]{1,0:T(8,128)S(1)} collective-permute-done((f32[64,512]{1,0:T(8,128)S(1)}, f32[64,512]{1,0:T(8,128)S(1)}, u32[]{:S(2)}, u32[]{:S(2)}) %collective-permute-start.23) | collective-permute-done | bytes 131104 | tf_op jit(solution)/shard_map/ppermute | solution.py:83
  181.8 7.2 %shard_map.99 = (f32[128,512]{1,0:T(8,128)}, f32[128,8192]{1,0:T(8,128)}) custom-call(f32[128,512]{1,0:T(8,128)S(1)} %pad_maximum_fusion.4.cross_ref, f32[512,512]{1,0:T(8,128)S(1)} %get-tuple-element.36.inverse_ref, bf16[16,512,512]{2,1,0:T(8,128)(2,1)S(1)} %bitcast.18, bf16[8,16,64,128]{3,2,1,0:T(8,128)(2,1)S(1)} %bitcast.20), custom_call_target="tpu_custom_call" | custom-call | flops 2147483648 | bytes 16777216 | tf_op jit(solution)/shard_map/pallas_call | solution.py:380
  (117 shorter events, 42.0 us)
Async XLA Ops:
  7.2 32.4 %copy-start.7 = (s32[1,8]{1,0:T(1,128)S(1)}, s32[1,8]{1,0:T(1,128)}, u32[]{:S(2)}) copy-start(s32[1,8]{1,0:T(1,128)} %count_ref.1) | copy-start | bytes 100
  7.2 32.4 %copy-start.8 = (s32[1,8]{1,0:T(1,128)S(1)}, s32[1,8]{1,0:T(1,128)}, u32[]{:S(2)}) copy-start(s32[1,8]{1,0:T(1,128)} %owner_ref.1) | copy-start | bytes 100
  7.2 102.3 %all-gather.5.cloned.1.call-start = ((), (), s32[]{:S(2)}) async-start(), calls=%async_computation.2 | async-start | bytes 2228224 | tf_op jit(solution)/shard_map/all_gather | solution.py:424
  8.8 147.7 %all-gather.7.cloned.1.call-start = ((), (), s32[]{:S(2)}) async-start(), calls=%async_computation.3 | async-start | bytes 8912896 | tf_op jit(solution)/shard_map/all_gather | solution.py:443
  9.6 5.9 %collective-permute-start.1 = (bf16[16,1024]{1,0:T(8,128)(2,1)S(1)}, bf16[16,1024]{1,0:T(8,128)(2,1)S(1)}, u32[]{:S(2)}, u32[]{:S(2)}) collective-permute-start(bf16[16,1024]{1,0:T(8,128)(2,1)S(1)} %constant_dynamic-slice_fusion.5), channel_id=1, source_target_pairs={{0,2},{1,3},{2,0},{3,1},{4,6},{5,7},{6,4},{7,5},{8,10},{9,11},{10,... | collective-permute-start | bytes 98312 | tf_op jit(solution)/shard_map/ppermute | solution.py:44
  14.1 2.8 %collective-permute-start.2 = (bf16[16,1024]{1,0:T(8,128)(2,1)S(1)}, bf16[16,1024]{1,0:T(8,128)(2,1)S(1)}, u32[]{:S(2)}, u32[]{:S(2)}) collective-permute-start(bf16[16,1024]{1,0:T(8,128)(2,1)S(1)} %constant_dynamic-slice_fusion.5), channel_id=1, source_target_pairs={{0,3},{1,0},{2,1},{3,2},{4,7},{5,4},{6,5},{7,6},{8,11},{9,8},{10,9... | collective-permute-start | bytes 98312 | tf_op jit(solution)/shard_map/ppermute | solution.py:44
  14.5 4.0 %collective-permute-start = (bf16[16,1024]{1,0:T(8,128)(2,1)S(1)}, bf16[16,1024]{1,0:T(8,128)(2,1)S(1)}, u32[]{:S(2)}, u32[]{:S(2)}) collective-permute-start(bf16[16,1024]{1,0:T(8,128)(2,1)S(1)} %constant_dynamic-slice_fusion.5), channel_id=1, source_target_pairs={{0,1},{1,2},{2,3},{3,0},{4,5},{5,6},{6,7},{7,4},{8,9},{9,10},{10,1... | collective-permute-start | bytes 98312 | tf_op jit(solution)/shard_map/ppermute | solution.py:44
  20.5 5.7 %collective-permute-start.4 = (bf16[64,1024]{1,0:T(8,128)(2,1)}, bf16[64,1024]{1,0:T(8,128)(2,1)S(1)}, u32[]{:S(2)}, u32[]{:S(2)}) collective-permute-start(bf16[64,1024]{1,0:T(8,128)(2,1)} %pad_maximum_fusion.5), channel_id=1, source_target_pairs={{0,8},{1,9},{2,10},{3,11},{4,12},{5,13},{6,14},{7,15},{8,0},{9,1},... | collective-permute-start | bytes 393224 | tf_op jit(solution)/shard_map/ppermute | solution.py:44
  23.3 5.9 %collective-permute-start.5 = (bf16[64,1024]{1,0:T(8,128)(2,1)}, bf16[64,1024]{1,0:T(8,128)(2,1)}, u32[]{:S(2)}, u32[]{:S(2)}) collective-permute-start(bf16[64,1024]{1,0:T(8,128)(2,1)} %pad_maximum_fusion.5), channel_id=1, source_target_pairs={{0,12},{1,13},{2,14},{3,15},{4,0},{5,1},{6,2},{7,3},{8,4},{9,5},{1... | collective-permute-start | bytes 393224 | tf_op jit(solution)/shard_map/ppermute | solution.py:44
  24.2 6.8 %collective-permute-start.3 = (bf16[64,1024]{1,0:T(8,128)(2,1)}, bf16[64,1024]{1,0:T(8,128)(2,1)}, u32[]{:S(2)}, u32[]{:S(2)}) collective-permute-start(bf16[64,1024]{1,0:T(8,128)(2,1)} %pad_maximum_fusion.5), channel_id=1, source_target_pairs={{0,4},{1,5},{2,6},{3,7},{4,8},{5,9},{6,10},{7,11},{8,12},{9,13},{1... | collective-permute-start | bytes 393224 | tf_op jit(solution)/shard_map/ppermute | solution.py:44
  34.2 7.7 %collective-permute-start.6 = (bf16[256,1024]{1,0:T(8,128)(2,1)}, bf16[256,1024]{1,0:T(8,128)(2,1)}, u32[]{:S(2)}, u32[]{:S(2)}) collective-permute-start(bf16[256,1024]{1,0:T(8,128)(2,1)} %pad_maximum_fusion.2), channel_id=1, source_target_pairs={{0,16},{16,0},{32,48},{48,32},{64,80},{80,64},{96,112},{112,96},{1... | collective-permute-start | bytes 1572872 | tf_op jit(solution)/shard_map/ppermute | solution.py:77
  59.5 2.7 %collective-permute-start.7 = (f32[256,512]{1,0:T(8,128)S(1)}, f32[256,512]{1,0:T(8,128)S(1)}, u32[]{:S(2)}, u32[]{:S(2)}) collective-permute-start(f32[256,512]{1,0:T(8,128)S(1)} %constant_dynamic-slice_fusion.4), channel_id=1, source_target_pairs={{0,16},{16,0},{32,48},{48,32},{64,80},{80,64},{96,112},{112,96},{1... | collective-permute-start | bytes 1572872 | tf_op jit(solution)/shard_map/ppermute | solution.py:73
  62.3 4.8 %collective-permute-start.10 = (f32[64,512]{1,0:T(8,128)S(1)}, f32[64,512]{1,0:T(8,128)S(1)}, u32[]{:S(2)}, u32[]{:S(2)}) collective-permute-start(f32[64,512]{1,0:T(8,128)S(1)} %get-tuple-element.48), channel_id=1, source_target_pairs={{0,96},{16,112},{32,0},{48,16},{64,32},{80,48},{96,64},{112,80},{1... | collective-permute-start | bytes 393224 | tf_op jit(solution)/shard_map/ppermute | solution.py:61
  63.3 5.9 %collective-permute-start.9 = (f32[64,512]{1,0:T(8,128)S(1)}, f32[64,512]{1,0:T(8,128)S(1)}, u32[]{:S(2)}, u32[]{:S(2)}) collective-permute-start(f32[64,512]{1,0:T(8,128)S(1)} %get-tuple-element.49), channel_id=1, source_target_pairs={{0,64},{16,80},{32,96},{48,112},{64,0},{80,16},{96,32},{112,48},{1... | collective-permute-start | bytes 393224 | tf_op jit(solution)/shard_map/ppermute | solution.py:61
  64.5 8.3 %collective-permute-start.8 = (f32[64,512]{1,0:T(8,128)S(1)}, f32[64,512]{1,0:T(8,128)S(1)}, u32[]{:S(2)}, u32[]{:S(2)}) collective-permute-start(f32[64,512]{1,0:T(8,128)S(1)} %get-tuple-element.47), channel_id=1, source_target_pairs={{0,32},{16,48},{32,64},{48,80},{64,96},{80,112},{96,0},{112,16},{1... | collective-permute-start | bytes 393224 | tf_op jit(solution)/shard_map/ppermute | solution.py:61
  72.9 7.2 %collective-permute-start.13 = (f32[64,512]{1,0:T(8,128)S(1)}, f32[64,512]{1,0:T(8,128)S(1)}, u32[]{:S(2)}, u32[]{:S(2)}) collective-permute-start(f32[64,512]{1,0:T(8,128)S(1)} %add_add_fusion.3), channel_id=1, source_target_pairs={{0,3},{1,0},{2,1},{3,2},{4,7},{5,4},{6,5},{7,6},{8,11},{9,8},{10,9... | collective-permute-start | bytes 393224 | tf_op jit(solution)/shard_map/ppermute | solution.py:83
  72.9 8.8 %collective-permute-start.12 = (f32[64,512]{1,0:T(8,128)S(1)}, f32[64,512]{1,0:T(8,128)S(1)}, u32[]{:S(2)}, u32[]{:S(2)}) collective-permute-start(f32[64,512]{1,0:T(8,128)S(1)} %add_add_fusion.3), channel_id=1, source_target_pairs={{0,2},{1,3},{2,0},{3,1},{4,6},{5,7},{6,4},{7,5},{8,10},{9,11},{10,... | collective-permute-start | bytes 393224 | tf_op jit(solution)/shard_map/ppermute | solution.py:83
  74.7 11.6 %collective-permute-start.11 = (f32[64,512]{1,0:T(8,128)S(1)}, f32[64,512]{1,0:T(8,128)S(1)}, u32[]{:S(2)}, u32[]{:S(2)}) collective-permute-start(f32[64,512]{1,0:T(8,128)S(1)} %add_add_fusion.3), channel_id=1, source_target_pairs={{0,1},{1,2},{2,3},{3,0},{4,5},{5,6},{6,7},{7,4},{8,9},{9,10},{10,1... | collective-permute-start | bytes 393224 | tf_op jit(solution)/shard_map/ppermute | solution.py:83
  86.2 5.9 %collective-permute-start.16 = (f32[64,512]{1,0:T(8,128)S(1)}, f32[64,512]{1,0:T(8,128)S(1)}, u32[]{:S(2)}, u32[]{:S(2)}) collective-permute-start(f32[64,512]{1,0:T(8,128)S(1)} %add_add_fusion.2), channel_id=1, source_target_pairs={{0,12},{1,13},{2,14},{3,15},{4,0},{5,1},{6,2},{7,3},{8,4},{9,5},{1... | collective-permute-start | bytes 393224 | tf_op jit(solution)/shard_map/ppermute | solution.py:83
  86.5 6.0 %collective-permute-start.15 = (f32[64,512]{1,0:T(8,128)S(1)}, f32[64,512]{1,0:T(8,128)S(1)}, u32[]{:S(2)}, u32[]{:S(2)}) collective-permute-start(f32[64,512]{1,0:T(8,128)S(1)} %add_add_fusion.2), channel_id=1, source_target_pairs={{0,8},{1,9},{2,10},{3,11},{4,12},{5,13},{6,14},{7,15},{8,0},{9,1},... | collective-permute-start | bytes 393224 | tf_op jit(solution)/shard_map/ppermute | solution.py:83
  87.3 8.6 %collective-permute-start.14 = (f32[64,512]{1,0:T(8,128)S(1)}, f32[64,512]{1,0:T(8,128)S(1)}, u32[]{:S(2)}, u32[]{:S(2)}) collective-permute-start(f32[64,512]{1,0:T(8,128)S(1)} %add_add_fusion.2), channel_id=1, source_target_pairs={{0,4},{1,5},{2,6},{3,7},{4,8},{5,9},{6,10},{7,11},{8,12},{9,13},{1... | collective-permute-start | bytes 393224 | tf_op jit(solution)/shard_map/ppermute | solution.py:83
  96.0 5.4 %collective-permute-start.18 = (f32[64,512]{1,0:T(8,128)S(1)}, f32[64,512]{1,0:T(8,128)S(1)}, u32[]{:S(2)}, u32[]{:S(2)}) collective-permute-start(f32[64,512]{1,0:T(8,128)S(1)} %add_add_fusion.1), channel_id=1, source_target_pairs={{0,64},{16,80},{32,96},{48,112},{64,0},{80,16},{96,32},{112,48},{1... | collective-permute-start | bytes 393224 | tf_op jit(solution)/shard_map/ppermute | solution.py:44
  98.0 4.2 %collective-permute-start.19 = (f32[64,512]{1,0:T(8,128)S(1)}, f32[64,512]{1,0:T(8,128)S(1)}, u32[]{:S(2)}, u32[]{:S(2)}) collective-permute-start(f32[64,512]{1,0:T(8,128)S(1)} %add_add_fusion.1), channel_id=1, source_target_pairs={{0,96},{16,112},{32,0},{48,16},{64,32},{80,48},{96,64},{112,80},{1... | collective-permute-start | bytes 393224 | tf_op jit(solution)/shard_map/ppermute | solution.py:44
  98.0 7.4 %collective-permute-start.17 = (f32[64,512]{1,0:T(8,128)S(1)}, f32[64,512]{1,0:T(8,128)S(1)}, u32[]{:S(2)}, u32[]{:S(2)}) collective-permute-start(f32[64,512]{1,0:T(8,128)S(1)} %add_add_fusion.1), channel_id=1, source_target_pairs={{0,32},{16,48},{32,64},{48,80},{64,96},{80,112},{96,0},{112,16},{1... | collective-permute-start | bytes 393224 | tf_op jit(solution)/shard_map/ppermute | solution.py:44
  105.5 2.8 %collective-permute-start.20 = (f32[256,512]{1,0:T(8,128)S(1)}, f32[256,512]{1,0:T(8,128)S(1)}, u32[]{:S(2)}, u32[]{:S(2)}) collective-permute-start(f32[256,512]{1,0:T(8,128)S(1)} %pad_maximum_fusion.3), channel_id=1, source_target_pairs={{0,16},{16,0},{32,48},{48,32},{64,80},{80,64},{96,112},{112,96},{1... | collective-permute-start | bytes 1572872 | tf_op jit(solution)/shard_map/ppermute | solution.py:77
  109.5 4.4 %collective-permute-start.21 = (bf16[16,64,1024]{2,1,0:T(8,128)(2,1)}, bf16[16,64,1024]{2,1,0:T(8,128)(2,1)S(1)}, u32[]{:S(2)}, u32[]{:S(2)}) collective-permute-start(bf16[16,64,1024]{2,1,0:T(8,128)(2,1)} %bitcast.25), channel_id=1, source_target_pairs={{0,16},{16,0},{32,48},{48,32},{64,80},{80,64},{96,112},{112,96},{1... | collective-permute-start | bytes 6291464 | tf_op jit(solution)/shard_map/ppermute | solution.py:447
  123.7 38.1 %all-to-all-start.1 = ((bf16[128,64,128]{2,1,0:T(8,128)(2,1)}), bf16[128,64,128]{2,1,0:T(8,128)(2,1)S(1)}, u32[]{:S(2)}, u32[]{:S(2)}) async-start(bf16[128,64,128]{2,1,0:T(8,128)(2,1)} %bitcast.22), calls=%async_computation.1 | async-start | bytes 4194304 | tf_op jit(solution)/shard_map/all_to_all | solution.py:450
  167.3 2.0 %collective-permute-start.22 = (f32[64,512]{1,0:T(8,128)S(1)}, f32[64,512]{1,0:T(8,128)S(1)}, u32[]{:S(2)}, u32[]{:S(2)}) collective-permute-start(f32[64,512]{1,0:T(8,128)S(1)} %constant_dynamic-slice_fusion), channel_id=1, source_target_pairs={{0,16},{16,0},{32,48},{48,32},{64,80},{80,64},{96,112},{112,96},{1... | collective-permute-start | bytes 393224 | tf_op jit(solution)/shard_map/ppermute | solution.py:73
  169.3 4.8 %collective-permute-start.25 = (f32[64,512]{1,0:T(8,128)S(1)}, f32[64,512]{1,0:T(8,128)S(1)}, u32[]{:S(2)}, u32[]{:S(2)}) collective-permute-start(f32[64,512]{1,0:T(8,128)S(1)} %dynamic-slice_add_fusion.1), channel_id=1, source_target_pairs={{0,96},{16,112},{32,0},{48,16},{64,32},{80,48},{96,64},{112,80},{1... | collective-permute-start | bytes 393224 | tf_op jit(solution)/shard_map/ppermute | solution.py:83
  170.4 5.9 %collective-permute-start.24 = (f32[64,512]{1,0:T(8,128)S(1)}, f32[64,512]{1,0:T(8,128)S(1)}, u32[]{:S(2)}, u32[]{:S(2)}) collective-permute-start(f32[64,512]{1,0:T(8,128)S(1)} %dynamic-slice_add_fusion.1), channel_id=1, source_target_pairs={{0,64},{16,80},{32,96},{48,112},{64,0},{80,16},{96,32},{112,48},{1... | collective-permute-start | bytes 393224 | tf_op jit(solution)/shard_map/ppermute | solution.py:83
  171.4 8.7 %collective-permute-start.23 = (f32[64,512]{1,0:T(8,128)S(1)}, f32[64,512]{1,0:T(8,128)S(1)}, u32[]{:S(2)}, u32[]{:S(2)}) collective-permute-start(f32[64,512]{1,0:T(8,128)S(1)} %dynamic-slice_add_fusion.1), channel_id=1, source_target_pairs={{0,32},{16,48},{32,64},{48,80},{64,96},{80,112},{96,0},{112,16},{1... | collective-permute-start | bytes 393224 | tf_op jit(solution)/shard_map/ppermute | solution.py:83
  180.1 1.6 collective-permute-start.26
  (25 other events, 110.2 us)
Sparse Core Ops, SparseCore 0:
  10.2 48.1 all-gather.4
  60.5 86.6 all-gather.6

commit v3 on v2

--- a/solution.py
+++ b/solution.py
@@ -30,6 +30,9 @@
     return [(x * 4 + z, ((x + s) % 4) * 4 + z) for x in range(4) for z in range(4)]
 
 
+UPPER = [(i, j) for i in range(4) for j in range(i, 4)]
+
+
 def dot(a, b, dims, precision=None):
     return lax.dot_general(a, b, dims, precision=precision, preferred_element_type=F32)
 
@@ -40,18 +43,13 @@
     )
 
 
+def shifted(v, axis, shift):
+    return [v] + [lax.ppermute(v, axis, shift(s)) for s in (1, 2, 3)]
+
+
 def gather4(v, axis, shift, index):
     pieces = [v] + [lax.ppermute(v, axis, shift(s)) for s in (1, 2, 3)]
     return in_order(pieces, index)
-
-
-def ring4(v, axis, shift, index):
-    h = v.shape[0] // 2
-    a = lax.ppermute(v, axis, shift(1))
-    b = lax.ppermute(v, axis, shift(3))
-    c = lax.ppermute(a[:h], axis, shift(1))
-    d = lax.ppermute(b[h:], axis, shift(3))
-    return in_order([v, a, jnp.concatenate([c, d], axis=0), b], index)
 
 
 def scatter4(v, axis, shift, index):
@@ -185,70 +183,140 @@
     return jnp.concatenate(parts, axis=0)
 
 
-def panel_kernel(env_ref, atoms_ref, grads_ref, mean_ref, order_ref, out_ref, gram_ref):
-    rows = compact_rows(env_ref[...], atoms_ref[...], grads_ref[...], mean_ref[...])
-    out_ref[...] = dot(order_ref[...], rows, NN).astype(BF16).reshape(out_ref.shape)
-    gram_ref[...] = dot(rows, rows, TN)
+def put_env(env, where, own, other, block, at):
+    core = where[3]
+    env[pl.ds(pl.multiple_of(at + core * 16, 16), 16)] = own[block]
+    env[pl.ds(pl.multiple_of(at + (1 - core) * 16, 16), 16)] = other[block]
+
+
+def panel_kernel(
+    where, own, other, atoms_ref, grads_ref, mean_ref, order_ref, near_ref, far_ref, gram_ref, env
+):
+    x, z, y, core = where[0], where[1], where[2], where[3]
+    for i in range(4):
+        for j in range(4):
+            place = ((x - i) & 3) * 4 + ((z - j) & 3)
+            put_env(env, where, own, other, (i, j), place * 32)
+    rows = compact_rows(env[...], atoms_ref[...], grads_ref[...], mean_ref[...])
+    full = dot(order_ref[...], rows, NN).astype(BF16)
+    first = core == 0
+    for i in range(4):
+        low, high = full[128 * i : 128 * i + 64], full[128 * i + 64 : 128 * i + 128]
+        s = (i - y) & 3
+        near_ref[s] = jnp.where(first, low, high)
+        far_ref[s] = jnp.where(first, high, low)
+    gram = dot(rows, rows, TN)
+    for n, (i, j) in enumerate(UPPER):
+        gram_ref[128 * n : 128 * n + 128] = gram[
+            128 * i : 128 * i + 128, 128 * j : 128 * j + 128
+        ]
 
 
 def trail_kernel(
-    core_ref, own_ref, other_ref, atoms_ref, grads_ref, mean_ref, order_ref, out_ref
+    where,
+    own0,
+    own1,
+    own2,
+    own3,
+    other0,
+    other1,
+    other2,
+    other3,
+    atoms_ref,
+    grads_ref,
+    mean_ref,
+    order_ref,
+    out_ref,
+    env,
 ):
-    first = core_ref[0] == 0
-    own, other = own_ref[...], other_ref[...]
-    low, high = jnp.where(first, own, other), jnp.where(first, other, own)
-    env = jnp.concatenate([low, high], axis=1).reshape(-1, 1024)
-    rows = compact_rows(env, atoms_ref[...], grads_ref[...], mean_ref[...])
+    z, y = where[1], where[2]
+    pairs = [(own0, other0), (own1, other1), (own2, other2), (own3, other3)]
+    for j in range(4):
+        place = ((z - j) & 3) * 128
+        for s in range(4):
+            own, other = pairs[s]
+            put_env(env, where, own, other, (0, j), place + ((y - s) & 3) * 32)
+    rows = compact_rows(env[...], atoms_ref[...], grads_ref[...], mean_ref[...])
     full = dot(order_ref[...], rows, NN).astype(BF16)
     for c in range(out_ref.shape[1]):
         out_ref[:, c] = full[:, c * 128 : c * 128 + 128].reshape(8, 64, 128)
 
 
+def assemble_kernel(where, near, far, got1, got2, got3, out):
+    y, core = where[2], where[3]
+    out[2 * y + core] = near[0]
+    out[2 * y + 1 - core] = far[0]
+    for s, got in ((1, got1), (2, got2), (3, got3)):
+        at = 2 * ((y - s) & 3)
+        out[at + core] = got[0]
+        out[at + 1 - core] = got[1]
+
+
 def params():
     return pltpu.CompilerParams(vmem_limit_bytes=40 << 20)
 
 
-def panel_rows(env, atoms, grads, mean, order):
-    m = env.shape[0]
+def in_smem():
+    return pl.BlockSpec(memory_space=pltpu.SMEM)
+
+
+def in_vmem():
+    return pl.BlockSpec(memory_space=pltpu.VMEM)
+
+
+def panel_rows(where, own, other, atoms, grads, mean, order):
     return pl.pallas_call(
         panel_kernel,
         out_shape=(
-            jax.ShapeDtypeStruct((8, 64, m), BF16),
-            jax.ShapeDtypeStruct((m, m), F32),
-        ),
+            jax.ShapeDtypeStruct((4, 64, 512), BF16),
+            jax.ShapeDtypeStruct((4, 64, 512), BF16),
+            jax.ShapeDtypeStruct((1280, 128), F32),
+        ),
+        in_specs=[in_smem()] + [in_vmem()] * 6,
+        out_specs=(in_vmem(),) * 3,
+        scratch_shapes=[pltpu.VMEM((512, 1024), BF16)],
         compiler_params=params(),
         cost_estimate=pl.CostEstimate(
-            flops=2 * m * 1024 * 1088, bytes_accessed=5 << 20, transcendentals=0
-        ),
-    )(env, atoms, grads, mean, order)
-
-
-def trail_rows(core, own, other, atoms, grads, mean, order):
-    blocks = own.shape[0]
-    step = 4
-    half = pl.BlockSpec((step, 64, 1024), lambda i, core: (i, 0, 0))
-    whole = lambda shape: pl.BlockSpec(shape, lambda i, core: (0, 0))
+            flops=2 * 512 * 1024 * 1088, bytes_accessed=5 << 20, transcendentals=0
+        ),
+    )(where, own, other, atoms, grads, mean, order)
+
+
+def assemble(where, near, far, got):
+    return pl.pallas_call(
+        assemble_kernel,
+        out_shape=jax.ShapeDtypeStruct((8, 64, 512), BF16),
+        in_specs=[in_smem()] + [in_vmem()] * 5,
+        out_specs=in_vmem(),
+        compiler_params=params(),
+        cost_estimate=pl.CostEstimate(flops=0, bytes_accessed=1 << 20, transcendentals=0),
+    )(where, near, far, *got)
+
+
+def trail_rows(where, own, other, atoms, grads, mean, order):
+    piece = pl.BlockSpec((1, 4, 16, 1024), lambda i, w: (i, 0, 0, 0))
+    whole = lambda shape: pl.BlockSpec(shape, lambda i, w: (0, 0))
     return pl.pallas_call(
         trail_kernel,
-        out_shape=jax.ShapeDtypeStruct((8, blocks, 64, 128), BF16),
+        out_shape=jax.ShapeDtypeStruct((8, 16, 64, 128), BF16),
         grid_spec=pltpu.PrefetchScalarGridSpec(
             num_scalar_prefetch=1,
-            grid=(blocks // step,),
-            in_specs=[
-                half,
-                half,
+            grid=(4,),
+            in_specs=[piece] * 8
+            + [
                 whole(atoms.shape),
                 whole(grads.shape),
                 whole(mean.shape),
                 whole(order.shape),
             ],
-            out_specs=pl.BlockSpec((8, step, 64, 128), lambda i, core: (0, i, 0, 0)),
+            out_specs=pl.BlockSpec((8, 4, 64, 128), lambda i, w: (0, (w[0] - i) & 3, 0, 0)),
+            scratch_shapes=[pltpu.VMEM((512, 1024), BF16)],
         ),
         compiler_params=params(),
         cost_estimate=pl.CostEstimate(
             flops=2 * 2048 * 1024 * 1088, bytes_accessed=9 << 20, transcendentals=0
         ),
-    )(core.reshape(1).astype(jnp.int32), own, other, atoms, grads, mean, order)
+    )(where, *own, *other, atoms, grads, mean, order)
 
 
 def eliminate(a):
@@ -288,10 +356,16 @@
 
 
 def factor_kernel(rows_total, gram_ref, factor_ref, inverse_ref, work):
-    n = gram_ref.shape[0]
+    n = factor_ref.shape[0]
     r = lax.broadcasted_iota(jnp.int32, (n, n), 0)
     c = lax.broadcasted_iota(jnp.int32, (n, n), 1)
-    work[:, :n] = gram_ref[...] / rows_total + jnp.where(r == c, ridge_value, 0.0)
+    same = r[:128, :128] == c[:128, :128]
+    work[:, :n] = jnp.zeros((n, n), F32)
+    for m, (i, j) in enumerate(UPPER):
+        block = gram_ref[128 * m : 128 * m + 128] / rows_total
+        if i == j:
+            block = block + jnp.where(same, ridge_value, 0.0)
+        work[128 * i : 128 * i + 128, 128 * j : 128 * j + 128] = block
     work[:, n:] = jnp.where(r == c, 1.0, 0.0)
 
     def step(b, carry):
@@ -310,7 +384,7 @@
 
 
 def factor_panel(gram, rows_total):
-    n = gram.shape[0]
+    n = 512
     return pl.pallas_call(
         functools.partial(factor_kernel, float(rows_total)),
         out_shape=(jax.ShapeDtypeStruct((n, n), F32), jax.ShapeDtypeStruct((n, n), F32)),
@@ -420,14 +494,20 @@
     x, z = col // 4, col % 4
     rows_total = 65536
 
-    trail_half = lax.dynamic_slice_in_dim(sparse_trail, core * 64, 64, 0)
-    trail_half = lax.all_gather(trail_half, "col", axis=0, tiled=False)
-    own = lax.dynamic_slice_in_dim(sparse_panel, core * 16, 16, 0)
-    own = gather4(gather4(own, "col", z_shift, z), "col", x_shift, x)
-    low, high = swap_gather(own, core)
-    env_panel = jnp.stack(
-        [low.reshape(16, 16, 1024), high.reshape(16, 16, 1024)], axis=1
-    ).reshape(512, 1024)
+    where = jnp.stack([x, z, y, core]).astype(jnp.int32)
+
+    piece = jnp.concatenate(
+        [
+            lax.dynamic_slice_in_dim(sparse_panel, core * 16, 16, 0),
+            lax.dynamic_slice_in_dim(sparse_trail, row * 16, 16, 0),
+        ],
+        axis=0,
+    )
+    piece = jnp.stack(shifted(piece, "col", z_shift))
+    pieces = shifted(piece, "col", x_shift)
+    own = jnp.stack([p[:, :16] for p in pieces])
+    other = lax.ppermute(own, "row", CORE_SWAP)
+    own_trail = jnp.stack([p[:, 16:] for p in pieces])
 
     atoms, grads, mean, order = prepare(
         atom_counts,
@@ -437,15 +517,18 @@
         gradients.reshape(12, 128, 1024),
     )
 
-    panel, gram = panel_rows(env_panel, atoms, grads, mean, order)
-    panel = lax.all_to_all(panel, "row", 0, 0, tiled=True).reshape(512, 512)
-    panel, gram = lax.optimization_barrier((panel, gram))
+    near, far, gram = panel_rows(where, own, other, atoms, grads, mean, order)
+    far = lax.ppermute(far, "row", CORE_SWAP)
+    got = [
+        lax.ppermute(jnp.stack([near[s], far[s]]), "row", y_shift(s)) for s in (1, 2, 3)
+    ]
+    panel = assemble(where, near, far, got).reshape(512, 512)
     segment = lax.all_gather(panel, "col", axis=0, tiled=False)
     gram = sum_all(gram, core, y)
 
-    trail_half, gram = lax.optimization_barrier((trail_half, gram))
-    other_half = lax.ppermute(trail_half, "row", CORE_SWAP)
-    trail = trail_rows(core, trail_half, other_half, atoms, grads, mean, order)
+    trail_own = shifted(own_trail, "row", y_shift)
+    trail_other = [lax.ppermute(p, "row", CORE_SWAP) for p in trail_own]
+    trail = trail_rows(where, trail_own, trail_other, atoms, grads, mean, order)
     trail, gram = lax.optimization_barrier((trail, gram))
     trail = lax.all_to_all(
         trail.reshape(128, 64, 128), ("row", "col"), 0, 0, tiled=True

time: 197 us -> 196 us (level)
  blocking collectives: 13.8 us -> 0 us
  starting transfers between devices: 34 us -> 46.5 us
  Pallas kernels: 46.1 us -> 51.8 us
  waiting for transfers between devices: 65.8 us -> 61.8 us
  other arithmetic: 7.97 us -> 5.36 us
  local copies, waits for them, and re-layouts: 13.7 us -> 15.8 us
    ppermute x1 -> x18, waiting for transfers between devices: 4 us -> 27.4 us  [the longest x9 20.8 us: shifted(): return [v] + [lax.ppermute(v, axis, shift(s)) for s in (1, 2, 3)]]
    ppermute x1 -> x18, starting transfers between devices: 0.37 us -> 23.5 us  [the longest x9 13.1 us: shifted(): return [v] + [lax.ppermute(v, axis, shift(s)) for s in (1, 2, 3)]]
    all_to_all x1 -> x0, blocking collectives: 13.8 us -> none  [per_device(): panel = lax.all_to_all(panel, 'row', 0, 0, tiled=True).reshape(512, 512)]
    ppermute x9 -> x3, starting transfers between devices: 13.6 us -> 1.71 us  [gather4(): pieces = [v] + [lax.ppermute(v, axis, shift(s)) for s in (1, 2, 3)]]
    ppermute x9 -> x3, waiting for transfers between devices: 15.1 us -> 4.9 us  [gather4(): pieces = [v] + [lax.ppermute(v, axis, shift(s)) for s in (1, 2, 3)]]
    ppermute x9, waiting for transfers between devices: 28.1 us -> 20.5 us  [spread4(): got = [lax.ppermute(v, axis, shift(s)) for s in (1, 2, 3)]]
    pallas_call x2 -> x3, Pallas kernels: 8.64 us -> 14.4 us  [the longest x1 9.14 us: trail_rows(): pl.pallas_call(trail_kernel, out_shape=jax.ShapeDtypeStruct((8, 16, 64, 1...]
    ppermute x3, waiting for transfers between devices: 8.34 us -> 3.62 us  [scatter4(): lax.ppermute(lax.dynamic_slice_in_dim(v, (index + s) % 4 * n, n, 0), axis...]
  transfers between devices with their start and end apart: 30 -> 39, of which waited for: 26 -> 23; matrix products, arithmetic and copies ran while one was open for 6% -> 4% of each run, Pallas kernels for 19% -> 19%
where the time goes in v3:
time: 196 us
  waiting for transfers between devices  61.8 us (32%)
  Pallas kernels  51.8 us (26%)
  starting transfers between devices  46.5 us (24%)
  local copies, waits for them, and re-layouts  15.8 us (8%)
  between operations  14.4 us (7%)
  other arithmetic  5.36 us (3%)
    pallas_call x1, Pallas kernels, factor_panel(): pl.pallas_call(functools.partial(factor_kernel, float(rows_total)), out_s...  26.7 us
    ppermute x9, waiting for transfers between devices, shifted(): return [v] + [lax.ppermute(v, axis, shift(s)) for s in (1, 2, 3)]  20.8 us
    ppermute x9, waiting for transfers between devices, spread4(): got = [lax.ppermute(v, axis, shift(s)) for s in (1, 2, 3)]  20.5 us
    ppermute x9, starting transfers between devices, shifted(): return [v] + [lax.ppermute(v, axis, shift(s)) for s in (1, 2, 3)]  13.1 us
    unnamed x35, local copies, waits for them, and re-layouts  11.2 us
    pallas_call x1, Pallas kernels, trail_rows(): pl.pallas_call(trail_kernel, out_shape=jax.ShapeDtypeStruct((8, 16, 64, 1...  9.14 us
    ppermute x9, starting transfers between devices, spread4(): got = [lax.ppermute(v, axis, shift(s)) for s in (1, 2, 3)]  8.14 us
    pallas_call x1, Pallas kernels, residual(): pl.pallas_call(functools.partial(residual_kernel, float(rows_total)), out...  7.19 us
  transfers between devices with their start and end apart: 39, of which 23 were waited for; matrix products, arithmetic and copies ran while one was open for 4% of the time, Pallas kernels for 19%

profile of v3, /device:TPU:1, one launch (start us, length us, event | category | flops | bytes accessed | tf_op | source)
XLA Modules:
  0.0 195.7 jit_solution(6829758612462934689)
XLA Ops:
  8.2 4.5 %collective-permute-start.1 = (bf16[32,1024]{1,0:T(8,128)(2,1)S(1)}, bf16[32,1024]{1,0:T(8,128)(2,1)S(1)}, u32[]{:S(2)}, u32[]{:S(2)}) collective-permute-start(bf16[32,1024]{1,0:T(8,128)(2,1)S(1)} %get-tuple-element.59), channel_id=1, source_target_pairs={{0,2},{1,3},{2,0},{3,1},{4,6},{5,7},{6,4},{7,5},{8,10},{9,11},{10,... | collective-permute-start | bytes 196616 | tf_op jit(solution)/shard_map/ppermute | solution.py:47
  13.5 1.9 collective-permute-start.2
  15.4 1.6 collective-permute-done
  17.1 2.5 %collective-permute-start.5 = (bf16[4,32,1024]{2,1,0:T(8,128)(2,1)S(1)}, bf16[4,32,1024]{2,1,0:T(8,128)(2,1)S(1)}, u32[]{:S(2)}, u32[]{:S(2)}) collective-permute-start(bf16[4,32,1024]{2,1,0:T(8,128)(2,1)S(1)} %pad_maximum_fusion.4), channel_id=1, source_target_pairs={{0,12},{1,13},{2,14},{3,15},{4,0},{5,1},{6,2},{7,3},{8,4},{9,5},{1... | collective-permute-start | bytes 786440 | tf_op jit(solution)/shard_map/ppermute | solution.py:47
  20.9 3.9 %collective-permute-done.5 = bf16[4,32,1024]{2,1,0:T(8,128)(2,1)S(1)} collective-permute-done((bf16[4,32,1024]{2,1,0:T(8,128)(2,1)S(1)}, bf16[4,32,1024]{2,1,0:T(8,128)(2,1)S(1)}, u32[]{:S(2)}, u32[]{:S(2)}) %collective-permute-start.5) | collective-permute-done | bytes 262176 | tf_op jit(solution)/shard_map/ppermute | solution.py:47
  27.1 7.5 %collective-permute-done.3 = bf16[4,32,1024]{2,1,0:T(8,128)(2,1)S(1)} collective-permute-done((bf16[4,32,1024]{2,1,0:T(8,128)(2,1)S(1)}, bf16[4,32,1024]{2,1,0:T(8,128)(2,1)S(1)}, u32[]{:S(2)}, u32[]{:S(2)}) %collective-permute-start.3) | collective-permute-done | bytes 262176 | tf_op jit(solution)/shard_map/ppermute | solution.py:47
  40.7 3.9 %shard_map.96 = (bf16[4,64,512]{2,1,0:T(8,128)(2,1)S(1)}, bf16[4,64,512]{2,1,0:T(8,128)(2,1)S(1)}, f32[1280,128]{1,0:T(8,128)S(1)}) custom-call(s32[4]{0:T(128)S(1)} %pad_add_fusion.where, bf16[4,4,16,1024]{3,2,1,0:T(8,128)(2,1)} %pad_maximum_fusion.2.own, bf16[4,4,16,1024]{3,2,1,0:T(8,128)(2,1)} %collective-permute-done.13.other, ...), custom_call_target="tpu_custom_call" | custom-call | flops 1140850688 | bytes 5242880 | tf_op jit(solution)/shard_map/pallas_call | solution.py:268
  44.8 1.5 collective-permute-done.28.far
  47.7 2.7 %collective-permute-start.30 = (bf16[2,64,512]{2,1,0:T(8,128)(2,1)S(1)}, bf16[2,64,512]{2,1,0:T(8,128)(2,1)S(1)}, u32[]{:S(2)}, u32[]{:S(2)}) collective-permute-start(bf16[2,64,512]{2,1,0:T(8,128)(2,1)S(1)} %pad_maximum_fusion.7), channel_id=1, source_target_pairs={{0,64},{16,80},{32,96},{48,112},{64,0},{80,16},{96,32},{112,48},{1... | collective-permute-start | bytes 393224 | tf_op jit(solution)/shard_map/ppermute | solution.py:523
  52.7 3.9 %collective-permute-done.30.got2 = bf16[2,64,512]{2,1,0:T(8,128)(2,1)S(1)} collective-permute-done((bf16[2,64,512]{2,1,0:T(8,128)(2,1)S(1)}, bf16[2,64,512]{2,1,0:T(8,128)(2,1)S(1)}, u32[]{:S(2)}, u32[]{:S(2)}) %collective-permute-start.30) | collective-permute-done | bytes 131104 | tf_op jit(solution)/shard_map/ppermute | solution.py:523
  62.7 1.6 collective-permute-start.17
  66.5 2.6 %collective-permute-done.16 = f32[160,128]{1,0:T(8,128)S(1)} collective-permute-done((f32[160,128]{1,0:T(8,128)S(1)}, f32[160,128]{1,0:T(8,128)S(1)}, u32[]{:S(2)}, u32[]{:S(2)}) %collective-permute-start.16) | collective-permute-done | bytes 81952 | tf_op jit(solution)/shard_map/ppermute | solution.py:59
  69.1 2.7 %collective-permute-start.20 = (f32[160,128]{1,0:T(8,128)S(1)}, f32[160,128]{1,0:T(8,128)S(1)}, u32[]{:S(2)}, u32[]{:S(2)}) collective-permute-start(f32[160,128]{1,0:T(8,128)S(1)} %add_add_fusion.3), channel_id=1, source_target_pairs={{0,3},{1,0},{2,1},{3,2},{4,7},{5,4},{6,5},{7,6},{8,11},{9,8},{10,9... | collective-permute-start | bytes 245768 | tf_op jit(solution)/shard_map/ppermute | solution.py:81
  78.4 2.5 %collective-permute-start.23 = (f32[160,128]{1,0:T(8,128)S(1)}, f32[160,128]{1,0:T(8,128)S(1)}, u32[]{:S(2)}, u32[]{:S(2)}) collective-permute-start(f32[160,128]{1,0:T(8,128)S(1)} %add_add_fusion.2), channel_id=1, source_target_pairs={{0,12},{1,13},{2,14},{3,15},{4,0},{5,1},{6,2},{7,3},{8,4},{9,5},{1... | collective-permute-start | bytes 245768 | tf_op jit(solution)/shard_map/ppermute | solution.py:81
  81.0 2.4 %collective-permute-done.23 = f32[160,128]{1,0:T(8,128)S(1)} collective-permute-done((f32[160,128]{1,0:T(8,128)S(1)}, f32[160,128]{1,0:T(8,128)S(1)}, u32[]{:S(2)}, u32[]{:S(2)}) %collective-permute-start.23) | collective-permute-done | bytes 81952 | tf_op jit(solution)/shard_map/ppermute | solution.py:81
  83.4 3.5 %collective-permute-done.22 = f32[160,128]{1,0:T(8,128)S(1)} collective-permute-done((f32[160,128]{1,0:T(8,128)S(1)}, f32[160,128]{1,0:T(8,128)S(1)}, u32[]{:S(2)}, u32[]{:S(2)}) %collective-permute-start.22) | collective-permute-done | bytes 81952 | tf_op jit(solution)/shard_map/ppermute | solution.py:81
  86.9 3.5 %collective-permute-done.21 = f32[160,128]{1,0:T(8,128)S(1)} collective-permute-done((f32[160,128]{1,0:T(8,128)S(1)}, f32[160,128]{1,0:T(8,128)S(1)}, u32[]{:S(2)}, u32[]{:S(2)}) %collective-permute-start.21) | collective-permute-done | bytes 81952 | tf_op jit(solution)/shard_map/ppermute | solution.py:81
  92.1 3.6 %collective-permute-start.9 = (bf16[4,4,16,1024]{3,2,1,0:T(8,128)(2,1)S(1)}, bf16[4,4,16,1024]{3,2,1,0:T(8,128)(2,1)}, u32[]{:S(2)}, u32[]{:S(2)}) collective-permute-start(bf16[4,4,16,1024]{3,2,1,0:T(8,128)(2,1)S(1)} %pad_maximum_fusion.1.own0), channel_id=1, source_target_pairs={{0,16},{16,0},{32,48},{48,32},{64,80},{80,64},{96,112},{112,96},{1... | collective-permute-start | bytes 1572872 | tf_op jit(solution)/shard_map/ppermute | solution.py:530
  95.8 6.7 %collective-permute-done.6.own1 = bf16[4,4,16,1024]{3,2,1,0:T(8,128)(2,1)} collective-permute-done((bf16[4,4,16,1024]{3,2,1,0:T(8,128)(2,1)S(1)}, bf16[4,4,16,1024]{3,2,1,0:T(8,128)(2,1)}, u32[]{:S(2)}, u32[]{:S(2)}) %collective-permute-start.6) | collective-permute-done | bytes 524320 | tf_op jit(solution)/shard_map/ppermute | solution.py:47
  103.8 4.9 %collective-permute-done.24 = f32[160,128]{1,0:T(8,128)} collective-permute-done((f32[160,128]{1,0:T(8,128)S(1)}, f32[160,128]{1,0:T(8,128)}, u32[]{:S(2)}, u32[]{:S(2)}) %collective-permute-start.24) | collective-permute-done | bytes 81952 | tf_op jit(solution)/shard_map/ppermute | solution.py:51
  109.7 1.7 collective-permute-start.27
  112.4 9.1 %shard_map.95 = bf16[8,16,64,128]{3,2,1,0:T(8,128)(2,1)S(1)} custom-call(s32[4]{0:T(128)S(1)} %pad_add_fusion.where, bf16[4,4,16,1024]{3,2,1,0:T(8,128)(2,1)S(1)} %pad_maximum_fusion.1.own0, bf16[4,4,16,1024]{3,2,1,0:T(8,128)(2,1)} %collective-permute-done.6.own1, bf16[4,4,16,1024]{3,2,1,0:T(8,128)(2,1)} %collective-permute-done.7.own2, ...), custom_call_target="tpu_custom_call" | custom-call | flops 4563402752 | bytes 9437184 | tf_op jit(solution)/shard_map/pallas_call | solution.py:299
  123.1 4.7 %all-to-all-start = ((bf16[128,64,128]{2,1,0:T(8,128)(2,1)}), bf16[128,64,128]{2,1,0:T(8,128)(2,1)S(1)}, u32[]{:S(2)}, u32[]{:S(2)}) async-start(bf16[128,64,128]{2,1,0:T(8,128)(2,1)} %bitcast.35), calls=%async_computation | async-start | bytes 4194304 | tf_op jit(solution)/shard_map/all_to_all | solution.py:533
  128.8 26.7 %shard_map.97 = (f32[512,512]{1,0:T(8,128)}, f32[512,512]{1,0:T(8,128)S(1)}) custom-call(f32[1280,128]{1,0:T(8,128)S(1)} %copy-done.4), custom_call_target="tpu_custom_call" | custom-call | flops 2684354560 | bytes 4194304 | tf_op jit(solution)/shard_map/pallas_call | solution.py:388
  155.6 1.8 all-to-all-done
  157.4 3.4 %copy-done = bf16[16,512,512]{2,1,0:T(8,128)(2,1)S(1)} copy-done((bf16[16,512,512]{2,1,0:T(8,128)(2,1)S(1)}, bf16[16,512,512]{2,1,0:T(8,128)(2,1)}, u32[]{:S(2)}) %copy-start) | copy-done | bytes 8388632
  160.8 2.1 %shard_map.99 = f32[128,512]{1,0:T(8,128)S(1)} custom-call(bf16[16,512,512]{2,1,0:T(8,128)(2,1)S(1)} %copy-done, bf16[8,16,64,128]{3,2,1,0:T(8,128)(2,1)S(1)} %bitcast.32), custom_call_target="tpu_custom_call" | custom-call | flops 1073741824 | bytes 11534336 | tf_op jit(solution)/shard_map/pallas_call | solution.py:413
  168.1 2.6 %collective-permute-done.35 = f32[64,512]{1,0:T(8,128)S(1)} collective-permute-done((f32[64,512]{1,0:T(8,128)S(1)}, f32[64,512]{1,0:T(8,128)S(1)}, u32[]{:S(2)}, u32[]{:S(2)}) %collective-permute-start.35) | collective-permute-done | bytes 131104 | tf_op jit(solution)/shard_map/ppermute | solution.py:81
  170.7 2.1 %collective-permute-done.34 = f32[64,512]{1,0:T(8,128)S(1)} collective-permute-done((f32[64,512]{1,0:T(8,128)S(1)}, f32[64,512]{1,0:T(8,128)S(1)}, u32[]{:S(2)}, u32[]{:S(2)}) %collective-permute-start.34) | collective-permute-done | bytes 131104 | tf_op jit(solution)/shard_map/ppermute | solution.py:81
  172.8 3.6 %collective-permute-done.33 = f32[64,512]{1,0:T(8,128)S(1)} collective-permute-done((f32[64,512]{1,0:T(8,128)S(1)}, f32[64,512]{1,0:T(8,128)S(1)}, u32[]{:S(2)}, u32[]{:S(2)}) %collective-permute-start.33) | collective-permute-done | bytes 131104 | tf_op jit(solution)/shard_map/ppermute | solution.py:81
  178.3 3.4 %copy-done.1 = bf16[16,512,512]{2,1,0:T(8,128)(2,1)S(1)} copy-done((bf16[16,512,512]{2,1,0:T(8,128)(2,1)S(1)}, bf16[16,512,512]{2,1,0:T(8,128)(2,1)}, u32[]{:S(2)}) %copy-start.1) | copy-done | bytes 8388632
  181.7 7.2 %shard_map.100 = (f32[128,512]{1,0:T(8,128)}, f32[128,8192]{1,0:T(8,128)}) custom-call(f32[128,512]{1,0:T(8,128)S(1)} %pad_maximum_fusion.5.cross_ref, f32[512,512]{1,0:T(8,128)S(1)} %get-tuple-element.30.inverse_ref, bf16[16,512,512]{2,1,0:T(8,128)(2,1)S(1)} %copy-done.1, bf16[8,16,64,128]{3,2,1,0:T(8,128)(2,1)S(1)} %bitcast.33), custom_call_target="tpu_custom_call" | custom-call | flops 2147483648 | bytes 16777216 | tf_op jit(solution)/shard_map/pallas_call | solution.py:454
  (120 shorter events, 44.7 us)
Async XLA Ops:
  7.2 148.4 %all-gather.2.cloned.1.call-start = ((), (), s32[]{:S(2)}) async-start(), calls=%async_computation.1 | async-start | bytes 8912896 | tf_op jit(solution)/shard_map/all_gather | solution.py:526
  8.2 7.2 %collective-permute-start.1 = (bf16[32,1024]{1,0:T(8,128)(2,1)S(1)}, bf16[32,1024]{1,0:T(8,128)(2,1)S(1)}, u32[]{:S(2)}, u32[]{:S(2)}) collective-permute-start(bf16[32,1024]{1,0:T(8,128)(2,1)S(1)} %get-tuple-element.59), channel_id=1, source_target_pairs={{0,2},{1,3},{2,0},{3,1},{4,6},{5,7},{6,4},{7,5},{8,10},{9,11},{10,... | collective-permute-start | bytes 196616 | tf_op jit(solution)/shard_map/ppermute | solution.py:47
  17.1 7.7 %collective-permute-start.5 = (bf16[4,32,1024]{2,1,0:T(8,128)(2,1)S(1)}, bf16[4,32,1024]{2,1,0:T(8,128)(2,1)S(1)}, u32[]{:S(2)}, u32[]{:S(2)}) collective-permute-start(bf16[4,32,1024]{2,1,0:T(8,128)(2,1)S(1)} %pad_maximum_fusion.4), channel_id=1, source_target_pairs={{0,12},{1,13},{2,14},{3,15},{4,0},{5,1},{6,2},{7,3},{8,4},{9,5},{1... | collective-permute-start | bytes 786440 | tf_op jit(solution)/shard_map/ppermute | solution.py:47
  19.6 6.8 %collective-permute-start.4 = (bf16[4,32,1024]{2,1,0:T(8,128)(2,1)S(1)}, bf16[4,32,1024]{2,1,0:T(8,128)(2,1)S(1)}, u32[]{:S(2)}, u32[]{:S(2)}) collective-permute-start(bf16[4,32,1024]{2,1,0:T(8,128)(2,1)S(1)} %pad_maximum_fusion.4), channel_id=1, source_target_pairs={{0,8},{1,9},{2,10},{3,11},{4,12},{5,13},{6,14},{7,15},{8,0},{9,1},... | collective-permute-start | bytes 786440 | tf_op jit(solution)/shard_map/ppermute | solution.py:47
  20.2 14.5 %collective-permute-start.3 = (bf16[4,32,1024]{2,1,0:T(8,128)(2,1)S(1)}, bf16[4,32,1024]{2,1,0:T(8,128)(2,1)S(1)}, u32[]{:S(2)}, u32[]{:S(2)}) collective-permute-start(bf16[4,32,1024]{2,1,0:T(8,128)(2,1)S(1)} %pad_maximum_fusion.4), channel_id=1, source_target_pairs={{0,4},{1,5},{2,6},{3,7},{4,8},{5,9},{6,10},{7,11},{8,12},{9,13},{1... | collective-permute-start | bytes 786440 | tf_op jit(solution)/shard_map/ppermute | solution.py:47
  36.2 4.5 %collective-permute-start.13 = (bf16[4,4,16,1024]{3,2,1,0:T(8,128)(2,1)}, bf16[4,4,16,1024]{3,2,1,0:T(8,128)(2,1)}, u32[]{:S(2)}, u32[]{:S(2)}) collective-permute-start(bf16[4,4,16,1024]{3,2,1,0:T(8,128)(2,1)} %pad_maximum_fusion.2.own), channel_id=1, source_target_pairs={{0,16},{16,0},{32,48},{48,32},{64,80},{80,64},{96,112},{112,96},{1... | collective-permute-start | bytes 1572872 | tf_op jit(solution)/shard_map/ppermute | solution.py:509
  46.3 6.4 %collective-permute-start.29 = (bf16[2,64,512]{2,1,0:T(8,128)(2,1)S(1)}, bf16[2,64,512]{2,1,0:T(8,128)(2,1)S(1)}, u32[]{:S(2)}, u32[]{:S(2)}) collective-permute-start(bf16[2,64,512]{2,1,0:T(8,128)(2,1)S(1)} %pad_maximum_fusion.6), channel_id=1, source_target_pairs={{0,32},{16,48},{32,64},{48,80},{64,96},{80,112},{96,0},{112,16},{1... | collective-permute-start | bytes 393224 | tf_op jit(solution)/shard_map/ppermute | solution.py:523
  47.7 8.9 %collective-permute-start.30 = (bf16[2,64,512]{2,1,0:T(8,128)(2,1)S(1)}, bf16[2,64,512]{2,1,0:T(8,128)(2,1)S(1)}, u32[]{:S(2)}, u32[]{:S(2)}) collective-permute-start(bf16[2,64,512]{2,1,0:T(8,128)(2,1)S(1)} %pad_maximum_fusion.7), channel_id=1, source_target_pairs={{0,64},{16,80},{32,96},{48,112},{64,0},{80,16},{96,32},{112,48},{1... | collective-permute-start | bytes 393224 | tf_op jit(solution)/shard_map/ppermute | solution.py:523
  50.4 6.2 %collective-permute-start.31 = (bf16[2,64,512]{2,1,0:T(8,128)(2,1)S(1)}, bf16[2,64,512]{2,1,0:T(8,128)(2,1)S(1)}, u32[]{:S(2)}, u32[]{:S(2)}) collective-permute-start(bf16[2,64,512]{2,1,0:T(8,128)(2,1)S(1)} %pad_maximum_fusion.8), channel_id=1, source_target_pairs={{0,96},{16,112},{32,0},{48,16},{64,32},{80,48},{96,64},{112,80},{1... | collective-permute-start | bytes 393224 | tf_op jit(solution)/shard_map/ppermute | solution.py:523
  61.5 4.9 %collective-permute-start.15 = (f32[160,128]{1,0:T(8,128)S(1)}, f32[160,128]{1,0:T(8,128)S(1)}, u32[]{:S(2)}, u32[]{:S(2)}) collective-permute-start(f32[160,128]{1,0:T(8,128)S(1)} %get-tuple-element.39), channel_id=1, source_target_pairs={{0,32},{16,48},{32,64},{48,80},{64,96},{80,112},{96,0},{112,16},{1... | collective-permute-start | bytes 245768 | tf_op jit(solution)/shard_map/ppermute | solution.py:59
  64.3 4.8 %collective-permute-start.16 = (f32[160,128]{1,0:T(8,128)S(1)}, f32[160,128]{1,0:T(8,128)S(1)}, u32[]{:S(2)}, u32[]{:S(2)}) collective-permute-start(f32[160,128]{1,0:T(8,128)S(1)} %get-tuple-element.41), channel_id=1, source_target_pairs={{0,64},{16,80},{32,96},{48,112},{64,0},{80,16},{96,32},{112,48},{1... | collective-permute-start | bytes 245768 | tf_op jit(solution)/shard_map/ppermute | solution.py:59
  69.1 6.6 %collective-permute-start.20 = (f32[160,128]{1,0:T(8,128)S(1)}, f32[160,128]{1,0:T(8,128)S(1)}, u32[]{:S(2)}, u32[]{:S(2)}) collective-permute-start(f32[160,128]{1,0:T(8,128)S(1)} %add_add_fusion.3), channel_id=1, source_target_pairs={{0,3},{1,0},{2,1},{3,2},{4,7},{5,4},{6,5},{7,6},{8,11},{9,8},{10,9... | collective-permute-start | bytes 245768 | tf_op jit(solution)/shard_map/ppermute | solution.py:81
  71.8 5.2 %collective-permute-start.19 = (f32[160,128]{1,0:T(8,128)S(1)}, f32[160,128]{1,0:T(8,128)S(1)}, u32[]{:S(2)}, u32[]{:S(2)}) collective-permute-start(f32[160,128]{1,0:T(8,128)S(1)} %add_add_fusion.3), channel_id=1, source_target_pairs={{0,2},{1,3},{2,0},{3,1},{4,6},{5,7},{6,4},{7,5},{8,10},{9,11},{10,... | collective-permute-start | bytes 245768 | tf_op jit(solution)/shard_map/ppermute | solution.py:81
  71.8 6.6 %collective-permute-start.18 = (f32[160,128]{1,0:T(8,128)S(1)}, f32[160,128]{1,0:T(8,128)S(1)}, u32[]{:S(2)}, u32[]{:S(2)}) collective-permute-start(f32[160,128]{1,0:T(8,128)S(1)} %add_add_fusion.3), channel_id=1, source_target_pairs={{0,1},{1,2},{2,3},{3,0},{4,5},{5,6},{6,7},{7,4},{8,9},{9,10},{10,1... | collective-permute-start | bytes 245768 | tf_op jit(solution)/shard_map/ppermute | solution.py:81
  73.5 18.6 %collective-permute-start.8 = (bf16[4,4,16,1024]{3,2,1,0:T(8,128)(2,1)S(1)}, bf16[4,4,16,1024]{3,2,1,0:T(8,128)(2,1)S(1)}, u32[]{:S(2)}, u32[]{:S(2)}) collective-permute-start(bf16[4,4,16,1024]{3,2,1,0:T(8,128)(2,1)S(1)} %pad_maximum_fusion.1.own0), channel_id=1, source_target_pairs={{0,96},{16,112},{32,0},{48,16},{64,32},{80,48},{96,64},{112,80},{1... | collective-permute-start | bytes 1572872 | tf_op jit(solution)/shard_map/ppermute | solution.py:47
  75.0 20.8 %collective-permute-start.7 = (bf16[4,4,16,1024]{3,2,1,0:T(8,128)(2,1)S(1)}, bf16[4,4,16,1024]{3,2,1,0:T(8,128)(2,1)}, u32[]{:S(2)}, u32[]{:S(2)}) collective-permute-start(bf16[4,4,16,1024]{3,2,1,0:T(8,128)(2,1)S(1)} %pad_maximum_fusion.1.own0), channel_id=1, source_target_pairs={{0,64},{16,80},{32,96},{48,112},{64,0},{80,16},{96,32},{112,48},{1... | collective-permute-start | bytes 1572872 | tf_op jit(solution)/shard_map/ppermute | solution.py:47
  75.7 26.9 %collective-permute-start.6 = (bf16[4,4,16,1024]{3,2,1,0:T(8,128)(2,1)S(1)}, bf16[4,4,16,1024]{3,2,1,0:T(8,128)(2,1)}, u32[]{:S(2)}, u32[]{:S(2)}) collective-permute-start(bf16[4,4,16,1024]{3,2,1,0:T(8,128)(2,1)S(1)} %pad_maximum_fusion.1.own0), channel_id=1, source_target_pairs={{0,32},{16,48},{32,64},{48,80},{64,96},{80,112},{96,0},{112,16},{1... | collective-permute-start | bytes 1572872 | tf_op jit(solution)/shard_map/ppermute | solution.py:47
  78.4 5.0 %collective-permute-start.23 = (f32[160,128]{1,0:T(8,128)S(1)}, f32[160,128]{1,0:T(8,128)S(1)}, u32[]{:S(2)}, u32[]{:S(2)}) collective-permute-start(f32[160,128]{1,0:T(8,128)S(1)} %add_add_fusion.2), channel_id=1, source_target_pairs={{0,12},{1,13},{2,14},{3,15},{4,0},{5,1},{6,2},{7,3},{8,4},{9,5},{1... | collective-permute-start | bytes 245768 | tf_op jit(solution)/shard_map/ppermute | solution.py:81
  80.9 5.9 %collective-permute-start.22 = (f32[160,128]{1,0:T(8,128)S(1)}, f32[160,128]{1,0:T(8,128)S(1)}, u32[]{:S(2)}, u32[]{:S(2)}) collective-permute-start(f32[160,128]{1,0:T(8,128)S(1)} %add_add_fusion.2), channel_id=1, source_target_pairs={{0,8},{1,9},{2,10},{3,11},{4,12},{5,13},{6,14},{7,15},{8,0},{9,1},... | collective-permute-start | bytes 245768 | tf_op jit(solution)/shard_map/ppermute | solution.py:81
  83.4 7.0 %collective-permute-start.21 = (f32[160,128]{1,0:T(8,128)S(1)}, f32[160,128]{1,0:T(8,128)S(1)}, u32[]{:S(2)}, u32[]{:S(2)}) collective-permute-start(f32[160,128]{1,0:T(8,128)S(1)} %add_add_fusion.2), channel_id=1, source_target_pairs={{0,4},{1,5},{2,6},{3,7},{4,8},{5,9},{6,10},{7,11},{8,12},{9,13},{1... | collective-permute-start | bytes 245768 | tf_op jit(solution)/shard_map/ppermute | solution.py:81
  90.4 12.6 %collective-permute-start.26 = (f32[160,128]{1,0:T(8,128)S(1)}, f32[160,128]{1,0:T(8,128)S(1)}, u32[]{:S(2)}, u32[]{:S(2)}) collective-permute-start(f32[160,128]{1,0:T(8,128)S(1)} %add_add_fusion.1), channel_id=1, source_target_pairs={{0,96},{16,112},{32,0},{48,16},{64,32},{80,48},{96,64},{112,80},{1... | collective-permute-start | bytes 245768 | tf_op jit(solution)/shard_map/ppermute | solution.py:51
  91.8 11.4 %collective-permute-start.25 = (f32[160,128]{1,0:T(8,128)S(1)}, f32[160,128]{1,0:T(8,128)S(1)}, u32[]{:S(2)}, u32[]{:S(2)}) collective-permute-start(f32[160,128]{1,0:T(8,128)S(1)} %add_add_fusion.1), channel_id=1, source_target_pairs={{0,64},{16,80},{32,96},{48,112},{64,0},{80,16},{96,32},{112,48},{1... | collective-permute-start | bytes 245768 | tf_op jit(solution)/shard_map/ppermute | solution.py:51
  92.1 19.3 %collective-permute-start.9 = (bf16[4,4,16,1024]{3,2,1,0:T(8,128)(2,1)S(1)}, bf16[4,4,16,1024]{3,2,1,0:T(8,128)(2,1)}, u32[]{:S(2)}, u32[]{:S(2)}) collective-permute-start(bf16[4,4,16,1024]{3,2,1,0:T(8,128)(2,1)S(1)} %pad_maximum_fusion.1.own0), channel_id=1, source_target_pairs={{0,16},{16,0},{32,48},{48,32},{64,80},{80,64},{96,112},{112,96},{1... | collective-permute-start | bytes 1572872 | tf_op jit(solution)/shard_map/ppermute | solution.py:530
  95.7 15.7 %collective-permute-start.12 = (bf16[4,4,16,1024]{3,2,1,0:T(8,128)(2,1)S(1)}, bf16[4,4,16,1024]{3,2,1,0:T(8,128)(2,1)}, u32[]{:S(2)}, u32[]{:S(2)}) collective-permute-start(bf16[4,4,16,1024]{3,2,1,0:T(8,128)(2,1)S(1)} %collective-permute-done.8.own3), channel_id=1, source_target_pairs={{0,16},{16,0},{32,48},{48,32},{64,80},{80,64},{96,112},{112,96},{1... | collective-permute-start | bytes 1572872 | tf_op jit(solution)/shard_map/ppermute | solution.py:530
  102.5 8.8 %collective-permute-start.11 = (bf16[4,4,16,1024]{3,2,1,0:T(8,128)(2,1)}, bf16[4,4,16,1024]{3,2,1,0:T(8,128)(2,1)}, u32[]{:S(2)}, u32[]{:S(2)}) collective-permute-start(bf16[4,4,16,1024]{3,2,1,0:T(8,128)(2,1)} %collective-permute-done.7.own2), channel_id=1, source_target_pairs={{0,16},{16,0},{32,48},{48,32},{64,80},{80,64},{96,112},{112,96},{1... | collective-permute-start | bytes 1572872 | tf_op jit(solution)/shard_map/ppermute | solution.py:530
  103.0 8.4 %collective-permute-start.10 = (bf16[4,4,16,1024]{3,2,1,0:T(8,128)(2,1)}, bf16[4,4,16,1024]{3,2,1,0:T(8,128)(2,1)}, u32[]{:S(2)}, u32[]{:S(2)}) collective-permute-start(bf16[4,4,16,1024]{3,2,1,0:T(8,128)(2,1)} %collective-permute-done.6.own1), channel_id=1, source_target_pairs={{0,16},{16,0},{32,48},{48,32},{64,80},{80,64},{96,112},{112,96},{1... | collective-permute-start | bytes 1572872 | tf_op jit(solution)/shard_map/ppermute | solution.py:530
  103.8 4.9 %collective-permute-start.24 = (f32[160,128]{1,0:T(8,128)S(1)}, f32[160,128]{1,0:T(8,128)}, u32[]{:S(2)}, u32[]{:S(2)}) collective-permute-start(f32[160,128]{1,0:T(8,128)S(1)} %add_add_fusion.1), channel_id=1, source_target_pairs={{0,32},{16,48},{32,64},{48,80},{64,96},{80,112},{96,0},{112,16},{1... | collective-permute-start | bytes 245768 | tf_op jit(solution)/shard_map/ppermute | solution.py:51
  109.7 11.8 %collective-permute-start.27 = (f32[640,128]{1,0:T(8,128)S(1)}, f32[640,128]{1,0:T(8,128)S(1)}, u32[]{:S(2)}, u32[]{:S(2)}) collective-permute-start(f32[640,128]{1,0:T(8,128)S(1)} %pad_maximum_fusion.3), channel_id=1, source_target_pairs={{0,16},{16,0},{32,48},{48,32},{64,80},{80,64},{96,112},{112,96},{1... | collective-permute-start | bytes 983048 | tf_op jit(solution)/shard_map/ppermute | solution.py:75
  123.1 34.3 %all-to-all-start = ((bf16[128,64,128]{2,1,0:T(8,128)(2,1)}), bf16[128,64,128]{2,1,0:T(8,128)(2,1)S(1)}, u32[]{:S(2)}, u32[]{:S(2)}) async-start(bf16[128,64,128]{2,1,0:T(8,128)(2,1)} %bitcast.35), calls=%async_computation | async-start | bytes 4194304 | tf_op jit(solution)/shard_map/all_to_all | solution.py:533
  165.9 4.8 %collective-permute-start.35 = (f32[64,512]{1,0:T(8,128)S(1)}, f32[64,512]{1,0:T(8,128)S(1)}, u32[]{:S(2)}, u32[]{:S(2)}) collective-permute-start(f32[64,512]{1,0:T(8,128)S(1)} %dynamic-slice_add_fusion.1), channel_id=1, source_target_pairs={{0,96},{16,112},{32,0},{48,16},{64,32},{80,48},{96,64},{112,80},{1... | collective-permute-start | bytes 393224 | tf_op jit(solution)/shard_map/ppermute | solution.py:81
  166.9 5.9 %collective-permute-start.34 = (f32[64,512]{1,0:T(8,128)S(1)}, f32[64,512]{1,0:T(8,128)S(1)}, u32[]{:S(2)}, u32[]{:S(2)}) collective-permute-start(f32[64,512]{1,0:T(8,128)S(1)} %dynamic-slice_add_fusion.1), channel_id=1, source_target_pairs={{0,64},{16,80},{32,96},{48,112},{64,0},{80,16},{96,32},{112,48},{1... | collective-permute-start | bytes 393224 | tf_op jit(solution)/shard_map/ppermute | solution.py:81
  168.1 8.4 %collective-permute-start.33 = (f32[64,512]{1,0:T(8,128)S(1)}, f32[64,512]{1,0:T(8,128)S(1)}, u32[]{:S(2)}, u32[]{:S(2)}) collective-permute-start(f32[64,512]{1,0:T(8,128)S(1)} %dynamic-slice_add_fusion.1), channel_id=1, source_target_pairs={{0,32},{16,48},{32,64},{48,80},{64,96},{80,112},{96,0},{112,16},{1... | collective-permute-start | bytes 393224 | tf_op jit(solution)/shard_map/ppermute | solution.py:81
  (24 other events, 333.0 us)
Sparse Core Ops, SparseCore 0:
  58.1 73.3 all-gather.1

commit v4 on v3

--- a/solution.py
+++ b/solution.py
@@ -213,29 +213,13 @@
 
 
 def trail_kernel(
-    where,
-    own0,
-    own1,
-    own2,
-    own3,
-    other0,
-    other1,
-    other2,
-    other3,
-    atoms_ref,
-    grads_ref,
-    mean_ref,
-    order_ref,
-    out_ref,
-    env,
+    where, own, other, atoms_ref, grads_ref, mean_ref, order_ref, out_ref, env
 ):
     z, y = where[1], where[2]
-    pairs = [(own0, other0), (own1, other1), (own2, other2), (own3, other3)]
     for j in range(4):
         place = ((z - j) & 3) * 128
         for s in range(4):
-            own, other = pairs[s]
-            put_env(env, where, own, other, (0, j), place + ((y - s) & 3) * 32)
+            put_env(env, where, own, other, (s, 0, j), place + ((y - s) & 3) * 32)
     rows = compact_rows(env[...], atoms_ref[...], grads_ref[...], mean_ref[...])
     full = dot(order_ref[...], rows, NN).astype(BF16)
     for c in range(out_ref.shape[1]):
@@ -252,8 +236,8 @@
         out[at + 1 - core] = got[1]
 
 
-def params():
-    return pltpu.CompilerParams(vmem_limit_bytes=40 << 20)
+def params(mib=40):
+    return pltpu.CompilerParams(vmem_limit_bytes=mib << 20)
 
 
 def in_smem():
@@ -294,7 +278,7 @@
 
 
 def trail_rows(where, own, other, atoms, grads, mean, order):
-    piece = pl.BlockSpec((1, 4, 16, 1024), lambda i, w: (i, 0, 0, 0))
+    piece = pl.BlockSpec((4, 1, 4, 16, 1024), lambda i, w: (0, i, 0, 0, 0))
     whole = lambda shape: pl.BlockSpec(shape, lambda i, w: (0, 0))
     return pl.pallas_call(
         trail_kernel,
@@ -302,7 +286,7 @@
         grid_spec=pltpu.PrefetchScalarGridSpec(
             num_scalar_prefetch=1,
             grid=(4,),
-            in_specs=[piece] * 8
+            in_specs=[piece] * 2
             + [
                 whole(atoms.shape),
                 whole(grads.shape),
@@ -316,7 +300,7 @@
         cost_estimate=pl.CostEstimate(
             flops=2 * 2048 * 1024 * 1088, bytes_accessed=9 << 20, transcendentals=0
         ),
-    )(where, *own, *other, atoms, grads, mean, order)
+    )(where, own, other, atoms, grads, mean, order)
 
 
 def eliminate(a):
@@ -419,7 +403,7 @@
             pl.BlockSpec((8, 4, 64, 128), lambda i: (0, i, 0, 0)),
         ],
         out_specs=pl.BlockSpec((128, n), lambda i: (0, 0)),
-        compiler_params=params(),
+        compiler_params=params(58),
         cost_estimate=pl.CostEstimate(
             flops=2 * 128 * n * 8192, bytes_accessed=11 << 20, transcendentals=0
         ),
@@ -466,18 +450,11 @@
         ],
         out_specs=(whole((128, n)), pl.BlockSpec((128, 2048), lambda i: (0, i))),
         scratch_shapes=[pltpu.VMEM((256, n), BF16)],
-        compiler_params=params(),
+        compiler_params=params(58),
         cost_estimate=pl.CostEstimate(
             flops=4 * 128 * n * 8192, bytes_accessed=16 << 20, transcendentals=0
         ),
     )(cross, inverse, segment, trail)
-
-
-def sum_all(v, core, y):
-    v = scatter4(swap_add(v, core), "row", y_shift, y)
-    v = spread4(spread4(v, "col", z_shift), "col", x_shift)
-    v = gather4(v, "row", y_shift, y)
-    return jnp.concatenate(swap_gather(v, core), axis=0)
 
 
 def sum_row(v, core):
@@ -503,11 +480,13 @@
         ],
         axis=0,
     )
-    piece = jnp.stack(shifted(piece, "col", z_shift))
-    pieces = shifted(piece, "col", x_shift)
-    own = jnp.stack([p[:, :16] for p in pieces])
+    pieces = shifted(piece, "col", z_shift)
+    piece = jnp.stack([p[:16] for p in pieces])
+    piece_trail = jnp.stack([p[16:] for p in pieces])
+    own = jnp.stack(shifted(piece, "col", x_shift))
+    own, piece_trail = lax.optimization_barrier((own, piece_trail))
     other = lax.ppermute(own, "row", CORE_SWAP)
-    own_trail = jnp.stack([p[:, 16:] for p in pieces])
+    own_trail = jnp.stack(shifted(piece_trail, "col", x_shift))
 
     atoms, grads, mean, order = prepare(
         atom_counts,
@@ -518,18 +497,24 @@
     )
 
     near, far, gram = panel_rows(where, own, other, atoms, grads, mean, order)
+    far, own_trail = lax.optimization_barrier((far, own_trail))
     far = lax.ppermute(far, "row", CORE_SWAP)
     got = [
         lax.ppermute(jnp.stack([near[s], far[s]]), "row", y_shift(s)) for s in (1, 2, 3)
     ]
     panel = assemble(where, near, far, got).reshape(512, 512)
     segment = lax.all_gather(panel, "col", axis=0, tiled=False)
-    gram = sum_all(gram, core, y)
-
-    trail_own = shifted(own_trail, "row", y_shift)
-    trail_other = [lax.ppermute(p, "row", CORE_SWAP) for p in trail_own]
+    gram = scatter4(swap_add(gram, core), "row", y_shift, y)
+    trail_own = jnp.stack(shifted(own_trail, "row", y_shift))
+    trail_own, gram = lax.optimization_barrier((trail_own, gram))
+    trail_other = lax.ppermute(trail_own, "row", CORE_SWAP)
+    gram = spread4(gram, "col", z_shift)
+    trail_other, gram = lax.optimization_barrier((trail_other, gram))
+    gram = spread4(gram, "col", x_shift)
     trail = trail_rows(where, trail_own, trail_other, atoms, grads, mean, order)
     trail, gram = lax.optimization_barrier((trail, gram))
+    gram = gather4(gram, "row", y_shift, y)
+    gram = jnp.concatenate(swap_gather(gram, core), axis=0)
     trail = lax.all_to_all(
         trail.reshape(128, 64, 128), ("row", "col"), 0, 0, tiled=True
     ).reshape(8, 16, 64, 128)

time: 196 us -> 230 us (1.17)
  waiting for transfers between devices: 61.8 us -> 89 us
  local copies, waits for them, and re-layouts: 15.8 us -> 7.82 us
  starting transfers between devices: 46.5 us -> 53.7 us
  Pallas kernels: 51.8 us -> 57.6 us
    ppermute x3, waiting for transfers between devices: 3.62 us -> 25.4 us  [scatter4(): lax.ppermute(lax.dynamic_slice_in_dim(v, (index + s) % 4 * n, n, 0), axis...]
    ppermute x3, waiting for transfers between devices: 4.9 us -> 24.8 us  [gather4(): pieces = [v] + [lax.ppermute(v, axis, shift(s)) for s in (1, 2, 3)]]
    ppermute x9 -> x12, waiting for transfers between devices: 20.8 us -> 13.2 us  [shifted(): return [v] + [lax.ppermute(v, axis, shift(s)) for s in (1, 2, 3)]]
    unnamed x35 -> x21, local copies, waits for them, and re-layouts: 11.2 us -> 4.21 us
    ppermute x9 -> x12, starting transfers between devices: 13.1 us -> 17.8 us  [shifted(): return [v] + [lax.ppermute(v, axis, shift(s)) for s in (1, 2, 3)]]
    ppermute x9, waiting for transfers between devices: 20.5 us -> 16.4 us  [spread4(): got = [lax.ppermute(v, axis, shift(s)) for s in (1, 2, 3)]]
    all_to_all x1, starting transfers between devices: 4.67 us -> 8.65 us  [per_device(): lax.all_to_all(trail.reshape(128, 64, 128), ('row', 'col'), 0, 0, tiled=T...]
    pallas_call x1, Pallas kernels: 2.09 us -> 5.97 us  [cross_part(): pl.pallas_call(cross_kernel, out_shape=jax.ShapeDtypeStruct((128, n), F32...]
  transfers between devices with their start and end apart: 39 -> 39, of which waited for: 23 -> 24; matrix products, arithmetic and copies ran while one was open for 4% -> 3% of each run, Pallas kernels for 19% -> 16%
where the time goes in v4:
time: 230 us
  waiting for transfers between devices  89 us (39%)
  Pallas kernels  57.6 us (25%)
  starting transfers between devices  53.7 us (23%)
  between operations  14.3 us (6%)
  local copies, waits for them, and re-layouts  7.82 us (3%)
  other arithmetic  7.37 us (3%)
    pallas_call x1, Pallas kernels, factor_panel(): pl.pallas_call(functools.partial(factor_kernel, float(rows_total)), out_s...  26.7 us
    ppermute x3, waiting for transfers between devices, scatter4(): lax.ppermute(lax.dynamic_slice_in_dim(v, (index + s) % 4 * n, n, 0), axis...  25.4 us
    ppermute x3, waiting for transfers between devices, gather4(): pieces = [v] + [lax.ppermute(v, axis, shift(s)) for s in (1, 2, 3)]  24.8 us
    ppermute x12, starting transfers between devices, shifted(): return [v] + [lax.ppermute(v, axis, shift(s)) for s in (1, 2, 3)]  17.8 us
    ppermute x9, waiting for transfers between devices, spread4(): got = [lax.ppermute(v, axis, shift(s)) for s in (1, 2, 3)]  16.4 us
    ppermute x12, waiting for transfers between devices, shifted(): return [v] + [lax.ppermute(v, axis, shift(s)) for s in (1, 2, 3)]  13.2 us
    pallas_call x1, Pallas kernels, residual(): pl.pallas_call(functools.partial(residual_kernel, float(rows_total)), out...  10.3 us
    pallas_call x1, Pallas kernels, trail_rows(): pl.pallas_call(trail_kernel, out_shape=jax.ShapeDtypeStruct((8, 16, 64, 1...  8.87 us
  transfers between devices with their start and end apart: 39, of which 24 were waited for; matrix products, arithmetic and copies ran while one was open for 3% of the time, Pallas kernels for 16%

profile of v4, /device:TPU:1, one launch (start us, length us, event | category | flops | bytes accessed | tf_op | source)
XLA Modules:
  0.0 229.7 jit_solution(13673406882417935428)
XLA Ops:
  8.1 4.7 %collective-permute-start.2 = (bf16[32,1024]{1,0:T(8,128)(2,1)S(1)}, bf16[32,1024]{1,0:T(8,128)(2,1)S(1)}, u32[]{:S(2)}, u32[]{:S(2)}) collective-permute-start(bf16[32,1024]{1,0:T(8,128)(2,1)S(1)} %pad_maximum_fusion.11), channel_id=1, source_target_pairs={{0,3},{1,0},{2,1},{3,2},{4,7},{5,4},{6,5},{7,6},{8,11},{9,8},{10,9... | collective-permute-start | bytes 196616 | tf_op jit(solution)/shard_map/ppermute | solution.py:47
  14.1 3.4 %collective-permute-done.1 = bf16[32,1024]{1,0:T(8,128)(2,1)S(1)} collective-permute-done((bf16[32,1024]{1,0:T(8,128)(2,1)S(1)}, bf16[32,1024]{1,0:T(8,128)(2,1)S(1)}, u32[]{:S(2)}, u32[]{:S(2)}) %collective-permute-start.1) | collective-permute-done | bytes 65568 | tf_op jit(solution)/shard_map/ppermute | solution.py:47
  17.8 2.8 %collective-permute-start.4 = (bf16[4,16,1024]{2,1,0:T(8,128)(2,1)S(1)}, bf16[4,16,1024]{2,1,0:T(8,128)(2,1)S(1)}, u32[]{:S(2)}, u32[]{:S(2)}) collective-permute-start(bf16[4,16,1024]{2,1,0:T(8,128)(2,1)S(1)} %get-tuple-element.67), channel_id=1, source_target_pairs={{0,8},{1,9},{2,10},{3,11},{4,12},{5,13},{6,14},{7,15},{8,0},{9,1},... | collective-permute-start | bytes 393224 | tf_op jit(solution)/shard_map/ppermute | solution.py:47
  21.0 2.4 %collective-permute-start.5 = (bf16[4,16,1024]{2,1,0:T(8,128)(2,1)S(1)}, bf16[4,16,1024]{2,1,0:T(8,128)(2,1)S(1)}, u32[]{:S(2)}, u32[]{:S(2)}) collective-permute-start(bf16[4,16,1024]{2,1,0:T(8,128)(2,1)S(1)} %get-tuple-element.67), channel_id=1, source_target_pairs={{0,12},{1,13},{2,14},{3,15},{4,0},{5,1},{6,2},{7,3},{8,4},{9,5},{1... | collective-permute-start | bytes 393224 | tf_op jit(solution)/shard_map/ppermute | solution.py:47
  23.4 3.7 %collective-permute-done.3 = bf16[4,16,1024]{2,1,0:T(8,128)(2,1)S(1)} collective-permute-done((bf16[4,16,1024]{2,1,0:T(8,128)(2,1)S(1)}, bf16[4,16,1024]{2,1,0:T(8,128)(2,1)S(1)}, u32[]{:S(2)}, u32[]{:S(2)}) %collective-permute-start.3) | collective-permute-done | bytes 131104 | tf_op jit(solution)/shard_map/ppermute | solution.py:47
  27.2 2.2 collective-permute-start.6
  29.4 3.0 %collective-permute-start.9 = (bf16[4,16,1024]{2,1,0:T(8,128)(2,1)S(1)}, bf16[4,16,1024]{2,1,0:T(8,128)(2,1)S(1)}, u32[]{:S(2)}, u32[]{:S(2)}) collective-permute-start(bf16[4,16,1024]{2,1,0:T(8,128)(2,1)S(1)} %pad_maximum_fusion.7), channel_id=1, source_target_pairs={{0,12},{1,13},{2,14},{3,15},{4,0},{5,1},{6,2},{7,3},{8,4},{9,5},{1... | collective-permute-start | bytes 393224 | tf_op jit(solution)/shard_map/ppermute | solution.py:47
  33.1 1.9 copy-done
  38.7 2.9 %collective-permute-done.7 = bf16[4,16,1024]{2,1,0:T(8,128)(2,1)S(1)} collective-permute-done((bf16[4,16,1024]{2,1,0:T(8,128)(2,1)S(1)}, bf16[4,16,1024]{2,1,0:T(8,128)(2,1)S(1)}, u32[]{:S(2)}, u32[]{:S(2)}) %collective-permute-start.7) | collective-permute-done | bytes 131104 | tf_op jit(solution)/shard_map/ppermute | solution.py:47
  42.5 3.0 %shard_map.95 = (bf16[4,64,512]{2,1,0:T(8,128)(2,1)S(1)}, bf16[4,64,512]{2,1,0:T(8,128)(2,1)S(1)}, f32[1280,128]{1,0:T(8,128)S(1)}) custom-call(s32[4]{0:T(128)S(1)} %pad_add_fusion.where, bf16[4,4,16,1024]{3,2,1,0:T(8,128)(2,1)S(1)} %pad_maximum_fusion.2.own, bf16[4,4,16,1024]{3,2,1,0:T(8,128)(2,1)} %collective-permute-done.6.other, ...), custom_call_target="tpu_custom_call" | custom-call | flops 1140850688 | bytes 5242880 | tf_op jit(solution)/shard_map/pallas_call | solution.py:252
  48.9 2.7 %collective-permute-start.30 = (bf16[2,64,512]{2,1,0:T(8,128)(2,1)S(1)}, bf16[2,64,512]{2,1,0:T(8,128)(2,1)S(1)}, u32[]{:S(2)}, u32[]{:S(2)}) collective-permute-start(bf16[2,64,512]{2,1,0:T(8,128)(2,1)S(1)} %pad_maximum_fusion.9), channel_id=1, source_target_pairs={{0,64},{16,80},{32,96},{48,112},{64,0},{80,16},{96,32},{112,48},{1... | collective-permute-start | bytes 393224 | tf_op jit(solution)/shard_map/ppermute | solution.py:503
  53.6 3.9 %collective-permute-done.30.got2 = bf16[2,64,512]{2,1,0:T(8,128)(2,1)S(1)} collective-permute-done((bf16[2,64,512]{2,1,0:T(8,128)(2,1)S(1)}, bf16[2,64,512]{2,1,0:T(8,128)(2,1)S(1)}, u32[]{:S(2)}, u32[]{:S(2)}) %collective-permute-start.30) | collective-permute-done | bytes 131104 | tf_op jit(solution)/shard_map/ppermute | solution.py:503
  60.9 1.9 collective-permute-start.12
  64.2 1.7 dynamic-slice_add_fusion
  69.6 21.5 %collective-permute-done.14 = f32[160,128]{1,0:T(8,128)S(1)} collective-permute-done((f32[160,128]{1,0:T(8,128)S(1)}, f32[160,128]{1,0:T(8,128)S(1)}, u32[]{:S(2)}, u32[]{:S(2)}) %collective-permute-start.14) | collective-permute-done | bytes 81952 | tf_op jit(solution)/shard_map/ppermute | solution.py:59
  92.1 3.9 %collective-permute-done.15 = f32[160,128]{1,0:T(8,128)S(1)} collective-permute-done((f32[160,128]{1,0:T(8,128)S(1)}, f32[160,128]{1,0:T(8,128)S(1)}, u32[]{:S(2)}, u32[]{:S(2)}) %collective-permute-start.15) | collective-permute-done | bytes 81952 | tf_op jit(solution)/shard_map/ppermute | solution.py:59
  96.9 1.7 pad_maximum_fusion.own
  98.7 1.7 collective-permute-start.17
  102.5 4.0 %collective-permute-done.20 = f32[160,128]{1,0:T(8,128)S(1)} collective-permute-done((f32[160,128]{1,0:T(8,128)S(1)}, f32[160,128]{1,0:T(8,128)S(1)}, u32[]{:S(2)}, u32[]{:S(2)}) %collective-permute-start.20) | collective-permute-done | bytes 81952 | tf_op jit(solution)/shard_map/ppermute | solution.py:81
  106.5 1.8 collective-permute-done.19
  108.3 2.2 collective-permute-done.18
  112.3 8.9 %shard_map.96 = bf16[8,16,64,128]{3,2,1,0:T(8,128)(2,1)} custom-call(s32[4]{0:T(128)S(1)} %pad_add_fusion.where, bf16[4,4,4,16,1024]{4,3,2,1,0:T(8,128)(2,1)S(1)} %pad_maximum_fusion.own, bf16[4,4,4,16,1024]{4,3,2,1,0:T(8,128)(2,1)S(1)} %collective-permute-done.17.other, bf16[320,1024]{1,0:T(8,128)(2,1)S(1)} %get-tuple-element.27.atoms_ref, ...), custom_call_target="tpu_custom_call" | custom-call | flops 4563402752 | bytes 9437184 | tf_op jit(solution)/shard_map/pallas_call | solution.py:283
  121.2 8.7 %all-to-all-start = ((bf16[128,64,128]{2,1,0:T(8,128)(2,1)}), bf16[128,64,128]{2,1,0:T(8,128)(2,1)S(1)}, u32[]{:S(2)}, u32[]{:S(2)}) async-start(bf16[128,64,128]{2,1,0:T(8,128)(2,1)} %bitcast.27), calls=%async_computation | async-start | bytes 4194304 | tf_op jit(solution)/shard_map/all_to_all | solution.py:518
  129.9 2.7 %collective-permute-start.26 = (f32[160,128]{1,0:T(8,128)S(1)}, f32[160,128]{1,0:T(8,128)S(1)}, u32[]{:S(2)}, u32[]{:S(2)}) collective-permute-start(f32[160,128]{1,0:T(8,128)S(1)} %add_add_fusion.1), channel_id=1, source_target_pairs={{0,96},{16,112},{32,0},{48,16},{64,32},{80,48},{96,64},{112,80},{1... | collective-permute-start | bytes 245768 | tf_op jit(solution)/shard_map/ppermute | solution.py:51
  133.7 21.4 %collective-permute-done.26 = f32[160,128]{1,0:T(8,128)S(1)} collective-permute-done((f32[160,128]{1,0:T(8,128)S(1)}, f32[160,128]{1,0:T(8,128)S(1)}, u32[]{:S(2)}, u32[]{:S(2)}) %collective-permute-start.26) | collective-permute-done | bytes 81952 | tf_op jit(solution)/shard_map/ppermute | solution.py:51
  156.1 2.5 %collective-permute-done.24 = f32[160,128]{1,0:T(8,128)S(1)} collective-permute-done((f32[160,128]{1,0:T(8,128)S(1)}, f32[160,128]{1,0:T(8,128)S(1)}, u32[]{:S(2)}, u32[]{:S(2)}) %collective-permute-start.24) | collective-permute-done | bytes 81952 | tf_op jit(solution)/shard_map/ppermute | solution.py:51
  161.0 26.7 %shard_map.97 = (f32[512,512]{1,0:T(8,128)}, f32[512,512]{1,0:T(8,128)S(1)}) custom-call(f32[1280,128]{1,0:T(8,128)S(1)} %pad_maximum_fusion.1.gram_ref), custom_call_target="tpu_custom_call" | custom-call | flops 2684354560 | bytes 4194304 | tf_op jit(solution)/shard_map/pallas_call | solution.py:372
  190.1 6.0 %shard_map.99 = f32[128,512]{1,0:T(8,128)} custom-call(bf16[16,512,512]{2,1,0:T(8,128)(2,1)} %all-gather.2.cloned.1.call-done.panel_ref, bf16[8,16,64,128]{3,2,1,0:T(8,128)(2,1)} %bitcast.40), custom_call_target="tpu_custom_call" | custom-call | flops 1073741824 | bytes 11534336 | tf_op jit(solution)/shard_map/pallas_call | solution.py:397
  201.7 2.4 %collective-permute-done.35 = f32[64,512]{1,0:T(8,128)S(1)} collective-permute-done((f32[64,512]{1,0:T(8,128)S(1)}, f32[64,512]{1,0:T(8,128)S(1)}, u32[]{:S(2)}, u32[]{:S(2)}) %collective-permute-start.35) | collective-permute-done | bytes 131104 | tf_op jit(solution)/shard_map/ppermute | solution.py:81
  204.1 2.3 %collective-permute-done.34 = f32[64,512]{1,0:T(8,128)S(1)} collective-permute-done((f32[64,512]{1,0:T(8,128)S(1)}, f32[64,512]{1,0:T(8,128)S(1)}, u32[]{:S(2)}, u32[]{:S(2)}) %collective-permute-start.34) | collective-permute-done | bytes 131104 | tf_op jit(solution)/shard_map/ppermute | solution.py:81
  206.4 3.6 %collective-permute-done.33 = f32[64,512]{1,0:T(8,128)S(1)} collective-permute-done((f32[64,512]{1,0:T(8,128)S(1)}, f32[64,512]{1,0:T(8,128)S(1)}, u32[]{:S(2)}, u32[]{:S(2)}) %collective-permute-start.33) | collective-permute-done | bytes 131104 | tf_op jit(solution)/shard_map/ppermute | solution.py:81
  212.6 10.3 %shard_map.100 = (f32[128,512]{1,0:T(8,128)}, f32[128,8192]{1,0:T(8,128)}) custom-call(f32[128,512]{1,0:T(8,128)} %pad_maximum_fusion.5.cross_ref, f32[512,512]{1,0:T(8,128)} %copy-done.1, bf16[16,512,512]{2,1,0:T(8,128)(2,1)} %all-gather.2.cloned.1.call-done.panel_ref, bf16[8,16,64,128]{3,2,1,0:T(8,128)(2,1)} %bitcast.41), custom_call_target="tpu_custom_call" | custom-call | flops 2147483648 | bytes 16777216 | tf_op jit(solution)/shard_map/pallas_call | solution.py:438
  (107 shorter events, 43.1 us)
Async XLA Ops:
  7.2 181.5 %all-gather.2.cloned.1.call-start = ((), (), s32[]{:S(2)}) async-start(), calls=%async_computation.1 | async-start | bytes 8912896 | tf_op jit(solution)/shard_map/all_gather | solution.py:506
  8.1 6.0 %collective-permute-start.2 = (bf16[32,1024]{1,0:T(8,128)(2,1)S(1)}, bf16[32,1024]{1,0:T(8,128)(2,1)S(1)}, u32[]{:S(2)}, u32[]{:S(2)}) collective-permute-start(bf16[32,1024]{1,0:T(8,128)(2,1)S(1)} %pad_maximum_fusion.11), channel_id=1, source_target_pairs={{0,3},{1,0},{2,1},{3,2},{4,7},{5,4},{6,5},{7,6},{8,11},{9,8},{10,9... | collective-permute-start | bytes 196616 | tf_op jit(solution)/shard_map/ppermute | solution.py:47
  12.8 5.0 %collective-permute-start = (bf16[32,1024]{1,0:T(8,128)(2,1)S(1)}, bf16[32,1024]{1,0:T(8,128)(2,1)S(1)}, u32[]{:S(2)}, u32[]{:S(2)}) collective-permute-start(bf16[32,1024]{1,0:T(8,128)(2,1)S(1)} %pad_maximum_fusion.11), channel_id=1, source_target_pairs={{0,1},{1,2},{2,3},{3,0},{4,5},{5,6},{6,7},{7,4},{8,9},{9,10},{10,1... | collective-permute-start | bytes 196616 | tf_op jit(solution)/shard_map/ppermute | solution.py:47
  17.8 5.5 %collective-permute-start.4 = (bf16[4,16,1024]{2,1,0:T(8,128)(2,1)S(1)}, bf16[4,16,1024]{2,1,0:T(8,128)(2,1)S(1)}, u32[]{:S(2)}, u32[]{:S(2)}) collective-permute-start(bf16[4,16,1024]{2,1,0:T(8,128)(2,1)S(1)} %get-tuple-element.67), channel_id=1, source_target_pairs={{0,8},{1,9},{2,10},{3,11},{4,12},{5,13},{6,14},{7,15},{8,0},{9,1},... | collective-permute-start | bytes 393224 | tf_op jit(solution)/shard_map/ppermute | solution.py:47
  20.6 6.4 %collective-permute-start.3 = (bf16[4,16,1024]{2,1,0:T(8,128)(2,1)S(1)}, bf16[4,16,1024]{2,1,0:T(8,128)(2,1)S(1)}, u32[]{:S(2)}, u32[]{:S(2)}) collective-permute-start(bf16[4,16,1024]{2,1,0:T(8,128)(2,1)S(1)} %get-tuple-element.67), channel_id=1, source_target_pairs={{0,4},{1,5},{2,6},{3,7},{4,8},{5,9},{6,10},{7,11},{8,12},{9,13},{1... | collective-permute-start | bytes 393224 | tf_op jit(solution)/shard_map/ppermute | solution.py:47
  21.0 6.1 %collective-permute-start.5 = (bf16[4,16,1024]{2,1,0:T(8,128)(2,1)S(1)}, bf16[4,16,1024]{2,1,0:T(8,128)(2,1)S(1)}, u32[]{:S(2)}, u32[]{:S(2)}) collective-permute-start(bf16[4,16,1024]{2,1,0:T(8,128)(2,1)S(1)} %get-tuple-element.67), channel_id=1, source_target_pairs={{0,12},{1,13},{2,14},{3,15},{4,0},{5,1},{6,2},{7,3},{8,4},{9,5},{1... | collective-permute-start | bytes 393224 | tf_op jit(solution)/shard_map/ppermute | solution.py:47
  27.2 15.3 %collective-permute-start.6 = (bf16[4,4,16,1024]{3,2,1,0:T(8,128)(2,1)S(1)}, bf16[4,4,16,1024]{3,2,1,0:T(8,128)(2,1)}, u32[]{:S(2)}, u32[]{:S(2)}) collective-permute-start(bf16[4,4,16,1024]{3,2,1,0:T(8,128)(2,1)S(1)} %pad_maximum_fusion.2.own), channel_id=1, source_target_pairs={{0,16},{16,0},{32,48},{48,32},{64,80},{80,64},{96,112},{112,96},{1... | collective-permute-start | bytes 1572872 | tf_op jit(solution)/shard_map/ppermute | solution.py:488
  29.4 8.5 %collective-permute-start.9 = (bf16[4,16,1024]{2,1,0:T(8,128)(2,1)S(1)}, bf16[4,16,1024]{2,1,0:T(8,128)(2,1)S(1)}, u32[]{:S(2)}, u32[]{:S(2)}) collective-permute-start(bf16[4,16,1024]{2,1,0:T(8,128)(2,1)S(1)} %pad_maximum_fusion.7), channel_id=1, source_target_pairs={{0,12},{1,13},{2,14},{3,15},{4,0},{5,1},{6,2},{7,3},{8,4},{9,5},{1... | collective-permute-start | bytes 393224 | tf_op jit(solution)/shard_map/ppermute | solution.py:47
  32.4 6.3 %collective-permute-start.8 = (bf16[4,16,1024]{2,1,0:T(8,128)(2,1)S(1)}, bf16[4,16,1024]{2,1,0:T(8,128)(2,1)S(1)}, u32[]{:S(2)}, u32[]{:S(2)}) collective-permute-start(bf16[4,16,1024]{2,1,0:T(8,128)(2,1)S(1)} %pad_maximum_fusion.7), channel_id=1, source_target_pairs={{0,8},{1,9},{2,10},{3,11},{4,12},{5,13},{6,14},{7,15},{8,0},{9,1},... | collective-permute-start | bytes 393224 | tf_op jit(solution)/shard_map/ppermute | solution.py:47
  32.4 9.2 %collective-permute-start.7 = (bf16[4,16,1024]{2,1,0:T(8,128)(2,1)S(1)}, bf16[4,16,1024]{2,1,0:T(8,128)(2,1)S(1)}, u32[]{:S(2)}, u32[]{:S(2)}) collective-permute-start(bf16[4,16,1024]{2,1,0:T(8,128)(2,1)S(1)} %pad_maximum_fusion.7), channel_id=1, source_target_pairs={{0,4},{1,5},{2,6},{3,7},{4,8},{5,9},{6,10},{7,11},{8,12},{9,13},{1... | collective-permute-start | bytes 393224 | tf_op jit(solution)/shard_map/ppermute | solution.py:47
  47.5 6.1 %collective-permute-start.29 = (bf16[2,64,512]{2,1,0:T(8,128)(2,1)S(1)}, bf16[2,64,512]{2,1,0:T(8,128)(2,1)S(1)}, u32[]{:S(2)}, u32[]{:S(2)}) collective-permute-start(bf16[2,64,512]{2,1,0:T(8,128)(2,1)S(1)} %pad_maximum_fusion.8), channel_id=1, source_target_pairs={{0,32},{16,48},{32,64},{48,80},{64,96},{80,112},{96,0},{112,16},{1... | collective-permute-start | bytes 393224 | tf_op jit(solution)/shard_map/ppermute | solution.py:503
  48.9 8.7 %collective-permute-start.30 = (bf16[2,64,512]{2,1,0:T(8,128)(2,1)S(1)}, bf16[2,64,512]{2,1,0:T(8,128)(2,1)S(1)}, u32[]{:S(2)}, u32[]{:S(2)}) collective-permute-start(bf16[2,64,512]{2,1,0:T(8,128)(2,1)S(1)} %pad_maximum_fusion.9), channel_id=1, source_target_pairs={{0,64},{16,80},{32,96},{48,112},{64,0},{80,16},{96,32},{112,48},{1... | collective-permute-start | bytes 393224 | tf_op jit(solution)/shard_map/ppermute | solution.py:503
  51.6 5.9 %collective-permute-start.31 = (bf16[2,64,512]{2,1,0:T(8,128)(2,1)S(1)}, bf16[2,64,512]{2,1,0:T(8,128)(2,1)S(1)}, u32[]{:S(2)}, u32[]{:S(2)}) collective-permute-start(bf16[2,64,512]{2,1,0:T(8,128)(2,1)S(1)} %pad_maximum_fusion.10), channel_id=1, source_target_pairs={{0,96},{16,112},{32,0},{48,16},{64,32},{80,48},{96,64},{112,80},{1... | collective-permute-start | bytes 393224 | tf_op jit(solution)/shard_map/ppermute | solution.py:503
  60.9 36.0 %collective-permute-start.12 = (bf16[4,4,16,1024]{3,2,1,0:T(8,128)(2,1)S(1)}, bf16[4,4,16,1024]{3,2,1,0:T(8,128)(2,1)}, u32[]{:S(2)}, u32[]{:S(2)}) collective-permute-start(bf16[4,4,16,1024]{3,2,1,0:T(8,128)(2,1)S(1)} %copy-done.8), channel_id=1, source_target_pairs={{0,96},{16,112},{32,0},{48,16},{64,32},{80,48},{96,64},{112,80},{1... | collective-permute-start | bytes 1572872 | tf_op jit(solution)/shard_map/ppermute | solution.py:47
  62.8 34.1 %collective-permute-start.11 = (bf16[4,4,16,1024]{3,2,1,0:T(8,128)(2,1)S(1)}, bf16[4,4,16,1024]{3,2,1,0:T(8,128)(2,1)}, u32[]{:S(2)}, u32[]{:S(2)}) collective-permute-start(bf16[4,4,16,1024]{3,2,1,0:T(8,128)(2,1)S(1)} %copy-done.8), channel_id=1, source_target_pairs={{0,64},{16,80},{32,96},{48,112},{64,0},{80,16},{96,32},{112,48},{1... | collective-permute-start | bytes 1572872 | tf_op jit(solution)/shard_map/ppermute | solution.py:47
  63.8 33.2 %collective-permute-start.10 = (bf16[4,4,16,1024]{3,2,1,0:T(8,128)(2,1)S(1)}, bf16[4,4,16,1024]{3,2,1,0:T(8,128)(2,1)}, u32[]{:S(2)}, u32[]{:S(2)}) collective-permute-start(bf16[4,4,16,1024]{3,2,1,0:T(8,128)(2,1)S(1)} %copy-done.8), channel_id=1, source_target_pairs={{0,32},{16,48},{32,64},{48,80},{64,96},{80,112},{96,0},{112,16},{1... | collective-permute-start | bytes 1572872 | tf_op jit(solution)/shard_map/ppermute | solution.py:47
  66.9 24.2 %collective-permute-start.14 = (f32[160,128]{1,0:T(8,128)S(1)}, f32[160,128]{1,0:T(8,128)S(1)}, u32[]{:S(2)}, u32[]{:S(2)}) collective-permute-start(f32[160,128]{1,0:T(8,128)S(1)} %get-tuple-element.55), channel_id=1, source_target_pairs={{0,32},{16,48},{32,64},{48,80},{64,96},{80,112},{96,0},{112,16},{1... | collective-permute-start | bytes 245768 | tf_op jit(solution)/shard_map/ppermute | solution.py:59
  68.3 23.8 %collective-permute-start.16 = (f32[160,128]{1,0:T(8,128)S(1)}, f32[160,128]{1,0:T(8,128)S(1)}, u32[]{:S(2)}, u32[]{:S(2)}) collective-permute-start(f32[160,128]{1,0:T(8,128)S(1)} %get-tuple-element.56), channel_id=1, source_target_pairs={{0,96},{16,112},{32,0},{48,16},{64,32},{80,48},{96,64},{112,80},{1... | collective-permute-start | bytes 245768 | tf_op jit(solution)/shard_map/ppermute | solution.py:59
  91.1 4.8 %collective-permute-start.15 = (f32[160,128]{1,0:T(8,128)S(1)}, f32[160,128]{1,0:T(8,128)S(1)}, u32[]{:S(2)}, u32[]{:S(2)}) collective-permute-start(f32[160,128]{1,0:T(8,128)S(1)} %get-tuple-element.57), channel_id=1, source_target_pairs={{0,64},{16,80},{32,96},{48,112},{64,0},{80,16},{96,32},{112,48},{1... | collective-permute-start | bytes 245768 | tf_op jit(solution)/shard_map/ppermute | solution.py:59
  98.7 11.9 %collective-permute-start.17 = (bf16[4,4,4,16,1024]{4,3,2,1,0:T(8,128)(2,1)S(1)}, bf16[4,4,4,16,1024]{4,3,2,1,0:T(8,128)(2,1)S(1)}, u32[]{:S(2)}, u32[]{:S(2)}) collective-permute-start(bf16[4,4,4,16,1024]{4,3,2,1,0:T(8,128)(2,1)S(1)} %pad_maximum_fusion.own), channel_id=1, source_target_pairs={{0,16},{16,0},{32,48},{48,32},{64,80},{80,64},{96,112},{112,96},{1... | collective-permute-start | bytes 6291464 | tf_op jit(solution)/shard_map/ppermute | solution.py:510
  100.3 6.1 %collective-permute-start.20 = (f32[160,128]{1,0:T(8,128)S(1)}, f32[160,128]{1,0:T(8,128)S(1)}, u32[]{:S(2)}, u32[]{:S(2)}) collective-permute-start(f32[160,128]{1,0:T(8,128)S(1)} %add_add_fusion.3), channel_id=1, source_target_pairs={{0,3},{1,0},{2,1},{3,2},{4,7},{5,4},{6,5},{7,6},{8,11},{9,8},{10,9... | collective-permute-start | bytes 245768 | tf_op jit(solution)/shard_map/ppermute | solution.py:81
  100.9 7.4 %collective-permute-start.19 = (f32[160,128]{1,0:T(8,128)S(1)}, f32[160,128]{1,0:T(8,128)S(1)}, u32[]{:S(2)}, u32[]{:S(2)}) collective-permute-start(f32[160,128]{1,0:T(8,128)S(1)} %add_add_fusion.3), channel_id=1, source_target_pairs={{0,2},{1,3},{2,0},{3,1},{4,6},{5,7},{6,4},{7,5},{8,10},{9,11},{10,... | collective-permute-start | bytes 245768 | tf_op jit(solution)/shard_map/ppermute | solution.py:81
  101.6 8.9 %collective-permute-start.18 = (f32[160,128]{1,0:T(8,128)S(1)}, f32[160,128]{1,0:T(8,128)S(1)}, u32[]{:S(2)}, u32[]{:S(2)}) collective-permute-start(f32[160,128]{1,0:T(8,128)S(1)} %add_add_fusion.3), channel_id=1, source_target_pairs={{0,1},{1,2},{2,3},{3,0},{4,5},{5,6},{6,7},{7,4},{8,9},{9,10},{10,1... | collective-permute-start | bytes 245768 | tf_op jit(solution)/shard_map/ppermute | solution.py:81
  110.6 10.6 %collective-permute-start.23 = (f32[160,128]{1,0:T(8,128)S(1)}, f32[160,128]{1,0:T(8,128)S(1)}, u32[]{:S(2)}, u32[]{:S(2)}) collective-permute-start(f32[160,128]{1,0:T(8,128)S(1)} %add_add_fusion.2), channel_id=1, source_target_pairs={{0,12},{1,13},{2,14},{3,15},{4,0},{5,1},{6,2},{7,3},{8,4},{9,5},{1... | collective-permute-start | bytes 245768 | tf_op jit(solution)/shard_map/ppermute | solution.py:81
  111.5 9.7 %collective-permute-start.22 = (f32[160,128]{1,0:T(8,128)S(1)}, f32[160,128]{1,0:T(8,128)S(1)}, u32[]{:S(2)}, u32[]{:S(2)}) collective-permute-start(f32[160,128]{1,0:T(8,128)S(1)} %add_add_fusion.2), channel_id=1, source_target_pairs={{0,8},{1,9},{2,10},{3,11},{4,12},{5,13},{6,14},{7,15},{8,0},{9,1},... | collective-permute-start | bytes 245768 | tf_op jit(solution)/shard_map/ppermute | solution.py:81
  111.5 9.7 %collective-permute-start.21 = (f32[160,128]{1,0:T(8,128)S(1)}, f32[160,128]{1,0:T(8,128)S(1)}, u32[]{:S(2)}, u32[]{:S(2)}) collective-permute-start(f32[160,128]{1,0:T(8,128)S(1)} %add_add_fusion.2), channel_id=1, source_target_pairs={{0,4},{1,5},{2,6},{3,7},{4,8},{5,9},{6,10},{7,11},{8,12},{9,13},{1... | collective-permute-start | bytes 245768 | tf_op jit(solution)/shard_map/ppermute | solution.py:81
  121.2 67.5 %all-to-all-start = ((bf16[128,64,128]{2,1,0:T(8,128)(2,1)}), bf16[128,64,128]{2,1,0:T(8,128)(2,1)S(1)}, u32[]{:S(2)}, u32[]{:S(2)}) async-start(bf16[128,64,128]{2,1,0:T(8,128)(2,1)} %bitcast.27), calls=%async_computation | async-start | bytes 4194304 | tf_op jit(solution)/shard_map/all_to_all | solution.py:518
  129.9 25.2 %collective-permute-start.26 = (f32[160,128]{1,0:T(8,128)S(1)}, f32[160,128]{1,0:T(8,128)S(1)}, u32[]{:S(2)}, u32[]{:S(2)}) collective-permute-start(f32[160,128]{1,0:T(8,128)S(1)} %add_add_fusion.1), channel_id=1, source_target_pairs={{0,96},{16,112},{32,0},{48,16},{64,32},{80,48},{96,64},{112,80},{1... | collective-permute-start | bytes 245768 | tf_op jit(solution)/shard_map/ppermute | solution.py:51
  132.6 23.4 %collective-permute-start.25 = (f32[160,128]{1,0:T(8,128)S(1)}, f32[160,128]{1,0:T(8,128)S(1)}, u32[]{:S(2)}, u32[]{:S(2)}) collective-permute-start(f32[160,128]{1,0:T(8,128)S(1)} %add_add_fusion.1), channel_id=1, source_target_pairs={{0,64},{16,80},{32,96},{48,112},{64,0},{80,16},{96,32},{112,48},{1... | collective-permute-start | bytes 245768 | tf_op jit(solution)/shard_map/ppermute | solution.py:51
  133.1 25.4 %collective-permute-start.24 = (f32[160,128]{1,0:T(8,128)S(1)}, f32[160,128]{1,0:T(8,128)S(1)}, u32[]{:S(2)}, u32[]{:S(2)}) collective-permute-start(f32[160,128]{1,0:T(8,128)S(1)} %add_add_fusion.1), channel_id=1, source_target_pairs={{0,32},{16,48},{32,64},{48,80},{64,96},{80,112},{96,0},{112,16},{1... | collective-permute-start | bytes 245768 | tf_op jit(solution)/shard_map/ppermute | solution.py:51
  200.5 5.9 %collective-permute-start.34 = (f32[64,512]{1,0:T(8,128)S(1)}, f32[64,512]{1,0:T(8,128)S(1)}, u32[]{:S(2)}, u32[]{:S(2)}) collective-permute-start(f32[64,512]{1,0:T(8,128)S(1)} %dynamic-slice_add_fusion.1), channel_id=1, source_target_pairs={{0,64},{16,80},{32,96},{48,112},{64,0},{80,16},{96,32},{112,48},{1... | collective-permute-start | bytes 393224 | tf_op jit(solution)/shard_map/ppermute | solution.py:81
  201.7 8.3 %collective-permute-start.33 = (f32[64,512]{1,0:T(8,128)S(1)}, f32[64,512]{1,0:T(8,128)S(1)}, u32[]{:S(2)}, u32[]{:S(2)}) collective-permute-start(f32[64,512]{1,0:T(8,128)S(1)} %dynamic-slice_add_fusion.1), channel_id=1, source_target_pairs={{0,32},{16,48},{32,64},{48,80},{64,96},{80,112},{96,0},{112,16},{1... | collective-permute-start | bytes 393224 | tf_op jit(solution)/shard_map/ppermute | solution.py:81
  (17 other events, 164.7 us)
Sparse Core Ops, SparseCore 0:
  59.1 72.1 all-gather.1

commit v5 on v4

--- a/solution.py
+++ b/solution.py
@@ -213,14 +213,13 @@
 
 
 def trail_kernel(
-    where, own, other, atoms_ref, grads_ref, mean_ref, order_ref, out_ref, env
+    where, own_ref, other_ref, atoms_ref, grads_ref, mean_ref, order_ref, out_ref
 ):
-    z, y = where[1], where[2]
-    for j in range(4):
-        place = ((z - j) & 3) * 128
-        for s in range(4):
-            put_env(env, where, own, other, (s, 0, j), place + ((y - s) & 3) * 32)
-    rows = compact_rows(env[...], atoms_ref[...], grads_ref[...], mean_ref[...])
+    first = where[3] == 0
+    own, other = own_ref[...], other_ref[...]
+    low, high = jnp.where(first, own, other), jnp.where(first, other, own)
+    env = jnp.concatenate([low, high], axis=1).reshape(-1, 1024)
+    rows = compact_rows(env, atoms_ref[...], grads_ref[...], mean_ref[...])
     full = dot(order_ref[...], rows, NN).astype(BF16)
     for c in range(out_ref.shape[1]):
         out_ref[:, c] = full[:, c * 128 : c * 128 + 128].reshape(8, 64, 128)
@@ -278,23 +277,25 @@
 
 
 def trail_rows(where, own, other, atoms, grads, mean, order):
-    piece = pl.BlockSpec((4, 1, 4, 16, 1024), lambda i, w: (0, i, 0, 0, 0))
+    blocks = own.shape[0]
+    step = 4
+    half = pl.BlockSpec((step, 64, 1024), lambda i, w: (i, 0, 0))
     whole = lambda shape: pl.BlockSpec(shape, lambda i, w: (0, 0))
     return pl.pallas_call(
         trail_kernel,
-        out_shape=jax.ShapeDtypeStruct((8, 16, 64, 128), BF16),
+        out_shape=jax.ShapeDtypeStruct((8, blocks, 64, 128), BF16),
         grid_spec=pltpu.PrefetchScalarGridSpec(
             num_scalar_prefetch=1,
-            grid=(4,),
-            in_specs=[piece] * 2
-            + [
+            grid=(blocks // step,),
+            in_specs=[
+                half,
+                half,
                 whole(atoms.shape),
                 whole(grads.shape),
                 whole(mean.shape),
                 whole(order.shape),
             ],
-            out_specs=pl.BlockSpec((8, 4, 64, 128), lambda i, w: (0, (w[0] - i) & 3, 0, 0)),
-            scratch_shapes=[pltpu.VMEM((512, 1024), BF16)],
+            out_specs=pl.BlockSpec((8, step, 64, 128), lambda i, w: (0, i, 0, 0)),
         ),
         compiler_params=params(),
         cost_estimate=pl.CostEstimate(
@@ -403,7 +404,7 @@
             pl.BlockSpec((8, 4, 64, 128), lambda i: (0, i, 0, 0)),
         ],
         out_specs=pl.BlockSpec((128, n), lambda i: (0, 0)),
-        compiler_params=params(58),
+        compiler_params=params(),
         cost_estimate=pl.CostEstimate(
             flops=2 * 128 * n * 8192, bytes_accessed=11 << 20, transcendentals=0
         ),
@@ -450,7 +451,7 @@
         ],
         out_specs=(whole((128, n)), pl.BlockSpec((128, 2048), lambda i: (0, i))),
         scratch_shapes=[pltpu.VMEM((256, n), BF16)],
-        compiler_params=params(58),
+        compiler_params=params(),
         cost_estimate=pl.CostEstimate(
             flops=4 * 128 * n * 8192, bytes_accessed=16 << 20, transcendentals=0
         ),
@@ -473,20 +474,12 @@
 
     where = jnp.stack([x, z, y, core]).astype(jnp.int32)
 
-    piece = jnp.concatenate(
-        [
-            lax.dynamic_slice_in_dim(sparse_panel, core * 16, 16, 0),
-            lax.dynamic_slice_in_dim(sparse_trail, row * 16, 16, 0),
-        ],
-        axis=0,
-    )
-    pieces = shifted(piece, "col", z_shift)
-    piece = jnp.stack([p[:16] for p in pieces])
-    piece_trail = jnp.stack([p[16:] for p in pieces])
+    trail_own = lax.dynamic_slice_in_dim(sparse_trail, core * 64, 64, 0)
+    trail_own = lax.all_gather(trail_own, "col", axis=0, tiled=False)
+    piece = lax.dynamic_slice_in_dim(sparse_panel, core * 16, 16, 0)
+    piece = jnp.stack(shifted(piece, "col", z_shift))
     own = jnp.stack(shifted(piece, "col", x_shift))
-    own, piece_trail = lax.optimization_barrier((own, piece_trail))
     other = lax.ppermute(own, "row", CORE_SWAP)
-    own_trail = jnp.stack(shifted(piece_trail, "col", x_shift))
 
     atoms, grads, mean, order = prepare(
         atom_counts,
@@ -497,15 +490,16 @@
     )
 
     near, far, gram = panel_rows(where, own, other, atoms, grads, mean, order)
-    far, own_trail = lax.optimization_barrier((far, own_trail))
     far = lax.ppermute(far, "row", CORE_SWAP)
+    gram = swap_add(gram, core)
+    far, gram = lax.optimization_barrier((far, gram))
     got = [
         lax.ppermute(jnp.stack([near[s], far[s]]), "row", y_shift(s)) for s in (1, 2, 3)
     ]
     panel = assemble(where, near, far, got).reshape(512, 512)
+    panel, gram = lax.optimization_barrier((panel, gram))
     segment = lax.all_gather(panel, "col", axis=0, tiled=False)
-    gram = scatter4(swap_add(gram, core), "row", y_shift, y)
-    trail_own = jnp.stack(shifted(own_trail, "row", y_shift))
+    gram = scatter4(gram, "row", y_shift, y)
     trail_own, gram = lax.optimization_barrier((trail_own, gram))
     trail_other = lax.ppermute(trail_own, "row", CORE_SWAP)
     gram = spread4(gram, "col", z_shift)
@@ -515,6 +509,7 @@
     trail, gram = lax.optimization_barrier((trail, gram))
     gram = gather4(gram, "row", y_shift, y)
     gram = jnp.concatenate(swap_gather(gram, core), axis=0)
+    trail, gram = lax.optimization_barrier((trail, gram))
     trail = lax.all_to_all(
         trail.reshape(128, 64, 128), ("row", "col"), 0, 0, tiled=True
     ).reshape(8, 16, 64, 128)

time: 230 us -> 194 us (0.84)
  waiting for transfers between devices: 89 us -> 62.5 us
  Pallas kernels: 57.6 us -> 48.7 us
  local copies, waits for them, and re-layouts: 7.82 us -> 15.9 us
  starting transfers between devices: 53.7 us -> 48.9 us
  other arithmetic: 7.37 us -> 3.01 us
    ppermute x3, waiting for transfers between devices: 25.4 us -> 3.94 us  [scatter4(): lax.ppermute(lax.dynamic_slice_in_dim(v, (index + s) % 4 * n, n, 0), axis...]
    all_gather x1, waiting for transfers between devices: 0.01 us -> 21.2 us  [per_device(): segment = lax.all_gather(panel, 'col', axis=0, tiled=False)]
    ppermute x3, waiting for transfers between devices: 24.8 us -> 4.53 us  [gather4(): pieces = [v] + [lax.ppermute(v, axis, shift(s)) for s in (1, 2, 3)]]
    unnamed x21 -> x35, local copies, waits for them, and re-layouts: 4.21 us -> 12.8 us
    ppermute x12 -> x6, waiting for transfers between devices: 13.2 us -> 5.02 us  [shifted(): return [v] + [lax.ppermute(v, axis, shift(s)) for s in (1, 2, 3)]]
    ppermute x12 -> x6, starting transfers between devices: 17.8 us -> 12.6 us  [shifted(): return [v] + [lax.ppermute(v, axis, shift(s)) for s in (1, 2, 3)]]
    pallas_call x1, Pallas kernels: 5.97 us -> 2.09 us  [cross_part(): pl.pallas_call(cross_kernel, out_shape=jax.ShapeDtypeStruct((128, n), F32...]
    ppermute x9, starting transfers between devices: 6.32 us -> 9.64 us  [spread4(): got = [lax.ppermute(v, axis, shift(s)) for s in (1, 2, 3)]]
  transfers between devices with their start and end apart: 39 -> 34, of which waited for: 24 -> 21; matrix products, arithmetic and copies ran while one was open for 3% -> 3% of each run, Pallas kernels for 16% -> 20%
where the time goes in v5:
time: 194 us; the launch traced here: 193 us
  waiting for transfers between devices  62.5 us (32%)
  starting transfers between devices  48.9 us (25%)
  Pallas kernels  48.7 us (25%)
  local copies, waits for them, and re-layouts  15.9 us (8%)
  between operations  14.5 us (7%)
  other arithmetic  3.01 us (2%)
    pallas_call x1, Pallas kernels, factor_panel(): pl.pallas_call(functools.partial(factor_kernel, float(rows_total)), out_s...  26.7 us
    all_gather x1, waiting for transfers between devices, per_device(): segment = lax.all_gather(panel, 'col', axis=0, tiled=False)  21.2 us
    ppermute x9, waiting for transfers between devices, spread4(): got = [lax.ppermute(v, axis, shift(s)) for s in (1, 2, 3)]  15.2 us
    unnamed x35, local copies, waits for them, and re-layouts  12.8 us
    ppermute x6, starting transfers between devices, shifted(): return [v] + [lax.ppermute(v, axis, shift(s)) for s in (1, 2, 3)]  12.6 us
    ppermute x9, starting transfers between devices, spread4(): got = [lax.ppermute(v, axis, shift(s)) for s in (1, 2, 3)]  9.64 us
    pallas_call x1, Pallas kernels, trail_rows(): pl.pallas_call(trail_kernel, out_shape=jax.ShapeDtypeStruct((8, blocks, 6...  7.43 us
    pallas_call x1, Pallas kernels, residual(): pl.pallas_call(functools.partial(residual_kernel, float(rows_total)), out...  7.21 us
  transfers between devices with their start and end apart: 34, of which 21 were waited for; matrix products, arithmetic and copies ran while one was open for 3% of the time, Pallas kernels for 20%

profile of v5, /device:TPU:1, one launch (start us, length us, event | category | flops | bytes accessed | tf_op | source)
XLA Modules:
  0.0 193.4 jit_solution(17358750258708675440)
XLA Ops:
  9.6 4.4 %collective-permute-start.1 = (bf16[16,1024]{1,0:T(8,128)(2,1)S(1)}, bf16[16,1024]{1,0:T(8,128)(2,1)S(1)}, u32[]{:S(2)}, u32[]{:S(2)}) collective-permute-start(bf16[16,1024]{1,0:T(8,128)(2,1)S(1)} %constant_dynamic-slice_fusion.5), channel_id=1, source_target_pairs={{0,2},{1,3},{2,0},{3,1},{4,6},{5,7},{6,4},{7,5},{8,10},{9,11},{10,... | collective-permute-start | bytes 98312 | tf_op jit(solution)/shard_map/ppermute | solution.py:47
  14.8 1.9 %collective-permute-start.2 = (bf16[16,1024]{1,0:T(8,128)(2,1)S(1)}, bf16[16,1024]{1,0:T(8,128)(2,1)S(1)}, u32[]{:S(2)}, u32[]{:S(2)}) collective-permute-start(bf16[16,1024]{1,0:T(8,128)(2,1)S(1)} %constant_dynamic-slice_fusion.5), channel_id=1, source_target_pairs={{0,3},{1,0},{2,1},{3,2},{4,7},{5,4},{6,5},{7,6},{8,11},{9,8},{10,9... | collective-permute-start | bytes 98312 | tf_op jit(solution)/shard_map/ppermute | solution.py:47
  18.1 2.8 %collective-permute-start.4 = (bf16[4,16,1024]{2,1,0:T(8,128)(2,1)S(1)}, bf16[4,16,1024]{2,1,0:T(8,128)(2,1)S(1)}, u32[]{:S(2)}, u32[]{:S(2)}) collective-permute-start(bf16[4,16,1024]{2,1,0:T(8,128)(2,1)S(1)} %get-tuple-element.71), channel_id=1, source_target_pairs={{0,8},{1,9},{2,10},{3,11},{4,12},{5,13},{6,14},{7,15},{8,0},{9,1},... | collective-permute-start | bytes 393224 | tf_op jit(solution)/shard_map/ppermute | solution.py:47
  21.2 2.4 %collective-permute-start.5 = (bf16[4,16,1024]{2,1,0:T(8,128)(2,1)S(1)}, bf16[4,16,1024]{2,1,0:T(8,128)(2,1)S(1)}, u32[]{:S(2)}, u32[]{:S(2)}) collective-permute-start(bf16[4,16,1024]{2,1,0:T(8,128)(2,1)S(1)} %get-tuple-element.71), channel_id=1, source_target_pairs={{0,12},{1,13},{2,14},{3,15},{4,0},{5,1},{6,2},{7,3},{8,4},{9,5},{1... | collective-permute-start | bytes 393224 | tf_op jit(solution)/shard_map/ppermute | solution.py:47
  23.6 4.5 %collective-permute-done.3 = bf16[4,16,1024]{2,1,0:T(8,128)(2,1)S(1)} collective-permute-done((bf16[4,16,1024]{2,1,0:T(8,128)(2,1)S(1)}, bf16[4,16,1024]{2,1,0:T(8,128)(2,1)S(1)}, u32[]{:S(2)}, u32[]{:S(2)}) %collective-permute-start.3) | collective-permute-done | bytes 131104 | tf_op jit(solution)/shard_map/ppermute | solution.py:47
  28.1 2.2 %collective-permute-start.6 = (bf16[4,4,16,1024]{3,2,1,0:T(8,128)(2,1)S(1)}, bf16[4,4,16,1024]{3,2,1,0:T(8,128)(2,1)S(1)}, u32[]{:S(2)}, u32[]{:S(2)}) collective-permute-start(bf16[4,4,16,1024]{3,2,1,0:T(8,128)(2,1)S(1)} %pad_maximum_fusion.1.own), channel_id=1, source_target_pairs={{0,16},{16,0},{32,48},{48,32},{64,80},{80,64},{96,112},{112,96},{1... | collective-permute-start | bytes 1572872 | tf_op jit(solution)/shard_map/ppermute | solution.py:482
  30.5 1.9 copy-done.3
  35.8 2.4 %shard_map.95 = (bf16[4,64,512]{2,1,0:T(8,128)(2,1)S(1)}, bf16[4,64,512]{2,1,0:T(8,128)(2,1)S(1)}, f32[1280,128]{1,0:T(8,128)S(1)}) custom-call(s32[4]{0:T(128)S(1)} %pad_add_fusion.where, bf16[4,4,16,1024]{3,2,1,0:T(8,128)(2,1)S(1)} %pad_maximum_fusion.1.own, bf16[4,4,16,1024]{3,2,1,0:T(8,128)(2,1)S(1)} %copy-done.13, ...), custom_call_target="tpu_custom_call" | custom-call | flops 1140850688 | bytes 5242880 | tf_op jit(solution)/shard_map/pallas_call | solution.py:251
  43.7 2.7 %collective-permute-start.10 = (bf16[2,64,512]{2,1,0:T(8,128)(2,1)S(1)}, bf16[2,64,512]{2,1,0:T(8,128)(2,1)S(1)}, u32[]{:S(2)}, u32[]{:S(2)}) collective-permute-start(bf16[2,64,512]{2,1,0:T(8,128)(2,1)S(1)} %pad_maximum_fusion.6), channel_id=1, source_target_pairs={{0,64},{16,80},{32,96},{48,112},{64,0},{80,16},{96,32},{112,48},{1... | collective-permute-start | bytes 393224 | tf_op jit(solution)/shard_map/ppermute | solution.py:497
  48.8 3.8 %collective-permute-done.10.got2 = bf16[2,64,512]{2,1,0:T(8,128)(2,1)S(1)} collective-permute-done((bf16[2,64,512]{2,1,0:T(8,128)(2,1)S(1)}, bf16[2,64,512]{2,1,0:T(8,128)(2,1)S(1)}, u32[]{:S(2)}, u32[]{:S(2)}) %collective-permute-start.10) | collective-permute-done | bytes 131104 | tf_op jit(solution)/shard_map/ppermute | solution.py:497
  55.1 1.7 collective-permute-start.14
  59.0 2.7 %collective-permute-done.13 = f32[160,128]{1,0:T(8,128)} collective-permute-done((f32[160,128]{1,0:T(8,128)S(1)}, f32[160,128]{1,0:T(8,128)}, u32[]{:S(2)}, u32[]{:S(2)}) %collective-permute-start.13) | collective-permute-done | bytes 81952 | tf_op jit(solution)/shard_map/ppermute | solution.py:59
  62.7 2.7 %collective-permute-start.15 = (bf16[16,64,1024]{2,1,0:T(8,128)(2,1)}, bf16[16,64,1024]{2,1,0:T(8,128)(2,1)S(1)}, u32[]{:S(2)}, u32[]{:S(2)}) collective-permute-start(bf16[16,64,1024]{2,1,0:T(8,128)(2,1)} %bitcast.30), channel_id=1, source_target_pairs={{0,16},{16,0},{32,48},{48,32},{64,80},{80,64},{96,112},{112,96},{1... | collective-permute-start | bytes 6291464 | tf_op jit(solution)/shard_map/ppermute | solution.py:504
  65.4 2.8 %collective-permute-start.18 = (f32[160,128]{1,0:T(8,128)S(1)}, f32[160,128]{1,0:T(8,128)S(1)}, u32[]{:S(2)}, u32[]{:S(2)}) collective-permute-start(f32[160,128]{1,0:T(8,128)S(1)} %add_add_fusion.3), channel_id=1, source_target_pairs={{0,3},{1,0},{2,1},{3,2},{4,7},{5,4},{6,5},{7,6},{8,11},{9,8},{10,9... | collective-permute-start | bytes 245768 | tf_op jit(solution)/shard_map/ppermute | solution.py:81
  68.8 3.0 %collective-permute-done.18 = f32[160,128]{1,0:T(8,128)S(1)} collective-permute-done((f32[160,128]{1,0:T(8,128)S(1)}, f32[160,128]{1,0:T(8,128)S(1)}, u32[]{:S(2)}, u32[]{:S(2)}) %collective-permute-start.18) | collective-permute-done | bytes 81952 | tf_op jit(solution)/shard_map/ppermute | solution.py:81
  71.8 1.7 collective-permute-done.17
  73.5 1.8 collective-permute-done.16
  75.4 2.9 %collective-permute-start.21 = (f32[160,128]{1,0:T(8,128)S(1)}, f32[160,128]{1,0:T(8,128)S(1)}, u32[]{:S(2)}, u32[]{:S(2)}) collective-permute-start(f32[160,128]{1,0:T(8,128)S(1)} %add_add_fusion.2), channel_id=1, source_target_pairs={{0,12},{1,13},{2,14},{3,15},{4,0},{5,1},{6,2},{7,3},{8,4},{9,5},{1... | collective-permute-start | bytes 245768 | tf_op jit(solution)/shard_map/ppermute | solution.py:81
  80.5 7.4 %shard_map.97 = bf16[8,16,64,128]{3,2,1,0:T(8,128)(2,1)S(1)} custom-call(s32[4]{0:T(128)S(1)} %pad_add_fusion.where, bf16[16,64,1024]{2,1,0:T(8,128)(2,1)S(1)} %bitcast.31, bf16[16,64,1024]{2,1,0:T(8,128)(2,1)S(1)} %collective-permute-done.15.other_ref, bf16[320,1024]{1,0:T(8,128)(2,1)S(1)} %copy-done.11, bf16[768,1024]{1,0:T(8,128)(2,1)S(1)} %get-tuple-element.29.grads_ref, ...), custom_call_target="tpu_custom_call" | custom-call | flops 4563402752 | bytes 9437184 | tf_op jit(solution)/shard_map/pallas_call | solution.py:284
  92.9 2.4 %collective-permute-done.23 = f32[160,128]{1,0:T(8,128)S(1)} collective-permute-done((f32[160,128]{1,0:T(8,128)S(1)}, f32[160,128]{1,0:T(8,128)S(1)}, u32[]{:S(2)}, u32[]{:S(2)}) %collective-permute-start.23) | collective-permute-done | bytes 81952 | tf_op jit(solution)/shard_map/ppermute | solution.py:51
  96.2 2.9 %collective-permute-start.25 = (f32[640,128]{1,0:T(8,128)S(1)}, f32[640,128]{1,0:T(8,128)S(1)}, u32[]{:S(2)}, u32[]{:S(2)}) collective-permute-start(f32[640,128]{1,0:T(8,128)S(1)} %pad_maximum_fusion.2), channel_id=1, source_target_pairs={{0,16},{16,0},{32,48},{48,32},{64,80},{80,64},{96,112},{112,96},{1... | collective-permute-start | bytes 983048 | tf_op jit(solution)/shard_map/ppermute | solution.py:75
  101.2 6.0 %all-to-all-start = ((bf16[128,64,128]{2,1,0:T(8,128)(2,1)}), bf16[128,64,128]{2,1,0:T(8,128)(2,1)S(1)}, u32[]{:S(2)}, u32[]{:S(2)}) async-start(bf16[128,64,128]{2,1,0:T(8,128)(2,1)} %bitcast.28), calls=%async_computation | async-start | bytes 4194304 | tf_op jit(solution)/shard_map/all_to_all | solution.py:513
  108.3 26.7 %shard_map.98 = (f32[512,512]{1,0:T(8,128)}, f32[512,512]{1,0:T(8,128)S(1)}) custom-call(f32[1280,128]{1,0:T(8,128)S(1)} %copy-done.5), custom_call_target="tpu_custom_call" | custom-call | flops 2684354560 | bytes 4194304 | tf_op jit(solution)/shard_map/pallas_call | solution.py:373
  135.1 21.2 %all-gather.7.cloned.1.call-done = bf16[8192,512]{1,0:T(8,128)(2,1)} async-done(((bf16[512,512]{1,0:T(8,128)(2,1)}), bf16[8192,512]{1,0:T(8,128)(2,1)}) %all-gather.7.cloned.1.call-update) | async-done | bytes 8388624 | tf_op jit(solution)/shard_map/all_gather | solution.py:501
  156.3 3.0 %all-to-all-done = bf16[128,64,128]{2,1,0:T(8,128)(2,1)S(1)} async-done(((bf16[128,64,128]{2,1,0:T(8,128)(2,1)}), bf16[128,64,128]{2,1,0:T(8,128)(2,1)S(1)}, u32[]{:S(2)}, u32[]{:S(2)}) %all-to-all-start) | async-done | bytes 2097184 | tf_op jit(solution)/shard_map/all_to_all | solution.py:513
  159.3 3.4 %copy-done.1 = bf16[8192,512]{1,0:T(8,128)(2,1)S(1)} copy-done((bf16[8192,512]{1,0:T(8,128)(2,1)S(1)}, bf16[8192,512]{1,0:T(8,128)(2,1)}, u32[]{:S(2)}) %copy-start.1) | copy-done | bytes 8388632
  162.7 2.1 %shard_map.99 = f32[128,512]{1,0:T(8,128)S(1)} custom-call(bf16[16,512,512]{2,1,0:T(8,128)(2,1)S(1)} %bitcast.23, bf16[8,16,64,128]{3,2,1,0:T(8,128)(2,1)S(1)} %bitcast.25), custom_call_target="tpu_custom_call" | custom-call | flops 1073741824 | bytes 11534336 | tf_op jit(solution)/shard_map/pallas_call | solution.py:398
  166.3 1.6 collective-permute-start.29
  169.0 2.1 %collective-permute-done.29 = f32[64,512]{1,0:T(8,128)S(1)} collective-permute-done((f32[64,512]{1,0:T(8,128)S(1)}, f32[64,512]{1,0:T(8,128)S(1)}, u32[]{:S(2)}, u32[]{:S(2)}) %collective-permute-start.29) | collective-permute-done | bytes 131104 | tf_op jit(solution)/shard_map/ppermute | solution.py:81
  171.1 2.8 %collective-permute-done.28 = f32[64,512]{1,0:T(8,128)S(1)} collective-permute-done((f32[64,512]{1,0:T(8,128)S(1)}, f32[64,512]{1,0:T(8,128)S(1)}, u32[]{:S(2)}, u32[]{:S(2)}) %collective-permute-start.28) | collective-permute-done | bytes 131104 | tf_op jit(solution)/shard_map/ppermute | solution.py:81
  173.8 3.8 %collective-permute-done.27 = f32[64,512]{1,0:T(8,128)S(1)} collective-permute-done((f32[64,512]{1,0:T(8,128)S(1)}, f32[64,512]{1,0:T(8,128)S(1)}, u32[]{:S(2)}, u32[]{:S(2)}) %collective-permute-start.27) | collective-permute-done | bytes 131104 | tf_op jit(solution)/shard_map/ppermute | solution.py:81
  179.3 7.2 %shard_map.100 = (f32[128,512]{1,0:T(8,128)}, f32[128,8192]{1,0:T(8,128)}) custom-call(f32[128,512]{1,0:T(8,128)S(1)} %pad_maximum_fusion.3.cross_ref, f32[512,512]{1,0:T(8,128)S(1)} %get-tuple-element.50.inverse_ref, bf16[16,512,512]{2,1,0:T(8,128)(2,1)S(1)} %bitcast.24, bf16[8,16,64,128]{3,2,1,0:T(8,128)(2,1)S(1)} %bitcast.26), custom_call_target="tpu_custom_call" | custom-call | flops 2147483648 | bytes 16777216 | tf_op jit(solution)/shard_map/pallas_call | solution.py:439
  (107 shorter events, 37.8 us)
Async XLA Ops:
  7.2 55.5 %all-gather.5.cloned.1.call-start = ((), (), s32[]{:S(2)}) async-start(), calls=%async_computation.1 | async-start | bytes 2228224 | tf_op jit(solution)/shard_map/all_gather | solution.py:478
  8.8 147.5 %all-gather.7.cloned.1.call-start = ((), (), s32[]{:S(2)}) async-start(), calls=%async_computation.2 | async-start | bytes 8912896 | tf_op jit(solution)/shard_map/all_gather | solution.py:501
  9.6 7.9 %collective-permute-start.1 = (bf16[16,1024]{1,0:T(8,128)(2,1)S(1)}, bf16[16,1024]{1,0:T(8,128)(2,1)S(1)}, u32[]{:S(2)}, u32[]{:S(2)}) collective-permute-start(bf16[16,1024]{1,0:T(8,128)(2,1)S(1)} %constant_dynamic-slice_fusion.5), channel_id=1, source_target_pairs={{0,2},{1,3},{2,0},{3,1},{4,6},{5,7},{6,4},{7,5},{8,10},{9,11},{10,... | collective-permute-start | bytes 98312 | tf_op jit(solution)/shard_map/ppermute | solution.py:47
  14.1 4.0 %collective-permute-start = (bf16[16,1024]{1,0:T(8,128)(2,1)S(1)}, bf16[16,1024]{1,0:T(8,128)(2,1)S(1)}, u32[]{:S(2)}, u32[]{:S(2)}) collective-permute-start(bf16[16,1024]{1,0:T(8,128)(2,1)S(1)} %constant_dynamic-slice_fusion.5), channel_id=1, source_target_pairs={{0,1},{1,2},{2,3},{3,0},{4,5},{5,6},{6,7},{7,4},{8,9},{9,10},{10,1... | collective-permute-start | bytes 98312 | tf_op jit(solution)/shard_map/ppermute | solution.py:47
  14.8 3.2 %collective-permute-start.2 = (bf16[16,1024]{1,0:T(8,128)(2,1)S(1)}, bf16[16,1024]{1,0:T(8,128)(2,1)S(1)}, u32[]{:S(2)}, u32[]{:S(2)}) collective-permute-start(bf16[16,1024]{1,0:T(8,128)(2,1)S(1)} %constant_dynamic-slice_fusion.5), channel_id=1, source_target_pairs={{0,3},{1,0},{2,1},{3,2},{4,7},{5,4},{6,5},{7,6},{8,11},{9,8},{10,9... | collective-permute-start | bytes 98312 | tf_op jit(solution)/shard_map/ppermute | solution.py:47
  18.1 5.5 %collective-permute-start.4 = (bf16[4,16,1024]{2,1,0:T(8,128)(2,1)S(1)}, bf16[4,16,1024]{2,1,0:T(8,128)(2,1)S(1)}, u32[]{:S(2)}, u32[]{:S(2)}) collective-permute-start(bf16[4,16,1024]{2,1,0:T(8,128)(2,1)S(1)} %get-tuple-element.71), channel_id=1, source_target_pairs={{0,8},{1,9},{2,10},{3,11},{4,12},{5,13},{6,14},{7,15},{8,0},{9,1},... | collective-permute-start | bytes 393224 | tf_op jit(solution)/shard_map/ppermute | solution.py:47
  20.9 7.2 %collective-permute-start.3 = (bf16[4,16,1024]{2,1,0:T(8,128)(2,1)S(1)}, bf16[4,16,1024]{2,1,0:T(8,128)(2,1)S(1)}, u32[]{:S(2)}, u32[]{:S(2)}) collective-permute-start(bf16[4,16,1024]{2,1,0:T(8,128)(2,1)S(1)} %get-tuple-element.71), channel_id=1, source_target_pairs={{0,4},{1,5},{2,6},{3,7},{4,8},{5,9},{6,10},{7,11},{8,12},{9,13},{1... | collective-permute-start | bytes 393224 | tf_op jit(solution)/shard_map/ppermute | solution.py:47
  21.2 6.8 %collective-permute-start.5 = (bf16[4,16,1024]{2,1,0:T(8,128)(2,1)S(1)}, bf16[4,16,1024]{2,1,0:T(8,128)(2,1)S(1)}, u32[]{:S(2)}, u32[]{:S(2)}) collective-permute-start(bf16[4,16,1024]{2,1,0:T(8,128)(2,1)S(1)} %get-tuple-element.71), channel_id=1, source_target_pairs={{0,12},{1,13},{2,14},{3,15},{4,0},{5,1},{6,2},{7,3},{8,4},{9,5},{1... | collective-permute-start | bytes 393224 | tf_op jit(solution)/shard_map/ppermute | solution.py:47
  28.1 5.7 %collective-permute-start.6 = (bf16[4,4,16,1024]{3,2,1,0:T(8,128)(2,1)S(1)}, bf16[4,4,16,1024]{3,2,1,0:T(8,128)(2,1)S(1)}, u32[]{:S(2)}, u32[]{:S(2)}) collective-permute-start(bf16[4,4,16,1024]{3,2,1,0:T(8,128)(2,1)S(1)} %pad_maximum_fusion.1.own), channel_id=1, source_target_pairs={{0,16},{16,0},{32,48},{48,32},{64,80},{80,64},{96,112},{112,96},{1... | collective-permute-start | bytes 1572872 | tf_op jit(solution)/shard_map/ppermute | solution.py:482
  39.7 1.8 collective-permute-start.8
  39.7 2.5 %collective-permute-start.7 = (bf16[4,64,512]{2,1,0:T(8,128)(2,1)}, bf16[4,64,512]{2,1,0:T(8,128)(2,1)S(1)}, u32[]{:S(2)}, u32[]{:S(2)}) collective-permute-start(bf16[4,64,512]{2,1,0:T(8,128)(2,1)} %copy-done.14), channel_id=1, source_target_pairs={{0,16},{16,0},{32,48},{48,32},{64,80},{80,64},{96,112},{112,96},{1... | collective-permute-start | bytes 786440 | tf_op jit(solution)/shard_map/ppermute | solution.py:493
  42.3 6.5 %collective-permute-start.9 = (bf16[2,64,512]{2,1,0:T(8,128)(2,1)S(1)}, bf16[2,64,512]{2,1,0:T(8,128)(2,1)S(1)}, u32[]{:S(2)}, u32[]{:S(2)}) collective-permute-start(bf16[2,64,512]{2,1,0:T(8,128)(2,1)S(1)} %pad_maximum_fusion.5), channel_id=1, source_target_pairs={{0,32},{16,48},{32,64},{48,80},{64,96},{80,112},{96,0},{112,16},{1... | collective-permute-start | bytes 393224 | tf_op jit(solution)/shard_map/ppermute | solution.py:497
  43.7 8.9 %collective-permute-start.10 = (bf16[2,64,512]{2,1,0:T(8,128)(2,1)S(1)}, bf16[2,64,512]{2,1,0:T(8,128)(2,1)S(1)}, u32[]{:S(2)}, u32[]{:S(2)}) collective-permute-start(bf16[2,64,512]{2,1,0:T(8,128)(2,1)S(1)} %pad_maximum_fusion.6), channel_id=1, source_target_pairs={{0,64},{16,80},{32,96},{48,112},{64,0},{80,16},{96,32},{112,48},{1... | collective-permute-start | bytes 393224 | tf_op jit(solution)/shard_map/ppermute | solution.py:497
  46.4 6.2 %collective-permute-start.11 = (bf16[2,64,512]{2,1,0:T(8,128)(2,1)S(1)}, bf16[2,64,512]{2,1,0:T(8,128)(2,1)S(1)}, u32[]{:S(2)}, u32[]{:S(2)}) collective-permute-start(bf16[2,64,512]{2,1,0:T(8,128)(2,1)S(1)} %pad_maximum_fusion.7), channel_id=1, source_target_pairs={{0,96},{16,112},{32,0},{48,16},{64,32},{80,48},{96,64},{112,80},{1... | collective-permute-start | bytes 393224 | tf_op jit(solution)/shard_map/ppermute | solution.py:497
  54.1 4.9 %collective-permute-start.12 = (f32[160,128]{1,0:T(8,128)S(1)}, f32[160,128]{1,0:T(8,128)S(1)}, u32[]{:S(2)}, u32[]{:S(2)}) collective-permute-start(f32[160,128]{1,0:T(8,128)S(1)} %get-tuple-element.59), channel_id=1, source_target_pairs={{0,32},{16,48},{32,64},{48,80},{64,96},{80,112},{96,0},{112,16},{1... | collective-permute-start | bytes 245768 | tf_op jit(solution)/shard_map/ppermute | solution.py:59
  55.1 3.9 %collective-permute-start.14 = (f32[160,128]{1,0:T(8,128)S(1)}, f32[160,128]{1,0:T(8,128)S(1)}, u32[]{:S(2)}, u32[]{:S(2)}) collective-permute-start(f32[160,128]{1,0:T(8,128)S(1)} %get-tuple-element.60), channel_id=1, source_target_pairs={{0,96},{16,112},{32,0},{48,16},{64,32},{80,48},{96,64},{112,80},{1... | collective-permute-start | bytes 245768 | tf_op jit(solution)/shard_map/ppermute | solution.py:59
  56.9 4.9 %collective-permute-start.13 = (f32[160,128]{1,0:T(8,128)S(1)}, f32[160,128]{1,0:T(8,128)}, u32[]{:S(2)}, u32[]{:S(2)}) collective-permute-start(f32[160,128]{1,0:T(8,128)S(1)} %get-tuple-element.61), channel_id=1, source_target_pairs={{0,64},{16,80},{32,96},{48,112},{64,0},{80,16},{96,32},{112,48},{1... | collective-permute-start | bytes 245768 | tf_op jit(solution)/shard_map/ppermute | solution.py:59
  62.7 12.6 %collective-permute-start.15 = (bf16[16,64,1024]{2,1,0:T(8,128)(2,1)}, bf16[16,64,1024]{2,1,0:T(8,128)(2,1)S(1)}, u32[]{:S(2)}, u32[]{:S(2)}) collective-permute-start(bf16[16,64,1024]{2,1,0:T(8,128)(2,1)} %bitcast.30), channel_id=1, source_target_pairs={{0,16},{16,0},{32,48},{48,32},{64,80},{80,64},{96,112},{112,96},{1... | collective-permute-start | bytes 6291464 | tf_op jit(solution)/shard_map/ppermute | solution.py:504
  65.4 6.4 %collective-permute-start.18 = (f32[160,128]{1,0:T(8,128)S(1)}, f32[160,128]{1,0:T(8,128)S(1)}, u32[]{:S(2)}, u32[]{:S(2)}) collective-permute-start(f32[160,128]{1,0:T(8,128)S(1)} %add_add_fusion.3), channel_id=1, source_target_pairs={{0,3},{1,0},{2,1},{3,2},{4,7},{5,4},{6,5},{7,6},{8,11},{9,8},{10,9... | collective-permute-start | bytes 245768 | tf_op jit(solution)/shard_map/ppermute | solution.py:81
  68.3 5.2 %collective-permute-start.17 = (f32[160,128]{1,0:T(8,128)S(1)}, f32[160,128]{1,0:T(8,128)S(1)}, u32[]{:S(2)}, u32[]{:S(2)}) collective-permute-start(f32[160,128]{1,0:T(8,128)S(1)} %add_add_fusion.3), channel_id=1, source_target_pairs={{0,2},{1,3},{2,0},{3,1},{4,6},{5,7},{6,4},{7,5},{8,10},{9,11},{10,... | collective-permute-start | bytes 245768 | tf_op jit(solution)/shard_map/ppermute | solution.py:81
  68.3 7.1 %collective-permute-start.16 = (f32[160,128]{1,0:T(8,128)S(1)}, f32[160,128]{1,0:T(8,128)S(1)}, u32[]{:S(2)}, u32[]{:S(2)}) collective-permute-start(f32[160,128]{1,0:T(8,128)S(1)} %add_add_fusion.3), channel_id=1, source_target_pairs={{0,1},{1,2},{2,3},{3,0},{4,5},{5,6},{6,7},{7,4},{8,9},{9,10},{10,1... | collective-permute-start | bytes 245768 | tf_op jit(solution)/shard_map/ppermute | solution.py:81
  75.4 13.9 %collective-permute-start.21 = (f32[160,128]{1,0:T(8,128)S(1)}, f32[160,128]{1,0:T(8,128)S(1)}, u32[]{:S(2)}, u32[]{:S(2)}) collective-permute-start(f32[160,128]{1,0:T(8,128)S(1)} %add_add_fusion.2), channel_id=1, source_target_pairs={{0,12},{1,13},{2,14},{3,15},{4,0},{5,1},{6,2},{7,3},{8,4},{9,5},{1... | collective-permute-start | bytes 245768 | tf_op jit(solution)/shard_map/ppermute | solution.py:81
  78.2 11.1 %collective-permute-start.20 = (f32[160,128]{1,0:T(8,128)S(1)}, f32[160,128]{1,0:T(8,128)S(1)}, u32[]{:S(2)}, u32[]{:S(2)}) collective-permute-start(f32[160,128]{1,0:T(8,128)S(1)} %add_add_fusion.2), channel_id=1, source_target_pairs={{0,8},{1,9},{2,10},{3,11},{4,12},{5,13},{6,14},{7,15},{8,0},{9,1},... | collective-permute-start | bytes 245768 | tf_op jit(solution)/shard_map/ppermute | solution.py:81
  78.2 11.1 %collective-permute-start.19 = (f32[160,128]{1,0:T(8,128)S(1)}, f32[160,128]{1,0:T(8,128)S(1)}, u32[]{:S(2)}, u32[]{:S(2)}) collective-permute-start(f32[160,128]{1,0:T(8,128)S(1)} %add_add_fusion.2), channel_id=1, source_target_pairs={{0,4},{1,5},{2,6},{3,7},{4,8},{5,9},{6,10},{7,11},{8,12},{9,13},{1... | collective-permute-start | bytes 245768 | tf_op jit(solution)/shard_map/ppermute | solution.py:81
  89.3 3.5 %collective-permute-start.24 = (f32[160,128]{1,0:T(8,128)S(1)}, f32[160,128]{1,0:T(8,128)S(1)}, u32[]{:S(2)}, u32[]{:S(2)}) collective-permute-start(f32[160,128]{1,0:T(8,128)S(1)} %add_add_fusion.1), channel_id=1, source_target_pairs={{0,96},{16,112},{32,0},{48,16},{64,32},{80,48},{96,64},{112,80},{1... | collective-permute-start | bytes 245768 | tf_op jit(solution)/shard_map/ppermute | solution.py:51
  90.4 4.8 %collective-permute-start.23 = (f32[160,128]{1,0:T(8,128)S(1)}, f32[160,128]{1,0:T(8,128)S(1)}, u32[]{:S(2)}, u32[]{:S(2)}) collective-permute-start(f32[160,128]{1,0:T(8,128)S(1)} %add_add_fusion.1), channel_id=1, source_target_pairs={{0,64},{16,80},{32,96},{48,112},{64,0},{80,16},{96,32},{112,48},{1... | collective-permute-start | bytes 245768 | tf_op jit(solution)/shard_map/ppermute | solution.py:51
  91.3 4.8 %collective-permute-start.22 = (f32[160,128]{1,0:T(8,128)S(1)}, f32[160,128]{1,0:T(8,128)S(1)}, u32[]{:S(2)}, u32[]{:S(2)}) collective-permute-start(f32[160,128]{1,0:T(8,128)S(1)} %add_add_fusion.1), channel_id=1, source_target_pairs={{0,32},{16,48},{32,64},{48,80},{64,96},{80,112},{96,0},{112,16},{1... | collective-permute-start | bytes 245768 | tf_op jit(solution)/shard_map/ppermute | solution.py:51
  96.2 4.1 %collective-permute-start.25 = (f32[640,128]{1,0:T(8,128)S(1)}, f32[640,128]{1,0:T(8,128)S(1)}, u32[]{:S(2)}, u32[]{:S(2)}) collective-permute-start(f32[640,128]{1,0:T(8,128)S(1)} %pad_maximum_fusion.2), channel_id=1, source_target_pairs={{0,16},{16,0},{32,48},{48,32},{64,80},{80,64},{96,112},{112,96},{1... | collective-permute-start | bytes 983048 | tf_op jit(solution)/shard_map/ppermute | solution.py:75
  101.2 58.0 %all-to-all-start = ((bf16[128,64,128]{2,1,0:T(8,128)(2,1)}), bf16[128,64,128]{2,1,0:T(8,128)(2,1)S(1)}, u32[]{:S(2)}, u32[]{:S(2)}) async-start(bf16[128,64,128]{2,1,0:T(8,128)(2,1)} %bitcast.28), calls=%async_computation | async-start | bytes 4194304 | tf_op jit(solution)/shard_map/all_to_all | solution.py:513
  166.3 4.8 %collective-permute-start.29 = (f32[64,512]{1,0:T(8,128)S(1)}, f32[64,512]{1,0:T(8,128)S(1)}, u32[]{:S(2)}, u32[]{:S(2)}) collective-permute-start(f32[64,512]{1,0:T(8,128)S(1)} %dynamic-slice_add_fusion.1), channel_id=1, source_target_pairs={{0,96},{16,112},{32,0},{48,16},{64,32},{80,48},{96,64},{112,80},{1... | collective-permute-start | bytes 393224 | tf_op jit(solution)/shard_map/ppermute | solution.py:81
  167.9 5.9 %collective-permute-start.28 = (f32[64,512]{1,0:T(8,128)S(1)}, f32[64,512]{1,0:T(8,128)S(1)}, u32[]{:S(2)}, u32[]{:S(2)}) collective-permute-start(f32[64,512]{1,0:T(8,128)S(1)} %dynamic-slice_add_fusion.1), channel_id=1, source_target_pairs={{0,64},{16,80},{32,96},{48,112},{64,0},{80,16},{96,32},{112,48},{1... | collective-permute-start | bytes 393224 | tf_op jit(solution)/shard_map/ppermute | solution.py:81
  168.5 9.2 %collective-permute-start.27 = (f32[64,512]{1,0:T(8,128)S(1)}, f32[64,512]{1,0:T(8,128)S(1)}, u32[]{:S(2)}, u32[]{:S(2)}) collective-permute-start(f32[64,512]{1,0:T(8,128)S(1)} %dynamic-slice_add_fusion.1), channel_id=1, source_target_pairs={{0,32},{16,48},{32,64},{48,80},{64,96},{80,112},{96,0},{112,16},{1... | collective-permute-start | bytes 393224 | tf_op jit(solution)/shard_map/ppermute | solution.py:81
  (19 other events, 178.4 us)
Sparse Core Ops, SparseCore 0:
  10.2 47.9 all-gather.4
  60.3 95.9 all-gather.6

commit v6 on v5

--- a/solution.py
+++ b/solution.py
@@ -31,6 +31,18 @@
 
 
 UPPER = [(i, j) for i in range(4) for j in range(i, 4)]
+
+
+def y_pair(f):
+    return [(2 * y + c, 2 * (y ^ f) + c) for y in range(4) for c in range(2)]
+
+
+def z_pair(f):
+    return [(x * 4 + z, x * 4 + (z ^ f)) for x in range(4) for z in range(4)]
+
+
+def x_pair(f):
+    return [(x * 4 + z, (x ^ f) * 4 + z) for x in range(4) for z in range(4)]
 
 
 def dot(a, b, dims, precision=None):
@@ -77,9 +89,10 @@
     return jnp.where(first, v, other), jnp.where(first, other, v)
 
 
-def spread4(v, axis, shift):
-    got = [lax.ppermute(v, axis, shift(s)) for s in (1, 2, 3)]
-    return v + got[0] + got[1] + got[2]
+def sum4(v, axis, pairs):
+    for flip in (1, 3):
+        v = v + lax.ppermute(v, axis, pairs(flip))
+    return v
 
 
 def prep_kernel(
@@ -459,7 +472,7 @@
 
 
 def sum_row(v, core):
-    v = spread4(swap_add(v, core), "row", y_shift)
+    v = sum4(swap_add(v, core), "row", y_pair)
     return jnp.concatenate(swap_gather(v, core), axis=0)
 
 
@@ -496,20 +509,19 @@
     got = [
         lax.ppermute(jnp.stack([near[s], far[s]]), "row", y_shift(s)) for s in (1, 2, 3)
     ]
+    gram = scatter4(gram, "row", y_shift, y)
+    got, gram = lax.optimization_barrier((got, gram))
     panel = assemble(where, near, far, got).reshape(512, 512)
-    panel, gram = lax.optimization_barrier((panel, gram))
     segment = lax.all_gather(panel, "col", axis=0, tiled=False)
-    gram = scatter4(gram, "row", y_shift, y)
-    trail_own, gram = lax.optimization_barrier((trail_own, gram))
     trail_other = lax.ppermute(trail_own, "row", CORE_SWAP)
-    gram = spread4(gram, "col", z_shift)
+    gram = sum4(gram, "col", z_pair)
     trail_other, gram = lax.optimization_barrier((trail_other, gram))
-    gram = spread4(gram, "col", x_shift)
+    gram = sum4(gram, "col", x_pair)
     trail = trail_rows(where, trail_own, trail_other, atoms, grads, mean, order)
     trail, gram = lax.optimization_barrier((trail, gram))
     gram = gather4(gram, "row", y_shift, y)
+    trail, gram = lax.optimization_barrier((trail, gram))
     gram = jnp.concatenate(swap_gather(gram, core), axis=0)
-    trail, gram = lax.optimization_barrier((trail, gram))
     trail = lax.all_to_all(
         trail.reshape(128, 64, 128), ("row", "col"), 0, 0, tiled=True
     ).reshape(8, 16, 64, 128)

time: 194 us -> 191 us (0.985)
  starting transfers between devices: 48.9 us -> 53.9 us
  local copies, waits for them, and re-layouts: 15.9 us -> 12.1 us
  waiting for transfers between devices: 62.5 us -> 59.4 us
    all_to_all x1, starting transfers between devices: 5.98 us -> 11 us  [per_device(): lax.all_to_all(trail.reshape(128, 64, 128), ('row', 'col'), 0, 0, tiled=T...]
    unnamed x35 -> x27, local copies, waits for them, and re-layouts: 12.8 us -> 9.75 us
    ppermute x3, waiting for transfers between devices: 5.05 us -> 2.32 us  [per_device(): lax.ppermute(jnp.stack([near[s], far[s]]), 'row', y_shift(s))]
    ppermute x3, waiting for transfers between devices: 3.94 us -> 6.47 us  [scatter4(): lax.ppermute(lax.dynamic_slice_in_dim(v, (index + s) % 4 * n, n, 0), axis...]
    all_to_all x1, waiting for transfers between devices: 2.97 us -> 0.62 us  [per_device(): lax.all_to_all(trail.reshape(128, 64, 128), ('row', 'col'), 0, 0, tiled=T...]
    ppermute x9 -> x6, waiting for transfers between devices: 15.2 us -> 13.8 us  [sum4(): v = v + lax.ppermute(v, axis, pairs(flip))]
    ppermute x9 -> x6, starting transfers between devices: 9.64 us -> 10.8 us  [sum4(): v = v + lax.ppermute(v, axis, pairs(flip))]
  transfers between devices with their start and end apart: 34 -> 31, of which waited for: 21 -> 20; matrix products, arithmetic and copies ran while one was open for 3% -> 2% of each run, Pallas kernels for 20% -> 21%
where the time goes in v6:
time: 191 us
  waiting for transfers between devices  59.4 us (31%)
  starting transfers between devices  53.9 us (28%)
  Pallas kernels  49.3 us (26%)
  between operations  14.4 us (8%)
  local copies, waits for them, and re-layouts  12.1 us (6%)
    pallas_call x1, Pallas kernels, factor_panel(): pl.pallas_call(functools.partial(factor_kernel, float(rows_total)), out_s...  26.7 us
    all_gather x1, waiting for transfers between devices, per_device(): segment = lax.all_gather(panel, 'col', axis=0, tiled=False)  22.2 us
    ppermute x6, waiting for transfers between devices, sum4(): v = v + lax.ppermute(v, axis, pairs(flip))  13.8 us
    ppermute x6, starting transfers between devices, shifted(): return [v] + [lax.ppermute(v, axis, shift(s)) for s in (1, 2, 3)]  12.6 us
    all_to_all x1, starting transfers between devices, per_device(): lax.all_to_all(trail.reshape(128, 64, 128), ('row', 'col'), 0, 0, tiled=T...  11 us
    ppermute x6, starting transfers between devices, sum4(): v = v + lax.ppermute(v, axis, pairs(flip))  10.8 us
    unnamed x27, local copies, waits for them, and re-layouts  9.75 us
    pallas_call x1, Pallas kernels, trail_rows(): pl.pallas_call(trail_kernel, out_shape=jax.ShapeDtypeStruct((8, blocks, 6...  7.42 us
  transfers between devices with their start and end apart: 31, of which 20 were waited for; matrix products, arithmetic and copies ran while one was open for 2% of the time, Pallas kernels for 21%

profile of v6, /device:TPU:1, one launch (start us, length us, event | category | flops | bytes accessed | tf_op | source)
XLA Modules:
  0.0 190.7 jit_solution(8092249358251671171)
XLA Ops:
  9.6 4.4 %collective-permute-start.2 = (bf16[16,1024]{1,0:T(8,128)(2,1)S(1)}, bf16[16,1024]{1,0:T(8,128)(2,1)S(1)}, u32[]{:S(2)}, u32[]{:S(2)}) collective-permute-start(bf16[16,1024]{1,0:T(8,128)(2,1)S(1)} %constant_dynamic-slice_fusion.5), channel_id=1, source_target_pairs={{0,2},{1,3},{2,0},{3,1},{4,6},{5,7},{6,4},{7,5},{8,10},{9,11},{10,... | collective-permute-start | bytes 98312 | tf_op jit(solution)/shard_map/ppermute | solution.py:59
  14.8 1.9 %collective-permute-start.3 = (bf16[16,1024]{1,0:T(8,128)(2,1)S(1)}, bf16[16,1024]{1,0:T(8,128)(2,1)S(1)}, u32[]{:S(2)}, u32[]{:S(2)}) collective-permute-start(bf16[16,1024]{1,0:T(8,128)(2,1)S(1)} %constant_dynamic-slice_fusion.5), channel_id=1, source_target_pairs={{0,3},{1,0},{2,1},{3,2},{4,7},{5,4},{6,5},{7,6},{8,11},{9,8},{10,9... | collective-permute-start | bytes 98312 | tf_op jit(solution)/shard_map/ppermute | solution.py:59
  18.1 2.8 %collective-permute-start.5 = (bf16[4,16,1024]{2,1,0:T(8,128)(2,1)S(1)}, bf16[4,16,1024]{2,1,0:T(8,128)(2,1)S(1)}, u32[]{:S(2)}, u32[]{:S(2)}) collective-permute-start(bf16[4,16,1024]{2,1,0:T(8,128)(2,1)S(1)} %get-tuple-element.71), channel_id=1, source_target_pairs={{0,8},{1,9},{2,10},{3,11},{4,12},{5,13},{6,14},{7,15},{8,0},{9,1},... | collective-permute-start | bytes 393224 | tf_op jit(solution)/shard_map/ppermute | solution.py:59
  21.2 2.4 %collective-permute-start.6 = (bf16[4,16,1024]{2,1,0:T(8,128)(2,1)S(1)}, bf16[4,16,1024]{2,1,0:T(8,128)(2,1)S(1)}, u32[]{:S(2)}, u32[]{:S(2)}) collective-permute-start(bf16[4,16,1024]{2,1,0:T(8,128)(2,1)S(1)} %get-tuple-element.71), channel_id=1, source_target_pairs={{0,12},{1,13},{2,14},{3,15},{4,0},{5,1},{6,2},{7,3},{8,4},{9,5},{1... | collective-permute-start | bytes 393224 | tf_op jit(solution)/shard_map/ppermute | solution.py:59
  23.6 3.8 %collective-permute-done.4 = bf16[4,16,1024]{2,1,0:T(8,128)(2,1)S(1)} collective-permute-done((bf16[4,16,1024]{2,1,0:T(8,128)(2,1)S(1)}, bf16[4,16,1024]{2,1,0:T(8,128)(2,1)S(1)}, u32[]{:S(2)}, u32[]{:S(2)}) %collective-permute-start.4) | collective-permute-done | bytes 131104 | tf_op jit(solution)/shard_map/ppermute | solution.py:59
  27.9 2.4 %collective-permute-start.7 = (bf16[4,4,16,1024]{3,2,1,0:T(8,128)(2,1)S(1)}, bf16[4,4,16,1024]{3,2,1,0:T(8,128)(2,1)}, u32[]{:S(2)}, u32[]{:S(2)}) collective-permute-start(bf16[4,4,16,1024]{3,2,1,0:T(8,128)(2,1)S(1)} %pad_maximum_fusion.1.own), channel_id=1, source_target_pairs={{0,16},{16,0},{32,48},{48,32},{64,80},{80,64},{96,112},{112,96},{1... | collective-permute-start | bytes 1572872 | tf_op jit(solution)/shard_map/ppermute | solution.py:495
  30.4 1.9 copy-done.3
  33.8 3.1 %shard_map.95 = (bf16[4,64,512]{2,1,0:T(8,128)(2,1)S(1)}, bf16[4,64,512]{2,1,0:T(8,128)(2,1)S(1)}, f32[1280,128]{1,0:T(8,128)S(1)}) custom-call(s32[4]{0:T(128)S(1)} %pad_add_fusion.where, bf16[4,4,16,1024]{3,2,1,0:T(8,128)(2,1)S(1)} %pad_maximum_fusion.1.own, bf16[4,4,16,1024]{3,2,1,0:T(8,128)(2,1)} %collective-permute-done.7.other, ...), custom_call_target="tpu_custom_call" | custom-call | flops 1140850688 | bytes 5242880 | tf_op jit(solution)/shard_map/pallas_call | solution.py:264
  42.0 2.7 %collective-permute-start.11 = (bf16[2,64,512]{2,1,0:T(8,128)(2,1)S(1)}, bf16[2,64,512]{2,1,0:T(8,128)(2,1)S(1)}, u32[]{:S(2)}, u32[]{:S(2)}) collective-permute-start(bf16[2,64,512]{2,1,0:T(8,128)(2,1)S(1)} %pad_maximum_fusion.6), channel_id=1, source_target_pairs={{0,64},{16,80},{32,96},{48,112},{64,0},{80,16},{96,32},{112,48},{1... | collective-permute-start | bytes 393224 | tf_op jit(solution)/shard_map/ppermute | solution.py:510
  44.8 2.7 %collective-permute-start.15 = (f32[160,128]{1,0:T(8,128)S(1)}, f32[160,128]{1,0:T(8,128)S(1)}, u32[]{:S(2)}, u32[]{:S(2)}) collective-permute-start(f32[160,128]{1,0:T(8,128)S(1)} %get-tuple-element.60), channel_id=1, source_target_pairs={{0,96},{16,112},{32,0},{48,16},{64,32},{80,48},{96,64},{112,80},{1... | collective-permute-start | bytes 245768 | tf_op jit(solution)/shard_map/ppermute | solution.py:71
  47.5 5.1 %collective-permute-done.13 = f32[160,128]{1,0:T(8,128)S(1)} collective-permute-done((f32[160,128]{1,0:T(8,128)S(1)}, f32[160,128]{1,0:T(8,128)S(1)}, u32[]{:S(2)}, u32[]{:S(2)}) %collective-permute-start.13) | collective-permute-done | bytes 81952 | tf_op jit(solution)/shard_map/ppermute | solution.py:71
  54.5 2.3 %collective-permute-done.12.got3 = bf16[2,64,512]{2,1,0:T(8,128)(2,1)S(1)} collective-permute-done((bf16[2,64,512]{2,1,0:T(8,128)(2,1)S(1)}, bf16[2,64,512]{2,1,0:T(8,128)(2,1)S(1)}, u32[]{:S(2)}, u32[]{:S(2)}) %collective-permute-start.12) | collective-permute-done | bytes 131104 | tf_op jit(solution)/shard_map/ppermute | solution.py:510
  58.2 2.0 %collective-permute-start = (bf16[16,64,1024]{2,1,0:T(8,128)(2,1)}, bf16[16,64,1024]{2,1,0:T(8,128)(2,1)S(1)}, u32[]{:S(2)}, u32[]{:S(2)}) collective-permute-start(bf16[16,64,1024]{2,1,0:T(8,128)(2,1)} %bitcast.27), channel_id=1, source_target_pairs={{0,16},{16,0},{32,48},{48,32},{64,80},{80,64},{96,112},{112,96},{1... | collective-permute-start | bytes 6291464 | tf_op jit(solution)/shard_map/ppermute | solution.py:516
  61.1 3.2 %collective-permute-done.16 = f32[160,128]{1,0:T(8,128)S(1)} collective-permute-done((f32[160,128]{1,0:T(8,128)S(1)}, f32[160,128]{1,0:T(8,128)S(1)}, u32[]{:S(2)}, u32[]{:S(2)}) %collective-permute-start.16) | collective-permute-done | bytes 81952 | tf_op jit(solution)/shard_map/ppermute | solution.py:94
  64.3 2.7 %collective-permute-start.17 = (f32[160,128]{1,0:T(8,128)S(1)}, f32[160,128]{1,0:T(8,128)S(1)}, u32[]{:S(2)}, u32[]{:S(2)}) collective-permute-start(f32[160,128]{1,0:T(8,128)S(1)} %add.123), channel_id=1, source_target_pairs={{0,3},{1,2},{2,1},{3,0},{4,7},{5,6},{6,5},{7,4},{8,11},{9,10},{10,... | collective-permute-start | bytes 245768 | tf_op jit(solution)/shard_map/ppermute | solution.py:94
  67.0 1.9 %collective-permute-done.17 = f32[160,128]{1,0:T(8,128)S(1)} collective-permute-done((f32[160,128]{1,0:T(8,128)S(1)}, f32[160,128]{1,0:T(8,128)S(1)}, u32[]{:S(2)}, u32[]{:S(2)}) %collective-permute-start.17) | collective-permute-done | bytes 81952 | tf_op jit(solution)/shard_map/ppermute | solution.py:94
  69.9 2.4 %collective-permute-done.18 = f32[160,128]{1,0:T(8,128)S(1)} collective-permute-done((f32[160,128]{1,0:T(8,128)S(1)}, f32[160,128]{1,0:T(8,128)S(1)}, u32[]{:S(2)}, u32[]{:S(2)}) %collective-permute-start.18) | collective-permute-done | bytes 81952 | tf_op jit(solution)/shard_map/ppermute | solution.py:94
  72.3 2.7 %collective-permute-start.19 = (f32[160,128]{1,0:T(8,128)S(1)}, f32[160,128]{1,0:T(8,128)S(1)}, u32[]{:S(2)}, u32[]{:S(2)}) collective-permute-start(f32[160,128]{1,0:T(8,128)S(1)} %add.125), channel_id=1, source_target_pairs={{0,12},{1,13},{2,14},{3,15},{4,8},{5,9},{6,10},{7,11},{8,4},{9,5},... | collective-permute-start | bytes 245768 | tf_op jit(solution)/shard_map/ppermute | solution.py:94
  75.0 1.6 copy-done.8
  76.6 7.4 %shard_map.96 = bf16[8,16,64,128]{3,2,1,0:T(8,128)(2,1)S(1)} custom-call(s32[4]{0:T(128)S(1)} %pad_add_fusion.where, bf16[16,64,1024]{2,1,0:T(8,128)(2,1)S(1)} %bitcast.28, bf16[16,64,1024]{2,1,0:T(8,128)(2,1)S(1)} %collective-permute-done.other_ref, bf16[320,1024]{1,0:T(8,128)(2,1)S(1)} %copy-done.10, bf16[768,1024]{1,0:T(8,128)(2,1)S(1)} %get-tuple-element.29.grads_ref, ...), custom_call_target="tpu_custom_call" | custom-call | flops 4563402752 | bytes 9437184 | tf_op jit(solution)/shard_map/pallas_call | solution.py:297
  85.4 2.1 %collective-permute-start.22 = (f32[160,128]{1,0:T(8,128)S(1)}, f32[160,128]{1,0:T(8,128)S(1)}, u32[]{:S(2)}, u32[]{:S(2)}) collective-permute-start(f32[160,128]{1,0:T(8,128)S(1)} %add.126), channel_id=1, source_target_pairs={{0,96},{16,112},{32,0},{48,16},{64,32},{80,48},{96,64},{112,80},{1... | collective-permute-start | bytes 245768 | tf_op jit(solution)/shard_map/ppermute | solution.py:63
  89.0 3.4 %collective-permute-done.21 = f32[160,128]{1,0:T(8,128)S(1)} collective-permute-done((f32[160,128]{1,0:T(8,128)S(1)}, f32[160,128]{1,0:T(8,128)S(1)}, u32[]{:S(2)}, u32[]{:S(2)}) %collective-permute-start.21) | collective-permute-done | bytes 81952 | tf_op jit(solution)/shard_map/ppermute | solution.py:63
  93.2 11.0 %all-to-all-start = ((bf16[128,64,128]{2,1,0:T(8,128)(2,1)}), bf16[128,64,128]{2,1,0:T(8,128)(2,1)S(1)}, u32[]{:S(2)}, u32[]{:S(2)}) async-start(bf16[128,64,128]{2,1,0:T(8,128)(2,1)} %bitcast.25), calls=%async_computation | async-start | bytes 4194304 | tf_op jit(solution)/shard_map/all_to_all | solution.py:525
  106.7 26.7 %shard_map.97 = (f32[512,512]{1,0:T(8,128)}, f32[512,512]{1,0:T(8,128)S(1)}) custom-call(f32[1280,128]{1,0:T(8,128)S(1)} %pad_maximum_fusion.gram_ref), custom_call_target="tpu_custom_call" | custom-call | flops 2684354560 | bytes 4194304 | tf_op jit(solution)/shard_map/pallas_call | solution.py:386
  133.4 22.2 %all-gather.4.cloned.1.call-done.panel_ref = bf16[16,512,512]{2,1,0:T(8,128)(2,1)} async-done(((bf16[1,512,512]{2,1,0:T(8,128)(2,1)}), bf16[16,512,512]{2,1,0:T(8,128)(2,1)}) %all-gather.4.cloned.1.call-update) | async-done | bytes 8388624 | tf_op jit(solution)/shard_map/all_gather | solution.py:515
  156.2 3.4 %copy-done.1 = bf16[16,512,512]{2,1,0:T(8,128)(2,1)S(1)} copy-done((bf16[16,512,512]{2,1,0:T(8,128)(2,1)S(1)}, bf16[16,512,512]{2,1,0:T(8,128)(2,1)}, u32[]{:S(2)}) %copy-start.1) | copy-done | bytes 8388632
  159.6 2.1 %shard_map.99 = f32[128,512]{1,0:T(8,128)S(1)} custom-call(bf16[16,512,512]{2,1,0:T(8,128)(2,1)S(1)} %copy-done.1, bf16[8,16,64,128]{3,2,1,0:T(8,128)(2,1)S(1)} %bitcast.22), custom_call_target="tpu_custom_call" | custom-call | flops 1073741824 | bytes 11534336 | tf_op jit(solution)/shard_map/pallas_call | solution.py:411
  164.4 3.6 %collective-permute-done.25 = f32[64,512]{1,0:T(8,128)S(1)} collective-permute-done((f32[64,512]{1,0:T(8,128)S(1)}, f32[64,512]{1,0:T(8,128)S(1)}, u32[]{:S(2)}, u32[]{:S(2)}) %collective-permute-start.25) | collective-permute-done | bytes 131104 | tf_op jit(solution)/shard_map/ppermute | solution.py:94
  168.0 2.5 %collective-permute-start.26 = (f32[64,512]{1,0:T(8,128)S(1)}, f32[64,512]{1,0:T(8,128)S(1)}, u32[]{:S(2)}, u32[]{:S(2)}) collective-permute-start(f32[64,512]{1,0:T(8,128)S(1)} %add.133), channel_id=1, source_target_pairs={{0,96},{16,112},{32,64},{48,80},{64,32},{80,48},{96,0},{112,16},{1... | collective-permute-start | bytes 393224 | tf_op jit(solution)/shard_map/ppermute | solution.py:94
  170.5 2.6 %collective-permute-done.26 = f32[64,512]{1,0:T(8,128)S(1)} collective-permute-done((f32[64,512]{1,0:T(8,128)S(1)}, f32[64,512]{1,0:T(8,128)S(1)}, u32[]{:S(2)}, u32[]{:S(2)}) %collective-permute-start.26) | collective-permute-done | bytes 131104 | tf_op jit(solution)/shard_map/ppermute | solution.py:94
  173.2 2.4 %collective-permute-start.27 = (f32[64,512]{1,0:T(8,128)S(1)}, f32[64,512]{1,0:T(8,128)S(1)}, u32[]{:S(2)}, u32[]{:S(2)}) collective-permute-start(f32[64,512]{1,0:T(8,128)S(1)} %add.134), channel_id=1, source_target_pairs={{0,16},{16,0},{32,48},{48,32},{64,80},{80,64},{96,112},{112,96},{1... | collective-permute-start | bytes 393224 | tf_op jit(solution)/shard_map/ppermute | solution.py:87
  176.6 7.2 %shard_map.100 = (f32[128,512]{1,0:T(8,128)}, f32[128,8192]{1,0:T(8,128)}) custom-call(f32[128,512]{1,0:T(8,128)S(1)} %pad_maximum_fusion.3.cross_ref, f32[512,512]{1,0:T(8,128)S(1)} %get-tuple-element.50.inverse_ref, bf16[16,512,512]{2,1,0:T(8,128)(2,1)S(1)} %copy-done.2, bf16[8,16,64,128]{3,2,1,0:T(8,128)(2,1)S(1)} %bitcast.23), custom_call_target="tpu_custom_call" | custom-call | flops 2147483648 | bytes 16777216 | tf_op jit(solution)/shard_map/pallas_call | solution.py:452
  (96 shorter events, 27.6 us)
Async XLA Ops:
  7.2 51.0 %all-gather.6.cloned.1.call-start = ((), (), s32[]{:S(2)}) async-start(), calls=%async_computation.2 | async-start | bytes 2228224 | tf_op jit(solution)/shard_map/all_gather | solution.py:491
  8.8 146.8 %all-gather.4.cloned.1.call-start = ((), (), s32[]{:S(2)}) async-start(), calls=%async_computation.1 | async-start | bytes 8912896 | tf_op jit(solution)/shard_map/all_gather | solution.py:515
  9.6 7.9 %collective-permute-start.2 = (bf16[16,1024]{1,0:T(8,128)(2,1)S(1)}, bf16[16,1024]{1,0:T(8,128)(2,1)S(1)}, u32[]{:S(2)}, u32[]{:S(2)}) collective-permute-start(bf16[16,1024]{1,0:T(8,128)(2,1)S(1)} %constant_dynamic-slice_fusion.5), channel_id=1, source_target_pairs={{0,2},{1,3},{2,0},{3,1},{4,6},{5,7},{6,4},{7,5},{8,10},{9,11},{10,... | collective-permute-start | bytes 98312 | tf_op jit(solution)/shard_map/ppermute | solution.py:59
  14.1 4.0 %collective-permute-start.1 = (bf16[16,1024]{1,0:T(8,128)(2,1)S(1)}, bf16[16,1024]{1,0:T(8,128)(2,1)S(1)}, u32[]{:S(2)}, u32[]{:S(2)}) collective-permute-start(bf16[16,1024]{1,0:T(8,128)(2,1)S(1)} %constant_dynamic-slice_fusion.5), channel_id=1, source_target_pairs={{0,1},{1,2},{2,3},{3,0},{4,5},{5,6},{6,7},{7,4},{8,9},{9,10},{10,1... | collective-permute-start | bytes 98312 | tf_op jit(solution)/shard_map/ppermute | solution.py:59
  14.8 3.2 %collective-permute-start.3 = (bf16[16,1024]{1,0:T(8,128)(2,1)S(1)}, bf16[16,1024]{1,0:T(8,128)(2,1)S(1)}, u32[]{:S(2)}, u32[]{:S(2)}) collective-permute-start(bf16[16,1024]{1,0:T(8,128)(2,1)S(1)} %constant_dynamic-slice_fusion.5), channel_id=1, source_target_pairs={{0,3},{1,0},{2,1},{3,2},{4,7},{5,4},{6,5},{7,6},{8,11},{9,8},{10,9... | collective-permute-start | bytes 98312 | tf_op jit(solution)/shard_map/ppermute | solution.py:59
  18.1 5.5 %collective-permute-start.5 = (bf16[4,16,1024]{2,1,0:T(8,128)(2,1)S(1)}, bf16[4,16,1024]{2,1,0:T(8,128)(2,1)S(1)}, u32[]{:S(2)}, u32[]{:S(2)}) collective-permute-start(bf16[4,16,1024]{2,1,0:T(8,128)(2,1)S(1)} %get-tuple-element.71), channel_id=1, source_target_pairs={{0,8},{1,9},{2,10},{3,11},{4,12},{5,13},{6,14},{7,15},{8,0},{9,1},... | collective-permute-start | bytes 393224 | tf_op jit(solution)/shard_map/ppermute | solution.py:59
  20.9 6.4 %collective-permute-start.4 = (bf16[4,16,1024]{2,1,0:T(8,128)(2,1)S(1)}, bf16[4,16,1024]{2,1,0:T(8,128)(2,1)S(1)}, u32[]{:S(2)}, u32[]{:S(2)}) collective-permute-start(bf16[4,16,1024]{2,1,0:T(8,128)(2,1)S(1)} %get-tuple-element.71), channel_id=1, source_target_pairs={{0,4},{1,5},{2,6},{3,7},{4,8},{5,9},{6,10},{7,11},{8,12},{9,13},{1... | collective-permute-start | bytes 393224 | tf_op jit(solution)/shard_map/ppermute | solution.py:59
  21.2 6.6 %collective-permute-start.6 = (bf16[4,16,1024]{2,1,0:T(8,128)(2,1)S(1)}, bf16[4,16,1024]{2,1,0:T(8,128)(2,1)S(1)}, u32[]{:S(2)}, u32[]{:S(2)}) collective-permute-start(bf16[4,16,1024]{2,1,0:T(8,128)(2,1)S(1)} %get-tuple-element.71), channel_id=1, source_target_pairs={{0,12},{1,13},{2,14},{3,15},{4,0},{5,1},{6,2},{7,3},{8,4},{9,5},{1... | collective-permute-start | bytes 393224 | tf_op jit(solution)/shard_map/ppermute | solution.py:59
  27.9 5.9 %collective-permute-start.7 = (bf16[4,4,16,1024]{3,2,1,0:T(8,128)(2,1)S(1)}, bf16[4,4,16,1024]{3,2,1,0:T(8,128)(2,1)}, u32[]{:S(2)}, u32[]{:S(2)}) collective-permute-start(bf16[4,4,16,1024]{3,2,1,0:T(8,128)(2,1)S(1)} %pad_maximum_fusion.1.own), channel_id=1, source_target_pairs={{0,16},{16,0},{32,48},{48,32},{64,80},{80,64},{96,112},{112,96},{1... | collective-permute-start | bytes 1572872 | tf_op jit(solution)/shard_map/ppermute | solution.py:495
  37.7 1.8 collective-permute-start.9
  37.9 2.7 %collective-permute-start.8 = (bf16[4,64,512]{2,1,0:T(8,128)(2,1)}, bf16[4,64,512]{2,1,0:T(8,128)(2,1)S(1)}, u32[]{:S(2)}, u32[]{:S(2)}) collective-permute-start(bf16[4,64,512]{2,1,0:T(8,128)(2,1)} %copy-done.11), channel_id=1, source_target_pairs={{0,16},{16,0},{32,48},{48,32},{64,80},{80,64},{96,112},{112,96},{1... | collective-permute-start | bytes 786440 | tf_op jit(solution)/shard_map/ppermute | solution.py:506
  40.6 34.4 %copy-start.10 = (bf16[320,1024]{1,0:T(8,128)(2,1)S(1)}, bf16[320,1024]{1,0:T(8,128)(2,1)}, u32[]{:S(2)}) copy-start(bf16[320,1024]{1,0:T(8,128)(2,1)} %copy-done.9) | copy-start | bytes 1966084
  40.6 13.9 %collective-permute-start.10 = (bf16[2,64,512]{2,1,0:T(8,128)(2,1)S(1)}, bf16[2,64,512]{2,1,0:T(8,128)(2,1)S(1)}, u32[]{:S(2)}, u32[]{:S(2)}) collective-permute-start(bf16[2,64,512]{2,1,0:T(8,128)(2,1)S(1)} %pad_maximum_fusion.5), channel_id=1, source_target_pairs={{0,32},{16,48},{32,64},{48,80},{64,96},{80,112},{96,0},{112,16},{1... | collective-permute-start | bytes 393224 | tf_op jit(solution)/shard_map/ppermute | solution.py:510
  42.0 12.5 %collective-permute-start.11 = (bf16[2,64,512]{2,1,0:T(8,128)(2,1)S(1)}, bf16[2,64,512]{2,1,0:T(8,128)(2,1)S(1)}, u32[]{:S(2)}, u32[]{:S(2)}) collective-permute-start(bf16[2,64,512]{2,1,0:T(8,128)(2,1)S(1)} %pad_maximum_fusion.6), channel_id=1, source_target_pairs={{0,64},{16,80},{32,96},{48,112},{64,0},{80,16},{96,32},{112,48},{1... | collective-permute-start | bytes 393224 | tf_op jit(solution)/shard_map/ppermute | solution.py:510
  44.7 7.9 %collective-permute-start.13 = (f32[160,128]{1,0:T(8,128)S(1)}, f32[160,128]{1,0:T(8,128)S(1)}, u32[]{:S(2)}, u32[]{:S(2)}) collective-permute-start(f32[160,128]{1,0:T(8,128)S(1)} %get-tuple-element.59), channel_id=1, source_target_pairs={{0,32},{16,48},{32,64},{48,80},{64,96},{80,112},{96,0},{112,16},{1... | collective-permute-start | bytes 245768 | tf_op jit(solution)/shard_map/ppermute | solution.py:71
  44.8 8.3 %collective-permute-start.15 = (f32[160,128]{1,0:T(8,128)S(1)}, f32[160,128]{1,0:T(8,128)S(1)}, u32[]{:S(2)}, u32[]{:S(2)}) collective-permute-start(f32[160,128]{1,0:T(8,128)S(1)} %get-tuple-element.60), channel_id=1, source_target_pairs={{0,96},{16,112},{32,0},{48,16},{64,32},{80,48},{96,64},{112,80},{1... | collective-permute-start | bytes 245768 | tf_op jit(solution)/shard_map/ppermute | solution.py:71
  47.5 7.0 %collective-permute-start.14 = (f32[160,128]{1,0:T(8,128)S(1)}, f32[160,128]{1,0:T(8,128)S(1)}, u32[]{:S(2)}, u32[]{:S(2)}) collective-permute-start(f32[160,128]{1,0:T(8,128)S(1)} %get-tuple-element.61), channel_id=1, source_target_pairs={{0,64},{16,80},{32,96},{48,112},{64,0},{80,16},{96,32},{112,48},{1... | collective-permute-start | bytes 245768 | tf_op jit(solution)/shard_map/ppermute | solution.py:71
  52.6 4.2 %collective-permute-start.12 = (bf16[2,64,512]{2,1,0:T(8,128)(2,1)S(1)}, bf16[2,64,512]{2,1,0:T(8,128)(2,1)S(1)}, u32[]{:S(2)}, u32[]{:S(2)}) collective-permute-start(bf16[2,64,512]{2,1,0:T(8,128)(2,1)S(1)} %pad_maximum_fusion.7), channel_id=1, source_target_pairs={{0,96},{16,112},{32,0},{48,16},{64,32},{80,48},{96,64},{112,80},{1... | collective-permute-start | bytes 393224 | tf_op jit(solution)/shard_map/ppermute | solution.py:510
  58.2 10.7 %collective-permute-start = (bf16[16,64,1024]{2,1,0:T(8,128)(2,1)}, bf16[16,64,1024]{2,1,0:T(8,128)(2,1)S(1)}, u32[]{:S(2)}, u32[]{:S(2)}) collective-permute-start(bf16[16,64,1024]{2,1,0:T(8,128)(2,1)} %bitcast.27), channel_id=1, source_target_pairs={{0,16},{16,0},{32,48},{48,32},{64,80},{80,64},{96,112},{112,96},{1... | collective-permute-start | bytes 6291464 | tf_op jit(solution)/shard_map/ppermute | solution.py:516
  60.3 4.1 %collective-permute-start.16 = (f32[160,128]{1,0:T(8,128)S(1)}, f32[160,128]{1,0:T(8,128)S(1)}, u32[]{:S(2)}, u32[]{:S(2)}) collective-permute-start(f32[160,128]{1,0:T(8,128)S(1)} %add_add_fusion), channel_id=1, source_target_pairs={{0,1},{1,0},{2,3},{3,2},{4,5},{5,4},{6,7},{7,6},{8,9},{9,8},{10,11... | collective-permute-start | bytes 245768 | tf_op jit(solution)/shard_map/ppermute | solution.py:94
  64.3 4.6 %collective-permute-start.17 = (f32[160,128]{1,0:T(8,128)S(1)}, f32[160,128]{1,0:T(8,128)S(1)}, u32[]{:S(2)}, u32[]{:S(2)}) collective-permute-start(f32[160,128]{1,0:T(8,128)S(1)} %add.123), channel_id=1, source_target_pairs={{0,3},{1,2},{2,1},{3,0},{4,7},{5,6},{6,5},{7,4},{8,11},{9,10},{10,... | collective-permute-start | bytes 245768 | tf_op jit(solution)/shard_map/ppermute | solution.py:94
  68.9 3.4 %collective-permute-start.18 = (f32[160,128]{1,0:T(8,128)S(1)}, f32[160,128]{1,0:T(8,128)S(1)}, u32[]{:S(2)}, u32[]{:S(2)}) collective-permute-start(f32[160,128]{1,0:T(8,128)S(1)} %add.124), channel_id=1, source_target_pairs={{0,4},{1,5},{2,6},{3,7},{4,0},{5,1},{6,2},{7,3},{8,12},{9,13},{10,... | collective-permute-start | bytes 245768 | tf_op jit(solution)/shard_map/ppermute | solution.py:94
  72.3 13.0 %collective-permute-start.19 = (f32[160,128]{1,0:T(8,128)S(1)}, f32[160,128]{1,0:T(8,128)S(1)}, u32[]{:S(2)}, u32[]{:S(2)}) collective-permute-start(f32[160,128]{1,0:T(8,128)S(1)} %add.125), channel_id=1, source_target_pairs={{0,12},{1,13},{2,14},{3,15},{4,8},{5,9},{6,10},{7,11},{8,4},{9,5},... | collective-permute-start | bytes 245768 | tf_op jit(solution)/shard_map/ppermute | solution.py:94
  85.4 3.6 %collective-permute-start.22 = (f32[160,128]{1,0:T(8,128)S(1)}, f32[160,128]{1,0:T(8,128)S(1)}, u32[]{:S(2)}, u32[]{:S(2)}) collective-permute-start(f32[160,128]{1,0:T(8,128)S(1)} %add.126), channel_id=1, source_target_pairs={{0,96},{16,112},{32,0},{48,16},{64,32},{80,48},{96,64},{112,80},{1... | collective-permute-start | bytes 245768 | tf_op jit(solution)/shard_map/ppermute | solution.py:63
  87.5 4.9 %collective-permute-start.21 = (f32[160,128]{1,0:T(8,128)S(1)}, f32[160,128]{1,0:T(8,128)S(1)}, u32[]{:S(2)}, u32[]{:S(2)}) collective-permute-start(f32[160,128]{1,0:T(8,128)S(1)} %add.126), channel_id=1, source_target_pairs={{0,64},{16,80},{32,96},{48,112},{64,0},{80,16},{96,32},{112,48},{1... | collective-permute-start | bytes 245768 | tf_op jit(solution)/shard_map/ppermute | solution.py:63
  87.7 5.4 %collective-permute-start.20 = (f32[160,128]{1,0:T(8,128)S(1)}, f32[160,128]{1,0:T(8,128)S(1)}, u32[]{:S(2)}, u32[]{:S(2)}) collective-permute-start(f32[160,128]{1,0:T(8,128)S(1)} %add.126), channel_id=1, source_target_pairs={{0,32},{16,48},{32,64},{48,80},{64,96},{80,112},{96,0},{112,16},{1... | collective-permute-start | bytes 245768 | tf_op jit(solution)/shard_map/ppermute | solution.py:63
  93.2 63.0 %all-to-all-start = ((bf16[128,64,128]{2,1,0:T(8,128)(2,1)}), bf16[128,64,128]{2,1,0:T(8,128)(2,1)S(1)}, u32[]{:S(2)}, u32[]{:S(2)}) async-start(bf16[128,64,128]{2,1,0:T(8,128)(2,1)} %bitcast.25), calls=%async_computation | async-start | bytes 4194304 | tf_op jit(solution)/shard_map/all_to_all | solution.py:525
  104.2 2.4 %collective-permute-start.23 = (f32[640,128]{1,0:T(8,128)S(1)}, f32[640,128]{1,0:T(8,128)S(1)}, u32[]{:S(2)}, u32[]{:S(2)}) collective-permute-start(f32[640,128]{1,0:T(8,128)S(1)} %pad_maximum_fusion.2), channel_id=1, source_target_pairs={{0,16},{16,0},{32,48},{48,32},{64,80},{80,64},{96,112},{112,96},{1... | collective-permute-start | bytes 983048 | tf_op jit(solution)/shard_map/ppermute | solution.py:87
  161.7 1.5 collective-permute-start.24
  163.2 4.8 %collective-permute-start.25 = (f32[64,512]{1,0:T(8,128)S(1)}, f32[64,512]{1,0:T(8,128)S(1)}, u32[]{:S(2)}, u32[]{:S(2)}) collective-permute-start(f32[64,512]{1,0:T(8,128)S(1)} %dynamic-slice_add_fusion.1), channel_id=1, source_target_pairs={{0,32},{16,48},{32,0},{48,16},{64,96},{80,112},{96,64},{112,80},{1... | collective-permute-start | bytes 393224 | tf_op jit(solution)/shard_map/ppermute | solution.py:94
  168.0 5.1 %collective-permute-start.26 = (f32[64,512]{1,0:T(8,128)S(1)}, f32[64,512]{1,0:T(8,128)S(1)}, u32[]{:S(2)}, u32[]{:S(2)}) collective-permute-start(f32[64,512]{1,0:T(8,128)S(1)} %add.133), channel_id=1, source_target_pairs={{0,96},{16,112},{32,64},{48,80},{64,32},{80,48},{96,0},{112,16},{1... | collective-permute-start | bytes 393224 | tf_op jit(solution)/shard_map/ppermute | solution.py:94
  173.2 3.4 %collective-permute-start.27 = (f32[64,512]{1,0:T(8,128)S(1)}, f32[64,512]{1,0:T(8,128)S(1)}, u32[]{:S(2)}, u32[]{:S(2)}) collective-permute-start(f32[64,512]{1,0:T(8,128)S(1)} %add.134), channel_id=1, source_target_pairs={{0,16},{16,0},{32,48},{48,32},{64,80},{80,64},{96,112},{112,96},{1... | collective-permute-start | bytes 393224 | tf_op jit(solution)/shard_map/ppermute | solution.py:87
  (12 other events, 122.9 us)
Sparse Core Ops, SparseCore 0:
  10.8 46.9 all-gather.5
  59.9 95.6 all-gather.3

commit v7 on v6

--- a/solution.py
+++ b/solution.py
@@ -30,6 +30,8 @@
     return [(x * 4 + z, ((x + s) % 4) * 4 + z) for x in range(4) for z in range(4)]
 
 
+SENT = 56
+HELD = 400
 UPPER = [(i, j) for i in range(4) for j in range(i, 4)]
 
 
@@ -96,7 +98,7 @@
 
 
 def prep_kernel(
-    count_ref, owner_ref, neighbor_ref, desc_ref, grad_ref, atoms_ref, grads_ref, mean_ref, order_ref
+    where, count_ref, owner_ref, neighbor_ref, desc_ref, grad_ref, atoms_ref, grads_ref, mean_ref, order_ref
 ):
     counts = [count_ref[0, s] for s in range(8)]
     owners = [owner_ref[0, s] for s in range(8)]
@@ -142,10 +144,11 @@
     inside = (atom8 >= low) & (atom8 < low + size8)
     mean_ref[...] = jnp.where(inside, 1.0 / size8.astype(F32), 0.0)
 
-    r = lax.broadcasted_iota(jnp.int32, (64, 256), 0)
-    wanted = lax.broadcasted_iota(jnp.int32, (64, 256), 1)
-    third = ((r - 1) * 43) >> 7
-    part = (r - 1) - 3 * third
+    source = 2 * where[2] + where[3]
+    r = lax.broadcasted_iota(jnp.int32, (SENT, 256), 0)
+    wanted = lax.broadcasted_iota(jnp.int32, (SENT, 256), 1)
+    third = (r * 43) >> 7
+    part = r - 3 * third
     for g in range(8):
         struct_g, count_g, offset_g = jnp.int32(0), jnp.int32(0), jnp.int32(0)
         for s in range(8):
@@ -153,12 +156,12 @@
             struct_g = jnp.where(mine, s, struct_g)
             count_g = jnp.where(mine, counts[s], count_g)
             offset_g = jnp.where(mine, offsets[s], offset_g)
-        column = jnp.where(third < count_g, part * 64 + offset_g + third, -1)
-        column = jnp.where(r == 0, 192 + struct_g, column)
-        order_ref[64 * g : 64 * g + 64] = (column == wanted).astype(F32).astype(BF16)
-
-
-def prepare(count, owner, neighbors, descriptors, gradients):
+        column = jnp.where((third < count_g) & (r < 48), part * 64 + offset_g + third, -1)
+        column = jnp.where(r == 48 + source, 192 + struct_g, column)
+        order_ref[SENT * g : SENT * g + SENT] = (column == wanted).astype(F32)
+
+
+def prepare(where, count, owner, neighbors, descriptors, gradients):
     smem = pl.BlockSpec(memory_space=pltpu.SMEM)
     vmem = pl.BlockSpec(memory_space=pltpu.VMEM)
     return pl.pallas_call(
@@ -167,15 +170,15 @@
             jax.ShapeDtypeStruct((320, 1024), BF16),
             jax.ShapeDtypeStruct((768, 1024), BF16),
             jax.ShapeDtypeStruct((8, 64), F32),
-            jax.ShapeDtypeStruct((512, 256), BF16),
-        ),
-        in_specs=[smem, smem, vmem, vmem, vmem],
+            jax.ShapeDtypeStruct((8 * SENT, 256), F32),
+        ),
+        in_specs=[smem, smem, smem, vmem, vmem, vmem],
         out_specs=(vmem, vmem, vmem, vmem),
         compiler_params=params(),
         cost_estimate=pl.CostEstimate(
             flops=2 * 64 * 128 * 1024 * 17, bytes_accessed=6 << 20, transcendentals=0
         ),
-    )(count, owner, neighbors, descriptors, gradients)
+    )(where, count, owner, neighbors, descriptors, gradients)
 
 
 def compact_rows(env, atoms, grads, mean):
@@ -211,13 +214,14 @@
             place = ((x - i) & 3) * 4 + ((z - j) & 3)
             put_env(env, where, own, other, (i, j), place * 32)
     rows = compact_rows(env[...], atoms_ref[...], grads_ref[...], mean_ref[...])
-    full = dot(order_ref[...], rows, NN).astype(BF16)
+    full = dot(order_ref[...].astype(BF16), rows, NN)
     first = core == 0
     for i in range(4):
-        low, high = full[128 * i : 128 * i + 64], full[128 * i + 64 : 128 * i + 128]
+        at = 2 * SENT * i
+        low, high = full[at : at + SENT], full[at + SENT : at + 2 * SENT]
         s = (i - y) & 3
-        near_ref[s] = jnp.where(first, low, high)
-        far_ref[s] = jnp.where(first, high, low)
+        near_ref[s] = jnp.where(first, low, high).astype(BF16)
+        far_ref[s] = jnp.where(first, high, low).astype(BF16)
     gram = dot(rows, rows, TN)
     for n, (i, j) in enumerate(UPPER):
         gram_ref[128 * n : 128 * n + 128] = gram[
@@ -233,19 +237,31 @@
     low, high = jnp.where(first, own, other), jnp.where(first, other, own)
     env = jnp.concatenate([low, high], axis=1).reshape(-1, 1024)
     rows = compact_rows(env, atoms_ref[...], grads_ref[...], mean_ref[...])
-    full = dot(order_ref[...], rows, NN).astype(BF16)
+    full = dot(order_ref[...].astype(BF16), rows, NN)
     for c in range(out_ref.shape[1]):
-        out_ref[:, c] = full[:, c * 128 : c * 128 + 128].reshape(8, 64, 128)
+        part = full[:, c * 128 : c * 128 + 128].reshape(8, SENT, 128)
+        out_ref[:, c] = part.astype(BF16)
 
 
 def assemble_kernel(where, near, far, got1, got2, got3, out):
     y, core = where[2], where[3]
-    out[2 * y + core] = near[0]
-    out[2 * y + 1 - core] = far[0]
+    blocks = [(near, 0, 0, core), (far, 0, 0, 1 - core)]
     for s, got in ((1, got1), (2, got2), (3, got3)):
-        at = 2 * ((y - s) & 3)
-        out[at + core] = got[0]
-        out[at + 1 - core] = got[1]
+        blocks += [(got, 0, s, core), (got, 1, s, 1 - core)]
+    energy = jnp.zeros((8, out.shape[1]), F32)
+    for ref, i, s, c in blocks:
+        at = (2 * ((y - s) & 3) + c) * 48
+        out[pl.ds(pl.multiple_of(at, 16), 48)] = ref[i, :48]
+        energy = energy + ref[i, 48:].astype(F32)
+    out[384:] = jnp.concatenate([energy, jnp.zeros_like(energy)], axis=0).astype(BF16)
+
+
+def trail_chunk(ref, i):
+    rows = [ref[r, i, :48].astype(F32) for r in range(8)]
+    energy = ref[0, i, 48:].astype(F32)
+    for r in range(1, 8):
+        energy = energy + ref[r, i, 48:].astype(F32)
+    return jnp.concatenate(rows + [energy, jnp.zeros_like(energy)], axis=0).astype(BF16)
 
 
 def params(mib=40):
@@ -264,8 +280,8 @@
     return pl.pallas_call(
         panel_kernel,
         out_shape=(
-            jax.ShapeDtypeStruct((4, 64, 512), BF16),
-            jax.ShapeDtypeStruct((4, 64, 512), BF16),
+            jax.ShapeDtypeStruct((4, SENT, 512), BF16),
+            jax.ShapeDtypeStruct((4, SENT, 512), BF16),
             jax.ShapeDtypeStruct((1280, 128), F32),
         ),
         in_specs=[in_smem()] + [in_vmem()] * 6,
@@ -281,7 +297,7 @@
 def assemble(where, near, far, got):
     return pl.pallas_call(
         assemble_kernel,
-        out_shape=jax.ShapeDtypeStruct((8, 64, 512), BF16),
+        out_shape=jax.ShapeDtypeStruct((HELD, 512), BF16),
         in_specs=[in_smem()] + [in_vmem()] * 5,
         out_specs=in_vmem(),
         compiler_params=params(),
@@ -296,7 +312,7 @@
     whole = lambda shape: pl.BlockSpec(shape, lambda i, w: (0, 0))
     return pl.pallas_call(
         trail_kernel,
-        out_shape=jax.ShapeDtypeStruct((8, blocks, 64, 128), BF16),
+        out_shape=jax.ShapeDtypeStruct((8, blocks, SENT, 128), BF16),
         grid_spec=pltpu.PrefetchScalarGridSpec(
             num_scalar_prefetch=1,
             grid=(blocks // step,),
@@ -308,7 +324,7 @@
                 whole(mean.shape),
                 whole(order.shape),
             ],
-            out_specs=pl.BlockSpec((8, step, 64, 128), lambda i, w: (0, i, 0, 0)),
+            out_specs=pl.BlockSpec((8, step, SENT, 128), lambda i, w: (0, i, 0, 0)),
         ),
         compiler_params=params(),
         cost_estimate=pl.CostEstimate(
@@ -401,7 +417,7 @@
 
     n = panel_ref.shape[2]
     trail = jnp.concatenate(
-        [trail_ref[:, i].reshape(512, 128) for i in range(panel_ref.shape[0])], axis=0
+        [trail_chunk(trail_ref, i) for i in range(panel_ref.shape[0])], axis=0
     )
     out_ref[...] += dot(trail, panel_ref[...].reshape(-1, n), TN)
 
@@ -413,8 +429,8 @@
         out_shape=jax.ShapeDtypeStruct((128, n), F32),
         grid=(segment.shape[0] // 4,),
         in_specs=[
-            pl.BlockSpec((4, 512, n), lambda i: (i, 0, 0)),
-            pl.BlockSpec((8, 4, 64, 128), lambda i: (0, i, 0, 0)),
+            pl.BlockSpec((4, HELD, n), lambda i: (i, 0, 0)),
+            pl.BlockSpec((8, 4, SENT, 128), lambda i: (0, i, 0, 0)),
         ],
         out_specs=pl.BlockSpec((128, n), lambda i: (0, 0)),
         compiler_params=params(),
@@ -425,7 +441,7 @@
 
 
 def residual_kernel(
-    rows_total, cross_ref, inverse_ref, panel_ref, trail_ref, coupling_ref, out_ref, weights
+    rows_total, cross_ref, inverse_ref, panel_ref, trail_ref, coupling_ref, out_ref, weights, spread
 ):
     @pl.when(pl.program_id(0) == 0)
     def _():
@@ -435,14 +451,24 @@
         high = solved.astype(BF16)
         weights[:128] = high
         weights[128:] = (solved - high.astype(F32)).astype(BF16)
+        held = lax.broadcasted_iota(jnp.int32, (HELD, 512), 0)
+        column = lax.broadcasted_iota(jnp.int32, (HELD, 512), 1)
+        struct, place = column >> 6, column & 63
+        wanted = jnp.where(place <= 48, struct * 48 + place - 1, -1)
+        wanted = jnp.where(place == 0, 384 + struct, wanted)
+        spread[...] = (held == wanted).astype(F32).astype(BF16)
 
     r = lax.broadcasted_iota(jnp.int32, (128, 128), 0)
     c = lax.broadcasted_iota(jnp.int32, (128, 128), 1)
     same = (r == c).astype(BF16)
     for i in range(panel_ref.shape[0]):
         both = dot(weights[...], panel_ref[i], NT)
-        own = dot(same, trail_ref[:, i].reshape(512, 128), NT)
-        out_ref[:, i * 512 : i * 512 + 512] = own - both[:128] - both[128:]
+        own = dot(same, trail_chunk(trail_ref, i), NT)
+        rest = own - both[:128] - both[128:]
+        high = rest.astype(BF16)
+        low = (rest - high.astype(F32)).astype(BF16)
+        full = dot(jnp.concatenate([high, low], axis=0), spread[...], NN)
+        out_ref[:, i * 512 : i * 512 + 512] = full[:128] + full[128:]
 
 
 def residual(cross, inverse, segment, trail, rows_total):
@@ -459,11 +485,11 @@
         in_specs=[
             whole((128, n)),
             whole((n, n)),
-            pl.BlockSpec((4, 512, n), lambda i: (i, 0, 0)),
-            pl.BlockSpec((8, 4, 64, 128), lambda i: (0, i, 0, 0)),
+            pl.BlockSpec((4, HELD, n), lambda i: (i, 0, 0)),
+            pl.BlockSpec((8, 4, SENT, 128), lambda i: (0, i, 0, 0)),
         ],
         out_specs=(whole((128, n)), pl.BlockSpec((128, 2048), lambda i: (0, i))),
-        scratch_shapes=[pltpu.VMEM((256, n), BF16)],
+        scratch_shapes=[pltpu.VMEM((256, n), BF16), pltpu.VMEM((HELD, 512), BF16)],
         compiler_params=params(),
         cost_estimate=pl.CostEstimate(
             flops=4 * 128 * n * 8192, bytes_accessed=16 << 20, transcendentals=0
@@ -495,6 +521,7 @@
     other = lax.ppermute(own, "row", CORE_SWAP)
 
     atoms, grads, mean, order = prepare(
+        where,
         atom_counts,
         owner_rows,
         neighbor_ids.reshape(128, 4).T,
@@ -511,7 +538,7 @@
     ]
     gram = scatter4(gram, "row", y_shift, y)
     got, gram = lax.optimization_barrier((got, gram))
-    panel = assemble(where, near, far, got).reshape(512, 512)
+    panel = assemble(where, near, far, got)
     segment = lax.all_gather(panel, "col", axis=0, tiled=False)
     trail_other = lax.ppermute(trail_own, "row", CORE_SWAP)
     gram = sum4(gram, "col", z_pair)
@@ -523,8 +550,8 @@
     trail, gram = lax.optimization_barrier((trail, gram))
     gram = jnp.concatenate(swap_gather(gram, core), axis=0)
     trail = lax.all_to_all(
-        trail.reshape(128, 64, 128), ("row", "col"), 0, 0, tiled=True
-    ).reshape(8, 16, 64, 128)
+        trail.reshape(128, SENT, 128), ("row", "col"), 0, 0, tiled=True
+    ).reshape(8, 16, SENT, 128)
     factor, inverse = factor_panel(gram, rows_total)
 
     segment, inverse = lax.optimization_barrier((segment, inverse))

time: 191 us -> 186 us (0.974)
  waiting for transfers between devices: 59.4 us -> 55 us
  starting transfers between devices: 53.9 us -> 50.4 us
  Pallas kernels: 49.3 us -> 52.5 us
    all_gather x1, waiting for transfers between devices: 22.2 us -> 10.8 us  [per_device(): segment = lax.all_gather(panel, 'col', axis=0, tiled=False)]
    ppermute x6, waiting for transfers between devices: 4.8 us -> 8.87 us  [shifted(): return [v] + [lax.ppermute(v, axis, shift(s)) for s in (1, 2, 3)]]
    ppermute x6, starting transfers between devices: 12.6 us -> 8.96 us  [shifted(): return [v] + [lax.ppermute(v, axis, shift(s)) for s in (1, 2, 3)]]
    ppermute x6, starting transfers between devices: 10.8 us -> 7.27 us  [sum4(): v = v + lax.ppermute(v, axis, pairs(flip))]
    all_to_all x1, waiting for transfers between devices: 0.62 us -> 3.85 us  [per_device(): lax.all_to_all(trail.reshape(128, SENT, 128), ('row', 'col'), 0, 0, tiled...]
    pallas_call x1, Pallas kernels: 7.21 us -> 10.4 us  [residual(): pl.pallas_call(functools.partial(residual_kernel, float(rows_total)), out...]
    ppermute x6, waiting for transfers between devices: 13.8 us -> 16.6 us  [sum4(): v = v + lax.ppermute(v, axis, pairs(flip))]
    ppermute x3, waiting for transfers between devices: 2.32 us -> 0.01 us  [per_device(): lax.ppermute(jnp.stack([near[s], far[s]]), 'row', y_shift(s))]
  transfers between devices with their start and end apart: 31 -> 31, of which waited for: 20 -> 22; matrix products, arithmetic and copies ran while one was open for 2% -> 2% of each run, Pallas kernels for 21% -> 22%
where the time goes in v7:
time: 186 us; the launch traced here: 185 us
  waiting for transfers between devices  55 us (30%)
  Pallas kernels  52.5 us (28%)
  starting transfers between devices  50.4 us (27%)
  between operations  14.4 us (8%)
  local copies, waits for them, and re-layouts  12.3 us (7%)
    pallas_call x1, Pallas kernels, factor_panel(): pl.pallas_call(functools.partial(factor_kernel, float(rows_total)), out_s...  26.7 us
    ppermute x6, waiting for transfers between devices, sum4(): v = v + lax.ppermute(v, axis, pairs(flip))  16.6 us
    all_gather x1, waiting for transfers between devices, per_device(): segment = lax.all_gather(panel, 'col', axis=0, tiled=False)  10.8 us
    pallas_call x1, Pallas kernels, residual(): pl.pallas_call(functools.partial(residual_kernel, float(rows_total)), out...  10.4 us
    all_to_all x1, starting transfers between devices, per_device(): lax.all_to_all(trail.reshape(128, SENT, 128), ('row', 'col'), 0, 0, tiled...  10.3 us
    unnamed x27, local copies, waits for them, and re-layouts  9.19 us
    ppermute x6, starting transfers between devices, shifted(): return [v] + [lax.ppermute(v, axis, shift(s)) for s in (1, 2, 3)]  8.96 us
    ppermute x6, waiting for transfers between devices, shifted(): return [v] + [lax.ppermute(v, axis, shift(s)) for s in (1, 2, 3)]  8.87 us
  transfers between devices with their start and end apart: 31, of which 22 were waited for; matrix products, arithmetic and copies ran while one was open for 2% of the time, Pallas kernels for 22%

profile of v7, /device:TPU:1, one launch (start us, length us, event | category | flops | bytes accessed | tf_op | source)
XLA Modules:
  0.0 185.1 jit_solution(11246861888453347798)
XLA Ops:
  9.6 4.6 %collective-permute-start.3 = (bf16[16,1024]{1,0:T(8,128)(2,1)S(1)}, bf16[16,1024]{1,0:T(8,128)(2,1)S(1)}, u32[]{:S(2)}, u32[]{:S(2)}) collective-permute-start(bf16[16,1024]{1,0:T(8,128)(2,1)S(1)} %constant_dynamic-slice_fusion.5), channel_id=1, source_target_pairs={{0,3},{1,0},{2,1},{3,2},{4,7},{5,4},{6,5},{7,6},{8,11},{9,8},{10,9... | collective-permute-start | bytes 98312 | tf_op jit(solution)/shard_map/ppermute | solution.py:61
  15.7 2.9 %collective-permute-done.2 = bf16[16,1024]{1,0:T(8,128)(2,1)S(1)} collective-permute-done((bf16[16,1024]{1,0:T(8,128)(2,1)S(1)}, bf16[16,1024]{1,0:T(8,128)(2,1)S(1)}, u32[]{:S(2)}, u32[]{:S(2)}) %collective-permute-start.2) | collective-permute-done | bytes 32800 | tf_op jit(solution)/shard_map/ppermute | solution.py:61
  18.6 2.5 %collective-permute-start.6 = (bf16[4,16,1024]{2,1,0:T(8,128)(2,1)S(1)}, bf16[4,16,1024]{2,1,0:T(8,128)(2,1)S(1)}, u32[]{:S(2)}, u32[]{:S(2)}) collective-permute-start(bf16[4,16,1024]{2,1,0:T(8,128)(2,1)S(1)} %get-tuple-element.71), channel_id=1, source_target_pairs={{0,12},{1,13},{2,14},{3,15},{4,0},{5,1},{6,2},{7,3},{8,4},{9,5},{1... | collective-permute-start | bytes 393224 | tf_op jit(solution)/shard_map/ppermute | solution.py:61
  23.8 2.8 %collective-permute-done.5 = bf16[4,16,1024]{2,1,0:T(8,128)(2,1)S(1)} collective-permute-done((bf16[4,16,1024]{2,1,0:T(8,128)(2,1)S(1)}, bf16[4,16,1024]{2,1,0:T(8,128)(2,1)S(1)}, u32[]{:S(2)}, u32[]{:S(2)}) %collective-permute-start.5) | collective-permute-done | bytes 131104 | tf_op jit(solution)/shard_map/ppermute | solution.py:61
  26.6 1.7 collective-permute-done.4
  28.3 4.1 %collective-permute-start.7 = (bf16[4,4,16,1024]{3,2,1,0:T(8,128)(2,1)S(1)}, bf16[4,4,16,1024]{3,2,1,0:T(8,128)(2,1)}, u32[]{:S(2)}, u32[]{:S(2)}) collective-permute-start(bf16[4,4,16,1024]{3,2,1,0:T(8,128)(2,1)S(1)} %pad_maximum_fusion.1.own), channel_id=1, source_target_pairs={{0,16},{16,0},{32,48},{48,32},{64,80},{80,64},{96,112},{112,96},{1... | collective-permute-start | bytes 1572872 | tf_op jit(solution)/shard_map/ppermute | solution.py:521
  33.3 1.9 %copy-done.3 = bf16[3,4,128,1024]{3,2,1,0:T(8,128)(2,1)S(1)} copy-done((bf16[3,4,128,1024]{3,2,1,0:T(8,128)(2,1)S(1)}, bf16[3,4,128,1024]{3,2,1,0:T(8,128)(2,1)}, u32[]{:S(2)}) %copy-start.3) | copy-done | bytes 3145752
  36.6 3.3 %shard_map.95 = (bf16[4,56,512]{2,1,0:T(8,128)(2,1)S(1)}, bf16[4,56,512]{2,1,0:T(8,128)(2,1)S(1)}, f32[1280,128]{1,0:T(8,128)S(1)}) custom-call(s32[4]{0:T(128)S(1)} %pad_add_fusion.where, bf16[4,4,16,1024]{3,2,1,0:T(8,128)(2,1)S(1)} %pad_maximum_fusion.1.own, bf16[4,4,16,1024]{3,2,1,0:T(8,128)(2,1)} %collective-permute-done.7.other, ...), custom_call_target="tpu_custom_call" | custom-call | flops 1140850688 | bytes 5242880 | tf_op jit(solution)/shard_map/pallas_call | solution.py:280
  44.1 2.7 %collective-permute-start.11 = (bf16[2,56,512]{2,1,0:T(8,128)(2,1)S(1)}, bf16[2,56,512]{2,1,0:T(8,128)(2,1)S(1)}, u32[]{:S(2)}, u32[]{:S(2)}) collective-permute-start(bf16[2,56,512]{2,1,0:T(8,128)(2,1)S(1)} %pad_maximum_fusion.6), channel_id=1, source_target_pairs={{0,64},{16,80},{32,96},{48,112},{64,0},{80,16},{96,32},{112,48},{1... | collective-permute-start | bytes 344072 | tf_op jit(solution)/shard_map/ppermute | solution.py:537
  48.7 2.3 %collective-permute-done.15 = f32[160,128]{1,0:T(8,128)S(1)} collective-permute-done((f32[160,128]{1,0:T(8,128)S(1)}, f32[160,128]{1,0:T(8,128)S(1)}, u32[]{:S(2)}, u32[]{:S(2)}) %collective-permute-start.15) | collective-permute-done | bytes 81952 | tf_op jit(solution)/shard_map/ppermute | solution.py:73
  50.9 2.6 %collective-permute-start.12 = (bf16[2,56,512]{2,1,0:T(8,128)(2,1)S(1)}, bf16[2,56,512]{2,1,0:T(8,128)(2,1)S(1)}, u32[]{:S(2)}, u32[]{:S(2)}) collective-permute-start(bf16[2,56,512]{2,1,0:T(8,128)(2,1)S(1)} %pad_maximum_fusion.7), channel_id=1, source_target_pairs={{0,96},{16,112},{32,0},{48,16},{64,32},{80,48},{96,64},{112,80},{1... | collective-permute-start | bytes 344072 | tf_op jit(solution)/shard_map/ppermute | solution.py:537
  53.9 2.5 %collective-permute-done.13 = f32[160,128]{1,0:T(8,128)S(1)} collective-permute-done((f32[160,128]{1,0:T(8,128)S(1)}, f32[160,128]{1,0:T(8,128)S(1)}, u32[]{:S(2)}, u32[]{:S(2)}) %collective-permute-start.13) | collective-permute-done | bytes 81952 | tf_op jit(solution)/shard_map/ppermute | solution.py:73
  58.9 1.7 collective-permute-start
  61.6 3.2 %collective-permute-done.16 = f32[160,128]{1,0:T(8,128)S(1)} collective-permute-done((f32[160,128]{1,0:T(8,128)S(1)}, f32[160,128]{1,0:T(8,128)S(1)}, u32[]{:S(2)}, u32[]{:S(2)}) %collective-permute-start.16) | collective-permute-done | bytes 81952 | tf_op jit(solution)/shard_map/ppermute | solution.py:96
  64.8 2.2 %collective-permute-start.17 = (f32[160,128]{1,0:T(8,128)S(1)}, f32[160,128]{1,0:T(8,128)S(1)}, u32[]{:S(2)}, u32[]{:S(2)}) collective-permute-start(f32[160,128]{1,0:T(8,128)S(1)} %add.123), channel_id=1, source_target_pairs={{0,3},{1,2},{2,1},{3,0},{4,7},{5,6},{6,5},{7,4},{8,11},{9,10},{10,... | collective-permute-start | bytes 245768 | tf_op jit(solution)/shard_map/ppermute | solution.py:96
  67.0 2.4 %collective-permute-done.17 = f32[160,128]{1,0:T(8,128)S(1)} collective-permute-done((f32[160,128]{1,0:T(8,128)S(1)}, f32[160,128]{1,0:T(8,128)S(1)}, u32[]{:S(2)}, u32[]{:S(2)}) %collective-permute-start.17) | collective-permute-done | bytes 81952 | tf_op jit(solution)/shard_map/ppermute | solution.py:96
  70.1 2.6 %collective-permute-done.18 = f32[160,128]{1,0:T(8,128)S(1)} collective-permute-done((f32[160,128]{1,0:T(8,128)S(1)}, f32[160,128]{1,0:T(8,128)S(1)}, u32[]{:S(2)}, u32[]{:S(2)}) %collective-permute-start.18) | collective-permute-done | bytes 81952 | tf_op jit(solution)/shard_map/ppermute | solution.py:96
  72.8 2.0 %collective-permute-start.19 = (f32[160,128]{1,0:T(8,128)S(1)}, f32[160,128]{1,0:T(8,128)S(1)}, u32[]{:S(2)}, u32[]{:S(2)}) collective-permute-start(f32[160,128]{1,0:T(8,128)S(1)} %add.125), channel_id=1, source_target_pairs={{0,12},{1,13},{2,14},{3,15},{4,8},{5,9},{6,10},{7,11},{8,4},{9,5},... | collective-permute-start | bytes 245768 | tf_op jit(solution)/shard_map/ppermute | solution.py:96
  74.7 1.6 copy-done.8
  76.3 7.3 %shard_map.96 = bf16[8,16,56,128]{3,2,1,0:T(8,128)(2,1)S(1)} custom-call(s32[4]{0:T(128)S(1)} %pad_add_fusion.where, bf16[16,64,1024]{2,1,0:T(8,128)(2,1)S(1)} %bitcast.30, bf16[16,64,1024]{2,1,0:T(8,128)(2,1)S(1)} %collective-permute-done.other_ref, bf16[320,1024]{1,0:T(8,128)(2,1)S(1)} %copy-done.10, bf16[768,1024]{1,0:T(8,128)(2,1)S(1)} %get-tuple-element.29.grads_ref, ...), custom_call_target="tpu_custom_call" | custom-call | flops 4563402752 | bytes 9437184 | tf_op jit(solution)/shard_map/pallas_call | solution.py:313
  84.9 2.8 %collective-permute-start.21 = (f32[160,128]{1,0:T(8,128)S(1)}, f32[160,128]{1,0:T(8,128)S(1)}, u32[]{:S(2)}, u32[]{:S(2)}) collective-permute-start(f32[160,128]{1,0:T(8,128)S(1)} %add.126), channel_id=1, source_target_pairs={{0,64},{16,80},{32,96},{48,112},{64,0},{80,16},{96,32},{112,48},{1... | collective-permute-start | bytes 245768 | tf_op jit(solution)/shard_map/ppermute | solution.py:65
  91.0 2.1 %collective-permute-done.20 = f32[160,128]{1,0:T(8,128)S(1)} collective-permute-done((f32[160,128]{1,0:T(8,128)S(1)}, f32[160,128]{1,0:T(8,128)S(1)}, u32[]{:S(2)}, u32[]{:S(2)}) %collective-permute-start.20) | collective-permute-done | bytes 81952 | tf_op jit(solution)/shard_map/ppermute | solution.py:65
  93.2 10.3 %all-to-all-start = ((bf16[128,56,128]{2,1,0:T(8,128)(2,1)}), bf16[128,56,128]{2,1,0:T(8,128)(2,1)S(1)}, u32[]{:S(2)}, u32[]{:S(2)}) async-start(bf16[128,56,128]{2,1,0:T(8,128)(2,1)} %bitcast.27), calls=%async_computation | async-start | bytes 3670016 | tf_op jit(solution)/shard_map/all_to_all | solution.py:552
  106.1 26.7 %shard_map.97 = (f32[512,512]{1,0:T(8,128)}, f32[512,512]{1,0:T(8,128)S(1)}) custom-call(f32[1280,128]{1,0:T(8,128)S(1)} %pad_maximum_fusion.gram_ref), custom_call_target="tpu_custom_call" | custom-call | flops 2684354560 | bytes 4194304 | tf_op jit(solution)/shard_map/pallas_call | solution.py:402
  132.9 10.8 %all-gather.7.cloned.1.call-done = bf16[6400,512]{1,0:T(8,128)(2,1)} async-done(((bf16[400,512]{1,0:T(8,128)(2,1)}), bf16[6400,512]{1,0:T(8,128)(2,1)}) %all-gather.7.cloned.1.call-update) | async-done | bytes 6553616 | tf_op jit(solution)/shard_map/all_gather | solution.py:542
  143.7 3.9 %all-to-all-done = bf16[128,56,128]{2,1,0:T(8,128)(2,1)S(1)} async-done(((bf16[128,56,128]{2,1,0:T(8,128)(2,1)}), bf16[128,56,128]{2,1,0:T(8,128)(2,1)S(1)}, u32[]{:S(2)}, u32[]{:S(2)}) %all-to-all-start) | async-done | bytes 1835040 | tf_op jit(solution)/shard_map/all_to_all | solution.py:552
  147.5 2.9 %copy-done.1 = bf16[6400,512]{1,0:T(8,128)(2,1)S(1)} copy-done((bf16[6400,512]{1,0:T(8,128)(2,1)S(1)}, bf16[6400,512]{1,0:T(8,128)(2,1)}, u32[]{:S(2)}) %copy-start.1) | copy-done | bytes 6553624
  150.4 1.9 %shard_map.99 = f32[128,512]{1,0:T(8,128)S(1)} custom-call(bf16[16,400,512]{2,1,0:T(8,128)(2,1)S(1)} %bitcast.22, bf16[8,16,56,128]{3,2,1,0:T(8,128)(2,1)S(1)} %bitcast.24), custom_call_target="tpu_custom_call" | custom-call | flops 1073741824 | bytes 11534336 | tf_op jit(solution)/shard_map/pallas_call | solution.py:427
  154.8 4.4 %collective-permute-done.25 = f32[64,512]{1,0:T(8,128)S(1)} collective-permute-done((f32[64,512]{1,0:T(8,128)S(1)}, f32[64,512]{1,0:T(8,128)S(1)}, u32[]{:S(2)}, u32[]{:S(2)}) %collective-permute-start.25) | collective-permute-done | bytes 131104 | tf_op jit(solution)/shard_map/ppermute | solution.py:96
  160.3 4.0 %collective-permute-done.26 = f32[64,512]{1,0:T(8,128)S(1)} collective-permute-done((f32[64,512]{1,0:T(8,128)S(1)}, f32[64,512]{1,0:T(8,128)S(1)}, u32[]{:S(2)}, u32[]{:S(2)}) %collective-permute-start.26) | collective-permute-done | bytes 131104 | tf_op jit(solution)/shard_map/ppermute | solution.py:96
  164.4 2.4 %collective-permute-start.27 = (f32[64,512]{1,0:T(8,128)S(1)}, f32[64,512]{1,0:T(8,128)S(1)}, u32[]{:S(2)}, u32[]{:S(2)}) collective-permute-start(f32[64,512]{1,0:T(8,128)S(1)} %add.134), channel_id=1, source_target_pairs={{0,16},{16,0},{32,48},{48,32},{64,80},{80,64},{96,112},{112,96},{1... | collective-permute-start | bytes 393224 | tf_op jit(solution)/shard_map/ppermute | solution.py:89
  167.8 10.4 %shard_map.100 = (f32[128,512]{1,0:T(8,128)}, f32[128,8192]{1,0:T(8,128)}) custom-call(f32[128,512]{1,0:T(8,128)S(1)} %pad_maximum_fusion.3.cross_ref, f32[512,512]{1,0:T(8,128)S(1)} %get-tuple-element.50.inverse_ref, bf16[16,400,512]{2,1,0:T(8,128)(2,1)S(1)} %bitcast.23, bf16[8,16,56,128]{3,2,1,0:T(8,128)(2,1)S(1)} %bitcast.25), custom_call_target="tpu_custom_call" | custom-call | flops 2147483648 | bytes 16777216 | tf_op jit(solution)/shard_map/pallas_call | solution.py:478
  (96 shorter events, 31.2 us)
Async XLA Ops:
  7.2 51.7 %all-gather.5.cloned.1.call-start = ((), (), s32[]{:S(2)}) async-start(), calls=%async_computation.1 | async-start | bytes 2228224 | tf_op jit(solution)/shard_map/all_gather | solution.py:517
  8.8 134.8 %all-gather.7.cloned.1.call-start = ((), (), s32[]{:S(2)}) async-start(), calls=%async_computation.2 | async-start | bytes 6963200 | tf_op jit(solution)/shard_map/all_gather | solution.py:542
  9.6 6.1 %collective-permute-start.3 = (bf16[16,1024]{1,0:T(8,128)(2,1)S(1)}, bf16[16,1024]{1,0:T(8,128)(2,1)S(1)}, u32[]{:S(2)}, u32[]{:S(2)}) collective-permute-start(bf16[16,1024]{1,0:T(8,128)(2,1)S(1)} %constant_dynamic-slice_fusion.5), channel_id=1, source_target_pairs={{0,3},{1,0},{2,1},{3,2},{4,7},{5,4},{6,5},{7,6},{8,11},{9,8},{10,9... | collective-permute-start | bytes 98312 | tf_op jit(solution)/shard_map/ppermute | solution.py:61
  14.2 4.3 %collective-permute-start.2 = (bf16[16,1024]{1,0:T(8,128)(2,1)S(1)}, bf16[16,1024]{1,0:T(8,128)(2,1)S(1)}, u32[]{:S(2)}, u32[]{:S(2)}) collective-permute-start(bf16[16,1024]{1,0:T(8,128)(2,1)S(1)} %constant_dynamic-slice_fusion.5), channel_id=1, source_target_pairs={{0,2},{1,3},{2,0},{3,1},{4,6},{5,7},{6,4},{7,5},{8,10},{9,11},{10,... | collective-permute-start | bytes 98312 | tf_op jit(solution)/shard_map/ppermute | solution.py:61
  14.2 4.3 %collective-permute-start.1 = (bf16[16,1024]{1,0:T(8,128)(2,1)S(1)}, bf16[16,1024]{1,0:T(8,128)(2,1)S(1)}, u32[]{:S(2)}, u32[]{:S(2)}) collective-permute-start(bf16[16,1024]{1,0:T(8,128)(2,1)S(1)} %constant_dynamic-slice_fusion.5), channel_id=1, source_target_pairs={{0,1},{1,2},{2,3},{3,0},{4,5},{5,6},{6,7},{7,4},{8,9},{9,10},{10,1... | collective-permute-start | bytes 98312 | tf_op jit(solution)/shard_map/ppermute | solution.py:61
  18.6 5.2 %collective-permute-start.6 = (bf16[4,16,1024]{2,1,0:T(8,128)(2,1)S(1)}, bf16[4,16,1024]{2,1,0:T(8,128)(2,1)S(1)}, u32[]{:S(2)}, u32[]{:S(2)}) collective-permute-start(bf16[4,16,1024]{2,1,0:T(8,128)(2,1)S(1)} %get-tuple-element.71), channel_id=1, source_target_pairs={{0,12},{1,13},{2,14},{3,15},{4,0},{5,1},{6,2},{7,3},{8,4},{9,5},{1... | collective-permute-start | bytes 393224 | tf_op jit(solution)/shard_map/ppermute | solution.py:61
  21.1 5.4 %collective-permute-start.5 = (bf16[4,16,1024]{2,1,0:T(8,128)(2,1)S(1)}, bf16[4,16,1024]{2,1,0:T(8,128)(2,1)S(1)}, u32[]{:S(2)}, u32[]{:S(2)}) collective-permute-start(bf16[4,16,1024]{2,1,0:T(8,128)(2,1)S(1)} %get-tuple-element.71), channel_id=1, source_target_pairs={{0,8},{1,9},{2,10},{3,11},{4,12},{5,13},{6,14},{7,15},{8,0},{9,1},... | collective-permute-start | bytes 393224 | tf_op jit(solution)/shard_map/ppermute | solution.py:61
  21.7 6.6 %collective-permute-start.4 = (bf16[4,16,1024]{2,1,0:T(8,128)(2,1)S(1)}, bf16[4,16,1024]{2,1,0:T(8,128)(2,1)S(1)}, u32[]{:S(2)}, u32[]{:S(2)}) collective-permute-start(bf16[4,16,1024]{2,1,0:T(8,128)(2,1)S(1)} %get-tuple-element.71), channel_id=1, source_target_pairs={{0,4},{1,5},{2,6},{3,7},{4,8},{5,9},{6,10},{7,11},{8,12},{9,13},{1... | collective-permute-start | bytes 393224 | tf_op jit(solution)/shard_map/ppermute | solution.py:61
  28.3 8.3 %collective-permute-start.7 = (bf16[4,4,16,1024]{3,2,1,0:T(8,128)(2,1)S(1)}, bf16[4,4,16,1024]{3,2,1,0:T(8,128)(2,1)}, u32[]{:S(2)}, u32[]{:S(2)}) collective-permute-start(bf16[4,4,16,1024]{3,2,1,0:T(8,128)(2,1)S(1)} %pad_maximum_fusion.1.own), channel_id=1, source_target_pairs={{0,16},{16,0},{32,48},{48,32},{64,80},{80,64},{96,112},{112,96},{1... | collective-permute-start | bytes 1572872 | tf_op jit(solution)/shard_map/ppermute | solution.py:521
  40.7 2.0 %collective-permute-start.9 = (f32[640,128]{1,0:T(8,128)}, f32[640,128]{1,0:T(8,128)S(1)}, u32[]{:S(2)}, u32[]{:S(2)}) collective-permute-start(f32[640,128]{1,0:T(8,128)} %constant_dynamic-slice_fusion.4), channel_id=1, source_target_pairs={{0,16},{16,0},{32,48},{48,32},{64,80},{80,64},{96,112},{112,96},{1... | collective-permute-start | bytes 983048 | tf_op jit(solution)/shard_map/ppermute | solution.py:85
  40.8 2.0 %collective-permute-start.8 = (bf16[4,56,512]{2,1,0:T(8,128)(2,1)S(1)}, bf16[4,56,512]{2,1,0:T(8,128)(2,1)S(1)}, u32[]{:S(2)}, u32[]{:S(2)}) collective-permute-start(bf16[4,56,512]{2,1,0:T(8,128)(2,1)S(1)} %get-tuple-element.33), channel_id=1, source_target_pairs={{0,16},{16,0},{32,48},{48,32},{64,80},{80,64},{96,112},{112,96},{1... | collective-permute-start | bytes 688136 | tf_op jit(solution)/shard_map/ppermute | solution.py:533
  42.7 32.0 %copy-start.10 = (bf16[320,1024]{1,0:T(8,128)(2,1)S(1)}, bf16[320,1024]{1,0:T(8,128)(2,1)}, u32[]{:S(2)}) copy-start(bf16[320,1024]{1,0:T(8,128)(2,1)} %copy-done.9) | copy-start | bytes 1966084
  42.8 13.6 %collective-permute-start.10 = (bf16[2,56,512]{2,1,0:T(8,128)(2,1)S(1)}, bf16[2,56,512]{2,1,0:T(8,128)(2,1)S(1)}, u32[]{:S(2)}, u32[]{:S(2)}) collective-permute-start(bf16[2,56,512]{2,1,0:T(8,128)(2,1)S(1)} %pad_maximum_fusion.5), channel_id=1, source_target_pairs={{0,32},{16,48},{32,64},{48,80},{64,96},{80,112},{96,0},{112,16},{1... | collective-permute-start | bytes 344072 | tf_op jit(solution)/shard_map/ppermute | solution.py:537
  44.1 12.3 %collective-permute-start.11 = (bf16[2,56,512]{2,1,0:T(8,128)(2,1)S(1)}, bf16[2,56,512]{2,1,0:T(8,128)(2,1)S(1)}, u32[]{:S(2)}, u32[]{:S(2)}) collective-permute-start(bf16[2,56,512]{2,1,0:T(8,128)(2,1)S(1)} %pad_maximum_fusion.6), channel_id=1, source_target_pairs={{0,64},{16,80},{32,96},{48,112},{64,0},{80,16},{96,32},{112,48},{1... | collective-permute-start | bytes 344072 | tf_op jit(solution)/shard_map/ppermute | solution.py:537
  46.8 4.1 %collective-permute-start.15 = (f32[160,128]{1,0:T(8,128)S(1)}, f32[160,128]{1,0:T(8,128)S(1)}, u32[]{:S(2)}, u32[]{:S(2)}) collective-permute-start(f32[160,128]{1,0:T(8,128)S(1)} %get-tuple-element.60), channel_id=1, source_target_pairs={{0,96},{16,112},{32,0},{48,16},{64,32},{80,48},{96,64},{112,80},{1... | collective-permute-start | bytes 245768 | tf_op jit(solution)/shard_map/ppermute | solution.py:73
  48.0 5.9 %collective-permute-start.14 = (f32[160,128]{1,0:T(8,128)S(1)}, f32[160,128]{1,0:T(8,128)S(1)}, u32[]{:S(2)}, u32[]{:S(2)}) collective-permute-start(f32[160,128]{1,0:T(8,128)S(1)} %get-tuple-element.61), channel_id=1, source_target_pairs={{0,64},{16,80},{32,96},{48,112},{64,0},{80,16},{96,32},{112,48},{1... | collective-permute-start | bytes 245768 | tf_op jit(solution)/shard_map/ppermute | solution.py:73
  48.1 8.3 %collective-permute-start.13 = (f32[160,128]{1,0:T(8,128)S(1)}, f32[160,128]{1,0:T(8,128)S(1)}, u32[]{:S(2)}, u32[]{:S(2)}) collective-permute-start(f32[160,128]{1,0:T(8,128)S(1)} %get-tuple-element.59), channel_id=1, source_target_pairs={{0,32},{16,48},{32,64},{48,80},{64,96},{80,112},{96,0},{112,16},{1... | collective-permute-start | bytes 245768 | tf_op jit(solution)/shard_map/ppermute | solution.py:73
  50.9 5.5 %collective-permute-start.12 = (bf16[2,56,512]{2,1,0:T(8,128)(2,1)S(1)}, bf16[2,56,512]{2,1,0:T(8,128)(2,1)S(1)}, u32[]{:S(2)}, u32[]{:S(2)}) collective-permute-start(bf16[2,56,512]{2,1,0:T(8,128)(2,1)S(1)} %pad_maximum_fusion.7), channel_id=1, source_target_pairs={{0,96},{16,112},{32,0},{48,16},{64,32},{80,48},{96,64},{112,80},{1... | collective-permute-start | bytes 344072 | tf_op jit(solution)/shard_map/ppermute | solution.py:537
  58.9 10.4 %collective-permute-start = (bf16[16,64,1024]{2,1,0:T(8,128)(2,1)}, bf16[16,64,1024]{2,1,0:T(8,128)(2,1)S(1)}, u32[]{:S(2)}, u32[]{:S(2)}) collective-permute-start(bf16[16,64,1024]{2,1,0:T(8,128)(2,1)} %bitcast.29), channel_id=1, source_target_pairs={{0,16},{16,0},{32,48},{48,32},{64,80},{80,64},{96,112},{112,96},{1... | collective-permute-start | bytes 6291464 | tf_op jit(solution)/shard_map/ppermute | solution.py:543
  60.7 4.1 %collective-permute-start.16 = (f32[160,128]{1,0:T(8,128)S(1)}, f32[160,128]{1,0:T(8,128)S(1)}, u32[]{:S(2)}, u32[]{:S(2)}) collective-permute-start(f32[160,128]{1,0:T(8,128)S(1)} %add_add_fusion), channel_id=1, source_target_pairs={{0,1},{1,0},{2,3},{3,2},{4,5},{5,4},{6,7},{7,6},{8,9},{9,8},{10,11... | collective-permute-start | bytes 245768 | tf_op jit(solution)/shard_map/ppermute | solution.py:96
  64.8 4.6 %collective-permute-start.17 = (f32[160,128]{1,0:T(8,128)S(1)}, f32[160,128]{1,0:T(8,128)S(1)}, u32[]{:S(2)}, u32[]{:S(2)}) collective-permute-start(f32[160,128]{1,0:T(8,128)S(1)} %add.123), channel_id=1, source_target_pairs={{0,3},{1,2},{2,1},{3,0},{4,7},{5,6},{6,5},{7,4},{8,11},{9,10},{10,... | collective-permute-start | bytes 245768 | tf_op jit(solution)/shard_map/ppermute | solution.py:96
  69.4 3.4 %collective-permute-start.18 = (f32[160,128]{1,0:T(8,128)S(1)}, f32[160,128]{1,0:T(8,128)S(1)}, u32[]{:S(2)}, u32[]{:S(2)}) collective-permute-start(f32[160,128]{1,0:T(8,128)S(1)} %add.124), channel_id=1, source_target_pairs={{0,4},{1,5},{2,6},{3,7},{4,0},{5,1},{6,2},{7,3},{8,12},{9,13},{10,... | collective-permute-start | bytes 245768 | tf_op jit(solution)/shard_map/ppermute | solution.py:96
  72.8 12.1 %collective-permute-start.19 = (f32[160,128]{1,0:T(8,128)S(1)}, f32[160,128]{1,0:T(8,128)S(1)}, u32[]{:S(2)}, u32[]{:S(2)}) collective-permute-start(f32[160,128]{1,0:T(8,128)S(1)} %add.125), channel_id=1, source_target_pairs={{0,12},{1,13},{2,14},{3,15},{4,8},{5,9},{6,10},{7,11},{8,4},{9,5},... | collective-permute-start | bytes 245768 | tf_op jit(solution)/shard_map/ppermute | solution.py:96
  84.9 4.9 %collective-permute-start.21 = (f32[160,128]{1,0:T(8,128)S(1)}, f32[160,128]{1,0:T(8,128)S(1)}, u32[]{:S(2)}, u32[]{:S(2)}) collective-permute-start(f32[160,128]{1,0:T(8,128)S(1)} %add.126), channel_id=1, source_target_pairs={{0,64},{16,80},{32,96},{48,112},{64,0},{80,16},{96,32},{112,48},{1... | collective-permute-start | bytes 245768 | tf_op jit(solution)/shard_map/ppermute | solution.py:65
  87.7 3.3 %collective-permute-start.22 = (f32[160,128]{1,0:T(8,128)S(1)}, f32[160,128]{1,0:T(8,128)S(1)}, u32[]{:S(2)}, u32[]{:S(2)}) collective-permute-start(f32[160,128]{1,0:T(8,128)S(1)} %add.126), channel_id=1, source_target_pairs={{0,96},{16,112},{32,0},{48,16},{64,32},{80,48},{96,64},{112,80},{1... | collective-permute-start | bytes 245768 | tf_op jit(solution)/shard_map/ppermute | solution.py:65
  88.6 4.5 %collective-permute-start.20 = (f32[160,128]{1,0:T(8,128)S(1)}, f32[160,128]{1,0:T(8,128)S(1)}, u32[]{:S(2)}, u32[]{:S(2)}) collective-permute-start(f32[160,128]{1,0:T(8,128)S(1)} %add.126), channel_id=1, source_target_pairs={{0,32},{16,48},{32,64},{48,80},{64,96},{80,112},{96,0},{112,16},{1... | collective-permute-start | bytes 245768 | tf_op jit(solution)/shard_map/ppermute | solution.py:65
  93.2 54.3 %all-to-all-start = ((bf16[128,56,128]{2,1,0:T(8,128)(2,1)}), bf16[128,56,128]{2,1,0:T(8,128)(2,1)S(1)}, u32[]{:S(2)}, u32[]{:S(2)}) async-start(bf16[128,56,128]{2,1,0:T(8,128)(2,1)} %bitcast.27), calls=%async_computation | async-start | bytes 3670016 | tf_op jit(solution)/shard_map/all_to_all | solution.py:552
  103.5 2.5 %collective-permute-start.23 = (f32[640,128]{1,0:T(8,128)S(1)}, f32[640,128]{1,0:T(8,128)S(1)}, u32[]{:S(2)}, u32[]{:S(2)}) collective-permute-start(f32[640,128]{1,0:T(8,128)S(1)} %pad_maximum_fusion.2), channel_id=1, source_target_pairs={{0,16},{16,0},{32,48},{48,32},{64,80},{80,64},{96,112},{112,96},{1... | collective-permute-start | bytes 983048 | tf_op jit(solution)/shard_map/ppermute | solution.py:89
  152.3 2.1 %collective-permute-start.24 = (f32[64,512]{1,0:T(8,128)S(1)}, f32[64,512]{1,0:T(8,128)S(1)}, u32[]{:S(2)}, u32[]{:S(2)}) collective-permute-start(f32[64,512]{1,0:T(8,128)S(1)} %constant_dynamic-slice_fusion), channel_id=1, source_target_pairs={{0,16},{16,0},{32,48},{48,32},{64,80},{80,64},{96,112},{112,96},{1... | collective-permute-start | bytes 393224 | tf_op jit(solution)/shard_map/ppermute | solution.py:85
  154.4 4.8 %collective-permute-start.25 = (f32[64,512]{1,0:T(8,128)S(1)}, f32[64,512]{1,0:T(8,128)S(1)}, u32[]{:S(2)}, u32[]{:S(2)}) collective-permute-start(f32[64,512]{1,0:T(8,128)S(1)} %dynamic-slice_add_fusion.1), channel_id=1, source_target_pairs={{0,32},{16,48},{32,0},{48,16},{64,96},{80,112},{96,64},{112,80},{1... | collective-permute-start | bytes 393224 | tf_op jit(solution)/shard_map/ppermute | solution.py:96
  159.2 5.1 %collective-permute-start.26 = (f32[64,512]{1,0:T(8,128)S(1)}, f32[64,512]{1,0:T(8,128)S(1)}, u32[]{:S(2)}, u32[]{:S(2)}) collective-permute-start(f32[64,512]{1,0:T(8,128)S(1)} %add.133), channel_id=1, source_target_pairs={{0,96},{16,112},{32,64},{48,80},{64,32},{80,48},{96,0},{112,16},{1... | collective-permute-start | bytes 393224 | tf_op jit(solution)/shard_map/ppermute | solution.py:96
  164.4 3.4 %collective-permute-start.27 = (f32[64,512]{1,0:T(8,128)S(1)}, f32[64,512]{1,0:T(8,128)S(1)}, u32[]{:S(2)}, u32[]{:S(2)}) collective-permute-start(f32[64,512]{1,0:T(8,128)S(1)} %add.134), channel_id=1, source_target_pairs={{0,16},{16,0},{32,48},{48,32},{64,80},{80,64},{96,112},{112,96},{1... | collective-permute-start | bytes 393224 | tf_op jit(solution)/shard_map/ppermute | solution.py:89
  (12 other events, 143.0 us)
Sparse Core Ops, SparseCore 0:
  10.8 48.1 all-gather.4
  61.1 82.4 all-gather.6

commit v8 on v7

--- a/solution.py
+++ b/solution.py
@@ -230,13 +230,14 @@
 
 
 def trail_kernel(
-    where, own_ref, other_ref, atoms_ref, grads_ref, mean_ref, order_ref, out_ref
+    where, own, other, atoms_ref, grads_ref, mean_ref, order_ref, out_ref, env
 ):
-    first = where[3] == 0
-    own, other = own_ref[...], other_ref[...]
-    low, high = jnp.where(first, own, other), jnp.where(first, other, own)
-    env = jnp.concatenate([low, high], axis=1).reshape(-1, 1024)
-    rows = compact_rows(env, atoms_ref[...], grads_ref[...], mean_ref[...])
+    z, y = where[1], where[2]
+    for j in range(4):
+        place = ((z - j) & 3) * 128
+        for s in range(4):
+            put_env(env, where, own, other, (s, 0, j), place + ((y - s) & 3) * 32)
+    rows = compact_rows(env[...], atoms_ref[...], grads_ref[...], mean_ref[...])
     full = dot(order_ref[...].astype(BF16), rows, NN)
     for c in range(out_ref.shape[1]):
         part = full[:, c * 128 : c * 128 + 128].reshape(8, SENT, 128)
@@ -306,25 +307,23 @@
 
 
 def trail_rows(where, own, other, atoms, grads, mean, order):
-    blocks = own.shape[0]
-    step = 4
-    half = pl.BlockSpec((step, 64, 1024), lambda i, w: (i, 0, 0))
+    piece = pl.BlockSpec((4, 1, 4, 16, 1024), lambda i, w: (0, i, 0, 0, 0))
     whole = lambda shape: pl.BlockSpec(shape, lambda i, w: (0, 0))
     return pl.pallas_call(
         trail_kernel,
-        out_shape=jax.ShapeDtypeStruct((8, blocks, SENT, 128), BF16),
+        out_shape=jax.ShapeDtypeStruct((8, 16, SENT, 128), BF16),
         grid_spec=pltpu.PrefetchScalarGridSpec(
             num_scalar_prefetch=1,
-            grid=(blocks // step,),
-            in_specs=[
-                half,
-                half,
+            grid=(4,),
+            in_specs=[piece] * 2
+            + [
                 whole(atoms.shape),
                 whole(grads.shape),
                 whole(mean.shape),
                 whole(order.shape),
             ],
-            out_specs=pl.BlockSpec((8, step, SENT, 128), lambda i, w: (0, i, 0, 0)),
+            out_specs=pl.BlockSpec((8, 4, SENT, 128), lambda i, w: (0, (w[0] - i) & 3, 0, 0)),
+            scratch_shapes=[pltpu.VMEM((512, 1024), BF16)],
         ),
         compiler_params=params(),
         cost_estimate=pl.CostEstimate(
@@ -513,12 +512,20 @@
 
     where = jnp.stack([x, z, y, core]).astype(jnp.int32)
 
-    trail_own = lax.dynamic_slice_in_dim(sparse_trail, core * 64, 64, 0)
-    trail_own = lax.all_gather(trail_own, "col", axis=0, tiled=False)
-    piece = lax.dynamic_slice_in_dim(sparse_panel, core * 16, 16, 0)
-    piece = jnp.stack(shifted(piece, "col", z_shift))
+    piece = jnp.concatenate(
+        [
+            lax.dynamic_slice_in_dim(sparse_panel, core * 16, 16, 0),
+            lax.dynamic_slice_in_dim(sparse_trail, row * 16, 16, 0),
+        ],
+        axis=0,
+    )
+    pieces = shifted(piece, "col", z_shift)
+    piece = jnp.stack([p[:16] for p in pieces])
+    piece_trail = jnp.stack([p[16:] for p in pieces])
     own = jnp.stack(shifted(piece, "col", x_shift))
+    own, piece_trail = lax.optimization_barrier((own, piece_trail))
     other = lax.ppermute(own, "row", CORE_SWAP)
+    own_trail = jnp.stack(shifted(piece_trail, "col", x_shift))
 
     atoms, grads, mean, order = prepare(
         where,
@@ -532,23 +539,23 @@
     near, far, gram = panel_rows(where, own, other, atoms, grads, mean, order)
     far = lax.ppermute(far, "row", CORE_SWAP)
     gram = swap_add(gram, core)
-    far, gram = lax.optimization_barrier((far, gram))
+    far, gram, own_trail = lax.optimization_barrier((far, gram, own_trail))
     got = [
         lax.ppermute(jnp.stack([near[s], far[s]]), "row", y_shift(s)) for s in (1, 2, 3)
     ]
     gram = scatter4(gram, "row", y_shift, y)
-    got, gram = lax.optimization_barrier((got, gram))
+    got, gram, own_trail = lax.optimization_barrier((got, gram, own_trail))
     panel = assemble(where, near, far, got)
     segment = lax.all_gather(panel, "col", axis=0, tiled=False)
+    trail_own = jnp.stack(shifted(own_trail, "row", y_shift))
+    gram = sum4(gram, "col", z_pair)
+    gram = sum4(gram, "col", x_pair)
+    trail_own, gram = lax.optimization_barrier((trail_own, gram))
     trail_other = lax.ppermute(trail_own, "row", CORE_SWAP)
-    gram = sum4(gram, "col", z_pair)
-    trail_other, gram = lax.optimization_barrier((trail_other, gram))
-    gram = sum4(gram, "col", x_pair)
     trail = trail_rows(where, trail_own, trail_other, atoms, grads, mean, order)
+    gram = gather4(gram, "row", y_shift, y)
+    gram = jnp.concatenate(swap_gather(gram, core), axis=0)
     trail, gram = lax.optimization_barrier((trail, gram))
-    gram = gather4(gram, "row", y_shift, y)
-    trail, gram = lax.optimization_barrier((trail, gram))
-    gram = jnp.concatenate(swap_gather(gram, core), axis=0)
     trail = lax.all_to_all(
         trail.reshape(128, SENT, 128), ("row", "col"), 0, 0, tiled=True
     ).reshape(8, 16, SENT, 128)

time: 186 us -> 188 us (1.011)
  waiting for transfers between devices: 55 us -> 63.8 us
  starting transfers between devices: 50.4 us -> 43 us
    ppermute x6 -> x12, waiting for transfers between devices: 8.87 us -> 20.6 us  [shifted(): return [v] + [lax.ppermute(v, axis, shift(s)) for s in (1, 2, 3)]]
    all_gather x1, waiting for transfers between devices: 10.8 us -> 0.01 us  [per_device(): segment = lax.all_gather(panel, 'col', axis=0, tiled=False)]
    ppermute x6, waiting for transfers between devices: 16.6 us -> 27.2 us  [sum4(): v = v + lax.ppermute(v, axis, pairs(flip))]
    all_to_all x1, starting transfers between devices: 10.3 us -> 3.92 us  [per_device(): lax.all_to_all(trail.reshape(128, SENT, 128), ('row', 'col'), 0, 0, tiled...]
    ppermute x6, starting transfers between devices: 7.27 us -> 2.9 us  [sum4(): v = v + lax.ppermute(v, axis, pairs(flip))]
    ppermute x6 -> x12, starting transfers between devices: 8.96 us -> 12.8 us  [shifted(): return [v] + [lax.ppermute(v, axis, shift(s)) for s in (1, 2, 3)]]
    all_to_all x1, waiting for transfers between devices: 3.85 us -> 1.77 us  [per_device(): lax.all_to_all(trail.reshape(128, SENT, 128), ('row', 'col'), 0, 0, tiled...]
    unnamed x27 -> x25, local copies, waits for them, and re-layouts: 9.19 us -> 9.87 us
  transfers between devices with their start and end apart: 31 -> 36, of which waited for: 22 -> 26; matrix products, arithmetic and copies ran while one was open for 2% -> 1% of each run, Pallas kernels for 22% -> 21%
where the time goes in v8:
time: 188 us; the launch traced here: 187 us
  waiting for transfers between devices  63.8 us (34%)
  Pallas kernels  53.2 us (28%)
  starting transfers between devices  43 us (23%)
  between operations  14.4 us (8%)
  local copies, waits for them, and re-layouts  10.9 us (6%)
  other arithmetic  1.9 us (1%)
    ppermute x6, waiting for transfers between devices, sum4(): v = v + lax.ppermute(v, axis, pairs(flip))  27.2 us
    pallas_call x1, Pallas kernels, factor_panel(): pl.pallas_call(functools.partial(factor_kernel, float(rows_total)), out_s...  26.7 us
    ppermute x12, waiting for transfers between devices, shifted(): return [v] + [lax.ppermute(v, axis, shift(s)) for s in (1, 2, 3)]  20.6 us
    ppermute x12, starting transfers between devices, shifted(): return [v] + [lax.ppermute(v, axis, shift(s)) for s in (1, 2, 3)]  12.8 us
    pallas_call x1, Pallas kernels, residual(): pl.pallas_call(functools.partial(residual_kernel, float(rows_total)), out...  10.4 us
    unnamed x25, local copies, waits for them, and re-layouts  9.87 us
    pallas_call x1, Pallas kernels, trail_rows(): pl.pallas_call(trail_kernel, out_shape=jax.ShapeDtypeStruct((8, 16, SENT,...  8.91 us
    ppermute x3, starting transfers between devices, per_device(): lax.ppermute(jnp.stack([near[s], far[s]]), 'row', y_shift(s))  6.46 us
  transfers between devices with their start and end apart: 36, of which 26 were waited for; matrix products, arithmetic and copies ran while one was open for 1% of the time, Pallas kernels for 21%

profile of v8, /device:TPU:1, one launch (start us, length us, event | category | flops | bytes accessed | tf_op | source)
XLA Modules:
  0.0 187.2 jit_solution(15787351120740502471)
XLA Ops:
  8.1 4.7 %collective-permute-start.2 = (bf16[32,1024]{1,0:T(8,128)(2,1)S(1)}, bf16[32,1024]{1,0:T(8,128)(2,1)S(1)}, u32[]{:S(2)}, u32[]{:S(2)}) collective-permute-start(bf16[32,1024]{1,0:T(8,128)(2,1)S(1)} %pad_maximum_fusion.11), channel_id=1, source_target_pairs={{0,3},{1,0},{2,1},{3,2},{4,7},{5,4},{6,5},{7,6},{8,11},{9,8},{10,9... | collective-permute-start | bytes 196616 | tf_op jit(solution)/shard_map/ppermute | solution.py:61
  14.1 3.4 %collective-permute-done.1 = bf16[32,1024]{1,0:T(8,128)(2,1)S(1)} collective-permute-done((bf16[32,1024]{1,0:T(8,128)(2,1)S(1)}, bf16[32,1024]{1,0:T(8,128)(2,1)S(1)}, u32[]{:S(2)}, u32[]{:S(2)}) %collective-permute-start.1) | collective-permute-done | bytes 65568 | tf_op jit(solution)/shard_map/ppermute | solution.py:61
  17.8 2.5 %collective-permute-start.5 = (bf16[4,16,1024]{2,1,0:T(8,128)(2,1)S(1)}, bf16[4,16,1024]{2,1,0:T(8,128)(2,1)S(1)}, u32[]{:S(2)}, u32[]{:S(2)}) collective-permute-start(bf16[4,16,1024]{2,1,0:T(8,128)(2,1)S(1)} %get-tuple-element.75), channel_id=1, source_target_pairs={{0,12},{1,13},{2,14},{3,15},{4,0},{5,1},{6,2},{7,3},{8,4},{9,5},{1... | collective-permute-start | bytes 393224 | tf_op jit(solution)/shard_map/ppermute | solution.py:61
  23.0 2.8 %collective-permute-done.4 = bf16[4,16,1024]{2,1,0:T(8,128)(2,1)S(1)} collective-permute-done((bf16[4,16,1024]{2,1,0:T(8,128)(2,1)S(1)}, bf16[4,16,1024]{2,1,0:T(8,128)(2,1)S(1)}, u32[]{:S(2)}, u32[]{:S(2)}) %collective-permute-start.4) | collective-permute-done | bytes 131104 | tf_op jit(solution)/shard_map/ppermute | solution.py:61
  27.2 3.6 %collective-permute-start.6 = (bf16[4,4,16,1024]{3,2,1,0:T(8,128)(2,1)S(1)}, bf16[4,4,16,1024]{3,2,1,0:T(8,128)(2,1)S(1)}, u32[]{:S(2)}, u32[]{:S(2)}) collective-permute-start(bf16[4,4,16,1024]{3,2,1,0:T(8,128)(2,1)S(1)} %pad_maximum_fusion.2.own), channel_id=1, source_target_pairs={{0,16},{16,0},{32,48},{48,32},{64,80},{80,64},{96,112},{112,96},{1... | collective-permute-start | bytes 1572872 | tf_op jit(solution)/shard_map/ppermute | solution.py:527
  31.0 1.9 %copy-done.2 = bf16[3,4,128,1024]{3,2,1,0:T(8,128)(2,1)S(1)} copy-done((bf16[3,4,128,1024]{3,2,1,0:T(8,128)(2,1)S(1)}, bf16[3,4,128,1024]{3,2,1,0:T(8,128)(2,1)}, u32[]{:S(2)}) %copy-start.2) | copy-done | bytes 3145752
  35.8 2.4 %shard_map.95 = (bf16[4,56,512]{2,1,0:T(8,128)(2,1)S(1)}, bf16[4,56,512]{2,1,0:T(8,128)(2,1)S(1)}, f32[1280,128]{1,0:T(8,128)S(1)}) custom-call(s32[4]{0:T(128)S(1)} %pad_add_fusion.where, bf16[4,4,16,1024]{3,2,1,0:T(8,128)(2,1)S(1)} %pad_maximum_fusion.2.own, bf16[4,4,16,1024]{3,2,1,0:T(8,128)(2,1)S(1)} %collective-permute-done.6.other, ...), custom_call_target="tpu_custom_call" | custom-call | flops 1140850688 | bytes 5242880 | tf_op jit(solution)/shard_map/pallas_call | solution.py:281
  40.7 3.6 %collective-permute-done.9 = bf16[4,16,1024]{2,1,0:T(8,128)(2,1)S(1)} collective-permute-done((bf16[4,16,1024]{2,1,0:T(8,128)(2,1)S(1)}, bf16[4,16,1024]{2,1,0:T(8,128)(2,1)S(1)}, u32[]{:S(2)}, u32[]{:S(2)}) %collective-permute-start.9) | collective-permute-done | bytes 131104 | tf_op jit(solution)/shard_map/ppermute | solution.py:61
  47.5 2.7 %collective-permute-start.13 = (bf16[2,56,512]{2,1,0:T(8,128)(2,1)S(1)}, bf16[2,56,512]{2,1,0:T(8,128)(2,1)S(1)}, u32[]{:S(2)}, u32[]{:S(2)}) collective-permute-start(bf16[2,56,512]{2,1,0:T(8,128)(2,1)S(1)} %pad_maximum_fusion.9), channel_id=1, source_target_pairs={{0,64},{16,80},{32,96},{48,112},{64,0},{80,16},{96,32},{112,48},{1... | collective-permute-start | bytes 344072 | tf_op jit(solution)/shard_map/ppermute | solution.py:544
  52.1 1.9 collective-permute-done.17
  53.9 2.4 %collective-permute-start.14 = (bf16[2,56,512]{2,1,0:T(8,128)(2,1)S(1)}, bf16[2,56,512]{2,1,0:T(8,128)(2,1)S(1)}, u32[]{:S(2)}, u32[]{:S(2)}) collective-permute-start(bf16[2,56,512]{2,1,0:T(8,128)(2,1)S(1)} %pad_maximum_fusion.10), channel_id=1, source_target_pairs={{0,96},{16,112},{32,0},{48,16},{64,32},{80,48},{96,64},{112,80},{1... | collective-permute-start | bytes 344072 | tf_op jit(solution)/shard_map/ppermute | solution.py:544
  57.0 2.7 %collective-permute-done.15 = f32[160,128]{1,0:T(8,128)S(1)} collective-permute-done((f32[160,128]{1,0:T(8,128)S(1)}, f32[160,128]{1,0:T(8,128)S(1)}, u32[]{:S(2)}, u32[]{:S(2)}) %collective-permute-start.15) | collective-permute-done | bytes 81952 | tf_op jit(solution)/shard_map/ppermute | solution.py:73
  61.1 1.5 collective-permute-start.20
  63.3 3.6 %collective-permute-done.21 = f32[160,128]{1,0:T(8,128)S(1)} collective-permute-done((f32[160,128]{1,0:T(8,128)S(1)}, f32[160,128]{1,0:T(8,128)S(1)}, u32[]{:S(2)}, u32[]{:S(2)}) %collective-permute-start.21) | collective-permute-done | bytes 81952 | tf_op jit(solution)/shard_map/ppermute | solution.py:96
  67.8 4.0 %collective-permute-done.22 = f32[160,128]{1,0:T(8,128)S(1)} collective-permute-done((f32[160,128]{1,0:T(8,128)S(1)}, f32[160,128]{1,0:T(8,128)S(1)}, u32[]{:S(2)}, u32[]{:S(2)}) %collective-permute-start.22) | collective-permute-done | bytes 81952 | tf_op jit(solution)/shard_map/ppermute | solution.py:96
  71.9 5.0 %collective-permute-done.23 = f32[160,128]{1,0:T(8,128)S(1)} collective-permute-done((f32[160,128]{1,0:T(8,128)S(1)}, f32[160,128]{1,0:T(8,128)S(1)}, u32[]{:S(2)}, u32[]{:S(2)}) %collective-permute-start.23) | collective-permute-done | bytes 81952 | tf_op jit(solution)/shard_map/ppermute | solution.py:96
  77.3 6.2 %collective-permute-done.24 = f32[160,128]{1,0:T(8,128)S(1)} collective-permute-done((f32[160,128]{1,0:T(8,128)S(1)}, f32[160,128]{1,0:T(8,128)S(1)}, u32[]{:S(2)}, u32[]{:S(2)}) %collective-permute-start.24) | collective-permute-done | bytes 81952 | tf_op jit(solution)/shard_map/ppermute | solution.py:96
  83.5 5.7 %collective-permute-done.18 = bf16[4,4,16,1024]{3,2,1,0:T(8,128)(2,1)S(1)} collective-permute-done((bf16[4,4,16,1024]{3,2,1,0:T(8,128)(2,1)S(1)}, bf16[4,4,16,1024]{3,2,1,0:T(8,128)(2,1)S(1)}, u32[]{:S(2)}, u32[]{:S(2)}) %collective-permute-start.18) | collective-permute-done | bytes 524320 | tf_op jit(solution)/shard_map/ppermute | solution.py:61
  90.3 2.5 %collective-permute-start.27 = (f32[160,128]{1,0:T(8,128)S(1)}, f32[160,128]{1,0:T(8,128)S(1)}, u32[]{:S(2)}, u32[]{:S(2)}) collective-permute-start(f32[160,128]{1,0:T(8,128)S(1)} %add.128), channel_id=1, source_target_pairs={{0,64},{16,80},{32,96},{48,112},{64,0},{80,16},{96,32},{112,48},{1... | collective-permute-start | bytes 245768 | tf_op jit(solution)/shard_map/ppermute | solution.py:65
  94.3 1.6 collective-permute-done.27
  95.8 1.7 collective-permute-done.28
  104.0 8.9 %shard_map.96 = bf16[8,16,56,128]{3,2,1,0:T(8,128)(2,1)S(1)} custom-call(s32[4]{0:T(128)S(1)} %pad_add_fusion.where, bf16[4,4,4,16,1024]{4,3,2,1,0:T(8,128)(2,1)S(1)} %pad_maximum_fusion.own, bf16[4,4,4,16,1024]{4,3,2,1,0:T(8,128)(2,1)} %collective-permute-done.25.other, bf16[320,1024]{1,0:T(8,128)(2,1)S(1)} %get-tuple-element.31.atoms_ref, ...), custom_call_target="tpu_custom_call" | custom-call | flops 4563402752 | bytes 9437184 | tf_op jit(solution)/shard_map/pallas_call | solution.py:312
  114.1 3.9 %all-to-all-start = ((bf16[128,56,128]{2,1,0:T(8,128)(2,1)}), bf16[128,56,128]{2,1,0:T(8,128)(2,1)S(1)}, u32[]{:S(2)}, u32[]{:S(2)}) async-start(bf16[128,56,128]{2,1,0:T(8,128)(2,1)} %bitcast.43), calls=%async_computation | async-start | bytes 3670016 | tf_op jit(solution)/shard_map/all_to_all | solution.py:559
  118.1 26.7 %shard_map.97 = (f32[512,512]{1,0:T(8,128)}, f32[512,512]{1,0:T(8,128)S(1)}) custom-call(f32[1280,128]{1,0:T(8,128)S(1)} %pad_maximum_fusion.1.gram_ref), custom_call_target="tpu_custom_call" | custom-call | flops 2684354560 | bytes 4194304 | tf_op jit(solution)/shard_map/pallas_call | solution.py:401
  144.8 1.8 all-to-all-done
  146.6 2.9 %copy-done = bf16[6400,512]{1,0:T(8,128)(2,1)S(1)} copy-done((bf16[6400,512]{1,0:T(8,128)(2,1)S(1)}, bf16[6400,512]{1,0:T(8,128)(2,1)}, u32[]{:S(2)}) %copy-start) | copy-done | bytes 6553624
  149.4 1.9 %shard_map.99 = f32[128,512]{1,0:T(8,128)S(1)} custom-call(bf16[16,400,512]{2,1,0:T(8,128)(2,1)S(1)} %bitcast.38, bf16[8,16,56,128]{3,2,1,0:T(8,128)(2,1)S(1)} %bitcast.40), custom_call_target="tpu_custom_call" | custom-call | flops 1073741824 | bytes 11534336 | tf_op jit(solution)/shard_map/pallas_call | solution.py:426
  153.8 4.4 %collective-permute-done.31 = f32[64,512]{1,0:T(8,128)S(1)} collective-permute-done((f32[64,512]{1,0:T(8,128)S(1)}, f32[64,512]{1,0:T(8,128)S(1)}, u32[]{:S(2)}, u32[]{:S(2)}) %collective-permute-start.31) | collective-permute-done | bytes 131104 | tf_op jit(solution)/shard_map/ppermute | solution.py:96
  159.3 4.0 %collective-permute-done.32 = f32[64,512]{1,0:T(8,128)S(1)} collective-permute-done((f32[64,512]{1,0:T(8,128)S(1)}, f32[64,512]{1,0:T(8,128)S(1)}, u32[]{:S(2)}, u32[]{:S(2)}) %collective-permute-start.32) | collective-permute-done | bytes 131104 | tf_op jit(solution)/shard_map/ppermute | solution.py:96
  163.4 2.6 %collective-permute-start.33 = (f32[64,512]{1,0:T(8,128)S(1)}, f32[64,512]{1,0:T(8,128)S(1)}, u32[]{:S(2)}, u32[]{:S(2)}) collective-permute-start(f32[64,512]{1,0:T(8,128)S(1)} %add.137), channel_id=1, source_target_pairs={{0,16},{16,0},{32,48},{48,32},{64,80},{80,64},{96,112},{112,96},{1... | collective-permute-start | bytes 393224 | tf_op jit(solution)/shard_map/ppermute | solution.py:89
  167.1 2.9 %copy-done.1 = bf16[6400,512]{1,0:T(8,128)(2,1)S(1)} copy-done((bf16[6400,512]{1,0:T(8,128)(2,1)S(1)}, bf16[6400,512]{1,0:T(8,128)(2,1)}, u32[]{:S(2)}) %copy-start.1) | copy-done | bytes 6553624
  169.9 10.4 %shard_map.100 = (f32[128,512]{1,0:T(8,128)}, f32[128,8192]{1,0:T(8,128)}) custom-call(f32[128,512]{1,0:T(8,128)S(1)} %pad_maximum_fusion.5.cross_ref, f32[512,512]{1,0:T(8,128)S(1)} %get-tuple-element.54.inverse_ref, bf16[16,400,512]{2,1,0:T(8,128)(2,1)S(1)} %bitcast.39, bf16[8,16,56,128]{3,2,1,0:T(8,128)(2,1)S(1)} %bitcast.41), custom_call_target="tpu_custom_call" | custom-call | flops 2147483648 | bytes 16777216 | tf_op jit(solution)/shard_map/pallas_call | solution.py:477
  (108 shorter events, 36.1 us)
Async XLA Ops:
  7.2 137.6 %all-gather.3.cloned.1.call-start = ((), (), s32[]{:S(2)}) async-start(), calls=%async_computation.1 | async-start | bytes 6963200 | tf_op jit(solution)/shard_map/all_gather | solution.py:549
  8.1 6.0 %collective-permute-start.2 = (bf16[32,1024]{1,0:T(8,128)(2,1)S(1)}, bf16[32,1024]{1,0:T(8,128)(2,1)S(1)}, u32[]{:S(2)}, u32[]{:S(2)}) collective-permute-start(bf16[32,1024]{1,0:T(8,128)(2,1)S(1)} %pad_maximum_fusion.11), channel_id=1, source_target_pairs={{0,3},{1,0},{2,1},{3,2},{4,7},{5,4},{6,5},{7,6},{8,11},{9,8},{10,9... | collective-permute-start | bytes 196616 | tf_op jit(solution)/shard_map/ppermute | solution.py:61
  12.8 4.7 %collective-permute-start.1 = (bf16[32,1024]{1,0:T(8,128)(2,1)S(1)}, bf16[32,1024]{1,0:T(8,128)(2,1)S(1)}, u32[]{:S(2)}, u32[]{:S(2)}) collective-permute-start(bf16[32,1024]{1,0:T(8,128)(2,1)S(1)} %pad_maximum_fusion.11), channel_id=1, source_target_pairs={{0,2},{1,3},{2,0},{3,1},{4,6},{5,7},{6,4},{7,5},{8,10},{9,11},{10,... | collective-permute-start | bytes 196616 | tf_op jit(solution)/shard_map/ppermute | solution.py:61
  12.8 5.0 %collective-permute-start = (bf16[32,1024]{1,0:T(8,128)(2,1)S(1)}, bf16[32,1024]{1,0:T(8,128)(2,1)S(1)}, u32[]{:S(2)}, u32[]{:S(2)}) collective-permute-start(bf16[32,1024]{1,0:T(8,128)(2,1)S(1)} %pad_maximum_fusion.11), channel_id=1, source_target_pairs={{0,1},{1,2},{2,3},{3,0},{4,5},{5,6},{6,7},{7,4},{8,9},{9,10},{10,1... | collective-permute-start | bytes 196616 | tf_op jit(solution)/shard_map/ppermute | solution.py:61
  17.8 5.2 %collective-permute-start.5 = (bf16[4,16,1024]{2,1,0:T(8,128)(2,1)S(1)}, bf16[4,16,1024]{2,1,0:T(8,128)(2,1)S(1)}, u32[]{:S(2)}, u32[]{:S(2)}) collective-permute-start(bf16[4,16,1024]{2,1,0:T(8,128)(2,1)S(1)} %get-tuple-element.75), channel_id=1, source_target_pairs={{0,12},{1,13},{2,14},{3,15},{4,0},{5,1},{6,2},{7,3},{8,4},{9,5},{1... | collective-permute-start | bytes 393224 | tf_op jit(solution)/shard_map/ppermute | solution.py:61
  20.4 5.4 %collective-permute-start.4 = (bf16[4,16,1024]{2,1,0:T(8,128)(2,1)S(1)}, bf16[4,16,1024]{2,1,0:T(8,128)(2,1)S(1)}, u32[]{:S(2)}, u32[]{:S(2)}) collective-permute-start(bf16[4,16,1024]{2,1,0:T(8,128)(2,1)S(1)} %get-tuple-element.75), channel_id=1, source_target_pairs={{0,8},{1,9},{2,10},{3,11},{4,12},{5,13},{6,14},{7,15},{8,0},{9,1},... | collective-permute-start | bytes 393224 | tf_op jit(solution)/shard_map/ppermute | solution.py:61
  20.9 6.2 %collective-permute-start.3 = (bf16[4,16,1024]{2,1,0:T(8,128)(2,1)S(1)}, bf16[4,16,1024]{2,1,0:T(8,128)(2,1)S(1)}, u32[]{:S(2)}, u32[]{:S(2)}) collective-permute-start(bf16[4,16,1024]{2,1,0:T(8,128)(2,1)S(1)} %get-tuple-element.75), channel_id=1, source_target_pairs={{0,4},{1,5},{2,6},{3,7},{4,8},{5,9},{6,10},{7,11},{8,12},{9,13},{1... | collective-permute-start | bytes 393224 | tf_op jit(solution)/shard_map/ppermute | solution.py:61
  27.2 8.6 %collective-permute-start.6 = (bf16[4,4,16,1024]{3,2,1,0:T(8,128)(2,1)S(1)}, bf16[4,4,16,1024]{3,2,1,0:T(8,128)(2,1)S(1)}, u32[]{:S(2)}, u32[]{:S(2)}) collective-permute-start(bf16[4,4,16,1024]{3,2,1,0:T(8,128)(2,1)S(1)} %pad_maximum_fusion.2.own), channel_id=1, source_target_pairs={{0,16},{16,0},{32,48},{48,32},{64,80},{80,64},{96,112},{112,96},{1... | collective-permute-start | bytes 1572872 | tf_op jit(solution)/shard_map/ppermute | solution.py:527
  34.3 5.0 %collective-permute-start.11 = (bf16[4,16,1024]{2,1,0:T(8,128)(2,1)S(1)}, bf16[4,16,1024]{2,1,0:T(8,128)(2,1)S(1)}, u32[]{:S(2)}, u32[]{:S(2)}) collective-permute-start(bf16[4,16,1024]{2,1,0:T(8,128)(2,1)S(1)} %pad_maximum_fusion.7), channel_id=1, source_target_pairs={{0,12},{1,13},{2,14},{3,15},{4,0},{5,1},{6,2},{7,3},{8,4},{9,5},{1... | collective-permute-start | bytes 393224 | tf_op jit(solution)/shard_map/ppermute | solution.py:61
  34.6 6.1 %collective-permute-start.10 = (bf16[4,16,1024]{2,1,0:T(8,128)(2,1)S(1)}, bf16[4,16,1024]{2,1,0:T(8,128)(2,1)S(1)}, u32[]{:S(2)}, u32[]{:S(2)}) collective-permute-start(bf16[4,16,1024]{2,1,0:T(8,128)(2,1)S(1)} %pad_maximum_fusion.7), channel_id=1, source_target_pairs={{0,8},{1,9},{2,10},{3,11},{4,12},{5,13},{6,14},{7,15},{8,0},{9,1},... | collective-permute-start | bytes 393224 | tf_op jit(solution)/shard_map/ppermute | solution.py:61
  35.1 9.2 %collective-permute-start.9 = (bf16[4,16,1024]{2,1,0:T(8,128)(2,1)S(1)}, bf16[4,16,1024]{2,1,0:T(8,128)(2,1)S(1)}, u32[]{:S(2)}, u32[]{:S(2)}) collective-permute-start(bf16[4,16,1024]{2,1,0:T(8,128)(2,1)S(1)} %pad_maximum_fusion.7), channel_id=1, source_target_pairs={{0,4},{1,5},{2,6},{3,7},{4,8},{5,9},{6,10},{7,11},{8,12},{9,13},{1... | collective-permute-start | bytes 393224 | tf_op jit(solution)/shard_map/ppermute | solution.py:61
  38.3 6.7 %collective-permute-start.8 = (f32[640,128]{1,0:T(8,128)S(1)}, f32[640,128]{1,0:T(8,128)S(1)}, u32[]{:S(2)}, u32[]{:S(2)}) collective-permute-start(f32[640,128]{1,0:T(8,128)S(1)} %constant_dynamic-slice_fusion.4), channel_id=1, source_target_pairs={{0,16},{16,0},{32,48},{48,32},{64,80},{80,64},{96,112},{112,96},{1... | collective-permute-start | bytes 983048 | tf_op jit(solution)/shard_map/ppermute | solution.py:85
  46.1 13.5 %collective-permute-start.12 = (bf16[2,56,512]{2,1,0:T(8,128)(2,1)S(1)}, bf16[2,56,512]{2,1,0:T(8,128)(2,1)S(1)}, u32[]{:S(2)}, u32[]{:S(2)}) collective-permute-start(bf16[2,56,512]{2,1,0:T(8,128)(2,1)S(1)} %pad_maximum_fusion.8), channel_id=1, source_target_pairs={{0,32},{16,48},{32,64},{48,80},{64,96},{80,112},{96,0},{112,16},{1... | collective-permute-start | bytes 344072 | tf_op jit(solution)/shard_map/ppermute | solution.py:544
  47.5 12.2 %collective-permute-start.13 = (bf16[2,56,512]{2,1,0:T(8,128)(2,1)S(1)}, bf16[2,56,512]{2,1,0:T(8,128)(2,1)S(1)}, u32[]{:S(2)}, u32[]{:S(2)}) collective-permute-start(bf16[2,56,512]{2,1,0:T(8,128)(2,1)S(1)} %pad_maximum_fusion.9), channel_id=1, source_target_pairs={{0,64},{16,80},{32,96},{48,112},{64,0},{80,16},{96,32},{112,48},{1... | collective-permute-start | bytes 344072 | tf_op jit(solution)/shard_map/ppermute | solution.py:544
  50.2 3.7 %collective-permute-start.17 = (f32[160,128]{1,0:T(8,128)S(1)}, f32[160,128]{1,0:T(8,128)S(1)}, u32[]{:S(2)}, u32[]{:S(2)}) collective-permute-start(f32[160,128]{1,0:T(8,128)S(1)} %get-tuple-element.64), channel_id=1, source_target_pairs={{0,96},{16,112},{32,0},{48,16},{64,32},{80,48},{96,64},{112,80},{1... | collective-permute-start | bytes 245768 | tf_op jit(solution)/shard_map/ppermute | solution.py:73
  51.4 5.6 %collective-permute-start.16 = (f32[160,128]{1,0:T(8,128)S(1)}, f32[160,128]{1,0:T(8,128)S(1)}, u32[]{:S(2)}, u32[]{:S(2)}) collective-permute-start(f32[160,128]{1,0:T(8,128)S(1)} %get-tuple-element.65), channel_id=1, source_target_pairs={{0,64},{16,80},{32,96},{48,112},{64,0},{80,16},{96,32},{112,48},{1... | collective-permute-start | bytes 245768 | tf_op jit(solution)/shard_map/ppermute | solution.py:73
  51.5 8.1 %collective-permute-start.15 = (f32[160,128]{1,0:T(8,128)S(1)}, f32[160,128]{1,0:T(8,128)S(1)}, u32[]{:S(2)}, u32[]{:S(2)}) collective-permute-start(f32[160,128]{1,0:T(8,128)S(1)} %get-tuple-element.63), channel_id=1, source_target_pairs={{0,32},{16,48},{32,64},{48,80},{64,96},{80,112},{96,0},{112,16},{1... | collective-permute-start | bytes 245768 | tf_op jit(solution)/shard_map/ppermute | solution.py:73
  53.9 5.8 %collective-permute-start.14 = (bf16[2,56,512]{2,1,0:T(8,128)(2,1)S(1)}, bf16[2,56,512]{2,1,0:T(8,128)(2,1)S(1)}, u32[]{:S(2)}, u32[]{:S(2)}) collective-permute-start(bf16[2,56,512]{2,1,0:T(8,128)(2,1)S(1)} %pad_maximum_fusion.10), channel_id=1, source_target_pairs={{0,96},{16,112},{32,0},{48,16},{64,32},{80,48},{96,64},{112,80},{1... | collective-permute-start | bytes 344072 | tf_op jit(solution)/shard_map/ppermute | solution.py:544
  61.1 22.4 %collective-permute-start.20 = (bf16[4,4,16,1024]{3,2,1,0:T(8,128)(2,1)S(1)}, bf16[4,4,16,1024]{3,2,1,0:T(8,128)(2,1)S(1)}, u32[]{:S(2)}, u32[]{:S(2)}) collective-permute-start(bf16[4,4,16,1024]{3,2,1,0:T(8,128)(2,1)S(1)} %pad_maximum_fusion.3), channel_id=1, source_target_pairs={{0,96},{16,112},{32,0},{48,16},{64,32},{80,48},{96,64},{112,80},{1... | collective-permute-start | bytes 1572872 | tf_op jit(solution)/shard_map/ppermute | solution.py:61
  62.6 20.9 %collective-permute-start.19 = (bf16[4,4,16,1024]{3,2,1,0:T(8,128)(2,1)S(1)}, bf16[4,4,16,1024]{3,2,1,0:T(8,128)(2,1)S(1)}, u32[]{:S(2)}, u32[]{:S(2)}) collective-permute-start(bf16[4,4,16,1024]{3,2,1,0:T(8,128)(2,1)S(1)} %pad_maximum_fusion.3), channel_id=1, source_target_pairs={{0,64},{16,80},{32,96},{48,112},{64,0},{80,16},{96,32},{112,48},{1... | collective-permute-start | bytes 1572872 | tf_op jit(solution)/shard_map/ppermute | solution.py:61
  63.0 26.2 %collective-permute-start.18 = (bf16[4,4,16,1024]{3,2,1,0:T(8,128)(2,1)S(1)}, bf16[4,4,16,1024]{3,2,1,0:T(8,128)(2,1)S(1)}, u32[]{:S(2)}, u32[]{:S(2)}) collective-permute-start(bf16[4,4,16,1024]{3,2,1,0:T(8,128)(2,1)S(1)} %pad_maximum_fusion.3), channel_id=1, source_target_pairs={{0,32},{16,48},{32,64},{48,80},{64,96},{80,112},{96,0},{112,16},{1... | collective-permute-start | bytes 1572872 | tf_op jit(solution)/shard_map/ppermute | solution.py:61
  66.9 4.9 %collective-permute-start.22 = (f32[160,128]{1,0:T(8,128)S(1)}, f32[160,128]{1,0:T(8,128)S(1)}, u32[]{:S(2)}, u32[]{:S(2)}) collective-permute-start(f32[160,128]{1,0:T(8,128)S(1)} %add.125), channel_id=1, source_target_pairs={{0,3},{1,2},{2,1},{3,0},{4,7},{5,6},{6,5},{7,4},{8,11},{9,10},{10,... | collective-permute-start | bytes 245768 | tf_op jit(solution)/shard_map/ppermute | solution.py:96
  71.8 5.1 %collective-permute-start.23 = (f32[160,128]{1,0:T(8,128)S(1)}, f32[160,128]{1,0:T(8,128)S(1)}, u32[]{:S(2)}, u32[]{:S(2)}) collective-permute-start(f32[160,128]{1,0:T(8,128)S(1)} %add.126), channel_id=1, source_target_pairs={{0,4},{1,5},{2,6},{3,7},{4,0},{5,1},{6,2},{7,3},{8,12},{9,13},{10,... | collective-permute-start | bytes 245768 | tf_op jit(solution)/shard_map/ppermute | solution.py:96
  76.9 6.6 %collective-permute-start.24 = (f32[160,128]{1,0:T(8,128)S(1)}, f32[160,128]{1,0:T(8,128)S(1)}, u32[]{:S(2)}, u32[]{:S(2)}) collective-permute-start(f32[160,128]{1,0:T(8,128)S(1)} %add.127), channel_id=1, source_target_pairs={{0,12},{1,13},{2,14},{3,15},{4,8},{5,9},{6,10},{7,11},{8,4},{9,5},... | collective-permute-start | bytes 245768 | tf_op jit(solution)/shard_map/ppermute | solution.py:96
  89.5 13.5 %collective-permute-start.25 = (bf16[4,4,4,16,1024]{4,3,2,1,0:T(8,128)(2,1)S(1)}, bf16[4,4,4,16,1024]{4,3,2,1,0:T(8,128)(2,1)}, u32[]{:S(2)}, u32[]{:S(2)}) collective-permute-start(bf16[4,4,4,16,1024]{4,3,2,1,0:T(8,128)(2,1)S(1)} %pad_maximum_fusion.own), channel_id=1, source_target_pairs={{0,16},{16,0},{32,48},{48,32},{64,80},{80,64},{96,112},{112,96},{1... | collective-permute-start | bytes 6291464 | tf_op jit(solution)/shard_map/ppermute | solution.py:554
  90.3 5.5 %collective-permute-start.27 = (f32[160,128]{1,0:T(8,128)S(1)}, f32[160,128]{1,0:T(8,128)S(1)}, u32[]{:S(2)}, u32[]{:S(2)}) collective-permute-start(f32[160,128]{1,0:T(8,128)S(1)} %add.128), channel_id=1, source_target_pairs={{0,64},{16,80},{32,96},{48,112},{64,0},{80,16},{96,32},{112,48},{1... | collective-permute-start | bytes 245768 | tf_op jit(solution)/shard_map/ppermute | solution.py:65
  92.8 4.7 %collective-permute-start.28 = (f32[160,128]{1,0:T(8,128)S(1)}, f32[160,128]{1,0:T(8,128)S(1)}, u32[]{:S(2)}, u32[]{:S(2)}) collective-permute-start(f32[160,128]{1,0:T(8,128)S(1)} %add.128), channel_id=1, source_target_pairs={{0,96},{16,112},{32,0},{48,16},{64,32},{80,48},{96,64},{112,80},{1... | collective-permute-start | bytes 245768 | tf_op jit(solution)/shard_map/ppermute | solution.py:65
  94.0 4.9 %collective-permute-start.26 = (f32[160,128]{1,0:T(8,128)S(1)}, f32[160,128]{1,0:T(8,128)S(1)}, u32[]{:S(2)}, u32[]{:S(2)}) collective-permute-start(f32[160,128]{1,0:T(8,128)S(1)} %add.128), channel_id=1, source_target_pairs={{0,32},{16,48},{32,64},{48,80},{64,96},{80,112},{96,0},{112,16},{1... | collective-permute-start | bytes 245768 | tf_op jit(solution)/shard_map/ppermute | solution.py:65
  114.1 32.4 %all-to-all-start = ((bf16[128,56,128]{2,1,0:T(8,128)(2,1)}), bf16[128,56,128]{2,1,0:T(8,128)(2,1)S(1)}, u32[]{:S(2)}, u32[]{:S(2)}) async-start(bf16[128,56,128]{2,1,0:T(8,128)(2,1)} %bitcast.43), calls=%async_computation | async-start | bytes 3670016 | tf_op jit(solution)/shard_map/all_to_all | solution.py:559
  153.4 4.8 %collective-permute-start.31 = (f32[64,512]{1,0:T(8,128)S(1)}, f32[64,512]{1,0:T(8,128)S(1)}, u32[]{:S(2)}, u32[]{:S(2)}) collective-permute-start(f32[64,512]{1,0:T(8,128)S(1)} %dynamic-slice_add_fusion.1), channel_id=1, source_target_pairs={{0,32},{16,48},{32,0},{48,16},{64,96},{80,112},{96,64},{112,80},{1... | collective-permute-start | bytes 393224 | tf_op jit(solution)/shard_map/ppermute | solution.py:96
  158.2 5.1 %collective-permute-start.32 = (f32[64,512]{1,0:T(8,128)S(1)}, f32[64,512]{1,0:T(8,128)S(1)}, u32[]{:S(2)}, u32[]{:S(2)}) collective-permute-start(f32[64,512]{1,0:T(8,128)S(1)} %add.136), channel_id=1, source_target_pairs={{0,96},{16,112},{32,64},{48,80},{64,32},{80,48},{96,0},{112,16},{1... | collective-permute-start | bytes 393224 | tf_op jit(solution)/shard_map/ppermute | solution.py:96
  163.4 3.6 %collective-permute-start.33 = (f32[64,512]{1,0:T(8,128)S(1)}, f32[64,512]{1,0:T(8,128)S(1)}, u32[]{:S(2)}, u32[]{:S(2)}) collective-permute-start(f32[64,512]{1,0:T(8,128)S(1)} %add.137), channel_id=1, source_target_pairs={{0,16},{16,0},{32,48},{48,32},{64,80},{80,64},{96,112},{112,96},{1... | collective-permute-start | bytes 393224 | tf_op jit(solution)/shard_map/ppermute | solution.py:89
  (16 other events, 125.4 us)
Sparse Core Ops, SparseCore 0:
  61.2 68.8 all-gather.2

commit v9 on v7

--- a/solution.py
+++ b/solution.py
@@ -31,7 +31,8 @@
 
 
 SENT = 56
-HELD = 400
+FIRST, SECOND = 208, 192
+HELD = FIRST + SECOND
 UPPER = [(i, j) for i in range(4) for j in range(i, 4)]
 
 
@@ -89,6 +90,20 @@
     other = lax.ppermute(v, "row", CORE_SWAP)
     first = core == 0
     return jnp.where(first, v, other), jnp.where(first, other, v)
+
+
+def ring(v, axis, shift):
+    cut = v.shape[0] // 2
+    one = lax.ppermute(v, axis, shift(1))
+    three = lax.ppermute(v, axis, shift(3))
+    low = lax.ppermute(one[:cut], axis, shift(1))
+    high = lax.ppermute(three[cut:], axis, shift(3))
+    return one, low, high, three
+
+
+def ring_stack(v, axis, shift):
+    one, low, high, three = ring(v, axis, shift)
+    return jnp.stack([v, one, jnp.concatenate([low, high], axis=0), three])
 
 
 def sum4(v, axis, pairs):
@@ -243,25 +258,38 @@
         out_ref[:, c] = part.astype(BF16)
 
 
-def assemble_kernel(where, near, far, got1, got2, got3, out):
+def assemble_kernel(where, near, far, got1, got2, got3, first, second):
     y, core = where[2], where[3]
     blocks = [(near, 0, 0, core), (far, 0, 0, 1 - core)]
     for s, got in ((1, got1), (2, got2), (3, got3)):
         blocks += [(got, 0, s, core), (got, 1, s, 1 - core)]
-    energy = jnp.zeros((8, out.shape[1]), F32)
+    energy = jnp.zeros((8, first.shape[1]), F32)
     for ref, i, s, c in blocks:
-        at = (2 * ((y - s) & 3) + c) * 48
-        out[pl.ds(pl.multiple_of(at, 16), 48)] = ref[i, :48]
+        source = 2 * ((y - s) & 3) + c
+        at = pl.ds(pl.multiple_of((source & 3) * 48, 16), 48)
+
+        @pl.when(source < 4)
+        def _(ref=ref, i=i, at=at):
+            first[at] = ref[i, :48]
+
+        @pl.when(source >= 4)
+        def _(ref=ref, i=i, at=at):
+            second[at] = ref[i, :48]
+
         energy = energy + ref[i, 48:].astype(F32)
-    out[384:] = jnp.concatenate([energy, jnp.zeros_like(energy)], axis=0).astype(BF16)
-
-
-def trail_chunk(ref, i):
-    rows = [ref[r, i, :48].astype(F32) for r in range(8)]
-    energy = ref[0, i, 48:].astype(F32)
+    first[192:] = jnp.concatenate([energy, jnp.zeros_like(energy)], axis=0).astype(BF16)
+
+
+def trail_first(ref, c):
+    rows = [ref[r, c, :48].astype(F32) for r in range(4)]
+    energy = ref[0, c, 48:].astype(F32)
     for r in range(1, 8):
-        energy = energy + ref[r, i, 48:].astype(F32)
+        energy = energy + ref[r, c, 48:].astype(F32)
     return jnp.concatenate(rows + [energy, jnp.zeros_like(energy)], axis=0).astype(BF16)
+
+
+def trail_second(ref, c):
+    return jnp.concatenate([ref[r, c, :48] for r in range(4, 8)], axis=0)
 
 
 def params(mib=40):
@@ -297,9 +325,12 @@
 def assemble(where, near, far, got):
     return pl.pallas_call(
         assemble_kernel,
-        out_shape=jax.ShapeDtypeStruct((HELD, 512), BF16),
+        out_shape=(
+            jax.ShapeDtypeStruct((FIRST, 512), BF16),
+            jax.ShapeDtypeStruct((SECOND, 512), BF16),
+        ),
         in_specs=[in_smem()] + [in_vmem()] * 5,
-        out_specs=in_vmem(),
+        out_specs=(in_vmem(), in_vmem()),
         compiler_params=params(),
         cost_estimate=pl.CostEstimate(flops=0, bytes_accessed=1 << 20, transcendentals=0),
     )(where, near, far, *got)
@@ -385,11 +416,21 @@
     def step(b, carry):
         at = pl.multiple_of(b * 128, 128)
         low = eliminate(work[pl.ds(at, 128), pl.ds(at, 128)])
-        row = dot(low, work[pl.ds(at, 128), :], NN, HIGHEST)
-        lane = lax.broadcasted_iota(jnp.int32, (128, n), 1)
-        later = jnp.where(lane >= at + 128, row[:, :n], 0.0)
-        work[...] = work[...] - dot(later, row, TN, HIGHEST)
-        work[pl.ds(at, 128), :] = row
+        for k in range(n // 128):
+
+            @pl.when(b == k)
+            def _(k=k):
+                here, after = slice(128 * k, 128 * k + 128), slice(128 * k + 128, n)
+                left, right = slice(128 * k, n), slice(n, n + 128 * k + 128)
+                row = dot(low, work[here, left], NN, HIGHEST)
+                solved = dot(low, work[here, right], NN, HIGHEST)
+                work[here, left] = row
+                work[here, right] = solved
+                if k < n // 128 - 1:
+                    later = row[:, 128:]
+                    work[after, after] -= dot(later, later, TN, HIGHEST)
+                    work[after, right] -= dot(later, solved, TN, HIGHEST)
+
         return carry
 
     lax.fori_loop(0, n // 128, step, 0)
@@ -410,39 +451,54 @@
     )(gram)
 
 
-def cross_kernel(panel_ref, trail_ref, out_ref):
-    @pl.when(pl.program_id(0) == 0)
-    def _():
-        out_ref[...] = jnp.zeros_like(out_ref)
-
-    n = panel_ref.shape[2]
-    trail = jnp.concatenate(
-        [trail_chunk(trail_ref, i) for i in range(panel_ref.shape[0])], axis=0
-    )
-    out_ref[...] += dot(trail, panel_ref[...].reshape(-1, n), TN)
-
-
-def cross_part(segment, trail):
-    n = segment.shape[2]
+def chunk_place(where, i, j):
+    return ((where[0] - i) & 3) * 4 + ((where[1] - j) & 3)
+
+
+def first_pieces(refs):
+    own, one, low, high, three = refs
+    rows = [[(own, j) for j in range(4)], [(one, j) for j in range(4)]]
+    rows.append([(low, 0), (low, 1), (high, 0), (high, 1)])
+    return rows + [[(three, j) for j in range(4)]]
+
+
+def second_pieces(refs):
+    turned = first_pieces(refs)
+    return [[turned[j][i] for j in range(4)] for i in range(4)]
+
+
+def cross_kernel(where, *refs):
+    first, second = first_pieces(refs[:5]), second_pieces(refs[5:10])
+    trail_ref, out_ref = refs[10], refs[11]
+    total = jnp.zeros(out_ref.shape, F32)
+    for i in range(4):
+        for j in range(4):
+            c = chunk_place(where, i, j)
+            ref, at = first[i][j]
+            total = total + dot(trail_first(trail_ref, c), ref[at], TN)
+            ref, at = second[i][j]
+            total = total + dot(trail_second(trail_ref, c), ref[at], TN)
+    out_ref[...] = total
+
+
+def cross_part(where, segment, trail):
+    n = 512
     return pl.pallas_call(
         cross_kernel,
         out_shape=jax.ShapeDtypeStruct((128, n), F32),
-        grid=(segment.shape[0] // 4,),
-        in_specs=[
-            pl.BlockSpec((4, HELD, n), lambda i: (i, 0, 0)),
-            pl.BlockSpec((8, 4, SENT, 128), lambda i: (0, i, 0, 0)),
-        ],
-        out_specs=pl.BlockSpec((128, n), lambda i: (0, 0)),
+        in_specs=[in_smem()] + [in_vmem()] * 11,
+        out_specs=in_vmem(),
         compiler_params=params(),
         cost_estimate=pl.CostEstimate(
-            flops=2 * 128 * n * 8192, bytes_accessed=11 << 20, transcendentals=0
-        ),
-    )(segment, trail)
-
-
-def residual_kernel(
-    rows_total, cross_ref, inverse_ref, panel_ref, trail_ref, coupling_ref, out_ref, weights, spread
-):
+            flops=2 * 128 * n * 6400, bytes_accessed=9 << 20, transcendentals=0
+        ),
+    )(where, *segment, trail)
+
+
+def residual_kernel(rows_total, where, cross_ref, inverse_ref, *refs):
+    first, second = first_pieces(refs[:5]), second_pieces(refs[5:10])
+    trail_ref, coupling_ref, out_ref, weights, spread = refs[10:]
+
     @pl.when(pl.program_id(0) == 0)
     def _():
         coupling = dot(cross_ref[...] / rows_total, inverse_ref[...], NT, HIGHEST)
@@ -455,46 +511,62 @@
         column = lax.broadcasted_iota(jnp.int32, (HELD, 512), 1)
         struct, place = column >> 6, column & 63
         wanted = jnp.where(place <= 48, struct * 48 + place - 1, -1)
-        wanted = jnp.where(place == 0, 384 + struct, wanted)
+        wanted = jnp.where((place <= 48) & (struct >= 4), wanted + 16, wanted)
+        wanted = jnp.where(place == 0, 192 + struct, wanted)
         spread[...] = (held == wanted).astype(F32).astype(BF16)
 
     r = lax.broadcasted_iota(jnp.int32, (128, 128), 0)
     c = lax.broadcasted_iota(jnp.int32, (128, 128), 1)
     same = (r == c).astype(BF16)
-    for i in range(panel_ref.shape[0]):
-        both = dot(weights[...], panel_ref[i], NT)
-        own = dot(same, trail_chunk(trail_ref, i), NT)
-        rest = own - both[:128] - both[128:]
+
+    def piece(panel, trail):
+        both = dot(weights[...], panel, NT)
+        rest = dot(same, trail, NT) - both[:128] - both[128:]
         high = rest.astype(BF16)
         low = (rest - high.astype(F32)).astype(BF16)
-        full = dot(jnp.concatenate([high, low], axis=0), spread[...], NN)
-        out_ref[:, i * 512 : i * 512 + 512] = full[:128] + full[128:]
-
-
-def residual(cross, inverse, segment, trail, rows_total):
+        return jnp.concatenate([high, low], axis=0)
+
+    for i in range(4):
+
+        @pl.when(pl.program_id(0) == i)
+        def _(i=i):
+            for j in range(4):
+                c = chunk_place(where, i, j)
+                ref, at = first[i][j]
+                full = dot(piece(ref[at], trail_first(trail_ref, c)), spread[:FIRST], NN)
+                ref, at = second[i][j]
+                full = full + dot(
+                    piece(ref[at], trail_second(trail_ref, c)), spread[FIRST:], NN
+                )
+                at = pl.multiple_of(((where[1] - j) & 3) * 512, 512)
+                out_ref[:, pl.ds(at, 512)] = full[:128] + full[128:]
+
+
+def residual(where, cross, inverse, segment, trail, rows_total):
     n = inverse.shape[0]
-    chunks = segment.shape[0]
-    whole = lambda shape: pl.BlockSpec(shape, lambda i: (0, 0))
+    whole = lambda v: pl.BlockSpec(v.shape, lambda i, w: (0,) * v.ndim)
+    operands = [cross, inverse, *segment, trail]
     return pl.pallas_call(
         functools.partial(residual_kernel, float(rows_total)),
         out_shape=(
             jax.ShapeDtypeStruct((128, n), F32),
-            jax.ShapeDtypeStruct((128, 512 * chunks), F32),
-        ),
-        grid=(chunks // 4,),
-        in_specs=[
-            whole((128, n)),
-            whole((n, n)),
-            pl.BlockSpec((4, HELD, n), lambda i: (i, 0, 0)),
-            pl.BlockSpec((8, 4, SENT, 128), lambda i: (0, i, 0, 0)),
-        ],
-        out_specs=(whole((128, n)), pl.BlockSpec((128, 2048), lambda i: (0, i))),
-        scratch_shapes=[pltpu.VMEM((256, n), BF16), pltpu.VMEM((HELD, 512), BF16)],
+            jax.ShapeDtypeStruct((128, 8192), F32),
+        ),
+        grid_spec=pltpu.PrefetchScalarGridSpec(
+            num_scalar_prefetch=1,
+            grid=(4,),
+            in_specs=[whole(v) for v in operands],
+            out_specs=(
+                pl.BlockSpec((128, n), lambda i, w: (0, 0)),
+                pl.BlockSpec((128, 2048), lambda i, w: (0, (w[0] - i) & 3)),
+            ),
+            scratch_shapes=[pltpu.VMEM((256, n), BF16), pltpu.VMEM((HELD, 512), BF16)],
+        ),
         compiler_params=params(),
         cost_estimate=pl.CostEstimate(
-            flops=4 * 128 * n * 8192, bytes_accessed=16 << 20, transcendentals=0
-        ),
-    )(cross, inverse, segment, trail)
+            flops=4 * 128 * n * 6400, bytes_accessed=14 << 20, transcendentals=0
+        ),
+    )(where, *operands)
 
 
 def sum_row(v, core):
@@ -538,16 +610,23 @@
     ]
     gram = scatter4(gram, "row", y_shift, y)
     got, gram = lax.optimization_barrier((got, gram))
-    panel = assemble(where, near, far, got)
-    segment = lax.all_gather(panel, "col", axis=0, tiled=False)
+    first, second = assemble(where, near, far, got)
+    first = ring_stack(first, "col", z_shift)
+    second = ring_stack(second, "col", x_shift)
     trail_other = lax.ppermute(trail_own, "row", CORE_SWAP)
     gram = sum4(gram, "col", z_pair)
     trail_other, gram = lax.optimization_barrier((trail_other, gram))
     gram = sum4(gram, "col", x_pair)
     trail = trail_rows(where, trail_own, trail_other, atoms, grads, mean, order)
-    trail, gram = lax.optimization_barrier((trail, gram))
+    first, second, gram = lax.optimization_barrier((first, second, gram))
+    segment = (
+        first,
+        *ring(first, "col", x_shift),
+        second,
+        *ring(second, "col", z_shift),
+    )
     gram = gather4(gram, "row", y_shift, y)
-    trail, gram = lax.optimization_barrier((trail, gram))
+    trail, segment, gram = lax.optimization_barrier((trail, segment, gram))
     gram = jnp.concatenate(swap_gather(gram, core), axis=0)
     trail = lax.all_to_all(
         trail.reshape(128, SENT, 128), ("row", "col"), 0, 0, tiled=True
@@ -555,8 +634,8 @@
     factor, inverse = factor_panel(gram, rows_total)
 
     segment, inverse = lax.optimization_barrier((segment, inverse))
-    cross = sum_row(cross_part(segment, trail), core)
-    coupling, result = residual(cross, inverse, segment, trail, rows_total)
+    cross = sum_row(cross_part(where, segment, trail), core)
+    coupling, result = residual(where, cross, inverse, segment, trail, rows_total)
     return factor, coupling, result
 
 

time: 186 us -> 237 us (1.27)
  starting transfers between devices: 50.4 us -> 76.4 us
  waiting for transfers between devices: 55 us -> 68.7 us
  local copies, waits for them, and re-layouts: 12.3 us -> 23.1 us
  other arithmetic: 0.56 us -> 3.37 us
  Pallas kernels: 52.5 us -> 49.8 us
    all_gather x1, waiting for transfers between devices: 1.14 us -> 19.4 us  [per_device(): trail_own = lax.all_gather(trail_own, 'col', axis=0, tiled=False)]
    ppermute x0 -> x16, starting transfers between devices: none -> 13.7 us  [the longest x4 6.07 us: ring(): three = lax.ppermute(v, axis, shift(3))]
    ppermute x0 -> x16, waiting for transfers between devices: none -> 11.8 us  [the longest x4 5.52 us: ring(): three = lax.ppermute(v, axis, shift(3))]
    all_gather x1 -> x0, waiting for transfers between devices: 10.8 us -> none  [per_device(): segment = lax.all_gather(panel, 'col', axis=0, tiled=False)]
    all_to_all x1, starting transfers between devices: 10.3 us -> 20.9 us  [per_device(): lax.all_to_all(trail.reshape(128, SENT, 128), ('row', 'col'), 0, 0, tiled...]
    unnamed x27 -> x75, local copies, waits for them, and re-layouts: 9.19 us -> 18.6 us
    pallas_call x1, Pallas kernels: 26.7 us -> 20.5 us  [factor_panel(): pl.pallas_call(functools.partial(factor_kernel, float(rows_total)), out_s...]
    ppermute x6, waiting for transfers between devices: 8.87 us -> 4.8 us  [shifted(): return [v] + [lax.ppermute(v, axis, shift(s)) for s in (1, 2, 3)]]
  transfers between devices with their start and end apart: 31 -> 46, of which waited for: 22 -> 23; matrix products, arithmetic and copies ran while one was open for 2% -> 3% of each run, Pallas kernels for 22% -> 14%
where the time goes in v9:
time: 237 us; the launch traced here: 236 us
  starting transfers between devices  76.4 us (32%)
  waiting for transfers between devices  68.7 us (29%)
  Pallas kernels  49.8 us (21%)
  local copies, waits for them, and re-layouts  23.1 us (10%)
  between operations  14.7 us (6%)
  other arithmetic  3.37 us (1%)
    all_to_all x1, starting transfers between devices, per_device(): lax.all_to_all(trail.reshape(128, SENT, 128), ('row', 'col'), 0, 0, tiled...  20.9 us
    pallas_call x1, Pallas kernels, factor_panel(): pl.pallas_call(functools.partial(factor_kernel, float(rows_total)), out_s...  20.5 us
    all_gather x1, waiting for transfers between devices, per_device(): trail_own = lax.all_gather(trail_own, 'col', axis=0, tiled=False)  19.4 us
    unnamed x75, local copies, waits for them, and re-layouts  18.6 us
    ppermute x6, waiting for transfers between devices, sum4(): v = v + lax.ppermute(v, axis, pairs(flip))  18.1 us
    pallas_call x1, Pallas kernels, residual(): pl.pallas_call(functools.partial(residual_kernel, float(rows_total)), out...  13.7 us
    ppermute x6, starting transfers between devices, shifted(): return [v] + [lax.ppermute(v, axis, shift(s)) for s in (1, 2, 3)]  12.6 us
    pallas_call x1, Pallas kernels, trail_rows(): pl.pallas_call(trail_kernel, out_shape=jax.ShapeDtypeStruct((8, blocks, S...  8.37 us
  transfers between devices with their start and end apart: 46, of which 23 were waited for; matrix products, arithmetic and copies ran while one was open for 3% of the time, Pallas kernels for 14%

profile of v9, /device:TPU:1, one launch (start us, length us, event | category | flops | bytes accessed | tf_op | source)
XLA Modules:
  0.0 236.0 jit_solution(4210110511067142406)
XLA Ops:
  9.6 4.4 %collective-permute-start.2 = (bf16[16,1024]{1,0:T(8,128)(2,1)S(1)}, bf16[16,1024]{1,0:T(8,128)(2,1)S(1)}, u32[]{:S(2)}, u32[]{:S(2)}) collective-permute-start(bf16[16,1024]{1,0:T(8,128)(2,1)S(1)} %constant_dynamic-slice_fusion.5), channel_id=1, source_target_pairs={{0,2},{1,3},{2,0},{3,1},{4,6},{5,7},{6,4},{7,5},{8,10},{9,11},{10,... | collective-permute-start | bytes 98312 | tf_op jit(solution)/shard_map/ppermute | solution.py:62
  14.8 1.9 collective-permute-start.3
  18.0 2.8 %collective-permute-start.5 = (bf16[4,16,1024]{2,1,0:T(8,128)(2,1)S(1)}, bf16[4,16,1024]{2,1,0:T(8,128)(2,1)S(1)}, u32[]{:S(2)}, u32[]{:S(2)}) collective-permute-start(bf16[4,16,1024]{2,1,0:T(8,128)(2,1)S(1)} %get-tuple-element.115), channel_id=1, source_target_pairs={{0,8},{1,9},{2,10},{3,11},{4,12},{5,13},{6,14},{7,15},{8,0},{9,1},... | collective-permute-start | bytes 393224 | tf_op jit(solution)/shard_map/ppermute | solution.py:62
  21.2 2.4 %collective-permute-start.6 = (bf16[4,16,1024]{2,1,0:T(8,128)(2,1)S(1)}, bf16[4,16,1024]{2,1,0:T(8,128)(2,1)S(1)}, u32[]{:S(2)}, u32[]{:S(2)}) collective-permute-start(bf16[4,16,1024]{2,1,0:T(8,128)(2,1)S(1)} %get-tuple-element.115), channel_id=1, source_target_pairs={{0,12},{1,13},{2,14},{3,15},{4,0},{5,1},{6,2},{7,3},{8,4},{9,5},{1... | collective-permute-start | bytes 393224 | tf_op jit(solution)/shard_map/ppermute | solution.py:62
  23.5 3.8 %collective-permute-done.4 = bf16[4,16,1024]{2,1,0:T(8,128)(2,1)S(1)} collective-permute-done((bf16[4,16,1024]{2,1,0:T(8,128)(2,1)S(1)}, bf16[4,16,1024]{2,1,0:T(8,128)(2,1)S(1)}, u32[]{:S(2)}, u32[]{:S(2)}) %collective-permute-start.4) | collective-permute-done | bytes 131104 | tf_op jit(solution)/shard_map/ppermute | solution.py:62
  27.9 2.4 %collective-permute-start.7 = (bf16[4,4,16,1024]{3,2,1,0:T(8,128)(2,1)S(1)}, bf16[4,4,16,1024]{3,2,1,0:T(8,128)(2,1)S(1)}, u32[]{:S(2)}, u32[]{:S(2)}) collective-permute-start(bf16[4,4,16,1024]{3,2,1,0:T(8,128)(2,1)S(1)} %pad_maximum_fusion.3.own), channel_id=1, source_target_pairs={{0,16},{16,0},{32,48},{48,32},{64,80},{80,64},{96,112},{112,96},{1... | collective-permute-start | bytes 1572872 | tf_op jit(solution)/shard_map/ppermute | solution.py:593
  30.5 1.9 copy-done.10
  35.7 2.4 %shard_map.95 = (bf16[4,56,512]{2,1,0:T(8,128)(2,1)S(1)}, bf16[4,56,512]{2,1,0:T(8,128)(2,1)S(1)}, f32[1280,128]{1,0:T(8,128)S(1)}) custom-call(s32[4]{0:T(128)S(1)} %pad_add_fusion.where, bf16[4,4,16,1024]{3,2,1,0:T(8,128)(2,1)S(1)} %pad_maximum_fusion.3.own, bf16[4,4,16,1024]{3,2,1,0:T(8,128)(2,1)S(1)} %copy-done.33, ...), custom_call_target="tpu_custom_call" | custom-call | flops 1140850688 | bytes 5242880 | tf_op jit(solution)/shard_map/pallas_call | solution.py:308
  39.1 19.4 %all-gather.3.cloned.1.call-done = bf16[1024,1024]{1,0:T(8,128)(2,1)} async-done(((bf16[64,1024]{1,0:T(8,128)(2,1)}), bf16[1024,1024]{1,0:T(8,128)(2,1)}) %all-gather.3.cloned.1.call-update) | async-done | bytes 2097168 | tf_op jit(solution)/shard_map/all_gather | solution.py:589
  58.5 1.7 collective-permute-start
  60.3 3.9 %collective-permute-done.8.far = bf16[4,56,512]{2,1,0:T(8,128)(2,1)S(1)} collective-permute-done((bf16[4,56,512]{2,1,0:T(8,128)(2,1)S(1)}, bf16[4,56,512]{2,1,0:T(8,128)(2,1)S(1)}, u32[]{:S(2)}, u32[]{:S(2)}) %collective-permute-start.8) | collective-permute-done | bytes 229408 | tf_op jit(solution)/shard_map/ppermute | solution.py:605
  69.6 2.3 collective-permute-done.13
  74.7 2.4 %collective-permute-done.11.got2 = bf16[2,56,512]{2,1,0:T(8,128)(2,1)S(1)} collective-permute-done((bf16[2,56,512]{2,1,0:T(8,128)(2,1)S(1)}, bf16[2,56,512]{2,1,0:T(8,128)(2,1)S(1)}, u32[]{:S(2)}, u32[]{:S(2)}) %collective-permute-start.11) | collective-permute-done | bytes 114720 | tf_op jit(solution)/shard_map/ppermute | solution.py:609
  78.5 2.0 collective-permute-start.24
  83.8 2.8 %collective-permute-start.17 = (f32[160,128]{1,0:T(8,128)S(1)}, f32[160,128]{1,0:T(8,128)S(1)}, u32[]{:S(2)}, u32[]{:S(2)}) collective-permute-start(f32[160,128]{1,0:T(8,128)S(1)} %add.123), channel_id=1, source_target_pairs={{0,3},{1,2},{2,1},{3,0},{4,7},{5,6},{6,5},{7,4},{8,11},{9,10},{10,... | collective-permute-start | bytes 245768 | tf_op jit(solution)/shard_map/ppermute | solution.py:111
  87.7 2.8 %collective-permute-done.17 = f32[160,128]{1,0:T(8,128)S(1)} collective-permute-done((f32[160,128]{1,0:T(8,128)S(1)}, f32[160,128]{1,0:T(8,128)S(1)}, u32[]{:S(2)}, u32[]{:S(2)}) %collective-permute-start.17) | collective-permute-done | bytes 81952 | tf_op jit(solution)/shard_map/ppermute | solution.py:111
  92.6 2.6 %collective-permute-done.23 = bf16[96,512]{1,0:T(8,128)(2,1)S(1)} collective-permute-done((bf16[96,512]{1,0:T(8,128)(2,1)S(1)}, bf16[96,512]{1,0:T(8,128)(2,1)S(1)}, u32[]{:S(2)}, u32[]{:S(2)}) %collective-permute-start.23) | collective-permute-done | bytes 98336 | tf_op jit(solution)/shard_map/ppermute | solution.py:99
  95.5 1.9 collective-permute-done.19
  100.2 3.4 %collective-permute-done.27 = f32[160,128]{1,0:T(8,128)S(1)} collective-permute-done((f32[160,128]{1,0:T(8,128)S(1)}, f32[160,128]{1,0:T(8,128)S(1)}, u32[]{:S(2)}, u32[]{:S(2)}) %collective-permute-start.27) | collective-permute-done | bytes 81952 | tf_op jit(solution)/shard_map/ppermute | solution.py:111
  107.2 2.4 %collective-permute-start.38 = (f32[160,128]{1,0:T(8,128)}, f32[160,128]{1,0:T(8,128)}, u32[]{:S(2)}, u32[]{:S(2)}) collective-permute-start(f32[160,128]{1,0:T(8,128)} %add.126), channel_id=1, source_target_pairs={{0,96},{16,112},{32,0},{48,16},{64,32},{80,48},{96,64},{112,80},{1... | collective-permute-start | bytes 245768 | tf_op jit(solution)/shard_map/ppermute | solution.py:66
  109.6 5.5 %collective-permute-done.34.refs_9_ = bf16[4,192,512]{2,1,0:T(8,128)(2,1)S(1)} collective-permute-done((bf16[4,192,512]{2,1,0:T(8,128)(2,1)S(1)}, bf16[4,192,512]{2,1,0:T(8,128)(2,1)S(1)}, u32[]{:S(2)}, u32[]{:S(2)}) %collective-permute-start.34) | collective-permute-done | bytes 786464 | tf_op jit(solution)/shard_map/ppermute | solution.py:98
  115.1 2.4 %collective-permute-start.37 = (f32[160,128]{1,0:T(8,128)}, f32[160,128]{1,0:T(8,128)}, u32[]{:S(2)}, u32[]{:S(2)}) collective-permute-start(f32[160,128]{1,0:T(8,128)} %add.126), channel_id=1, source_target_pairs={{0,64},{16,80},{32,96},{48,112},{64,0},{80,16},{96,32},{112,48},{1... | collective-permute-start | bytes 245768 | tf_op jit(solution)/shard_map/ppermute | solution.py:66
  117.6 1.7 collective-permute-done.32.refs_6_
  124.7 2.5 %collective-permute-start.31 = (bf16[2,208,512]{2,1,0:T(8,128)(2,1)S(1)}, bf16[2,208,512]{2,1,0:T(8,128)(2,1)S(1)}, u32[]{:S(2)}, u32[]{:S(2)}) collective-permute-start(bf16[2,208,512]{2,1,0:T(8,128)(2,1)S(1)} %slice.61), channel_id=1, source_target_pairs={{0,12},{1,13},{2,14},{3,15},{4,0},{5,1},{6,2},{7,3},{8,4},{9,5},{1... | collective-permute-start | bytes 1277960 | tf_op jit(solution)/shard_map/ppermute | solution.py:100
  128.6 8.4 %shard_map.96 = bf16[8,16,56,128]{3,2,1,0:T(8,128)(2,1)S(1)} custom-call(s32[4]{0:T(128)S(1)} %pad_add_fusion.where, bf16[16,64,1024]{2,1,0:T(8,128)(2,1)S(1)} %bitcast.39, bf16[16,64,1024]{2,1,0:T(8,128)(2,1)} %collective-permute-done.other_ref, bf16[320,1024]{1,0:T(8,128)(2,1)S(1)} %copy-done.31, bf16[768,1024]{1,0:T(8,128)(2,1)S(1)} %copy-done.29, ...), custom_call_target="tpu_custom_call" | custom-call | flops 4563402752 | bytes 9437184 | tf_op jit(solution)/shard_map/pallas_call | solution.py:344
  142.3 20.9 %all-to-all-start = ((bf16[128,56,128]{2,1,0:T(8,128)(2,1)}), bf16[128,56,128]{2,1,0:T(8,128)(2,1)S(1)}, u32[]{:S(2)}, u32[]{:S(2)}) async-start(bf16[128,56,128]{2,1,0:T(8,128)(2,1)} %bitcast.34), calls=%async_computation | async-start | bytes 3670016 | tf_op jit(solution)/shard_map/all_to_all | solution.py:631
  167.1 20.5 %shard_map.98 = (f32[512,512]{1,0:T(8,128)}, f32[512,512]{1,0:T(8,128)S(1)}) custom-call(f32[1280,128]{1,0:T(8,128)S(1)} %pad_maximum_fusion.2.gram_ref), custom_call_target="tpu_custom_call" | custom-call | flops 2684354560 | bytes 4194304 | tf_op jit(solution)/shard_map/pallas_call | solution.py:443
  196.5 2.9 %shard_map.99 = f32[128,512]{1,0:T(8,128)S(1)} custom-call(s32[4]{0:T(128)S(1)} %pad_add_fusion.where, bf16[4,208,512]{2,1,0:T(8,128)(2,1)S(1)} %pad_maximum_fusion.refs_0_, bf16[4,208,512]{2,1,0:T(8,128)(2,1)} %collective-permute-done.28.refs_1_, bf16[2,208,512]{2,1,0:T(8,128)(2,1)S(1)} %copy-done.15, bf16[2,208,512]{2,1,0:T(8,128)(2,1)S(1)} %copy-done.13, ...), custom_call_target="tpu_custom_call" | custom-call | flops 838860800 | bytes 9437184 | tf_op jit(solution)/shard_map/pallas_call | solution.py:486
  202.2 4.4 %collective-permute-done.41 = f32[64,512]{1,0:T(8,128)S(1)} collective-permute-done((f32[64,512]{1,0:T(8,128)S(1)}, f32[64,512]{1,0:T(8,128)S(1)}, u32[]{:S(2)}, u32[]{:S(2)}) %collective-permute-start.41) | collective-permute-done | bytes 131104 | tf_op jit(solution)/shard_map/ppermute | solution.py:111
  207.5 4.2 %collective-permute-done.42 = f32[64,512]{1,0:T(8,128)S(1)} collective-permute-done((f32[64,512]{1,0:T(8,128)S(1)}, f32[64,512]{1,0:T(8,128)S(1)}, u32[]{:S(2)}, u32[]{:S(2)}) %collective-permute-start.42) | collective-permute-done | bytes 131104 | tf_op jit(solution)/shard_map/ppermute | solution.py:111
  211.8 2.7 %collective-permute-start.43 = (f32[64,512]{1,0:T(8,128)S(1)}, f32[64,512]{1,0:T(8,128)S(1)}, u32[]{:S(2)}, u32[]{:S(2)}) collective-permute-start(f32[64,512]{1,0:T(8,128)S(1)} %add.134), channel_id=1, source_target_pairs={{0,16},{16,0},{32,48},{48,32},{64,80},{80,64},{96,112},{112,96},{1... | collective-permute-start | bytes 393224 | tf_op jit(solution)/shard_map/ppermute | solution.py:90
  215.5 13.7 %shard_map.100 = (f32[128,512]{1,0:T(8,128)}, f32[128,8192]{1,0:T(8,128)}) custom-call(s32[4]{0:T(128)S(1)} %pad_add_fusion.where, f32[128,512]{1,0:T(8,128)S(1)} %pad_maximum_fusion.5.cross_ref, f32[512,512]{1,0:T(8,128)S(1)} %copy-done.23, bf16[4,208,512]{2,1,0:T(8,128)(2,1)S(1)} %pad_maximum_fusion.refs_0_, ...), custom_call_target="tpu_custom_call" | custom-call | flops 1677721600 | bytes 14680064 | tf_op jit(solution)/shard_map/pallas_call | solution.py:549
  (185 shorter events, 62.1 us)
Async XLA Ops:
  7.2 51.3 %all-gather.3.cloned.1.call-start = ((), (), s32[]{:S(2)}) async-start(), calls=%async_computation.1 | async-start | bytes 2228224 | tf_op jit(solution)/shard_map/all_gather | solution.py:589
  9.6 7.9 %collective-permute-start.2 = (bf16[16,1024]{1,0:T(8,128)(2,1)S(1)}, bf16[16,1024]{1,0:T(8,128)(2,1)S(1)}, u32[]{:S(2)}, u32[]{:S(2)}) collective-permute-start(bf16[16,1024]{1,0:T(8,128)(2,1)S(1)} %constant_dynamic-slice_fusion.5), channel_id=1, source_target_pairs={{0,2},{1,3},{2,0},{3,1},{4,6},{5,7},{6,4},{7,5},{8,10},{9,11},{10,... | collective-permute-start | bytes 98312 | tf_op jit(solution)/shard_map/ppermute | solution.py:62
  18.0 5.5 %collective-permute-start.5 = (bf16[4,16,1024]{2,1,0:T(8,128)(2,1)S(1)}, bf16[4,16,1024]{2,1,0:T(8,128)(2,1)S(1)}, u32[]{:S(2)}, u32[]{:S(2)}) collective-permute-start(bf16[4,16,1024]{2,1,0:T(8,128)(2,1)S(1)} %get-tuple-element.115), channel_id=1, source_target_pairs={{0,8},{1,9},{2,10},{3,11},{4,12},{5,13},{6,14},{7,15},{8,0},{9,1},... | collective-permute-start | bytes 393224 | tf_op jit(solution)/shard_map/ppermute | solution.py:62
  20.8 6.4 %collective-permute-start.4 = (bf16[4,16,1024]{2,1,0:T(8,128)(2,1)S(1)}, bf16[4,16,1024]{2,1,0:T(8,128)(2,1)S(1)}, u32[]{:S(2)}, u32[]{:S(2)}) collective-permute-start(bf16[4,16,1024]{2,1,0:T(8,128)(2,1)S(1)} %get-tuple-element.115), channel_id=1, source_target_pairs={{0,4},{1,5},{2,6},{3,7},{4,8},{5,9},{6,10},{7,11},{8,12},{9,13},{1... | collective-permute-start | bytes 393224 | tf_op jit(solution)/shard_map/ppermute | solution.py:62
  21.2 6.6 %collective-permute-start.6 = (bf16[4,16,1024]{2,1,0:T(8,128)(2,1)S(1)}, bf16[4,16,1024]{2,1,0:T(8,128)(2,1)S(1)}, u32[]{:S(2)}, u32[]{:S(2)}) collective-permute-start(bf16[4,16,1024]{2,1,0:T(8,128)(2,1)S(1)} %get-tuple-element.115), channel_id=1, source_target_pairs={{0,12},{1,13},{2,14},{3,15},{4,0},{5,1},{6,2},{7,3},{8,4},{9,5},{1... | collective-permute-start | bytes 393224 | tf_op jit(solution)/shard_map/ppermute | solution.py:62
  27.9 5.9 %collective-permute-start.7 = (bf16[4,4,16,1024]{3,2,1,0:T(8,128)(2,1)S(1)}, bf16[4,4,16,1024]{3,2,1,0:T(8,128)(2,1)S(1)}, u32[]{:S(2)}, u32[]{:S(2)}) collective-permute-start(bf16[4,4,16,1024]{3,2,1,0:T(8,128)(2,1)S(1)} %pad_maximum_fusion.3.own), channel_id=1, source_target_pairs={{0,16},{16,0},{32,48},{48,32},{64,80},{80,64},{96,112},{112,96},{1... | collective-permute-start | bytes 1572872 | tf_op jit(solution)/shard_map/ppermute | solution.py:593
  38.9 21.3 %collective-permute-start.9 = (f32[640,128]{1,0:T(8,128)S(1)}, f32[640,128]{1,0:T(8,128)S(1)}, u32[]{:S(2)}, u32[]{:S(2)}) collective-permute-start(f32[640,128]{1,0:T(8,128)S(1)} %constant_dynamic-slice_fusion.4), channel_id=1, source_target_pairs={{0,16},{16,0},{32,48},{48,32},{64,80},{80,64},{96,112},{112,96},{1... | collective-permute-start | bytes 983048 | tf_op jit(solution)/shard_map/ppermute | solution.py:86
  58.5 36.8 %collective-permute-start = (bf16[16,64,1024]{2,1,0:T(8,128)(2,1)}, bf16[16,64,1024]{2,1,0:T(8,128)(2,1)}, u32[]{:S(2)}, u32[]{:S(2)}) collective-permute-start(bf16[16,64,1024]{2,1,0:T(8,128)(2,1)} %bitcast.38), channel_id=1, source_target_pairs={{0,16},{16,0},{32,48},{48,32},{64,80},{80,64},{96,112},{112,96},{1... | collective-permute-start | bytes 6291464 | tf_op jit(solution)/shard_map/ppermute | solution.py:616
  64.3 10.4 %collective-permute-start.10 = (bf16[2,56,512]{2,1,0:T(8,128)(2,1)S(1)}, bf16[2,56,512]{2,1,0:T(8,128)(2,1)S(1)}, u32[]{:S(2)}, u32[]{:S(2)}) collective-permute-start(bf16[2,56,512]{2,1,0:T(8,128)(2,1)S(1)} %pad_maximum_fusion.7), channel_id=1, source_target_pairs={{0,32},{16,48},{32,64},{48,80},{64,96},{80,112},{96,0},{112,16},{1... | collective-permute-start | bytes 344072 | tf_op jit(solution)/shard_map/ppermute | solution.py:609
  65.5 6.3 %collective-permute-start.13 = (f32[160,128]{1,0:T(8,128)S(1)}, f32[160,128]{1,0:T(8,128)S(1)}, u32[]{:S(2)}, u32[]{:S(2)}) collective-permute-start(f32[160,128]{1,0:T(8,128)S(1)} %get-tuple-element.103), channel_id=1, source_target_pairs={{0,32},{16,48},{32,64},{48,80},{64,96},{80,112},{96,0},{112,16},{1... | collective-permute-start | bytes 245768 | tf_op jit(solution)/shard_map/ppermute | solution.py:74
  66.8 6.6 %collective-permute-start.15 = (f32[160,128]{1,0:T(8,128)S(1)}, f32[160,128]{1,0:T(8,128)S(1)}, u32[]{:S(2)}, u32[]{:S(2)}) collective-permute-start(f32[160,128]{1,0:T(8,128)S(1)} %get-tuple-element.104), channel_id=1, source_target_pairs={{0,96},{16,112},{32,0},{48,16},{64,32},{80,48},{96,64},{112,80},{1... | collective-permute-start | bytes 245768 | tf_op jit(solution)/shard_map/ppermute | solution.py:74
  68.3 6.3 %collective-permute-start.14 = (f32[160,128]{1,0:T(8,128)S(1)}, f32[160,128]{1,0:T(8,128)S(1)}, u32[]{:S(2)}, u32[]{:S(2)}) collective-permute-start(f32[160,128]{1,0:T(8,128)S(1)} %get-tuple-element.105), channel_id=1, source_target_pairs={{0,64},{16,80},{32,96},{48,112},{64,0},{80,16},{96,32},{112,48},{1... | collective-permute-start | bytes 245768 | tf_op jit(solution)/shard_map/ppermute | solution.py:74
  71.9 5.1 %collective-permute-start.11 = (bf16[2,56,512]{2,1,0:T(8,128)(2,1)S(1)}, bf16[2,56,512]{2,1,0:T(8,128)(2,1)S(1)}, u32[]{:S(2)}, u32[]{:S(2)}) collective-permute-start(bf16[2,56,512]{2,1,0:T(8,128)(2,1)S(1)} %pad_maximum_fusion.8), channel_id=1, source_target_pairs={{0,64},{16,80},{32,96},{48,112},{64,0},{80,16},{96,32},{112,48},{1... | collective-permute-start | bytes 344072 | tf_op jit(solution)/shard_map/ppermute | solution.py:609
  78.5 5.3 %collective-permute-start.24 = (bf16[192,512]{1,0:T(8,128)(2,1)S(1)}, bf16[192,512]{1,0:T(8,128)(2,1)S(1)}, u32[]{:S(2)}, u32[]{:S(2)}) collective-permute-start(bf16[192,512]{1,0:T(8,128)(2,1)S(1)} %get-tuple-element.65), channel_id=1, source_target_pairs={{0,12},{1,13},{2,14},{3,15},{4,0},{5,1},{6,2},{7,3},{8,4},{9,5},{1... | collective-permute-start | bytes 589832 | tf_op jit(solution)/shard_map/ppermute | solution.py:98
  80.5 6.1 %collective-permute-start.22 = (bf16[192,512]{1,0:T(8,128)(2,1)S(1)}, bf16[192,512]{1,0:T(8,128)(2,1)S(1)}, u32[]{:S(2)}, u32[]{:S(2)}) collective-permute-start(bf16[192,512]{1,0:T(8,128)(2,1)S(1)} %get-tuple-element.65), channel_id=1, source_target_pairs={{0,4},{1,5},{2,6},{3,7},{4,8},{5,9},{6,10},{7,11},{8,12},{9,13},{1... | collective-permute-start | bytes 589832 | tf_op jit(solution)/shard_map/ppermute | solution.py:97
  80.9 9.6 %collective-permute-start.20 = (bf16[208,512]{1,0:T(8,128)(2,1)S(1)}, bf16[208,512]{1,0:T(8,128)(2,1)S(1)}, u32[]{:S(2)}, u32[]{:S(2)}) collective-permute-start(bf16[208,512]{1,0:T(8,128)(2,1)S(1)} %get-tuple-element.64), channel_id=1, source_target_pairs={{0,3},{1,0},{2,1},{3,2},{4,7},{5,4},{6,5},{7,6},{8,11},{9,8},{10,9... | collective-permute-start | bytes 638984 | tf_op jit(solution)/shard_map/ppermute | solution.py:98
  83.7 8.6 %collective-permute-start.18 = (bf16[208,512]{1,0:T(8,128)(2,1)S(1)}, bf16[208,512]{1,0:T(8,128)(2,1)S(1)}, u32[]{:S(2)}, u32[]{:S(2)}) collective-permute-start(bf16[208,512]{1,0:T(8,128)(2,1)S(1)} %get-tuple-element.64), channel_id=1, source_target_pairs={{0,1},{1,2},{2,3},{3,0},{4,5},{5,6},{6,7},{7,4},{8,9},{9,10},{10,1... | collective-permute-start | bytes 638984 | tf_op jit(solution)/shard_map/ppermute | solution.py:97
  83.8 6.8 %collective-permute-start.17 = (f32[160,128]{1,0:T(8,128)S(1)}, f32[160,128]{1,0:T(8,128)S(1)}, u32[]{:S(2)}, u32[]{:S(2)}) collective-permute-start(f32[160,128]{1,0:T(8,128)S(1)} %add.123), channel_id=1, source_target_pairs={{0,3},{1,2},{2,1},{3,0},{4,7},{5,6},{6,5},{7,4},{8,11},{9,10},{10,... | collective-permute-start | bytes 245768 | tf_op jit(solution)/shard_map/ppermute | solution.py:111
  86.5 6.0 %collective-permute-start.25 = (bf16[96,512]{1,0:T(8,128)(2,1)S(1)}, bf16[96,512]{1,0:T(8,128)(2,1)S(1)}, u32[]{:S(2)}, u32[]{:S(2)}) collective-permute-start(bf16[96,512]{1,0:T(8,128)(2,1)S(1)} %slice.59), channel_id=1, source_target_pairs={{0,12},{1,13},{2,14},{3,15},{4,0},{5,1},{6,2},{7,3},{8,4},{9,5},{1... | collective-permute-start | bytes 294920 | tf_op jit(solution)/shard_map/ppermute | solution.py:100
  104.3 10.8 %collective-permute-start.34 = (bf16[4,192,512]{2,1,0:T(8,128)(2,1)S(1)}, bf16[4,192,512]{2,1,0:T(8,128)(2,1)S(1)}, u32[]{:S(2)}, u32[]{:S(2)}) collective-permute-start(bf16[4,192,512]{2,1,0:T(8,128)(2,1)S(1)} %pad_maximum_fusion.1.refs_5_), channel_id=1, source_target_pairs={{0,3},{1,0},{2,1},{3,2},{4,7},{5,4},{6,5},{7,6},{8,11},{9,8},{10,9... | collective-permute-start | bytes 2359304 | tf_op jit(solution)/shard_map/ppermute | solution.py:98
  105.6 16.3 %collective-permute-start.30 = (bf16[4,208,512]{2,1,0:T(8,128)(2,1)S(1)}, bf16[4,208,512]{2,1,0:T(8,128)(2,1)S(1)}, u32[]{:S(2)}, u32[]{:S(2)}) collective-permute-start(bf16[4,208,512]{2,1,0:T(8,128)(2,1)S(1)} %pad_maximum_fusion.refs_0_), channel_id=1, source_target_pairs={{0,12},{1,13},{2,14},{3,15},{4,0},{5,1},{6,2},{7,3},{8,4},{9,5},{1... | collective-permute-start | bytes 2555912 | tf_op jit(solution)/shard_map/ppermute | solution.py:98
  107.2 14.9 %collective-permute-start.28 = (bf16[4,208,512]{2,1,0:T(8,128)(2,1)S(1)}, bf16[4,208,512]{2,1,0:T(8,128)(2,1)}, u32[]{:S(2)}, u32[]{:S(2)}) collective-permute-start(bf16[4,208,512]{2,1,0:T(8,128)(2,1)S(1)} %pad_maximum_fusion.refs_0_), channel_id=1, source_target_pairs={{0,4},{1,5},{2,6},{3,7},{4,8},{5,9},{6,10},{7,11},{8,12},{9,13},{1... | collective-permute-start | bytes 2555912 | tf_op jit(solution)/shard_map/ppermute | solution.py:97
  107.2 12.2 %collective-permute-start.32 = (bf16[4,192,512]{2,1,0:T(8,128)(2,1)S(1)}, bf16[4,192,512]{2,1,0:T(8,128)(2,1)}, u32[]{:S(2)}, u32[]{:S(2)}) collective-permute-start(bf16[4,192,512]{2,1,0:T(8,128)(2,1)S(1)} %pad_maximum_fusion.1.refs_5_), channel_id=1, source_target_pairs={{0,1},{1,2},{2,3},{3,0},{4,5},{5,6},{6,7},{7,4},{8,9},{9,10},{10,1... | collective-permute-start | bytes 2359304 | tf_op jit(solution)/shard_map/ppermute | solution.py:97
  107.2 17.5 %collective-permute-start.38 = (f32[160,128]{1,0:T(8,128)}, f32[160,128]{1,0:T(8,128)}, u32[]{:S(2)}, u32[]{:S(2)}) collective-permute-start(f32[160,128]{1,0:T(8,128)} %add.126), channel_id=1, source_target_pairs={{0,96},{16,112},{32,0},{48,16},{64,32},{80,48},{96,64},{112,80},{1... | collective-permute-start | bytes 245768 | tf_op jit(solution)/shard_map/ppermute | solution.py:66
  115.1 12.0 %collective-permute-start.37 = (f32[160,128]{1,0:T(8,128)}, f32[160,128]{1,0:T(8,128)}, u32[]{:S(2)}, u32[]{:S(2)}) collective-permute-start(f32[160,128]{1,0:T(8,128)} %add.126), channel_id=1, source_target_pairs={{0,64},{16,80},{32,96},{48,112},{64,0},{80,16},{96,32},{112,48},{1... | collective-permute-start | bytes 245768 | tf_op jit(solution)/shard_map/ppermute | solution.py:66
  119.3 18.9 %collective-permute-start.36 = (f32[160,128]{1,0:T(8,128)}, f32[160,128]{1,0:T(8,128)S(1)}, u32[]{:S(2)}, u32[]{:S(2)}) collective-permute-start(f32[160,128]{1,0:T(8,128)} %add.126), channel_id=1, source_target_pairs={{0,32},{16,48},{32,64},{48,80},{64,96},{80,112},{96,0},{112,16},{1... | collective-permute-start | bytes 245768 | tf_op jit(solution)/shard_map/ppermute | solution.py:66
  122.0 17.3 %collective-permute-start.35 = (bf16[2,192,512]{2,1,0:T(8,128)(2,1)S(1)}, bf16[2,192,512]{2,1,0:T(8,128)(2,1)S(1)}, u32[]{:S(2)}, u32[]{:S(2)}) collective-permute-start(bf16[2,192,512]{2,1,0:T(8,128)(2,1)S(1)} %slice.63), channel_id=1, source_target_pairs={{0,3},{1,0},{2,1},{3,2},{4,7},{5,4},{6,5},{7,6},{8,11},{9,8},{10,9... | collective-permute-start | bytes 1179656 | tf_op jit(solution)/shard_map/ppermute | solution.py:100
  122.1 17.9 %collective-permute-start.33 = (bf16[2,192,512]{2,1,0:T(8,128)(2,1)S(1)}, bf16[2,192,512]{2,1,0:T(8,128)(2,1)S(1)}, u32[]{:S(2)}, u32[]{:S(2)}) collective-permute-start(bf16[2,192,512]{2,1,0:T(8,128)(2,1)S(1)} %slice.62), channel_id=1, source_target_pairs={{0,1},{1,2},{2,3},{3,0},{4,5},{5,6},{6,7},{7,4},{8,9},{9,10},{10,1... | collective-permute-start | bytes 1179656 | tf_op jit(solution)/shard_map/ppermute | solution.py:99
  124.7 16.1 %collective-permute-start.31 = (bf16[2,208,512]{2,1,0:T(8,128)(2,1)S(1)}, bf16[2,208,512]{2,1,0:T(8,128)(2,1)S(1)}, u32[]{:S(2)}, u32[]{:S(2)}) collective-permute-start(bf16[2,208,512]{2,1,0:T(8,128)(2,1)S(1)} %slice.61), channel_id=1, source_target_pairs={{0,12},{1,13},{2,14},{3,15},{4,0},{5,1},{6,2},{7,3},{8,4},{9,5},{1... | collective-permute-start | bytes 1277960 | tf_op jit(solution)/shard_map/ppermute | solution.py:100
  127.1 14.4 %collective-permute-start.29 = (bf16[2,208,512]{2,1,0:T(8,128)(2,1)S(1)}, bf16[2,208,512]{2,1,0:T(8,128)(2,1)S(1)}, u32[]{:S(2)}, u32[]{:S(2)}) collective-permute-start(bf16[2,208,512]{2,1,0:T(8,128)(2,1)S(1)} %slice.60), channel_id=1, source_target_pairs={{0,4},{1,5},{2,6},{3,7},{4,8},{5,9},{6,10},{7,11},{8,12},{9,13},{1... | collective-permute-start | bytes 1277960 | tf_op jit(solution)/shard_map/ppermute | solution.py:99
  142.3 47.7 %all-to-all-start = ((bf16[128,56,128]{2,1,0:T(8,128)(2,1)}), bf16[128,56,128]{2,1,0:T(8,128)(2,1)S(1)}, u32[]{:S(2)}, u32[]{:S(2)}) async-start(bf16[128,56,128]{2,1,0:T(8,128)(2,1)} %bitcast.34), calls=%async_computation | async-start | bytes 3670016 | tf_op jit(solution)/shard_map/all_to_all | solution.py:631
  206.6 5.1 %collective-permute-start.42 = (f32[64,512]{1,0:T(8,128)S(1)}, f32[64,512]{1,0:T(8,128)S(1)}, u32[]{:S(2)}, u32[]{:S(2)}) collective-permute-start(f32[64,512]{1,0:T(8,128)S(1)} %add.133), channel_id=1, source_target_pairs={{0,96},{16,112},{32,64},{48,80},{64,32},{80,48},{96,0},{112,16},{1... | collective-permute-start | bytes 393224 | tf_op jit(solution)/shard_map/ppermute | solution.py:111
  (51 other events, 396.4 us)
Sparse Core Ops, SparseCore 0:
  10.8 47.6 all-gather.2

commit v10 on v7

--- a/solution.py
+++ b/solution.py
@@ -385,11 +385,21 @@
     def step(b, carry):
         at = pl.multiple_of(b * 128, 128)
         low = eliminate(work[pl.ds(at, 128), pl.ds(at, 128)])
-        row = dot(low, work[pl.ds(at, 128), :], NN, HIGHEST)
-        lane = lax.broadcasted_iota(jnp.int32, (128, n), 1)
-        later = jnp.where(lane >= at + 128, row[:, :n], 0.0)
-        work[...] = work[...] - dot(later, row, TN, HIGHEST)
-        work[pl.ds(at, 128), :] = row
+        for k in range(n // 128):
+
+            @pl.when(b == k)
+            def _(k=k):
+                here, after = slice(128 * k, 128 * k + 128), slice(128 * k + 128, n)
+                left, right = slice(128 * k, n), slice(n, n + 128 * k + 128)
+                row = dot(low, work[here, left], NN, HIGHEST)
+                solved = dot(low, work[here, right], NN, HIGHEST)
+                work[here, left] = row
+                work[here, right] = solved
+                if k < n // 128 - 1:
+                    later = row[:, 128:]
+                    work[after, after] -= dot(later, later, TN, HIGHEST)
+                    work[after, right] -= dot(later, solved, TN, HIGHEST)
+
         return carry
 
     lax.fori_loop(0, n // 128, step, 0)
@@ -440,8 +450,26 @@
     )(segment, trail)
 
 
+def spread_pair(rest, k, lane):
+    full = jnp.zeros((128, 128), F32)
+    for m in (0, 1):
+        struct, at = 2 * k + m, 64 * m
+        start = 48 * struct
+        turn = (at + 1 - start) % 128
+        part = start // 128
+        split = at + 1 + min(48, 128 * (part + 1) - start)
+        force = pltpu.roll(rest[:, 128 * part : 128 * part + 128], turn, 1)
+        full = jnp.where((lane > at) & (lane < split), force, full)
+        if split < at + 49:
+            force = pltpu.roll(rest[:, 128 * part + 128 : 128 * part + 256], turn, 1)
+            full = jnp.where((lane >= split) & (lane < at + 49), force, full)
+        energy = jnp.broadcast_to(rest[:, 384 + struct : 385 + struct], (128, 128))
+        full = jnp.where(lane == at, energy, full)
+    return full
+
+
 def residual_kernel(
-    rows_total, cross_ref, inverse_ref, panel_ref, trail_ref, coupling_ref, out_ref, weights, spread
+    rows_total, cross_ref, inverse_ref, panel_ref, trail_ref, coupling_ref, out_ref, weights
 ):
     @pl.when(pl.program_id(0) == 0)
     def _():
@@ -451,12 +479,6 @@
         high = solved.astype(BF16)
         weights[:128] = high
         weights[128:] = (solved - high.astype(F32)).astype(BF16)
-        held = lax.broadcasted_iota(jnp.int32, (HELD, 512), 0)
-        column = lax.broadcasted_iota(jnp.int32, (HELD, 512), 1)
-        struct, place = column >> 6, column & 63
-        wanted = jnp.where(place <= 48, struct * 48 + place - 1, -1)
-        wanted = jnp.where(place == 0, 384 + struct, wanted)
-        spread[...] = (held == wanted).astype(F32).astype(BF16)
 
     r = lax.broadcasted_iota(jnp.int32, (128, 128), 0)
     c = lax.broadcasted_iota(jnp.int32, (128, 128), 1)
@@ -465,10 +487,9 @@
         both = dot(weights[...], panel_ref[i], NT)
         own = dot(same, trail_chunk(trail_ref, i), NT)
         rest = own - both[:128] - both[128:]
-        high = rest.astype(BF16)
-        low = (rest - high.astype(F32)).astype(BF16)
-        full = dot(jnp.concatenate([high, low], axis=0), spread[...], NN)
-        out_ref[:, i * 512 : i * 512 + 512] = full[:128] + full[128:]
+        for k in range(4):
+            at = i * 512 + k * 128
+            out_ref[:, at : at + 128] = spread_pair(rest, k, c)
 
 
 def residual(cross, inverse, segment, trail, rows_total):
@@ -489,7 +510,7 @@
             pl.BlockSpec((8, 4, SENT, 128), lambda i: (0, i, 0, 0)),
         ],
         out_specs=(whole((128, n)), pl.BlockSpec((128, 2048), lambda i: (0, i))),
-        scratch_shapes=[pltpu.VMEM((256, n), BF16), pltpu.VMEM((HELD, 512), BF16)],
+        scratch_shapes=[pltpu.VMEM((256, n), BF16)],
         compiler_params=params(),
         cost_estimate=pl.CostEstimate(
             flops=4 * 128 * n * 8192, bytes_accessed=16 << 20, transcendentals=0
@@ -542,10 +563,9 @@
     segment = lax.all_gather(panel, "col", axis=0, tiled=False)
     trail_other = lax.ppermute(trail_own, "row", CORE_SWAP)
     gram = sum4(gram, "col", z_pair)
+    gram = sum4(gram, "col", x_pair)
     trail_other, gram = lax.optimization_barrier((trail_other, gram))
-    gram = sum4(gram, "col", x_pair)
     trail = trail_rows(where, trail_own, trail_other, atoms, grads, mean, order)
-    trail, gram = lax.optimization_barrier((trail, gram))
     gram = gather4(gram, "row", y_shift, y)
     trail, gram = lax.optimization_barrier((trail, gram))
     gram = jnp.concatenate(swap_gather(gram, core), axis=0)

time: 186 us -> 186 us (level)
  Pallas kernels: 52.5 us -> 45.1 us
  other arithmetic: 0.56 us -> 3.65 us
  waiting for transfers between devices: 55 us -> 57.1 us
    pallas_call x1, Pallas kernels: 26.7 us -> 20.5 us  [factor_panel(): pl.pallas_call(functools.partial(factor_kernel, float(rows_total)), out_s...]
    ppermute x3, waiting for transfers between devices: 3.9 us -> 0.01 us  [gather4(): pieces = [v] + [lax.ppermute(v, axis, shift(s)) for s in (1, 2, 3)]]
    ppermute x6, waiting for transfers between devices: 16.6 us -> 20.4 us  [sum4(): v = v + lax.ppermute(v, axis, pairs(flip))]
    add x6, other arithmetic: 0.08 us -> 2.53 us  [sum4(): v = v + lax.ppermute(v, axis, pairs(flip))]
    unnamed x27 -> x25, local copies, waits for them, and re-layouts: 9.19 us -> 11.3 us
    all_gather x1, waiting for transfers between devices: 10.8 us -> 12.8 us  [per_device(): segment = lax.all_gather(panel, 'col', axis=0, tiled=False)]
  transfers between devices with their start and end apart: 31 -> 31, of which waited for: 22 -> 21; matrix products, arithmetic and copies ran while one was open for 2% -> 3% of each run, Pallas kernels for 22% -> 18%
where the time goes in v10:
time: 186 us; the launch traced here: 185 us
  waiting for transfers between devices  57.1 us (31%)
  starting transfers between devices  51.4 us (28%)
  Pallas kernels  45.1 us (24%)
  between operations  14.4 us (8%)
  local copies, waits for them, and re-layouts  13.6 us (7%)
  other arithmetic  3.65 us (2%)
    pallas_call x1, Pallas kernels, factor_panel(): pl.pallas_call(functools.partial(factor_kernel, float(rows_total)), out_s...  20.5 us
    ppermute x6, waiting for transfers between devices, sum4(): v = v + lax.ppermute(v, axis, pairs(flip))  20.4 us
    all_gather x1, waiting for transfers between devices, per_device(): segment = lax.all_gather(panel, 'col', axis=0, tiled=False)  12.8 us
    all_to_all x1, starting transfers between devices, per_device(): lax.all_to_all(trail.reshape(128, SENT, 128), ('row', 'col'), 0, 0, tiled...  11.3 us
    unnamed x25, local copies, waits for them, and re-layouts  11.3 us
    pallas_call x1, Pallas kernels, residual(): pl.pallas_call(functools.partial(residual_kernel, float(rows_total)), out...  10.2 us
    ppermute x6, starting transfers between devices, shifted(): return [v] + [lax.ppermute(v, axis, shift(s)) for s in (1, 2, 3)]  8.96 us
    ppermute x6, waiting for transfers between devices, shifted(): return [v] + [lax.ppermute(v, axis, shift(s)) for s in (1, 2, 3)]  8.87 us
  transfers between devices with their start and end apart: 31, of which 21 were waited for; matrix products, arithmetic and copies ran while one was open for 3% of the time, Pallas kernels for 18%

profile of v10, /device:TPU:1, one launch (start us, length us, event | category | flops | bytes accessed | tf_op | source)
XLA Modules:
  0.0 185.3 jit_solution(9663874787975081664)
XLA Ops:
  9.6 4.6 %collective-permute-start.3 = (bf16[16,1024]{1,0:T(8,128)(2,1)S(1)}, bf16[16,1024]{1,0:T(8,128)(2,1)S(1)}, u32[]{:S(2)}, u32[]{:S(2)}) collective-permute-start(bf16[16,1024]{1,0:T(8,128)(2,1)S(1)} %constant_dynamic-slice_fusion.5), channel_id=1, source_target_pairs={{0,3},{1,0},{2,1},{3,2},{4,7},{5,4},{6,5},{7,6},{8,11},{9,8},{10,9... | collective-permute-start | bytes 98312 | tf_op jit(solution)/shard_map/ppermute | solution.py:61
  15.7 2.9 %collective-permute-done.2 = bf16[16,1024]{1,0:T(8,128)(2,1)S(1)} collective-permute-done((bf16[16,1024]{1,0:T(8,128)(2,1)S(1)}, bf16[16,1024]{1,0:T(8,128)(2,1)S(1)}, u32[]{:S(2)}, u32[]{:S(2)}) %collective-permute-start.2) | collective-permute-done | bytes 32800 | tf_op jit(solution)/shard_map/ppermute | solution.py:61
  18.6 2.5 %collective-permute-start.6 = (bf16[4,16,1024]{2,1,0:T(8,128)(2,1)S(1)}, bf16[4,16,1024]{2,1,0:T(8,128)(2,1)S(1)}, u32[]{:S(2)}, u32[]{:S(2)}) collective-permute-start(bf16[4,16,1024]{2,1,0:T(8,128)(2,1)S(1)} %get-tuple-element.67), channel_id=1, source_target_pairs={{0,12},{1,13},{2,14},{3,15},{4,0},{5,1},{6,2},{7,3},{8,4},{9,5},{1... | collective-permute-start | bytes 393224 | tf_op jit(solution)/shard_map/ppermute | solution.py:61
  23.8 2.8 %collective-permute-done.5 = bf16[4,16,1024]{2,1,0:T(8,128)(2,1)S(1)} collective-permute-done((bf16[4,16,1024]{2,1,0:T(8,128)(2,1)S(1)}, bf16[4,16,1024]{2,1,0:T(8,128)(2,1)S(1)}, u32[]{:S(2)}, u32[]{:S(2)}) %collective-permute-start.5) | collective-permute-done | bytes 131104 | tf_op jit(solution)/shard_map/ppermute | solution.py:61
  26.6 1.7 collective-permute-done.4
  28.3 4.1 %collective-permute-start.7 = (bf16[4,4,16,1024]{3,2,1,0:T(8,128)(2,1)S(1)}, bf16[4,4,16,1024]{3,2,1,0:T(8,128)(2,1)S(1)}, u32[]{:S(2)}, u32[]{:S(2)}) collective-permute-start(bf16[4,4,16,1024]{3,2,1,0:T(8,128)(2,1)S(1)} %pad_maximum_fusion.1.own), channel_id=1, source_target_pairs={{0,16},{16,0},{32,48},{48,32},{64,80},{80,64},{96,112},{112,96},{1... | collective-permute-start | bytes 1572872 | tf_op jit(solution)/shard_map/ppermute | solution.py:542
  33.3 1.9 %copy-done.3 = bf16[3,4,128,1024]{3,2,1,0:T(8,128)(2,1)S(1)} copy-done((bf16[3,4,128,1024]{3,2,1,0:T(8,128)(2,1)S(1)}, bf16[3,4,128,1024]{3,2,1,0:T(8,128)(2,1)}, u32[]{:S(2)}) %copy-start.3) | copy-done | bytes 3145752
  36.6 2.4 %shard_map.95 = (bf16[4,56,512]{2,1,0:T(8,128)(2,1)S(1)}, bf16[4,56,512]{2,1,0:T(8,128)(2,1)S(1)}, f32[1280,128]{1,0:T(8,128)S(1)}) custom-call(s32[4]{0:T(128)S(1)} %pad_add_fusion.where, bf16[4,4,16,1024]{3,2,1,0:T(8,128)(2,1)S(1)} %pad_maximum_fusion.1.own, bf16[4,4,16,1024]{3,2,1,0:T(8,128)(2,1)S(1)} %collective-permute-done.7.other, ...), custom_call_target="tpu_custom_call" | custom-call | flops 1140850688 | bytes 5242880 | tf_op jit(solution)/shard_map/pallas_call | solution.py:280
  43.4 2.7 %collective-permute-start.11 = (bf16[2,56,512]{2,1,0:T(8,128)(2,1)S(1)}, bf16[2,56,512]{2,1,0:T(8,128)(2,1)S(1)}, u32[]{:S(2)}, u32[]{:S(2)}) collective-permute-start(bf16[2,56,512]{2,1,0:T(8,128)(2,1)S(1)} %pad_maximum_fusion.6), channel_id=1, source_target_pairs={{0,64},{16,80},{32,96},{48,112},{64,0},{80,16},{96,32},{112,48},{1... | collective-permute-start | bytes 344072 | tf_op jit(solution)/shard_map/ppermute | solution.py:558
  47.9 2.3 %collective-permute-done.15 = f32[160,128]{1,0:T(8,128)S(1)} collective-permute-done((f32[160,128]{1,0:T(8,128)S(1)}, f32[160,128]{1,0:T(8,128)S(1)}, u32[]{:S(2)}, u32[]{:S(2)}) %collective-permute-start.15) | collective-permute-done | bytes 81952 | tf_op jit(solution)/shard_map/ppermute | solution.py:73
  50.2 2.6 %collective-permute-start.12 = (bf16[2,56,512]{2,1,0:T(8,128)(2,1)S(1)}, bf16[2,56,512]{2,1,0:T(8,128)(2,1)S(1)}, u32[]{:S(2)}, u32[]{:S(2)}) collective-permute-start(bf16[2,56,512]{2,1,0:T(8,128)(2,1)S(1)} %pad_maximum_fusion.7), channel_id=1, source_target_pairs={{0,96},{16,112},{32,0},{48,16},{64,32},{80,48},{96,64},{112,80},{1... | collective-permute-start | bytes 344072 | tf_op jit(solution)/shard_map/ppermute | solution.py:558
  53.1 2.5 %collective-permute-done.13 = f32[160,128]{1,0:T(8,128)S(1)} collective-permute-done((f32[160,128]{1,0:T(8,128)S(1)}, f32[160,128]{1,0:T(8,128)S(1)}, u32[]{:S(2)}, u32[]{:S(2)}) %collective-permute-start.13) | collective-permute-done | bytes 81952 | tf_op jit(solution)/shard_map/ppermute | solution.py:73
  58.9 1.7 collective-permute-start
  61.6 3.4 %collective-permute-done.16 = f32[160,128]{1,0:T(8,128)S(1)} collective-permute-done((f32[160,128]{1,0:T(8,128)}, f32[160,128]{1,0:T(8,128)S(1)}, u32[]{:S(2)}, u32[]{:S(2)}) %collective-permute-start.16) | collective-permute-done | bytes 81952 | tf_op jit(solution)/shard_map/ppermute | solution.py:96
  65.9 2.2 %collective-permute-start.17 = (f32[160,128]{1,0:T(8,128)S(1)}, f32[160,128]{1,0:T(8,128)S(1)}, u32[]{:S(2)}, u32[]{:S(2)}) collective-permute-start(f32[160,128]{1,0:T(8,128)S(1)} %add.123), channel_id=1, source_target_pairs={{0,3},{1,2},{2,1},{3,0},{4,7},{5,6},{6,5},{7,4},{8,11},{9,10},{10,... | collective-permute-start | bytes 245768 | tf_op jit(solution)/shard_map/ppermute | solution.py:96
  68.0 2.4 %collective-permute-done.17 = f32[160,128]{1,0:T(8,128)S(1)} collective-permute-done((f32[160,128]{1,0:T(8,128)S(1)}, f32[160,128]{1,0:T(8,128)S(1)}, u32[]{:S(2)}, u32[]{:S(2)}) %collective-permute-start.17) | collective-permute-done | bytes 81952 | tf_op jit(solution)/shard_map/ppermute | solution.py:96
  71.2 2.6 %collective-permute-done.18 = f32[160,128]{1,0:T(8,128)S(1)} collective-permute-done((f32[160,128]{1,0:T(8,128)S(1)}, f32[160,128]{1,0:T(8,128)S(1)}, u32[]{:S(2)}, u32[]{:S(2)}) %collective-permute-start.18) | collective-permute-done | bytes 81952 | tf_op jit(solution)/shard_map/ppermute | solution.py:96
  74.5 1.9 %collective-permute-start.19 = (f32[160,128]{1,0:T(8,128)}, f32[160,128]{1,0:T(8,128)}, u32[]{:S(2)}, u32[]{:S(2)}) collective-permute-start(f32[160,128]{1,0:T(8,128)} %add.125), channel_id=1, source_target_pairs={{0,12},{1,13},{2,14},{3,15},{4,8},{5,9},{6,10},{7,11},{8,4},{9,5},... | collective-permute-start | bytes 245768 | tf_op jit(solution)/shard_map/ppermute | solution.py:96
  76.4 3.5 %collective-permute-done.19 = f32[160,128]{1,0:T(8,128)} collective-permute-done((f32[160,128]{1,0:T(8,128)}, f32[160,128]{1,0:T(8,128)}, u32[]{:S(2)}, u32[]{:S(2)}) %collective-permute-start.19) | collective-permute-done | bytes 81952 | tf_op jit(solution)/shard_map/ppermute | solution.py:96
  80.8 2.8 %collective-permute-start.21 = (f32[160,128]{1,0:T(8,128)S(1)}, f32[160,128]{1,0:T(8,128)S(1)}, u32[]{:S(2)}, u32[]{:S(2)}) collective-permute-start(f32[160,128]{1,0:T(8,128)S(1)} %add.126), channel_id=1, source_target_pairs={{0,64},{16,80},{32,96},{48,112},{64,0},{80,16},{96,32},{112,48},{1... | collective-permute-start | bytes 245768 | tf_op jit(solution)/shard_map/ppermute | solution.py:65
  85.1 1.6 copy-done.8
  88.1 7.3 %shard_map.96 = bf16[8,16,56,128]{3,2,1,0:T(8,128)(2,1)S(1)} custom-call(s32[4]{0:T(128)S(1)} %pad_add_fusion.where, bf16[16,64,1024]{2,1,0:T(8,128)(2,1)S(1)} %bitcast.30, bf16[16,64,1024]{2,1,0:T(8,128)(2,1)S(1)} %collective-permute-done.other_ref, bf16[320,1024]{1,0:T(8,128)(2,1)S(1)} %get-tuple-element.26.atoms_ref, bf16[768,1024]{1,0:T(8,128)(2,1)S(1)} %copy-done.10, ...), custom_call_target="tpu_custom_call" | custom-call | flops 4563402752 | bytes 9437184 | tf_op jit(solution)/shard_map/pallas_call | solution.py:313
  96.8 11.3 %all-to-all-start = ((bf16[128,56,128]{2,1,0:T(8,128)(2,1)}), bf16[128,56,128]{2,1,0:T(8,128)(2,1)S(1)}, u32[]{:S(2)}, u32[]{:S(2)}) async-start(bf16[128,56,128]{2,1,0:T(8,128)(2,1)} %bitcast.27), calls=%async_computation | async-start | bytes 3670016 | tf_op jit(solution)/shard_map/all_to_all | solution.py:572
  110.5 20.5 %shard_map.97 = (f32[512,512]{1,0:T(8,128)}, f32[512,512]{1,0:T(8,128)S(1)}) custom-call(f32[1280,128]{1,0:T(8,128)S(1)} %pad_maximum_fusion.gram_ref), custom_call_target="tpu_custom_call" | custom-call | flops 2684354560 | bytes 4194304 | tf_op jit(solution)/shard_map/pallas_call | solution.py:412
  131.0 12.8 %all-gather.7.cloned.1.call-done = bf16[6400,512]{1,0:T(8,128)(2,1)} async-done(((bf16[400,512]{1,0:T(8,128)(2,1)}), bf16[6400,512]{1,0:T(8,128)(2,1)}) %all-gather.7.cloned.1.call-update) | async-done | bytes 6553616 | tf_op jit(solution)/shard_map/all_gather | solution.py:563
  143.8 3.9 %all-to-all-done = bf16[128,56,128]{2,1,0:T(8,128)(2,1)S(1)} async-done(((bf16[128,56,128]{2,1,0:T(8,128)(2,1)}), bf16[128,56,128]{2,1,0:T(8,128)(2,1)S(1)}, u32[]{:S(2)}, u32[]{:S(2)}) %all-to-all-start) | async-done | bytes 1835040 | tf_op jit(solution)/shard_map/all_to_all | solution.py:572
  147.7 2.9 %copy-done.1 = bf16[6400,512]{1,0:T(8,128)(2,1)S(1)} copy-done((bf16[6400,512]{1,0:T(8,128)(2,1)S(1)}, bf16[6400,512]{1,0:T(8,128)(2,1)}, u32[]{:S(2)}) %copy-start.1) | copy-done | bytes 6553624
  150.6 1.9 %shard_map.99 = f32[128,512]{1,0:T(8,128)S(1)} custom-call(bf16[16,400,512]{2,1,0:T(8,128)(2,1)S(1)} %bitcast.22, bf16[8,16,56,128]{3,2,1,0:T(8,128)(2,1)S(1)} %bitcast.24), custom_call_target="tpu_custom_call" | custom-call | flops 1073741824 | bytes 11534336 | tf_op jit(solution)/shard_map/pallas_call | solution.py:437
  155.0 4.4 %collective-permute-done.25 = f32[64,512]{1,0:T(8,128)S(1)} collective-permute-done((f32[64,512]{1,0:T(8,128)S(1)}, f32[64,512]{1,0:T(8,128)S(1)}, u32[]{:S(2)}, u32[]{:S(2)}) %collective-permute-start.25) | collective-permute-done | bytes 131104 | tf_op jit(solution)/shard_map/ppermute | solution.py:96
  160.5 4.0 %collective-permute-done.26 = f32[64,512]{1,0:T(8,128)S(1)} collective-permute-done((f32[64,512]{1,0:T(8,128)S(1)}, f32[64,512]{1,0:T(8,128)S(1)}, u32[]{:S(2)}, u32[]{:S(2)}) %collective-permute-start.26) | collective-permute-done | bytes 131104 | tf_op jit(solution)/shard_map/ppermute | solution.py:96
  164.6 2.6 %collective-permute-start.27 = (f32[64,512]{1,0:T(8,128)S(1)}, f32[64,512]{1,0:T(8,128)S(1)}, u32[]{:S(2)}, u32[]{:S(2)}) collective-permute-start(f32[64,512]{1,0:T(8,128)S(1)} %add.134), channel_id=1, source_target_pairs={{0,16},{16,0},{32,48},{48,32},{64,80},{80,64},{96,112},{112,96},{1... | collective-permute-start | bytes 393224 | tf_op jit(solution)/shard_map/ppermute | solution.py:89
  168.3 10.2 %shard_map.100 = (f32[128,512]{1,0:T(8,128)}, f32[128,8192]{1,0:T(8,128)}) custom-call(f32[128,512]{1,0:T(8,128)S(1)} %pad_maximum_fusion.3.cross_ref, f32[512,512]{1,0:T(8,128)S(1)} %get-tuple-element.46.inverse_ref, bf16[16,400,512]{2,1,0:T(8,128)(2,1)S(1)} %bitcast.23, bf16[8,16,56,128]{3,2,1,0:T(8,128)(2,1)S(1)} %bitcast.25), custom_call_target="tpu_custom_call" | custom-call | flops 2147483648 | bytes 16777216 | tf_op jit(solution)/shard_map/pallas_call | solution.py:499
  (94 shorter events, 34.0 us)
Async XLA Ops:
  7.2 26.1 %copy-start.6 = (s32[1,8]{1,0:T(1,128)S(1)}, s32[1,8]{1,0:T(1,128)}, u32[]{:S(2)}) copy-start(s32[1,8]{1,0:T(1,128)} %count_ref.1) | copy-start | bytes 100
  7.2 51.7 %all-gather.5.cloned.1.call-start = ((), (), s32[]{:S(2)}) async-start(), calls=%async_computation.1 | async-start | bytes 2228224 | tf_op jit(solution)/shard_map/all_gather | solution.py:538
  8.8 135.0 %all-gather.7.cloned.1.call-start = ((), (), s32[]{:S(2)}) async-start(), calls=%async_computation.2 | async-start | bytes 6963200 | tf_op jit(solution)/shard_map/all_gather | solution.py:563
  9.6 6.1 %collective-permute-start.3 = (bf16[16,1024]{1,0:T(8,128)(2,1)S(1)}, bf16[16,1024]{1,0:T(8,128)(2,1)S(1)}, u32[]{:S(2)}, u32[]{:S(2)}) collective-permute-start(bf16[16,1024]{1,0:T(8,128)(2,1)S(1)} %constant_dynamic-slice_fusion.5), channel_id=1, source_target_pairs={{0,3},{1,0},{2,1},{3,2},{4,7},{5,4},{6,5},{7,6},{8,11},{9,8},{10,9... | collective-permute-start | bytes 98312 | tf_op jit(solution)/shard_map/ppermute | solution.py:61
  14.2 4.3 %collective-permute-start.2 = (bf16[16,1024]{1,0:T(8,128)(2,1)S(1)}, bf16[16,1024]{1,0:T(8,128)(2,1)S(1)}, u32[]{:S(2)}, u32[]{:S(2)}) collective-permute-start(bf16[16,1024]{1,0:T(8,128)(2,1)S(1)} %constant_dynamic-slice_fusion.5), channel_id=1, source_target_pairs={{0,2},{1,3},{2,0},{3,1},{4,6},{5,7},{6,4},{7,5},{8,10},{9,11},{10,... | collective-permute-start | bytes 98312 | tf_op jit(solution)/shard_map/ppermute | solution.py:61
  14.2 4.3 %collective-permute-start.1 = (bf16[16,1024]{1,0:T(8,128)(2,1)S(1)}, bf16[16,1024]{1,0:T(8,128)(2,1)S(1)}, u32[]{:S(2)}, u32[]{:S(2)}) collective-permute-start(bf16[16,1024]{1,0:T(8,128)(2,1)S(1)} %constant_dynamic-slice_fusion.5), channel_id=1, source_target_pairs={{0,1},{1,2},{2,3},{3,0},{4,5},{5,6},{6,7},{7,4},{8,9},{9,10},{10,1... | collective-permute-start | bytes 98312 | tf_op jit(solution)/shard_map/ppermute | solution.py:61
  18.6 5.2 %collective-permute-start.6 = (bf16[4,16,1024]{2,1,0:T(8,128)(2,1)S(1)}, bf16[4,16,1024]{2,1,0:T(8,128)(2,1)S(1)}, u32[]{:S(2)}, u32[]{:S(2)}) collective-permute-start(bf16[4,16,1024]{2,1,0:T(8,128)(2,1)S(1)} %get-tuple-element.67), channel_id=1, source_target_pairs={{0,12},{1,13},{2,14},{3,15},{4,0},{5,1},{6,2},{7,3},{8,4},{9,5},{1... | collective-permute-start | bytes 393224 | tf_op jit(solution)/shard_map/ppermute | solution.py:61
  21.1 5.4 %collective-permute-start.5 = (bf16[4,16,1024]{2,1,0:T(8,128)(2,1)S(1)}, bf16[4,16,1024]{2,1,0:T(8,128)(2,1)S(1)}, u32[]{:S(2)}, u32[]{:S(2)}) collective-permute-start(bf16[4,16,1024]{2,1,0:T(8,128)(2,1)S(1)} %get-tuple-element.67), channel_id=1, source_target_pairs={{0,8},{1,9},{2,10},{3,11},{4,12},{5,13},{6,14},{7,15},{8,0},{9,1},... | collective-permute-start | bytes 393224 | tf_op jit(solution)/shard_map/ppermute | solution.py:61
  21.7 6.6 %collective-permute-start.4 = (bf16[4,16,1024]{2,1,0:T(8,128)(2,1)S(1)}, bf16[4,16,1024]{2,1,0:T(8,128)(2,1)S(1)}, u32[]{:S(2)}, u32[]{:S(2)}) collective-permute-start(bf16[4,16,1024]{2,1,0:T(8,128)(2,1)S(1)} %get-tuple-element.67), channel_id=1, source_target_pairs={{0,4},{1,5},{2,6},{3,7},{4,8},{5,9},{6,10},{7,11},{8,12},{9,13},{1... | collective-permute-start | bytes 393224 | tf_op jit(solution)/shard_map/ppermute | solution.py:61
  28.3 8.3 %collective-permute-start.7 = (bf16[4,4,16,1024]{3,2,1,0:T(8,128)(2,1)S(1)}, bf16[4,4,16,1024]{3,2,1,0:T(8,128)(2,1)S(1)}, u32[]{:S(2)}, u32[]{:S(2)}) collective-permute-start(bf16[4,4,16,1024]{3,2,1,0:T(8,128)(2,1)S(1)} %pad_maximum_fusion.1.own), channel_id=1, source_target_pairs={{0,16},{16,0},{32,48},{48,32},{64,80},{80,64},{96,112},{112,96},{1... | collective-permute-start | bytes 1572872 | tf_op jit(solution)/shard_map/ppermute | solution.py:542
  39.7 1.7 collective-permute-start.9
  39.9 2.1 %collective-permute-start.8 = (bf16[4,56,512]{2,1,0:T(8,128)(2,1)}, bf16[4,56,512]{2,1,0:T(8,128)(2,1)S(1)}, u32[]{:S(2)}, u32[]{:S(2)}) collective-permute-start(bf16[4,56,512]{2,1,0:T(8,128)(2,1)} %copy-done.11), channel_id=1, source_target_pairs={{0,16},{16,0},{32,48},{48,32},{64,80},{80,64},{96,112},{112,96},{1... | collective-permute-start | bytes 688136 | tf_op jit(solution)/shard_map/ppermute | solution.py:554
  42.0 14.3 %collective-permute-start.10 = (bf16[2,56,512]{2,1,0:T(8,128)(2,1)S(1)}, bf16[2,56,512]{2,1,0:T(8,128)(2,1)S(1)}, u32[]{:S(2)}, u32[]{:S(2)}) collective-permute-start(bf16[2,56,512]{2,1,0:T(8,128)(2,1)S(1)} %pad_maximum_fusion.5), channel_id=1, source_target_pairs={{0,32},{16,48},{32,64},{48,80},{64,96},{80,112},{96,0},{112,16},{1... | collective-permute-start | bytes 344072 | tf_op jit(solution)/shard_map/ppermute | solution.py:558
  43.4 13.0 %collective-permute-start.11 = (bf16[2,56,512]{2,1,0:T(8,128)(2,1)S(1)}, bf16[2,56,512]{2,1,0:T(8,128)(2,1)S(1)}, u32[]{:S(2)}, u32[]{:S(2)}) collective-permute-start(bf16[2,56,512]{2,1,0:T(8,128)(2,1)S(1)} %pad_maximum_fusion.6), channel_id=1, source_target_pairs={{0,64},{16,80},{32,96},{48,112},{64,0},{80,16},{96,32},{112,48},{1... | collective-permute-start | bytes 344072 | tf_op jit(solution)/shard_map/ppermute | solution.py:558
  46.1 4.1 %collective-permute-start.15 = (f32[160,128]{1,0:T(8,128)S(1)}, f32[160,128]{1,0:T(8,128)S(1)}, u32[]{:S(2)}, u32[]{:S(2)}) collective-permute-start(f32[160,128]{1,0:T(8,128)S(1)} %get-tuple-element.56), channel_id=1, source_target_pairs={{0,96},{16,112},{32,0},{48,16},{64,32},{80,48},{96,64},{112,80},{1... | collective-permute-start | bytes 245768 | tf_op jit(solution)/shard_map/ppermute | solution.py:73
  47.3 5.9 %collective-permute-start.14 = (f32[160,128]{1,0:T(8,128)S(1)}, f32[160,128]{1,0:T(8,128)S(1)}, u32[]{:S(2)}, u32[]{:S(2)}) collective-permute-start(f32[160,128]{1,0:T(8,128)S(1)} %get-tuple-element.57), channel_id=1, source_target_pairs={{0,64},{16,80},{32,96},{48,112},{64,0},{80,16},{96,32},{112,48},{1... | collective-permute-start | bytes 245768 | tf_op jit(solution)/shard_map/ppermute | solution.py:73
  47.4 8.3 %collective-permute-start.13 = (f32[160,128]{1,0:T(8,128)S(1)}, f32[160,128]{1,0:T(8,128)S(1)}, u32[]{:S(2)}, u32[]{:S(2)}) collective-permute-start(f32[160,128]{1,0:T(8,128)S(1)} %get-tuple-element.55), channel_id=1, source_target_pairs={{0,32},{16,48},{32,64},{48,80},{64,96},{80,112},{96,0},{112,16},{1... | collective-permute-start | bytes 245768 | tf_op jit(solution)/shard_map/ppermute | solution.py:73
  50.2 6.2 %collective-permute-start.12 = (bf16[2,56,512]{2,1,0:T(8,128)(2,1)S(1)}, bf16[2,56,512]{2,1,0:T(8,128)(2,1)S(1)}, u32[]{:S(2)}, u32[]{:S(2)}) collective-permute-start(bf16[2,56,512]{2,1,0:T(8,128)(2,1)S(1)} %pad_maximum_fusion.7), channel_id=1, source_target_pairs={{0,96},{16,112},{32,0},{48,16},{64,32},{80,48},{96,64},{112,80},{1... | collective-permute-start | bytes 344072 | tf_op jit(solution)/shard_map/ppermute | solution.py:558
  58.9 21.9 %collective-permute-start = (bf16[16,64,1024]{2,1,0:T(8,128)(2,1)}, bf16[16,64,1024]{2,1,0:T(8,128)(2,1)S(1)}, u32[]{:S(2)}, u32[]{:S(2)}) collective-permute-start(bf16[16,64,1024]{2,1,0:T(8,128)(2,1)} %bitcast.29), channel_id=1, source_target_pairs={{0,16},{16,0},{32,48},{48,32},{64,80},{80,64},{96,112},{112,96},{1... | collective-permute-start | bytes 6291464 | tf_op jit(solution)/shard_map/ppermute | solution.py:564
  60.7 4.3 %collective-permute-start.16 = (f32[160,128]{1,0:T(8,128)}, f32[160,128]{1,0:T(8,128)S(1)}, u32[]{:S(2)}, u32[]{:S(2)}) collective-permute-start(f32[160,128]{1,0:T(8,128)} %add_add_fusion), channel_id=1, source_target_pairs={{0,1},{1,0},{2,3},{3,2},{4,5},{5,4},{6,7},{7,6},{8,9},{9,8},{10,11... | collective-permute-start | bytes 245768 | tf_op jit(solution)/shard_map/ppermute | solution.py:96
  65.9 4.6 %collective-permute-start.17 = (f32[160,128]{1,0:T(8,128)S(1)}, f32[160,128]{1,0:T(8,128)S(1)}, u32[]{:S(2)}, u32[]{:S(2)}) collective-permute-start(f32[160,128]{1,0:T(8,128)S(1)} %add.123), channel_id=1, source_target_pairs={{0,3},{1,2},{2,1},{3,0},{4,7},{5,6},{6,5},{7,4},{8,11},{9,10},{10,... | collective-permute-start | bytes 245768 | tf_op jit(solution)/shard_map/ppermute | solution.py:96
  70.5 3.4 %collective-permute-start.18 = (f32[160,128]{1,0:T(8,128)S(1)}, f32[160,128]{1,0:T(8,128)S(1)}, u32[]{:S(2)}, u32[]{:S(2)}) collective-permute-start(f32[160,128]{1,0:T(8,128)S(1)} %add.124), channel_id=1, source_target_pairs={{0,4},{1,5},{2,6},{3,7},{4,0},{5,1},{6,2},{7,3},{8,12},{9,13},{10,... | collective-permute-start | bytes 245768 | tf_op jit(solution)/shard_map/ppermute | solution.py:96
  74.5 5.4 %collective-permute-start.19 = (f32[160,128]{1,0:T(8,128)}, f32[160,128]{1,0:T(8,128)}, u32[]{:S(2)}, u32[]{:S(2)}) collective-permute-start(f32[160,128]{1,0:T(8,128)} %add.125), channel_id=1, source_target_pairs={{0,12},{1,13},{2,14},{3,15},{4,8},{5,9},{6,10},{7,11},{8,4},{9,5},... | collective-permute-start | bytes 245768 | tf_op jit(solution)/shard_map/ppermute | solution.py:96
  80.8 15.9 %collective-permute-start.21 = (f32[160,128]{1,0:T(8,128)S(1)}, f32[160,128]{1,0:T(8,128)S(1)}, u32[]{:S(2)}, u32[]{:S(2)}) collective-permute-start(f32[160,128]{1,0:T(8,128)S(1)} %add.126), channel_id=1, source_target_pairs={{0,64},{16,80},{32,96},{48,112},{64,0},{80,16},{96,32},{112,48},{1... | collective-permute-start | bytes 245768 | tf_op jit(solution)/shard_map/ppermute | solution.py:65
  83.6 13.1 %collective-permute-start.22 = (f32[160,128]{1,0:T(8,128)S(1)}, f32[160,128]{1,0:T(8,128)S(1)}, u32[]{:S(2)}, u32[]{:S(2)}) collective-permute-start(f32[160,128]{1,0:T(8,128)S(1)} %add.126), channel_id=1, source_target_pairs={{0,96},{16,112},{32,0},{48,16},{64,32},{80,48},{96,64},{112,80},{1... | collective-permute-start | bytes 245768 | tf_op jit(solution)/shard_map/ppermute | solution.py:65
  84.5 12.2 %collective-permute-start.20 = (f32[160,128]{1,0:T(8,128)S(1)}, f32[160,128]{1,0:T(8,128)S(1)}, u32[]{:S(2)}, u32[]{:S(2)}) collective-permute-start(f32[160,128]{1,0:T(8,128)S(1)} %add.126), channel_id=1, source_target_pairs={{0,32},{16,48},{32,64},{48,80},{64,96},{80,112},{96,0},{112,16},{1... | collective-permute-start | bytes 245768 | tf_op jit(solution)/shard_map/ppermute | solution.py:65
  96.8 50.9 %all-to-all-start = ((bf16[128,56,128]{2,1,0:T(8,128)(2,1)}), bf16[128,56,128]{2,1,0:T(8,128)(2,1)S(1)}, u32[]{:S(2)}, u32[]{:S(2)}) async-start(bf16[128,56,128]{2,1,0:T(8,128)(2,1)} %bitcast.27), calls=%async_computation | async-start | bytes 3670016 | tf_op jit(solution)/shard_map/all_to_all | solution.py:572
  108.0 2.4 %collective-permute-start.23 = (f32[640,128]{1,0:T(8,128)S(1)}, f32[640,128]{1,0:T(8,128)S(1)}, u32[]{:S(2)}, u32[]{:S(2)}) collective-permute-start(f32[640,128]{1,0:T(8,128)S(1)} %pad_maximum_fusion.2), channel_id=1, source_target_pairs={{0,16},{16,0},{32,48},{48,32},{64,80},{80,64},{96,112},{112,96},{1... | collective-permute-start | bytes 983048 | tf_op jit(solution)/shard_map/ppermute | solution.py:89
  152.5 2.1 %collective-permute-start.24 = (f32[64,512]{1,0:T(8,128)S(1)}, f32[64,512]{1,0:T(8,128)S(1)}, u32[]{:S(2)}, u32[]{:S(2)}) collective-permute-start(f32[64,512]{1,0:T(8,128)S(1)} %constant_dynamic-slice_fusion), channel_id=1, source_target_pairs={{0,16},{16,0},{32,48},{48,32},{64,80},{80,64},{96,112},{112,96},{1... | collective-permute-start | bytes 393224 | tf_op jit(solution)/shard_map/ppermute | solution.py:85
  154.6 4.8 %collective-permute-start.25 = (f32[64,512]{1,0:T(8,128)S(1)}, f32[64,512]{1,0:T(8,128)S(1)}, u32[]{:S(2)}, u32[]{:S(2)}) collective-permute-start(f32[64,512]{1,0:T(8,128)S(1)} %dynamic-slice_add_fusion.1), channel_id=1, source_target_pairs={{0,32},{16,48},{32,0},{48,16},{64,96},{80,112},{96,64},{112,80},{1... | collective-permute-start | bytes 393224 | tf_op jit(solution)/shard_map/ppermute | solution.py:96
  159.4 5.1 %collective-permute-start.26 = (f32[64,512]{1,0:T(8,128)S(1)}, f32[64,512]{1,0:T(8,128)S(1)}, u32[]{:S(2)}, u32[]{:S(2)}) collective-permute-start(f32[64,512]{1,0:T(8,128)S(1)} %add.133), channel_id=1, source_target_pairs={{0,96},{16,112},{32,64},{48,80},{64,32},{80,48},{96,0},{112,16},{1... | collective-permute-start | bytes 393224 | tf_op jit(solution)/shard_map/ppermute | solution.py:96
  164.6 3.6 %collective-permute-start.27 = (f32[64,512]{1,0:T(8,128)S(1)}, f32[64,512]{1,0:T(8,128)S(1)}, u32[]{:S(2)}, u32[]{:S(2)}) collective-permute-start(f32[64,512]{1,0:T(8,128)S(1)} %add.134), channel_id=1, source_target_pairs={{0,16},{16,0},{32,48},{48,32},{64,80},{80,64},{96,112},{112,96},{1... | collective-permute-start | bytes 393224 | tf_op jit(solution)/shard_map/ppermute | solution.py:89
  (11 other events, 82.9 us)
Sparse Core Ops, SparseCore 0:
  10.8 48.1 all-gather.4
  61.1 82.6 all-gather.6

commit v11 on v8

--- a/solution.py
+++ b/solution.py
@@ -384,11 +384,21 @@
     def step(b, carry):
         at = pl.multiple_of(b * 128, 128)
         low = eliminate(work[pl.ds(at, 128), pl.ds(at, 128)])
-        row = dot(low, work[pl.ds(at, 128), :], NN, HIGHEST)
-        lane = lax.broadcasted_iota(jnp.int32, (128, n), 1)
-        later = jnp.where(lane >= at + 128, row[:, :n], 0.0)
-        work[...] = work[...] - dot(later, row, TN, HIGHEST)
-        work[pl.ds(at, 128), :] = row
+        for k in range(n // 128):
+
+            @pl.when(b == k)
+            def _(k=k):
+                here, after = slice(128 * k, 128 * k + 128), slice(128 * k + 128, n)
+                left, right = slice(128 * k, n), slice(n, n + 128 * k + 128)
+                row = dot(low, work[here, left], NN, HIGHEST)
+                solved = dot(low, work[here, right], NN, HIGHEST)
+                work[here, left] = row
+                work[here, right] = solved
+                if k < n // 128 - 1:
+                    later = row[:, 128:]
+                    work[after, after] -= dot(later, later, TN, HIGHEST)
+                    work[after, right] -= dot(later, solved, TN, HIGHEST)
+
         return carry
 
     lax.fori_loop(0, n // 128, step, 0)
@@ -439,8 +449,26 @@
     )(segment, trail)
 
 
+def spread_pair(rest, k, lane):
+    full = jnp.zeros((128, 128), F32)
+    for m in (0, 1):
+        struct, at = 2 * k + m, 64 * m
+        start = 48 * struct
+        turn = (at + 1 - start) % 128
+        part = start // 128
+        split = at + 1 + min(48, 128 * (part + 1) - start)
+        force = pltpu.roll(rest[:, 128 * part : 128 * part + 128], turn, 1)
+        full = jnp.where((lane > at) & (lane < split), force, full)
+        if split < at + 49:
+            force = pltpu.roll(rest[:, 128 * part + 128 : 128 * part + 256], turn, 1)
+            full = jnp.where((lane >= split) & (lane < at + 49), force, full)
+        energy = jnp.broadcast_to(rest[:, 384 + struct : 385 + struct], (128, 128))
+        full = jnp.where(lane == at, energy, full)
+    return full
+
+
 def residual_kernel(
-    rows_total, cross_ref, inverse_ref, panel_ref, trail_ref, coupling_ref, out_ref, weights, spread
+    rows_total, cross_ref, inverse_ref, panel_ref, trail_ref, coupling_ref, out_ref, weights
 ):
     @pl.when(pl.program_id(0) == 0)
     def _():
@@ -450,12 +478,6 @@
         high = solved.astype(BF16)
         weights[:128] = high
         weights[128:] = (solved - high.astype(F32)).astype(BF16)
-        held = lax.broadcasted_iota(jnp.int32, (HELD, 512), 0)
-        column = lax.broadcasted_iota(jnp.int32, (HELD, 512), 1)
-        struct, place = column >> 6, column & 63
-        wanted = jnp.where(place <= 48, struct * 48 + place - 1, -1)
-        wanted = jnp.where(place == 0, 384 + struct, wanted)
-        spread[...] = (held == wanted).astype(F32).astype(BF16)
 
     r = lax.broadcasted_iota(jnp.int32, (128, 128), 0)
     c = lax.broadcasted_iota(jnp.int32, (128, 128), 1)
@@ -464,10 +486,9 @@
         both = dot(weights[...], panel_ref[i], NT)
         own = dot(same, trail_chunk(trail_ref, i), NT)
         rest = own - both[:128] - both[128:]
-        high = rest.astype(BF16)
-        low = (rest - high.astype(F32)).astype(BF16)
-        full = dot(jnp.concatenate([high, low], axis=0), spread[...], NN)
-        out_ref[:, i * 512 : i * 512 + 512] = full[:128] + full[128:]
+        for k in range(4):
+            at = i * 512 + k * 128
+            out_ref[:, at : at + 128] = spread_pair(rest, k, c)
 
 
 def residual(cross, inverse, segment, trail, rows_total):
@@ -488,8 +509,8 @@
             pl.BlockSpec((8, 4, SENT, 128), lambda i: (0, i, 0, 0)),
         ],
         out_specs=(whole((128, n)), pl.BlockSpec((128, 2048), lambda i: (0, i))),
-        scratch_shapes=[pltpu.VMEM((256, n), BF16), pltpu.VMEM((HELD, 512), BF16)],
-        compiler_params=params(),
+        scratch_shapes=[pltpu.VMEM((256, n), BF16)],
+        compiler_params=params(58),
         cost_estimate=pl.CostEstimate(
             flops=4 * 128 * n * 8192, bytes_accessed=16 << 20, transcendentals=0
         ),
@@ -547,8 +568,13 @@
     got, gram, own_trail = lax.optimization_barrier((got, gram, own_trail))
     panel = assemble(where, near, far, got)
     segment = lax.all_gather(panel, "col", axis=0, tiled=False)
-    trail_own = jnp.stack(shifted(own_trail, "row", y_shift))
+    one = lax.ppermute(own_trail, "row", y_shift(1))
+    three = lax.ppermute(own_trail, "row", y_shift(3))
     gram = sum4(gram, "col", z_pair)
+    one, three, gram = lax.optimization_barrier((one, three, gram))
+    low = lax.ppermute(one[:2], "row", y_shift(1))
+    high = lax.ppermute(three[2:], "row", y_shift(3))
+    trail_own = jnp.stack([own_trail, one, jnp.concatenate([low, high], axis=0), three])
     gram = sum4(gram, "col", x_pair)
     trail_own, gram = lax.optimization_barrier((trail_own, gram))
     trail_other = lax.ppermute(trail_own, "row", CORE_SWAP)

time: 188 us -> 188 us (level)
  starting transfers between devices: 43 us -> 49.6 us
  Pallas kernels: 53.2 us -> 49 us
    pallas_call x1, Pallas kernels: 26.7 us -> 20.5 us  [factor_panel(): pl.pallas_call(functools.partial(factor_kernel, float(rows_total)), out_s...]
    ppermute x12 -> x9, waiting for transfers between devices: 20.6 us -> 14.4 us  [shifted(): return [v] + [lax.ppermute(v, axis, shift(s)) for s in (1, 2, 3)]]
    ppermute x0 -> x4, starting transfers between devices: none -> 5.21 us  [the longest x1 2.63 us: per_device(): three = lax.ppermute(own_trail, 'row', y_shift(3))]
    all_to_all x1, waiting for transfers between devices: 1.77 us -> 6.27 us  [per_device(): lax.all_to_all(trail.reshape(128, SENT, 128), ('row', 'col'), 0, 0, tiled...]
    ppermute x1, starting transfers between devices: 0.88 us -> 5.12 us  [per_device(): trail_other = lax.ppermute(trail_own, 'row', CORE_SWAP)]
    ppermute x12 -> x9, starting transfers between devices: 12.8 us -> 10.6 us  [shifted(): return [v] + [lax.ppermute(v, axis, shift(s)) for s in (1, 2, 3)]]
    unnamed x25 -> x27, local copies, waits for them, and re-layouts: 9.87 us -> 8.64 us
  transfers between devices with their start and end apart: 36 -> 37, of which waited for: 26 -> 25; matrix products, arithmetic and copies ran while one was open for 1% -> 1% of each run, Pallas kernels for 21% -> 18%
where the time goes in v11:
time: 188 us
  waiting for transfers between devices  62.2 us (33%)
  starting transfers between devices  49.6 us (26%)
  Pallas kernels  49 us (26%)
  between operations  14.5 us (8%)
  local copies, waits for them, and re-layouts  9.68 us (5%)
  other arithmetic  2.66 us (1%)
    ppermute x6, waiting for transfers between devices, sum4(): v = v + lax.ppermute(v, axis, pairs(flip))  26 us
    pallas_call x1, Pallas kernels, factor_panel(): pl.pallas_call(functools.partial(factor_kernel, float(rows_total)), out_s...  20.5 us
    ppermute x9, waiting for transfers between devices, shifted(): return [v] + [lax.ppermute(v, axis, shift(s)) for s in (1, 2, 3)]  14.4 us
    pallas_call x1, Pallas kernels, residual(): pl.pallas_call(functools.partial(residual_kernel, float(rows_total)), out...  12 us
    ppermute x9, starting transfers between devices, shifted(): return [v] + [lax.ppermute(v, axis, shift(s)) for s in (1, 2, 3)]  10.6 us
    pallas_call x1, Pallas kernels, trail_rows(): pl.pallas_call(trail_kernel, out_shape=jax.ShapeDtypeStruct((8, 16, SENT,...  8.91 us
    unnamed x27, local copies, waits for them, and re-layouts  8.64 us
    ppermute x3, starting transfers between devices, per_device(): lax.ppermute(jnp.stack([near[s], far[s]]), 'row', y_shift(s))  6.46 us
  transfers between devices with their start and end apart: 37, of which 25 were waited for; matrix products, arithmetic and copies ran while one was open for 1% of the time, Pallas kernels for 18%

profile of v11, /device:TPU:1, one launch (start us, length us, event | category | flops | bytes accessed | tf_op | source)
XLA Modules:
  0.0 187.5 jit_solution(17449098701416302587)
XLA Ops:
  8.1 4.7 %collective-permute-start.2 = (bf16[32,1024]{1,0:T(8,128)(2,1)S(1)}, bf16[32,1024]{1,0:T(8,128)(2,1)S(1)}, u32[]{:S(2)}, u32[]{:S(2)}) collective-permute-start(bf16[32,1024]{1,0:T(8,128)(2,1)S(1)} %pad_maximum_fusion.11), channel_id=1, source_target_pairs={{0,3},{1,0},{2,1},{3,2},{4,7},{5,4},{6,5},{7,6},{8,11},{9,8},{10,9... | collective-permute-start | bytes 196616 | tf_op jit(solution)/shard_map/ppermute | solution.py:61
  14.1 3.4 %collective-permute-done.1 = bf16[32,1024]{1,0:T(8,128)(2,1)S(1)} collective-permute-done((bf16[32,1024]{1,0:T(8,128)(2,1)S(1)}, bf16[32,1024]{1,0:T(8,128)(2,1)S(1)}, u32[]{:S(2)}, u32[]{:S(2)}) %collective-permute-start.1) | collective-permute-done | bytes 65568 | tf_op jit(solution)/shard_map/ppermute | solution.py:61
  17.8 2.5 %collective-permute-start.5 = (bf16[4,16,1024]{2,1,0:T(8,128)(2,1)S(1)}, bf16[4,16,1024]{2,1,0:T(8,128)(2,1)S(1)}, u32[]{:S(2)}, u32[]{:S(2)}) collective-permute-start(bf16[4,16,1024]{2,1,0:T(8,128)(2,1)S(1)} %get-tuple-element.81), channel_id=1, source_target_pairs={{0,12},{1,13},{2,14},{3,15},{4,0},{5,1},{6,2},{7,3},{8,4},{9,5},{1... | collective-permute-start | bytes 393224 | tf_op jit(solution)/shard_map/ppermute | solution.py:61
  23.0 2.8 %collective-permute-done.4 = bf16[4,16,1024]{2,1,0:T(8,128)(2,1)S(1)} collective-permute-done((bf16[4,16,1024]{2,1,0:T(8,128)(2,1)S(1)}, bf16[4,16,1024]{2,1,0:T(8,128)(2,1)S(1)}, u32[]{:S(2)}, u32[]{:S(2)}) %collective-permute-start.4) | collective-permute-done | bytes 131104 | tf_op jit(solution)/shard_map/ppermute | solution.py:61
  27.2 3.6 %collective-permute-start.6 = (bf16[4,4,16,1024]{3,2,1,0:T(8,128)(2,1)S(1)}, bf16[4,4,16,1024]{3,2,1,0:T(8,128)(2,1)}, u32[]{:S(2)}, u32[]{:S(2)}) collective-permute-start(bf16[4,4,16,1024]{3,2,1,0:T(8,128)(2,1)S(1)} %pad_maximum_fusion.2.own), channel_id=1, source_target_pairs={{0,16},{16,0},{32,48},{48,32},{64,80},{80,64},{96,112},{112,96},{1... | collective-permute-start | bytes 1572872 | tf_op jit(solution)/shard_map/ppermute | solution.py:548
  31.0 1.9 %copy-done.2 = bf16[3,4,128,1024]{3,2,1,0:T(8,128)(2,1)S(1)} copy-done((bf16[3,4,128,1024]{3,2,1,0:T(8,128)(2,1)S(1)}, bf16[3,4,128,1024]{3,2,1,0:T(8,128)(2,1)}, u32[]{:S(2)}) %copy-start.2) | copy-done | bytes 3145752
  35.8 2.9 %shard_map.95 = (bf16[4,56,512]{2,1,0:T(8,128)(2,1)S(1)}, bf16[4,56,512]{2,1,0:T(8,128)(2,1)S(1)}, f32[1280,128]{1,0:T(8,128)S(1)}) custom-call(s32[4]{0:T(128)S(1)} %pad_add_fusion.where, bf16[4,4,16,1024]{3,2,1,0:T(8,128)(2,1)S(1)} %pad_maximum_fusion.2.own, bf16[4,4,16,1024]{3,2,1,0:T(8,128)(2,1)} %collective-permute-done.6.other, ...), custom_call_target="tpu_custom_call" | custom-call | flops 1140850688 | bytes 5242880 | tf_op jit(solution)/shard_map/pallas_call | solution.py:281
  40.7 3.6 %collective-permute-done.9 = bf16[4,16,1024]{2,1,0:T(8,128)(2,1)S(1)} collective-permute-done((bf16[4,16,1024]{2,1,0:T(8,128)(2,1)S(1)}, bf16[4,16,1024]{2,1,0:T(8,128)(2,1)S(1)}, u32[]{:S(2)}, u32[]{:S(2)}) %collective-permute-start.9) | collective-permute-done | bytes 131104 | tf_op jit(solution)/shard_map/ppermute | solution.py:61
  47.5 2.7 %collective-permute-start.13 = (bf16[2,56,512]{2,1,0:T(8,128)(2,1)S(1)}, bf16[2,56,512]{2,1,0:T(8,128)(2,1)S(1)}, u32[]{:S(2)}, u32[]{:S(2)}) collective-permute-start(bf16[2,56,512]{2,1,0:T(8,128)(2,1)S(1)} %pad_maximum_fusion.9), channel_id=1, source_target_pairs={{0,64},{16,80},{32,96},{48,112},{64,0},{80,16},{96,32},{112,48},{1... | collective-permute-start | bytes 344072 | tf_op jit(solution)/shard_map/ppermute | solution.py:565
  52.1 1.9 collective-permute-done.17
  53.9 2.4 %collective-permute-start.14 = (bf16[2,56,512]{2,1,0:T(8,128)(2,1)S(1)}, bf16[2,56,512]{2,1,0:T(8,128)(2,1)S(1)}, u32[]{:S(2)}, u32[]{:S(2)}) collective-permute-start(bf16[2,56,512]{2,1,0:T(8,128)(2,1)S(1)} %pad_maximum_fusion.10), channel_id=1, source_target_pairs={{0,96},{16,112},{32,0},{48,16},{64,32},{80,48},{96,64},{112,80},{1... | collective-permute-start | bytes 344072 | tf_op jit(solution)/shard_map/ppermute | solution.py:565
  57.0 2.7 %collective-permute-done.15 = f32[160,128]{1,0:T(8,128)S(1)} collective-permute-done((f32[160,128]{1,0:T(8,128)S(1)}, f32[160,128]{1,0:T(8,128)S(1)}, u32[]{:S(2)}, u32[]{:S(2)}) %collective-permute-start.15) | collective-permute-done | bytes 81952 | tf_op jit(solution)/shard_map/ppermute | solution.py:73
  61.2 2.6 %collective-permute-start.19 = (bf16[4,4,16,1024]{3,2,1,0:T(8,128)(2,1)S(1)}, bf16[4,4,16,1024]{3,2,1,0:T(8,128)(2,1)S(1)}, u32[]{:S(2)}, u32[]{:S(2)}) collective-permute-start(bf16[4,4,16,1024]{3,2,1,0:T(8,128)(2,1)S(1)} %pad_maximum_fusion.3), channel_id=1, source_target_pairs={{0,96},{16,112},{32,0},{48,16},{64,32},{80,48},{96,64},{112,80},{1... | collective-permute-start | bytes 1572872 | tf_op jit(solution)/shard_map/ppermute | solution.py:572
  63.8 3.6 %collective-permute-done.20 = f32[160,128]{1,0:T(8,128)S(1)} collective-permute-done((f32[160,128]{1,0:T(8,128)S(1)}, f32[160,128]{1,0:T(8,128)S(1)}, u32[]{:S(2)}, u32[]{:S(2)}) %collective-permute-start.20) | collective-permute-done | bytes 81952 | tf_op jit(solution)/shard_map/ppermute | solution.py:96
  68.3 4.0 %collective-permute-done.21 = f32[160,128]{1,0:T(8,128)S(1)} collective-permute-done((f32[160,128]{1,0:T(8,128)S(1)}, f32[160,128]{1,0:T(8,128)S(1)}, u32[]{:S(2)}, u32[]{:S(2)}) %collective-permute-start.21) | collective-permute-done | bytes 81952 | tf_op jit(solution)/shard_map/ppermute | solution.py:96
  73.7 2.4 %collective-permute-start.23 = (bf16[2,4,16,1024]{3,2,1,0:T(8,128)(2,1)S(1)}, bf16[2,4,16,1024]{3,2,1,0:T(8,128)(2,1)S(1)}, u32[]{:S(2)}, u32[]{:S(2)}) collective-permute-start(bf16[2,4,16,1024]{3,2,1,0:T(8,128)(2,1)S(1)} %slice.55), channel_id=1, source_target_pairs={{0,96},{16,112},{32,0},{48,16},{64,32},{80,48},{96,64},{112,80},{1... | collective-permute-start | bytes 786440 | tf_op jit(solution)/shard_map/ppermute | solution.py:576
  76.3 5.2 %collective-permute-done.24 = f32[160,128]{1,0:T(8,128)S(1)} collective-permute-done((f32[160,128]{1,0:T(8,128)S(1)}, f32[160,128]{1,0:T(8,128)S(1)}, u32[]{:S(2)}, u32[]{:S(2)}) %collective-permute-start.24) | collective-permute-done | bytes 81952 | tf_op jit(solution)/shard_map/ppermute | solution.py:96
  81.7 4.8 %collective-permute-done.25 = f32[160,128]{1,0:T(8,128)S(1)} collective-permute-done((f32[160,128]{1,0:T(8,128)S(1)}, f32[160,128]{1,0:T(8,128)S(1)}, u32[]{:S(2)}, u32[]{:S(2)}) %collective-permute-start.25) | collective-permute-done | bytes 81952 | tf_op jit(solution)/shard_map/ppermute | solution.py:96
  86.9 5.1 %collective-permute-start.26 = (bf16[4,4,4,16,1024]{4,3,2,1,0:T(8,128)(2,1)S(1)}, bf16[4,4,4,16,1024]{4,3,2,1,0:T(8,128)(2,1)}, u32[]{:S(2)}, u32[]{:S(2)}) collective-permute-start(bf16[4,4,4,16,1024]{4,3,2,1,0:T(8,128)(2,1)S(1)} %pad_maximum_fusion.own), channel_id=1, source_target_pairs={{0,16},{16,0},{32,48},{48,32},{64,80},{80,64},{96,112},{112,96},{1... | collective-permute-start | bytes 6291464 | tf_op jit(solution)/shard_map/ppermute | solution.py:580
  92.6 1.9 %collective-permute-start.29 = (f32[160,128]{1,0:T(8,128)S(1)}, f32[160,128]{1,0:T(8,128)S(1)}, u32[]{:S(2)}, u32[]{:S(2)}) collective-permute-start(f32[160,128]{1,0:T(8,128)S(1)} %add.128), channel_id=1, source_target_pairs={{0,96},{16,112},{32,0},{48,16},{64,32},{80,48},{96,64},{112,80},{1... | collective-permute-start | bytes 245768 | tf_op jit(solution)/shard_map/ppermute | solution.py:65
  95.0 2.5 %collective-permute-done.28 = f32[160,128]{1,0:T(8,128)S(1)} collective-permute-done((f32[160,128]{1,0:T(8,128)S(1)}, f32[160,128]{1,0:T(8,128)S(1)}, u32[]{:S(2)}, u32[]{:S(2)}) %collective-permute-start.28) | collective-permute-done | bytes 81952 | tf_op jit(solution)/shard_map/ppermute | solution.py:65
  97.5 2.0 %collective-permute-done.29 = f32[160,128]{1,0:T(8,128)S(1)} collective-permute-done((f32[160,128]{1,0:T(8,128)S(1)}, f32[160,128]{1,0:T(8,128)S(1)}, u32[]{:S(2)}, u32[]{:S(2)}) %collective-permute-start.29) | collective-permute-done | bytes 81952 | tf_op jit(solution)/shard_map/ppermute | solution.py:65
  104.2 8.9 %shard_map.96 = bf16[8,16,56,128]{3,2,1,0:T(8,128)(2,1)S(1)} custom-call(s32[4]{0:T(128)S(1)} %pad_add_fusion.where, bf16[4,4,4,16,1024]{4,3,2,1,0:T(8,128)(2,1)S(1)} %pad_maximum_fusion.own, bf16[4,4,4,16,1024]{4,3,2,1,0:T(8,128)(2,1)} %collective-permute-done.26.other, bf16[320,1024]{1,0:T(8,128)(2,1)S(1)} %get-tuple-element.34.atoms_ref, ...), custom_call_target="tpu_custom_call" | custom-call | flops 4563402752 | bytes 9437184 | tf_op jit(solution)/shard_map/pallas_call | solution.py:312
  114.4 4.7 %all-to-all-start = ((bf16[128,56,128]{2,1,0:T(8,128)(2,1)}), bf16[128,56,128]{2,1,0:T(8,128)(2,1)S(1)}, u32[]{:S(2)}, u32[]{:S(2)}) async-start(bf16[128,56,128]{2,1,0:T(8,128)(2,1)} %bitcast.44), calls=%async_computation | async-start | bytes 3670016 | tf_op jit(solution)/shard_map/all_to_all | solution.py:585
  119.1 20.5 %shard_map.97 = (f32[512,512]{1,0:T(8,128)}, f32[512,512]{1,0:T(8,128)S(1)}) custom-call(f32[1280,128]{1,0:T(8,128)S(1)} %pad_maximum_fusion.1.gram_ref), custom_call_target="tpu_custom_call" | custom-call | flops 2684354560 | bytes 4194304 | tf_op jit(solution)/shard_map/pallas_call | solution.py:411
  140.6 6.3 %all-to-all-done = bf16[128,56,128]{2,1,0:T(8,128)(2,1)S(1)} async-done(((bf16[128,56,128]{2,1,0:T(8,128)(2,1)}), bf16[128,56,128]{2,1,0:T(8,128)(2,1)S(1)}, u32[]{:S(2)}, u32[]{:S(2)}) %all-to-all-start) | async-done | bytes 1835040 | tf_op jit(solution)/shard_map/all_to_all | solution.py:585
  146.9 3.5 %copy-done = bf16[6400,512]{1,0:T(8,128)(2,1)S(1)} copy-done((bf16[6400,512]{1,0:T(8,128)(2,1)S(1)}, bf16[6400,512]{1,0:T(8,128)(2,1)}, u32[]{:S(2)}) %copy-start) | copy-done | bytes 6553624
  150.4 1.9 %shard_map.99 = f32[128,512]{1,0:T(8,128)S(1)} custom-call(bf16[16,400,512]{2,1,0:T(8,128)(2,1)S(1)} %bitcast.40, bf16[8,16,56,128]{3,2,1,0:T(8,128)(2,1)S(1)} %bitcast.41), custom_call_target="tpu_custom_call" | custom-call | flops 1073741824 | bytes 11534336 | tf_op jit(solution)/shard_map/pallas_call | solution.py:436
  154.7 4.5 %collective-permute-done.32 = f32[64,512]{1,0:T(8,128)S(1)} collective-permute-done((f32[64,512]{1,0:T(8,128)S(1)}, f32[64,512]{1,0:T(8,128)S(1)}, u32[]{:S(2)}, u32[]{:S(2)}) %collective-permute-start.32) | collective-permute-done | bytes 131104 | tf_op jit(solution)/shard_map/ppermute | solution.py:96
  160.3 4.0 %collective-permute-done.33 = f32[64,512]{1,0:T(8,128)S(1)} collective-permute-done((f32[64,512]{1,0:T(8,128)S(1)}, f32[64,512]{1,0:T(8,128)S(1)}, u32[]{:S(2)}, u32[]{:S(2)}) %collective-permute-start.33) | collective-permute-done | bytes 131104 | tf_op jit(solution)/shard_map/ppermute | solution.py:96
  164.3 2.6 %collective-permute-start.34 = (f32[64,512]{1,0:T(8,128)S(1)}, f32[64,512]{1,0:T(8,128)S(1)}, u32[]{:S(2)}, u32[]{:S(2)}) collective-permute-start(f32[64,512]{1,0:T(8,128)S(1)} %add.137), channel_id=1, source_target_pairs={{0,16},{16,0},{32,48},{48,32},{64,80},{80,64},{96,112},{112,96},{1... | collective-permute-start | bytes 393224 | tf_op jit(solution)/shard_map/ppermute | solution.py:89
  168.7 12.0 %shard_map.100 = (f32[128,512]{1,0:T(8,128)}, f32[128,8192]{1,0:T(8,128)}) custom-call(f32[128,512]{1,0:T(8,128)} %pad_maximum_fusion.5.cross_ref, f32[512,512]{1,0:T(8,128)} %copy-done.4, bf16[16,400,512]{2,1,0:T(8,128)(2,1)} %bitcast.39, bf16[8,16,56,128]{3,2,1,0:T(8,128)(2,1)} %bitcast.42), custom_call_target="tpu_custom_call" | custom-call | flops 2147483648 | bytes 16777216 | tf_op jit(solution)/shard_map/pallas_call | solution.py:498
  (115 shorter events, 35.1 us)
Async XLA Ops:
  7.2 133.4 %all-gather.3.cloned.1.call-start = ((), (), s32[]{:S(2)}) async-start(), calls=%async_computation.1 | async-start | bytes 6963200 | tf_op jit(solution)/shard_map/all_gather | solution.py:570
  8.1 6.0 %collective-permute-start.2 = (bf16[32,1024]{1,0:T(8,128)(2,1)S(1)}, bf16[32,1024]{1,0:T(8,128)(2,1)S(1)}, u32[]{:S(2)}, u32[]{:S(2)}) collective-permute-start(bf16[32,1024]{1,0:T(8,128)(2,1)S(1)} %pad_maximum_fusion.11), channel_id=1, source_target_pairs={{0,3},{1,0},{2,1},{3,2},{4,7},{5,4},{6,5},{7,6},{8,11},{9,8},{10,9... | collective-permute-start | bytes 196616 | tf_op jit(solution)/shard_map/ppermute | solution.py:61
  12.8 4.7 %collective-permute-start.1 = (bf16[32,1024]{1,0:T(8,128)(2,1)S(1)}, bf16[32,1024]{1,0:T(8,128)(2,1)S(1)}, u32[]{:S(2)}, u32[]{:S(2)}) collective-permute-start(bf16[32,1024]{1,0:T(8,128)(2,1)S(1)} %pad_maximum_fusion.11), channel_id=1, source_target_pairs={{0,2},{1,3},{2,0},{3,1},{4,6},{5,7},{6,4},{7,5},{8,10},{9,11},{10,... | collective-permute-start | bytes 196616 | tf_op jit(solution)/shard_map/ppermute | solution.py:61
  12.8 5.0 %collective-permute-start = (bf16[32,1024]{1,0:T(8,128)(2,1)S(1)}, bf16[32,1024]{1,0:T(8,128)(2,1)S(1)}, u32[]{:S(2)}, u32[]{:S(2)}) collective-permute-start(bf16[32,1024]{1,0:T(8,128)(2,1)S(1)} %pad_maximum_fusion.11), channel_id=1, source_target_pairs={{0,1},{1,2},{2,3},{3,0},{4,5},{5,6},{6,7},{7,4},{8,9},{9,10},{10,1... | collective-permute-start | bytes 196616 | tf_op jit(solution)/shard_map/ppermute | solution.py:61
  17.8 5.2 %collective-permute-start.5 = (bf16[4,16,1024]{2,1,0:T(8,128)(2,1)S(1)}, bf16[4,16,1024]{2,1,0:T(8,128)(2,1)S(1)}, u32[]{:S(2)}, u32[]{:S(2)}) collective-permute-start(bf16[4,16,1024]{2,1,0:T(8,128)(2,1)S(1)} %get-tuple-element.81), channel_id=1, source_target_pairs={{0,12},{1,13},{2,14},{3,15},{4,0},{5,1},{6,2},{7,3},{8,4},{9,5},{1... | collective-permute-start | bytes 393224 | tf_op jit(solution)/shard_map/ppermute | solution.py:61
  20.4 5.4 %collective-permute-start.4 = (bf16[4,16,1024]{2,1,0:T(8,128)(2,1)S(1)}, bf16[4,16,1024]{2,1,0:T(8,128)(2,1)S(1)}, u32[]{:S(2)}, u32[]{:S(2)}) collective-permute-start(bf16[4,16,1024]{2,1,0:T(8,128)(2,1)S(1)} %get-tuple-element.81), channel_id=1, source_target_pairs={{0,8},{1,9},{2,10},{3,11},{4,12},{5,13},{6,14},{7,15},{8,0},{9,1},... | collective-permute-start | bytes 393224 | tf_op jit(solution)/shard_map/ppermute | solution.py:61
  20.9 6.2 %collective-permute-start.3 = (bf16[4,16,1024]{2,1,0:T(8,128)(2,1)S(1)}, bf16[4,16,1024]{2,1,0:T(8,128)(2,1)S(1)}, u32[]{:S(2)}, u32[]{:S(2)}) collective-permute-start(bf16[4,16,1024]{2,1,0:T(8,128)(2,1)S(1)} %get-tuple-element.81), channel_id=1, source_target_pairs={{0,4},{1,5},{2,6},{3,7},{4,8},{5,9},{6,10},{7,11},{8,12},{9,13},{1... | collective-permute-start | bytes 393224 | tf_op jit(solution)/shard_map/ppermute | solution.py:61
  27.2 8.6 %collective-permute-start.6 = (bf16[4,4,16,1024]{3,2,1,0:T(8,128)(2,1)S(1)}, bf16[4,4,16,1024]{3,2,1,0:T(8,128)(2,1)}, u32[]{:S(2)}, u32[]{:S(2)}) collective-permute-start(bf16[4,4,16,1024]{3,2,1,0:T(8,128)(2,1)S(1)} %pad_maximum_fusion.2.own), channel_id=1, source_target_pairs={{0,16},{16,0},{32,48},{48,32},{64,80},{80,64},{96,112},{112,96},{1... | collective-permute-start | bytes 1572872 | tf_op jit(solution)/shard_map/ppermute | solution.py:548
  34.3 5.5 %collective-permute-start.11 = (bf16[4,16,1024]{2,1,0:T(8,128)(2,1)S(1)}, bf16[4,16,1024]{2,1,0:T(8,128)(2,1)S(1)}, u32[]{:S(2)}, u32[]{:S(2)}) collective-permute-start(bf16[4,16,1024]{2,1,0:T(8,128)(2,1)S(1)} %pad_maximum_fusion.7), channel_id=1, source_target_pairs={{0,12},{1,13},{2,14},{3,15},{4,0},{5,1},{6,2},{7,3},{8,4},{9,5},{1... | collective-permute-start | bytes 393224 | tf_op jit(solution)/shard_map/ppermute | solution.py:61
  34.6 6.1 %collective-permute-start.10 = (bf16[4,16,1024]{2,1,0:T(8,128)(2,1)S(1)}, bf16[4,16,1024]{2,1,0:T(8,128)(2,1)S(1)}, u32[]{:S(2)}, u32[]{:S(2)}) collective-permute-start(bf16[4,16,1024]{2,1,0:T(8,128)(2,1)S(1)} %pad_maximum_fusion.7), channel_id=1, source_target_pairs={{0,8},{1,9},{2,10},{3,11},{4,12},{5,13},{6,14},{7,15},{8,0},{9,1},... | collective-permute-start | bytes 393224 | tf_op jit(solution)/shard_map/ppermute | solution.py:61
  35.1 9.2 %collective-permute-start.9 = (bf16[4,16,1024]{2,1,0:T(8,128)(2,1)S(1)}, bf16[4,16,1024]{2,1,0:T(8,128)(2,1)S(1)}, u32[]{:S(2)}, u32[]{:S(2)}) collective-permute-start(bf16[4,16,1024]{2,1,0:T(8,128)(2,1)S(1)} %pad_maximum_fusion.7), channel_id=1, source_target_pairs={{0,4},{1,5},{2,6},{3,7},{4,8},{5,9},{6,10},{7,11},{8,12},{9,13},{1... | collective-permute-start | bytes 393224 | tf_op jit(solution)/shard_map/ppermute | solution.py:61
  38.8 6.2 %collective-permute-start.8 = (f32[640,128]{1,0:T(8,128)S(1)}, f32[640,128]{1,0:T(8,128)S(1)}, u32[]{:S(2)}, u32[]{:S(2)}) collective-permute-start(f32[640,128]{1,0:T(8,128)S(1)} %constant_dynamic-slice_fusion.4), channel_id=1, source_target_pairs={{0,16},{16,0},{32,48},{48,32},{64,80},{80,64},{96,112},{112,96},{1... | collective-permute-start | bytes 983048 | tf_op jit(solution)/shard_map/ppermute | solution.py:85
  46.1 13.5 %collective-permute-start.12 = (bf16[2,56,512]{2,1,0:T(8,128)(2,1)S(1)}, bf16[2,56,512]{2,1,0:T(8,128)(2,1)S(1)}, u32[]{:S(2)}, u32[]{:S(2)}) collective-permute-start(bf16[2,56,512]{2,1,0:T(8,128)(2,1)S(1)} %pad_maximum_fusion.8), channel_id=1, source_target_pairs={{0,32},{16,48},{32,64},{48,80},{64,96},{80,112},{96,0},{112,16},{1... | collective-permute-start | bytes 344072 | tf_op jit(solution)/shard_map/ppermute | solution.py:565
  47.5 12.2 %collective-permute-start.13 = (bf16[2,56,512]{2,1,0:T(8,128)(2,1)S(1)}, bf16[2,56,512]{2,1,0:T(8,128)(2,1)S(1)}, u32[]{:S(2)}, u32[]{:S(2)}) collective-permute-start(bf16[2,56,512]{2,1,0:T(8,128)(2,1)S(1)} %pad_maximum_fusion.9), channel_id=1, source_target_pairs={{0,64},{16,80},{32,96},{48,112},{64,0},{80,16},{96,32},{112,48},{1... | collective-permute-start | bytes 344072 | tf_op jit(solution)/shard_map/ppermute | solution.py:565
  50.2 3.7 %collective-permute-start.17 = (f32[160,128]{1,0:T(8,128)S(1)}, f32[160,128]{1,0:T(8,128)S(1)}, u32[]{:S(2)}, u32[]{:S(2)}) collective-permute-start(f32[160,128]{1,0:T(8,128)S(1)} %get-tuple-element.70), channel_id=1, source_target_pairs={{0,96},{16,112},{32,0},{48,16},{64,32},{80,48},{96,64},{112,80},{1... | collective-permute-start | bytes 245768 | tf_op jit(solution)/shard_map/ppermute | solution.py:73
  51.4 5.6 %collective-permute-start.16 = (f32[160,128]{1,0:T(8,128)S(1)}, f32[160,128]{1,0:T(8,128)S(1)}, u32[]{:S(2)}, u32[]{:S(2)}) collective-permute-start(f32[160,128]{1,0:T(8,128)S(1)} %get-tuple-element.71), channel_id=1, source_target_pairs={{0,64},{16,80},{32,96},{48,112},{64,0},{80,16},{96,32},{112,48},{1... | collective-permute-start | bytes 245768 | tf_op jit(solution)/shard_map/ppermute | solution.py:73
  51.5 8.1 %collective-permute-start.15 = (f32[160,128]{1,0:T(8,128)S(1)}, f32[160,128]{1,0:T(8,128)S(1)}, u32[]{:S(2)}, u32[]{:S(2)}) collective-permute-start(f32[160,128]{1,0:T(8,128)S(1)} %get-tuple-element.69), channel_id=1, source_target_pairs={{0,32},{16,48},{32,64},{48,80},{64,96},{80,112},{96,0},{112,16},{1... | collective-permute-start | bytes 245768 | tf_op jit(solution)/shard_map/ppermute | solution.py:73
  53.9 5.8 %collective-permute-start.14 = (bf16[2,56,512]{2,1,0:T(8,128)(2,1)S(1)}, bf16[2,56,512]{2,1,0:T(8,128)(2,1)S(1)}, u32[]{:S(2)}, u32[]{:S(2)}) collective-permute-start(bf16[2,56,512]{2,1,0:T(8,128)(2,1)S(1)} %pad_maximum_fusion.10), channel_id=1, source_target_pairs={{0,96},{16,112},{32,0},{48,16},{64,32},{80,48},{96,64},{112,80},{1... | collective-permute-start | bytes 344072 | tf_op jit(solution)/shard_map/ppermute | solution.py:565
  61.1 12.6 %collective-permute-start.18 = (bf16[4,4,16,1024]{3,2,1,0:T(8,128)(2,1)S(1)}, bf16[4,4,16,1024]{3,2,1,0:T(8,128)(2,1)S(1)}, u32[]{:S(2)}, u32[]{:S(2)}) collective-permute-start(bf16[4,4,16,1024]{3,2,1,0:T(8,128)(2,1)S(1)} %pad_maximum_fusion.3), channel_id=1, source_target_pairs={{0,32},{16,48},{32,64},{48,80},{64,96},{80,112},{96,0},{112,16},{1... | collective-permute-start | bytes 1572872 | tf_op jit(solution)/shard_map/ppermute | solution.py:571
  61.2 12.5 %collective-permute-start.19 = (bf16[4,4,16,1024]{3,2,1,0:T(8,128)(2,1)S(1)}, bf16[4,4,16,1024]{3,2,1,0:T(8,128)(2,1)S(1)}, u32[]{:S(2)}, u32[]{:S(2)}) collective-permute-start(bf16[4,4,16,1024]{3,2,1,0:T(8,128)(2,1)S(1)} %pad_maximum_fusion.3), channel_id=1, source_target_pairs={{0,96},{16,112},{32,0},{48,16},{64,32},{80,48},{96,64},{112,80},{1... | collective-permute-start | bytes 1572872 | tf_op jit(solution)/shard_map/ppermute | solution.py:572
  67.4 4.9 %collective-permute-start.21 = (f32[160,128]{1,0:T(8,128)S(1)}, f32[160,128]{1,0:T(8,128)S(1)}, u32[]{:S(2)}, u32[]{:S(2)}) collective-permute-start(f32[160,128]{1,0:T(8,128)S(1)} %add.125), channel_id=1, source_target_pairs={{0,3},{1,2},{2,1},{3,0},{4,7},{5,6},{6,5},{7,4},{8,11},{9,10},{10,... | collective-permute-start | bytes 245768 | tf_op jit(solution)/shard_map/ppermute | solution.py:96
  73.7 12.8 %collective-permute-start.23 = (bf16[2,4,16,1024]{3,2,1,0:T(8,128)(2,1)S(1)}, bf16[2,4,16,1024]{3,2,1,0:T(8,128)(2,1)S(1)}, u32[]{:S(2)}, u32[]{:S(2)}) collective-permute-start(bf16[2,4,16,1024]{3,2,1,0:T(8,128)(2,1)S(1)} %slice.55), channel_id=1, source_target_pairs={{0,96},{16,112},{32,0},{48,16},{64,32},{80,48},{96,64},{112,80},{1... | collective-permute-start | bytes 786440 | tf_op jit(solution)/shard_map/ppermute | solution.py:576
  76.1 10.4 %collective-permute-start.22 = (bf16[2,4,16,1024]{3,2,1,0:T(8,128)(2,1)S(1)}, bf16[2,4,16,1024]{3,2,1,0:T(8,128)(2,1)S(1)}, u32[]{:S(2)}, u32[]{:S(2)}) collective-permute-start(bf16[2,4,16,1024]{3,2,1,0:T(8,128)(2,1)S(1)} %slice.54), channel_id=1, source_target_pairs={{0,32},{16,48},{32,64},{48,80},{64,96},{80,112},{96,0},{112,16},{1... | collective-permute-start | bytes 786440 | tf_op jit(solution)/shard_map/ppermute | solution.py:575
  76.2 5.3 %collective-permute-start.24 = (f32[160,128]{1,0:T(8,128)S(1)}, f32[160,128]{1,0:T(8,128)S(1)}, u32[]{:S(2)}, u32[]{:S(2)}) collective-permute-start(f32[160,128]{1,0:T(8,128)S(1)} %add.126), channel_id=1, source_target_pairs={{0,4},{1,5},{2,6},{3,7},{4,0},{5,1},{6,2},{7,3},{8,12},{9,13},{10,... | collective-permute-start | bytes 245768 | tf_op jit(solution)/shard_map/ppermute | solution.py:96
  81.5 5.1 %collective-permute-start.25 = (f32[160,128]{1,0:T(8,128)S(1)}, f32[160,128]{1,0:T(8,128)S(1)}, u32[]{:S(2)}, u32[]{:S(2)}) collective-permute-start(f32[160,128]{1,0:T(8,128)S(1)} %add.127), channel_id=1, source_target_pairs={{0,12},{1,13},{2,14},{3,15},{4,8},{5,9},{6,10},{7,11},{8,4},{9,5},... | collective-permute-start | bytes 245768 | tf_op jit(solution)/shard_map/ppermute | solution.py:96
  86.9 16.3 %collective-permute-start.26 = (bf16[4,4,4,16,1024]{4,3,2,1,0:T(8,128)(2,1)S(1)}, bf16[4,4,4,16,1024]{4,3,2,1,0:T(8,128)(2,1)}, u32[]{:S(2)}, u32[]{:S(2)}) collective-permute-start(bf16[4,4,4,16,1024]{4,3,2,1,0:T(8,128)(2,1)S(1)} %pad_maximum_fusion.own), channel_id=1, source_target_pairs={{0,16},{16,0},{32,48},{48,32},{64,80},{80,64},{96,112},{112,96},{1... | collective-permute-start | bytes 6291464 | tf_op jit(solution)/shard_map/ppermute | solution.py:580
  92.0 5.5 %collective-permute-start.28 = (f32[160,128]{1,0:T(8,128)S(1)}, f32[160,128]{1,0:T(8,128)S(1)}, u32[]{:S(2)}, u32[]{:S(2)}) collective-permute-start(f32[160,128]{1,0:T(8,128)S(1)} %add.128), channel_id=1, source_target_pairs={{0,64},{16,80},{32,96},{48,112},{64,0},{80,16},{96,32},{112,48},{1... | collective-permute-start | bytes 245768 | tf_op jit(solution)/shard_map/ppermute | solution.py:65
  92.6 6.9 %collective-permute-start.29 = (f32[160,128]{1,0:T(8,128)S(1)}, f32[160,128]{1,0:T(8,128)S(1)}, u32[]{:S(2)}, u32[]{:S(2)}) collective-permute-start(f32[160,128]{1,0:T(8,128)S(1)} %add.128), channel_id=1, source_target_pairs={{0,96},{16,112},{32,0},{48,16},{64,32},{80,48},{96,64},{112,80},{1... | collective-permute-start | bytes 245768 | tf_op jit(solution)/shard_map/ppermute | solution.py:65
  94.5 5.0 %collective-permute-start.27 = (f32[160,128]{1,0:T(8,128)S(1)}, f32[160,128]{1,0:T(8,128)S(1)}, u32[]{:S(2)}, u32[]{:S(2)}) collective-permute-start(f32[160,128]{1,0:T(8,128)S(1)} %add.128), channel_id=1, source_target_pairs={{0,32},{16,48},{32,64},{48,80},{64,96},{80,112},{96,0},{112,16},{1... | collective-permute-start | bytes 245768 | tf_op jit(solution)/shard_map/ppermute | solution.py:65
  114.4 32.5 %all-to-all-start = ((bf16[128,56,128]{2,1,0:T(8,128)(2,1)}), bf16[128,56,128]{2,1,0:T(8,128)(2,1)S(1)}, u32[]{:S(2)}, u32[]{:S(2)}) async-start(bf16[128,56,128]{2,1,0:T(8,128)(2,1)} %bitcast.44), calls=%async_computation | async-start | bytes 3670016 | tf_op jit(solution)/shard_map/all_to_all | solution.py:585
  154.4 4.8 %collective-permute-start.32 = (f32[64,512]{1,0:T(8,128)S(1)}, f32[64,512]{1,0:T(8,128)S(1)}, u32[]{:S(2)}, u32[]{:S(2)}) collective-permute-start(f32[64,512]{1,0:T(8,128)S(1)} %dynamic-slice_add_fusion.1), channel_id=1, source_target_pairs={{0,32},{16,48},{32,0},{48,16},{64,96},{80,112},{96,64},{112,80},{1... | collective-permute-start | bytes 393224 | tf_op jit(solution)/shard_map/ppermute | solution.py:96
  159.2 5.1 %collective-permute-start.33 = (f32[64,512]{1,0:T(8,128)S(1)}, f32[64,512]{1,0:T(8,128)S(1)}, u32[]{:S(2)}, u32[]{:S(2)}) collective-permute-start(f32[64,512]{1,0:T(8,128)S(1)} %add.136), channel_id=1, source_target_pairs={{0,96},{16,112},{32,64},{48,80},{64,32},{80,48},{96,0},{112,16},{1... | collective-permute-start | bytes 393224 | tf_op jit(solution)/shard_map/ppermute | solution.py:96
  (18 other events, 134.0 us)
Sparse Core Ops, SparseCore 0:
  61.2 63.3 all-gather.2

commit v12 on v11

--- a/solution.py
+++ b/solution.py
@@ -230,13 +230,14 @@
 
 
 def trail_kernel(
-    where, own, other, atoms_ref, grads_ref, mean_ref, order_ref, out_ref, env
+    where, own, other, own2, other2, atoms_ref, grads_ref, mean_ref, order_ref, out_ref, env
 ):
     z, y = where[1], where[2]
     for j in range(4):
         place = ((z - j) & 3) * 128
-        for s in range(4):
-            put_env(env, where, own, other, (s, 0, j), place + ((y - s) & 3) * 32)
+        for k, s in enumerate((0, 1, 3)):
+            put_env(env, where, own, other, (k, 0, j), place + ((y - s) & 3) * 32)
+        put_env(env, where, own2, other2, (0, j), place + ((y - 2) & 3) * 32)
     rows = compact_rows(env[...], atoms_ref[...], grads_ref[...], mean_ref[...])
     full = dot(order_ref[...].astype(BF16), rows, NN)
     for c in range(out_ref.shape[1]):
@@ -306,8 +307,9 @@
     )(where, near, far, *got)
 
 
-def trail_rows(where, own, other, atoms, grads, mean, order):
-    piece = pl.BlockSpec((4, 1, 4, 16, 1024), lambda i, w: (0, i, 0, 0, 0))
+def trail_rows(where, own, other, own2, other2, atoms, grads, mean, order):
+    piece = pl.BlockSpec((3, 1, 4, 16, 1024), lambda i, w: (0, i, 0, 0, 0))
+    last = pl.BlockSpec((1, 4, 16, 1024), lambda i, w: (i, 0, 0, 0))
     whole = lambda shape: pl.BlockSpec(shape, lambda i, w: (0, 0))
     return pl.pallas_call(
         trail_kernel,
@@ -315,7 +317,7 @@
         grid_spec=pltpu.PrefetchScalarGridSpec(
             num_scalar_prefetch=1,
             grid=(4,),
-            in_specs=[piece] * 2
+            in_specs=[piece, piece, last, last]
             + [
                 whole(atoms.shape),
                 whole(grads.shape),
@@ -329,7 +331,7 @@
         cost_estimate=pl.CostEstimate(
             flops=2 * 2048 * 1024 * 1088, bytes_accessed=9 << 20, transcendentals=0
         ),
-    )(where, own, other, atoms, grads, mean, order)
+    )(where, own, other, own2, other2, atoms, grads, mean, order)
 
 
 def eliminate(a):
@@ -574,11 +576,16 @@
     one, three, gram = lax.optimization_barrier((one, three, gram))
     low = lax.ppermute(one[:2], "row", y_shift(1))
     high = lax.ppermute(three[2:], "row", y_shift(3))
-    trail_own = jnp.stack([own_trail, one, jnp.concatenate([low, high], axis=0), three])
+    trail_own = jnp.stack([own_trail, one, three])
+    trail_other = lax.ppermute(trail_own, "row", CORE_SWAP)
+    last = jnp.concatenate([low, high], axis=0)
     gram = sum4(gram, "col", x_pair)
-    trail_own, gram = lax.optimization_barrier((trail_own, gram))
-    trail_other = lax.ppermute(trail_own, "row", CORE_SWAP)
-    trail = trail_rows(where, trail_own, trail_other, atoms, grads, mean, order)
+    last, gram = lax.optimization_barrier((last, gram))
+    last_other = lax.ppermute(last, "row", CORE_SWAP)
+    trail_other, last_other, gram = lax.optimization_barrier((trail_other, last_other, gram))
+    trail = trail_rows(
+        where, trail_own, trail_other, last, last_other, atoms, grads, mean, order
+    )
     gram = gather4(gram, "row", y_shift, y)
     gram = jnp.concatenate(swap_gather(gram, core), axis=0)
     trail, gram = lax.optimization_barrier((trail, gram))

time: 188 us -> 191 us (1.016)
  local copies, waits for them, and re-layouts: 9.68 us -> 13.6 us
    unnamed x27 -> x31, local copies, waits for them, and re-layouts: 8.64 us -> 12.6 us
    ppermute x0 -> x1, starting transfers between devices: none -> 2.2 us  [per_device(): last_other = lax.ppermute(last, 'row', CORE_SWAP)]
  transfers between devices with their start and end apart: 37 -> 38, of which waited for: 25 -> 26; matrix products, arithmetic and copies ran while one was open for 1% -> 1% of each run, Pallas kernels for 18% -> 17%
where the time goes in v12:
time: 191 us; the launch traced here: 190 us
  waiting for transfers between devices  61.1 us (32%)
  starting transfers between devices  50.8 us (27%)
  Pallas kernels  47.6 us (25%)
  between operations  14.4 us (8%)
  local copies, waits for them, and re-layouts  13.6 us (7%)
  other arithmetic  2.47 us (1%)
    ppermute x6, waiting for transfers between devices, sum4(): v = v + lax.ppermute(v, axis, pairs(flip))  24.9 us
    pallas_call x1, Pallas kernels, factor_panel(): pl.pallas_call(functools.partial(factor_kernel, float(rows_total)), out_s...  20.5 us
    ppermute x9, waiting for transfers between devices, shifted(): return [v] + [lax.ppermute(v, axis, shift(s)) for s in (1, 2, 3)]  14.9 us
    unnamed x31, local copies, waits for them, and re-layouts  12.6 us
    pallas_call x1, Pallas kernels, residual(): pl.pallas_call(functools.partial(residual_kernel, float(rows_total)), out...  12 us
    ppermute x9, starting transfers between devices, shifted(): return [v] + [lax.ppermute(v, axis, shift(s)) for s in (1, 2, 3)]  10.6 us
    pallas_call x1, Pallas kernels, trail_rows(): pl.pallas_call(trail_kernel, out_shape=jax.ShapeDtypeStruct((8, 16, SENT,...  7.99 us
    ppermute x3, starting transfers between devices, per_device(): lax.ppermute(jnp.stack([near[s], far[s]]), 'row', y_shift(s))  6.46 us
  transfers between devices with their start and end apart: 38, of which 26 were waited for; matrix products, arithmetic and copies ran while one was open for 1% of the time, Pallas kernels for 17%

profile of v12, /device:TPU:1, one launch (start us, length us, event | category | flops | bytes accessed | tf_op | source)
XLA Modules:
  0.0 190.1 jit_solution(9116893770899441175)
XLA Ops:
  8.1 4.7 %collective-permute-start.2 = (bf16[32,1024]{1,0:T(8,128)(2,1)S(1)}, bf16[32,1024]{1,0:T(8,128)(2,1)S(1)}, u32[]{:S(2)}, u32[]{:S(2)}) collective-permute-start(bf16[32,1024]{1,0:T(8,128)(2,1)S(1)} %pad_maximum_fusion.12), channel_id=1, source_target_pairs={{0,3},{1,0},{2,1},{3,2},{4,7},{5,4},{6,5},{7,6},{8,11},{9,8},{10,9... | collective-permute-start | bytes 196616 | tf_op jit(solution)/shard_map/ppermute | solution.py:61
  14.1 3.4 %collective-permute-done.1 = bf16[32,1024]{1,0:T(8,128)(2,1)S(1)} collective-permute-done((bf16[32,1024]{1,0:T(8,128)(2,1)S(1)}, bf16[32,1024]{1,0:T(8,128)(2,1)S(1)}, u32[]{:S(2)}, u32[]{:S(2)}) %collective-permute-start.1) | collective-permute-done | bytes 65568 | tf_op jit(solution)/shard_map/ppermute | solution.py:61
  17.8 2.5 %collective-permute-start.5 = (bf16[4,16,1024]{2,1,0:T(8,128)(2,1)S(1)}, bf16[4,16,1024]{2,1,0:T(8,128)(2,1)S(1)}, u32[]{:S(2)}, u32[]{:S(2)}) collective-permute-start(bf16[4,16,1024]{2,1,0:T(8,128)(2,1)S(1)} %get-tuple-element.87), channel_id=1, source_target_pairs={{0,12},{1,13},{2,14},{3,15},{4,0},{5,1},{6,2},{7,3},{8,4},{9,5},{1... | collective-permute-start | bytes 393224 | tf_op jit(solution)/shard_map/ppermute | solution.py:61
  23.0 2.8 %collective-permute-done.4 = bf16[4,16,1024]{2,1,0:T(8,128)(2,1)S(1)} collective-permute-done((bf16[4,16,1024]{2,1,0:T(8,128)(2,1)S(1)}, bf16[4,16,1024]{2,1,0:T(8,128)(2,1)S(1)}, u32[]{:S(2)}, u32[]{:S(2)}) %collective-permute-start.4) | collective-permute-done | bytes 131104 | tf_op jit(solution)/shard_map/ppermute | solution.py:61
  27.2 3.6 %collective-permute-start.6 = (bf16[4,4,16,1024]{3,2,1,0:T(8,128)(2,1)S(1)}, bf16[4,4,16,1024]{3,2,1,0:T(8,128)(2,1)S(1)}, u32[]{:S(2)}, u32[]{:S(2)}) collective-permute-start(bf16[4,4,16,1024]{3,2,1,0:T(8,128)(2,1)S(1)} %pad_maximum_fusion.2.own), channel_id=1, source_target_pairs={{0,16},{16,0},{32,48},{48,32},{64,80},{80,64},{96,112},{112,96},{1... | collective-permute-start | bytes 1572872 | tf_op jit(solution)/shard_map/ppermute | solution.py:550
  31.0 1.9 copy-done.2
  35.8 2.4 %shard_map.95 = (bf16[4,56,512]{2,1,0:T(8,128)(2,1)S(1)}, bf16[4,56,512]{2,1,0:T(8,128)(2,1)S(1)}, f32[1280,128]{1,0:T(8,128)S(1)}) custom-call(s32[4]{0:T(128)S(1)} %pad_add_fusion.where, bf16[4,4,16,1024]{3,2,1,0:T(8,128)(2,1)S(1)} %pad_maximum_fusion.2.own, bf16[4,4,16,1024]{3,2,1,0:T(8,128)(2,1)S(1)} %collective-permute-done.6.other, ...), custom_call_target="tpu_custom_call" | custom-call | flops 1140850688 | bytes 5242880 | tf_op jit(solution)/shard_map/pallas_call | solution.py:282
  40.7 3.6 %collective-permute-done.9 = bf16[4,16,1024]{2,1,0:T(8,128)(2,1)S(1)} collective-permute-done((bf16[4,16,1024]{2,1,0:T(8,128)(2,1)S(1)}, bf16[4,16,1024]{2,1,0:T(8,128)(2,1)S(1)}, u32[]{:S(2)}, u32[]{:S(2)}) %collective-permute-start.9) | collective-permute-done | bytes 131104 | tf_op jit(solution)/shard_map/ppermute | solution.py:61
  47.5 2.7 %collective-permute-start.13 = (bf16[2,56,512]{2,1,0:T(8,128)(2,1)S(1)}, bf16[2,56,512]{2,1,0:T(8,128)(2,1)S(1)}, u32[]{:S(2)}, u32[]{:S(2)}) collective-permute-start(bf16[2,56,512]{2,1,0:T(8,128)(2,1)S(1)} %pad_maximum_fusion.10), channel_id=1, source_target_pairs={{0,64},{16,80},{32,96},{48,112},{64,0},{80,16},{96,32},{112,48},{1... | collective-permute-start | bytes 344072 | tf_op jit(solution)/shard_map/ppermute | solution.py:567
  52.1 1.9 collective-permute-done.17
  53.9 2.4 %collective-permute-start.14 = (bf16[2,56,512]{2,1,0:T(8,128)(2,1)S(1)}, bf16[2,56,512]{2,1,0:T(8,128)(2,1)S(1)}, u32[]{:S(2)}, u32[]{:S(2)}) collective-permute-start(bf16[2,56,512]{2,1,0:T(8,128)(2,1)S(1)} %pad_maximum_fusion.11), channel_id=1, source_target_pairs={{0,96},{16,112},{32,0},{48,16},{64,32},{80,48},{96,64},{112,80},{1... | collective-permute-start | bytes 344072 | tf_op jit(solution)/shard_map/ppermute | solution.py:567
  57.0 2.7 %collective-permute-done.15 = f32[160,128]{1,0:T(8,128)S(1)} collective-permute-done((f32[160,128]{1,0:T(8,128)S(1)}, f32[160,128]{1,0:T(8,128)S(1)}, u32[]{:S(2)}, u32[]{:S(2)}) %collective-permute-start.15) | collective-permute-done | bytes 81952 | tf_op jit(solution)/shard_map/ppermute | solution.py:73
  61.2 2.6 %collective-permute-start.19 = (bf16[4,4,16,1024]{3,2,1,0:T(8,128)(2,1)S(1)}, bf16[4,4,16,1024]{3,2,1,0:T(8,128)(2,1)S(1)}, u32[]{:S(2)}, u32[]{:S(2)}) collective-permute-start(bf16[4,4,16,1024]{3,2,1,0:T(8,128)(2,1)S(1)} %pad_maximum_fusion.3), channel_id=1, source_target_pairs={{0,96},{16,112},{32,0},{48,16},{64,32},{80,48},{96,64},{112,80},{1... | collective-permute-start | bytes 1572872 | tf_op jit(solution)/shard_map/ppermute | solution.py:574
  63.8 3.6 %collective-permute-done.20 = f32[160,128]{1,0:T(8,128)S(1)} collective-permute-done((f32[160,128]{1,0:T(8,128)S(1)}, f32[160,128]{1,0:T(8,128)S(1)}, u32[]{:S(2)}, u32[]{:S(2)}) %collective-permute-start.20) | collective-permute-done | bytes 81952 | tf_op jit(solution)/shard_map/ppermute | solution.py:96
  68.3 4.0 %collective-permute-done.21 = f32[160,128]{1,0:T(8,128)S(1)} collective-permute-done((f32[160,128]{1,0:T(8,128)S(1)}, f32[160,128]{1,0:T(8,128)S(1)}, u32[]{:S(2)}, u32[]{:S(2)}) %collective-permute-start.21) | collective-permute-done | bytes 81952 | tf_op jit(solution)/shard_map/ppermute | solution.py:96
  73.9 4.8 %collective-permute-start.22 = (bf16[3,4,4,16,1024]{4,3,2,1,0:T(8,128)(2,1)S(1)}, bf16[3,4,4,16,1024]{4,3,2,1,0:T(8,128)(2,1)S(1)}, u32[]{:S(2)}, u32[]{:S(2)}) collective-permute-start(bf16[3,4,4,16,1024]{4,3,2,1,0:T(8,128)(2,1)S(1)} %pad_maximum_fusion.own), channel_id=1, source_target_pairs={{0,16},{16,0},{32,48},{48,32},{64,80},{80,64},{96,112},{112,96},{1... | collective-permute-start | bytes 4718600 | tf_op jit(solution)/shard_map/ppermute | solution.py:580
  80.3 4.9 %collective-permute-done.25 = f32[160,128]{1,0:T(8,128)S(1)} collective-permute-done((f32[160,128]{1,0:T(8,128)S(1)}, f32[160,128]{1,0:T(8,128)S(1)}, u32[]{:S(2)}, u32[]{:S(2)}) %collective-permute-start.25) | collective-permute-done | bytes 81952 | tf_op jit(solution)/shard_map/ppermute | solution.py:96
  86.0 3.8 %collective-permute-done.26 = f32[160,128]{1,0:T(8,128)S(1)} collective-permute-done((f32[160,128]{1,0:T(8,128)S(1)}, f32[160,128]{1,0:T(8,128)S(1)}, u32[]{:S(2)}, u32[]{:S(2)}) %collective-permute-start.26) | collective-permute-done | bytes 81952 | tf_op jit(solution)/shard_map/ppermute | solution.py:96
  89.9 2.2 %collective-permute-start.27 = (bf16[4,4,16,1024]{3,2,1,0:T(8,128)(2,1)S(1)}, bf16[4,4,16,1024]{3,2,1,0:T(8,128)(2,1)S(1)}, u32[]{:S(2)}, u32[]{:S(2)}) collective-permute-start(bf16[4,4,16,1024]{3,2,1,0:T(8,128)(2,1)S(1)} %pad_maximum_fusion.4.own2), channel_id=1, source_target_pairs={{0,16},{16,0},{32,48},{48,32},{64,80},{80,64},{96,112},{112,96},{1... | collective-permute-start | bytes 1572872 | tf_op jit(solution)/shard_map/ppermute | solution.py:584
  95.8 1.7 collective-permute-start.30
  97.6 2.4 %collective-permute-done.29 = f32[160,128]{1,0:T(8,128)S(1)} collective-permute-done((f32[160,128]{1,0:T(8,128)S(1)}, f32[160,128]{1,0:T(8,128)S(1)}, u32[]{:S(2)}, u32[]{:S(2)}) %collective-permute-start.29) | collective-permute-done | bytes 81952 | tf_op jit(solution)/shard_map/ppermute | solution.py:65
  103.4 1.9 collective-permute-start.31
  109.2 8.0 %shard_map.96 = bf16[8,16,56,128]{3,2,1,0:T(8,128)(2,1)S(1)} custom-call(s32[4]{0:T(128)S(1)} %pad_add_fusion.where, bf16[3,4,4,16,1024]{4,3,2,1,0:T(8,128)(2,1)S(1)} %pad_maximum_fusion.own, bf16[3,4,4,16,1024]{4,3,2,1,0:T(8,128)(2,1)S(1)} %copy-done.11, bf16[4,4,16,1024]{3,2,1,0:T(8,128)(2,1)S(1)} %pad_maximum_fusion.4.own2, ...), custom_call_target="tpu_custom_call" | custom-call | flops 4563402752 | bytes 9437184 | tf_op jit(solution)/shard_map/pallas_call | solution.py:314
  118.4 3.7 %all-to-all-start = ((bf16[128,56,128]{2,1,0:T(8,128)(2,1)}), bf16[128,56,128]{2,1,0:T(8,128)(2,1)S(1)}, u32[]{:S(2)}, u32[]{:S(2)}) async-start(bf16[128,56,128]{2,1,0:T(8,128)(2,1)} %bitcast.42), calls=%async_computation | async-start | bytes 3670016 | tf_op jit(solution)/shard_map/all_to_all | solution.py:592
  122.2 20.5 %shard_map.97 = (f32[512,512]{1,0:T(8,128)}, f32[512,512]{1,0:T(8,128)S(1)}) custom-call(f32[1280,128]{1,0:T(8,128)S(1)} %pad_maximum_fusion.1.gram_ref), custom_call_target="tpu_custom_call" | custom-call | flops 2684354560 | bytes 4194304 | tf_op jit(solution)/shard_map/pallas_call | solution.py:413
  143.7 5.3 %all-to-all-done = bf16[128,56,128]{2,1,0:T(8,128)(2,1)S(1)} async-done(((bf16[128,56,128]{2,1,0:T(8,128)(2,1)}), bf16[128,56,128]{2,1,0:T(8,128)(2,1)S(1)}, u32[]{:S(2)}, u32[]{:S(2)}) %all-to-all-start) | async-done | bytes 1835040 | tf_op jit(solution)/shard_map/all_to_all | solution.py:592
  149.0 3.5 %copy-done = bf16[6400,512]{1,0:T(8,128)(2,1)S(1)} copy-done((bf16[6400,512]{1,0:T(8,128)(2,1)S(1)}, bf16[6400,512]{1,0:T(8,128)(2,1)}, u32[]{:S(2)}) %copy-start) | copy-done | bytes 6553624
  152.5 1.9 %shard_map.99 = f32[128,512]{1,0:T(8,128)S(1)} custom-call(bf16[16,400,512]{2,1,0:T(8,128)(2,1)S(1)} %bitcast.38, bf16[8,16,56,128]{3,2,1,0:T(8,128)(2,1)S(1)} %bitcast.39), custom_call_target="tpu_custom_call" | custom-call | flops 1073741824 | bytes 11534336 | tf_op jit(solution)/shard_map/pallas_call | solution.py:438
  157.3 4.4 %collective-permute-done.33 = f32[64,512]{1,0:T(8,128)S(1)} collective-permute-done((f32[64,512]{1,0:T(8,128)S(1)}, f32[64,512]{1,0:T(8,128)S(1)}, u32[]{:S(2)}, u32[]{:S(2)}) %collective-permute-start.33) | collective-permute-done | bytes 131104 | tf_op jit(solution)/shard_map/ppermute | solution.py:96
  162.6 4.2 %collective-permute-done.34 = f32[64,512]{1,0:T(8,128)S(1)} collective-permute-done((f32[64,512]{1,0:T(8,128)S(1)}, f32[64,512]{1,0:T(8,128)S(1)}, u32[]{:S(2)}, u32[]{:S(2)}) %collective-permute-start.34) | collective-permute-done | bytes 131104 | tf_op jit(solution)/shard_map/ppermute | solution.py:96
  166.9 2.6 %collective-permute-start.35 = (f32[64,512]{1,0:T(8,128)S(1)}, f32[64,512]{1,0:T(8,128)S(1)}, u32[]{:S(2)}, u32[]{:S(2)}) collective-permute-start(f32[64,512]{1,0:T(8,128)S(1)} %add.137), channel_id=1, source_target_pairs={{0,16},{16,0},{32,48},{48,32},{64,80},{80,64},{96,112},{112,96},{1... | collective-permute-start | bytes 393224 | tf_op jit(solution)/shard_map/ppermute | solution.py:89
  171.2 12.0 %shard_map.100 = (f32[128,512]{1,0:T(8,128)}, f32[128,8192]{1,0:T(8,128)}) custom-call(f32[128,512]{1,0:T(8,128)} %pad_maximum_fusion.6.cross_ref, f32[512,512]{1,0:T(8,128)} %copy-done.4, bf16[16,400,512]{2,1,0:T(8,128)(2,1)} %bitcast.37, bf16[8,16,56,128]{3,2,1,0:T(8,128)(2,1)} %bitcast.40), custom_call_target="tpu_custom_call" | custom-call | flops 2147483648 | bytes 16777216 | tf_op jit(solution)/shard_map/pallas_call | solution.py:500
  (121 shorter events, 43.0 us)
Async XLA Ops:
  7.2 136.5 %all-gather.3.cloned.1.call-start = ((), (), s32[]{:S(2)}) async-start(), calls=%async_computation.1 | async-start | bytes 6963200 | tf_op jit(solution)/shard_map/all_gather | solution.py:572
  8.1 6.0 %collective-permute-start.2 = (bf16[32,1024]{1,0:T(8,128)(2,1)S(1)}, bf16[32,1024]{1,0:T(8,128)(2,1)S(1)}, u32[]{:S(2)}, u32[]{:S(2)}) collective-permute-start(bf16[32,1024]{1,0:T(8,128)(2,1)S(1)} %pad_maximum_fusion.12), channel_id=1, source_target_pairs={{0,3},{1,0},{2,1},{3,2},{4,7},{5,4},{6,5},{7,6},{8,11},{9,8},{10,9... | collective-permute-start | bytes 196616 | tf_op jit(solution)/shard_map/ppermute | solution.py:61
  12.8 4.7 %collective-permute-start.1 = (bf16[32,1024]{1,0:T(8,128)(2,1)S(1)}, bf16[32,1024]{1,0:T(8,128)(2,1)S(1)}, u32[]{:S(2)}, u32[]{:S(2)}) collective-permute-start(bf16[32,1024]{1,0:T(8,128)(2,1)S(1)} %pad_maximum_fusion.12), channel_id=1, source_target_pairs={{0,2},{1,3},{2,0},{3,1},{4,6},{5,7},{6,4},{7,5},{8,10},{9,11},{10,... | collective-permute-start | bytes 196616 | tf_op jit(solution)/shard_map/ppermute | solution.py:61
  12.8 5.0 %collective-permute-start = (bf16[32,1024]{1,0:T(8,128)(2,1)S(1)}, bf16[32,1024]{1,0:T(8,128)(2,1)S(1)}, u32[]{:S(2)}, u32[]{:S(2)}) collective-permute-start(bf16[32,1024]{1,0:T(8,128)(2,1)S(1)} %pad_maximum_fusion.12), channel_id=1, source_target_pairs={{0,1},{1,2},{2,3},{3,0},{4,5},{5,6},{6,7},{7,4},{8,9},{9,10},{10,1... | collective-permute-start | bytes 196616 | tf_op jit(solution)/shard_map/ppermute | solution.py:61
  17.8 5.2 %collective-permute-start.5 = (bf16[4,16,1024]{2,1,0:T(8,128)(2,1)S(1)}, bf16[4,16,1024]{2,1,0:T(8,128)(2,1)S(1)}, u32[]{:S(2)}, u32[]{:S(2)}) collective-permute-start(bf16[4,16,1024]{2,1,0:T(8,128)(2,1)S(1)} %get-tuple-element.87), channel_id=1, source_target_pairs={{0,12},{1,13},{2,14},{3,15},{4,0},{5,1},{6,2},{7,3},{8,4},{9,5},{1... | collective-permute-start | bytes 393224 | tf_op jit(solution)/shard_map/ppermute | solution.py:61
  20.4 5.4 %collective-permute-start.4 = (bf16[4,16,1024]{2,1,0:T(8,128)(2,1)S(1)}, bf16[4,16,1024]{2,1,0:T(8,128)(2,1)S(1)}, u32[]{:S(2)}, u32[]{:S(2)}) collective-permute-start(bf16[4,16,1024]{2,1,0:T(8,128)(2,1)S(1)} %get-tuple-element.87), channel_id=1, source_target_pairs={{0,8},{1,9},{2,10},{3,11},{4,12},{5,13},{6,14},{7,15},{8,0},{9,1},... | collective-permute-start | bytes 393224 | tf_op jit(solution)/shard_map/ppermute | solution.py:61
  20.9 6.2 %collective-permute-start.3 = (bf16[4,16,1024]{2,1,0:T(8,128)(2,1)S(1)}, bf16[4,16,1024]{2,1,0:T(8,128)(2,1)S(1)}, u32[]{:S(2)}, u32[]{:S(2)}) collective-permute-start(bf16[4,16,1024]{2,1,0:T(8,128)(2,1)S(1)} %get-tuple-element.87), channel_id=1, source_target_pairs={{0,4},{1,5},{2,6},{3,7},{4,8},{5,9},{6,10},{7,11},{8,12},{9,13},{1... | collective-permute-start | bytes 393224 | tf_op jit(solution)/shard_map/ppermute | solution.py:61
  27.2 8.6 %collective-permute-start.6 = (bf16[4,4,16,1024]{3,2,1,0:T(8,128)(2,1)S(1)}, bf16[4,4,16,1024]{3,2,1,0:T(8,128)(2,1)S(1)}, u32[]{:S(2)}, u32[]{:S(2)}) collective-permute-start(bf16[4,4,16,1024]{3,2,1,0:T(8,128)(2,1)S(1)} %pad_maximum_fusion.2.own), channel_id=1, source_target_pairs={{0,16},{16,0},{32,48},{48,32},{64,80},{80,64},{96,112},{112,96},{1... | collective-permute-start | bytes 1572872 | tf_op jit(solution)/shard_map/ppermute | solution.py:550
  34.3 5.0 %collective-permute-start.11 = (bf16[4,16,1024]{2,1,0:T(8,128)(2,1)S(1)}, bf16[4,16,1024]{2,1,0:T(8,128)(2,1)S(1)}, u32[]{:S(2)}, u32[]{:S(2)}) collective-permute-start(bf16[4,16,1024]{2,1,0:T(8,128)(2,1)S(1)} %pad_maximum_fusion.8), channel_id=1, source_target_pairs={{0,12},{1,13},{2,14},{3,15},{4,0},{5,1},{6,2},{7,3},{8,4},{9,5},{1... | collective-permute-start | bytes 393224 | tf_op jit(solution)/shard_map/ppermute | solution.py:61
  34.6 6.1 %collective-permute-start.10 = (bf16[4,16,1024]{2,1,0:T(8,128)(2,1)S(1)}, bf16[4,16,1024]{2,1,0:T(8,128)(2,1)S(1)}, u32[]{:S(2)}, u32[]{:S(2)}) collective-permute-start(bf16[4,16,1024]{2,1,0:T(8,128)(2,1)S(1)} %pad_maximum_fusion.8), channel_id=1, source_target_pairs={{0,8},{1,9},{2,10},{3,11},{4,12},{5,13},{6,14},{7,15},{8,0},{9,1},... | collective-permute-start | bytes 393224 | tf_op jit(solution)/shard_map/ppermute | solution.py:61
  35.1 9.2 %collective-permute-start.9 = (bf16[4,16,1024]{2,1,0:T(8,128)(2,1)S(1)}, bf16[4,16,1024]{2,1,0:T(8,128)(2,1)S(1)}, u32[]{:S(2)}, u32[]{:S(2)}) collective-permute-start(bf16[4,16,1024]{2,1,0:T(8,128)(2,1)S(1)} %pad_maximum_fusion.8), channel_id=1, source_target_pairs={{0,4},{1,5},{2,6},{3,7},{4,8},{5,9},{6,10},{7,11},{8,12},{9,13},{1... | collective-permute-start | bytes 393224 | tf_op jit(solution)/shard_map/ppermute | solution.py:61
  38.3 6.7 %collective-permute-start.8 = (f32[640,128]{1,0:T(8,128)S(1)}, f32[640,128]{1,0:T(8,128)S(1)}, u32[]{:S(2)}, u32[]{:S(2)}) collective-permute-start(f32[640,128]{1,0:T(8,128)S(1)} %constant_dynamic-slice_fusion.4), channel_id=1, source_target_pairs={{0,16},{16,0},{32,48},{48,32},{64,80},{80,64},{96,112},{112,96},{1... | collective-permute-start | bytes 983048 | tf_op jit(solution)/shard_map/ppermute | solution.py:85
  46.1 13.5 %collective-permute-start.12 = (bf16[2,56,512]{2,1,0:T(8,128)(2,1)S(1)}, bf16[2,56,512]{2,1,0:T(8,128)(2,1)S(1)}, u32[]{:S(2)}, u32[]{:S(2)}) collective-permute-start(bf16[2,56,512]{2,1,0:T(8,128)(2,1)S(1)} %pad_maximum_fusion.9), channel_id=1, source_target_pairs={{0,32},{16,48},{32,64},{48,80},{64,96},{80,112},{96,0},{112,16},{1... | collective-permute-start | bytes 344072 | tf_op jit(solution)/shard_map/ppermute | solution.py:567
  47.5 12.2 %collective-permute-start.13 = (bf16[2,56,512]{2,1,0:T(8,128)(2,1)S(1)}, bf16[2,56,512]{2,1,0:T(8,128)(2,1)S(1)}, u32[]{:S(2)}, u32[]{:S(2)}) collective-permute-start(bf16[2,56,512]{2,1,0:T(8,128)(2,1)S(1)} %pad_maximum_fusion.10), channel_id=1, source_target_pairs={{0,64},{16,80},{32,96},{48,112},{64,0},{80,16},{96,32},{112,48},{1... | collective-permute-start | bytes 344072 | tf_op jit(solution)/shard_map/ppermute | solution.py:567
  51.4 5.6 %collective-permute-start.16 = (f32[160,128]{1,0:T(8,128)S(1)}, f32[160,128]{1,0:T(8,128)S(1)}, u32[]{:S(2)}, u32[]{:S(2)}) collective-permute-start(f32[160,128]{1,0:T(8,128)S(1)} %get-tuple-element.77), channel_id=1, source_target_pairs={{0,64},{16,80},{32,96},{48,112},{64,0},{80,16},{96,32},{112,48},{1... | collective-permute-start | bytes 245768 | tf_op jit(solution)/shard_map/ppermute | solution.py:73
  51.5 8.1 %collective-permute-start.15 = (f32[160,128]{1,0:T(8,128)S(1)}, f32[160,128]{1,0:T(8,128)S(1)}, u32[]{:S(2)}, u32[]{:S(2)}) collective-permute-start(f32[160,128]{1,0:T(8,128)S(1)} %get-tuple-element.75), channel_id=1, source_target_pairs={{0,32},{16,48},{32,64},{48,80},{64,96},{80,112},{96,0},{112,16},{1... | collective-permute-start | bytes 245768 | tf_op jit(solution)/shard_map/ppermute | solution.py:73
  53.9 5.8 %collective-permute-start.14 = (bf16[2,56,512]{2,1,0:T(8,128)(2,1)S(1)}, bf16[2,56,512]{2,1,0:T(8,128)(2,1)S(1)}, u32[]{:S(2)}, u32[]{:S(2)}) collective-permute-start(bf16[2,56,512]{2,1,0:T(8,128)(2,1)S(1)} %pad_maximum_fusion.11), channel_id=1, source_target_pairs={{0,96},{16,112},{32,0},{48,16},{64,32},{80,48},{96,64},{112,80},{1... | collective-permute-start | bytes 344072 | tf_op jit(solution)/shard_map/ppermute | solution.py:567
  61.1 12.6 %collective-permute-start.18 = (bf16[4,4,16,1024]{3,2,1,0:T(8,128)(2,1)S(1)}, bf16[4,4,16,1024]{3,2,1,0:T(8,128)(2,1)S(1)}, u32[]{:S(2)}, u32[]{:S(2)}) collective-permute-start(bf16[4,4,16,1024]{3,2,1,0:T(8,128)(2,1)S(1)} %pad_maximum_fusion.3), channel_id=1, source_target_pairs={{0,32},{16,48},{32,64},{48,80},{64,96},{80,112},{96,0},{112,16},{1... | collective-permute-start | bytes 1572872 | tf_op jit(solution)/shard_map/ppermute | solution.py:573
  61.2 12.5 %collective-permute-start.19 = (bf16[4,4,16,1024]{3,2,1,0:T(8,128)(2,1)S(1)}, bf16[4,4,16,1024]{3,2,1,0:T(8,128)(2,1)S(1)}, u32[]{:S(2)}, u32[]{:S(2)}) collective-permute-start(bf16[4,4,16,1024]{3,2,1,0:T(8,128)(2,1)S(1)} %pad_maximum_fusion.3), channel_id=1, source_target_pairs={{0,96},{16,112},{32,0},{48,16},{64,32},{80,48},{96,64},{112,80},{1... | collective-permute-start | bytes 1572872 | tf_op jit(solution)/shard_map/ppermute | solution.py:574
  67.4 4.9 %collective-permute-start.21 = (f32[160,128]{1,0:T(8,128)S(1)}, f32[160,128]{1,0:T(8,128)S(1)}, u32[]{:S(2)}, u32[]{:S(2)}) collective-permute-start(f32[160,128]{1,0:T(8,128)S(1)} %add.125), channel_id=1, source_target_pairs={{0,3},{1,2},{2,1},{3,0},{4,7},{5,6},{6,5},{7,4},{8,11},{9,10},{10,... | collective-permute-start | bytes 245768 | tf_op jit(solution)/shard_map/ppermute | solution.py:96
  73.9 19.8 %collective-permute-start.22 = (bf16[3,4,4,16,1024]{4,3,2,1,0:T(8,128)(2,1)S(1)}, bf16[3,4,4,16,1024]{4,3,2,1,0:T(8,128)(2,1)S(1)}, u32[]{:S(2)}, u32[]{:S(2)}) collective-permute-start(bf16[3,4,4,16,1024]{4,3,2,1,0:T(8,128)(2,1)S(1)} %pad_maximum_fusion.own), channel_id=1, source_target_pairs={{0,16},{16,0},{32,48},{48,32},{64,80},{80,64},{96,112},{112,96},{1... | collective-permute-start | bytes 4718600 | tf_op jit(solution)/shard_map/ppermute | solution.py:580
  78.7 11.1 %collective-permute-start.24 = (bf16[2,4,16,1024]{3,2,1,0:T(8,128)(2,1)S(1)}, bf16[2,4,16,1024]{3,2,1,0:T(8,128)(2,1)S(1)}, u32[]{:S(2)}, u32[]{:S(2)}) collective-permute-start(bf16[2,4,16,1024]{3,2,1,0:T(8,128)(2,1)S(1)} %slice.55), channel_id=1, source_target_pairs={{0,96},{16,112},{32,0},{48,16},{64,32},{80,48},{96,64},{112,80},{1... | collective-permute-start | bytes 786440 | tf_op jit(solution)/shard_map/ppermute | solution.py:578
  79.8 10.1 %collective-permute-start.23 = (bf16[2,4,16,1024]{3,2,1,0:T(8,128)(2,1)S(1)}, bf16[2,4,16,1024]{3,2,1,0:T(8,128)(2,1)S(1)}, u32[]{:S(2)}, u32[]{:S(2)}) collective-permute-start(bf16[2,4,16,1024]{3,2,1,0:T(8,128)(2,1)S(1)} %slice.54), channel_id=1, source_target_pairs={{0,32},{16,48},{32,64},{48,80},{64,96},{80,112},{96,0},{112,16},{1... | collective-permute-start | bytes 786440 | tf_op jit(solution)/shard_map/ppermute | solution.py:577
  80.3 4.9 %collective-permute-start.25 = (f32[160,128]{1,0:T(8,128)S(1)}, f32[160,128]{1,0:T(8,128)S(1)}, u32[]{:S(2)}, u32[]{:S(2)}) collective-permute-start(f32[160,128]{1,0:T(8,128)S(1)} %add.126), channel_id=1, source_target_pairs={{0,4},{1,5},{2,6},{3,7},{4,0},{5,1},{6,2},{7,3},{8,12},{9,13},{10,... | collective-permute-start | bytes 245768 | tf_op jit(solution)/shard_map/ppermute | solution.py:96
  85.2 4.6 %collective-permute-start.26 = (f32[160,128]{1,0:T(8,128)S(1)}, f32[160,128]{1,0:T(8,128)S(1)}, u32[]{:S(2)}, u32[]{:S(2)}) collective-permute-start(f32[160,128]{1,0:T(8,128)S(1)} %add.127), channel_id=1, source_target_pairs={{0,12},{1,13},{2,14},{3,15},{4,8},{5,9},{6,10},{7,11},{8,4},{9,5},... | collective-permute-start | bytes 245768 | tf_op jit(solution)/shard_map/ppermute | solution.py:96
  94.8 5.2 %collective-permute-start.29 = (f32[160,128]{1,0:T(8,128)S(1)}, f32[160,128]{1,0:T(8,128)S(1)}, u32[]{:S(2)}, u32[]{:S(2)}) collective-permute-start(f32[160,128]{1,0:T(8,128)S(1)} %add.128), channel_id=1, source_target_pairs={{0,64},{16,80},{32,96},{48,112},{64,0},{80,16},{96,32},{112,48},{1... | collective-permute-start | bytes 245768 | tf_op jit(solution)/shard_map/ppermute | solution.py:65
  95.8 5.8 %collective-permute-start.30 = (f32[160,128]{1,0:T(8,128)S(1)}, f32[160,128]{1,0:T(8,128)S(1)}, u32[]{:S(2)}, u32[]{:S(2)}) collective-permute-start(f32[160,128]{1,0:T(8,128)S(1)} %add.128), channel_id=1, source_target_pairs={{0,96},{16,112},{32,0},{48,16},{64,32},{80,48},{96,64},{112,80},{1... | collective-permute-start | bytes 245768 | tf_op jit(solution)/shard_map/ppermute | solution.py:65
  97.5 4.9 %collective-permute-start.28 = (f32[160,128]{1,0:T(8,128)S(1)}, f32[160,128]{1,0:T(8,128)}, u32[]{:S(2)}, u32[]{:S(2)}) collective-permute-start(f32[160,128]{1,0:T(8,128)S(1)} %add.128), channel_id=1, source_target_pairs={{0,32},{16,48},{32,64},{48,80},{64,96},{80,112},{96,0},{112,16},{1... | collective-permute-start | bytes 245768 | tf_op jit(solution)/shard_map/ppermute | solution.py:65
  103.4 13.8 %collective-permute-start.31 = (f32[640,128]{1,0:T(8,128)S(1)}, f32[640,128]{1,0:T(8,128)S(1)}, u32[]{:S(2)}, u32[]{:S(2)}) collective-permute-start(f32[640,128]{1,0:T(8,128)S(1)} %pad_maximum_fusion.5), channel_id=1, source_target_pairs={{0,16},{16,0},{32,48},{48,32},{64,80},{80,64},{96,112},{112,96},{1... | collective-permute-start | bytes 983048 | tf_op jit(solution)/shard_map/ppermute | solution.py:89
  118.4 30.5 %all-to-all-start = ((bf16[128,56,128]{2,1,0:T(8,128)(2,1)}), bf16[128,56,128]{2,1,0:T(8,128)(2,1)S(1)}, u32[]{:S(2)}, u32[]{:S(2)}) async-start(bf16[128,56,128]{2,1,0:T(8,128)(2,1)} %bitcast.42), calls=%async_computation | async-start | bytes 3670016 | tf_op jit(solution)/shard_map/all_to_all | solution.py:592
  156.9 4.8 %collective-permute-start.33 = (f32[64,512]{1,0:T(8,128)S(1)}, f32[64,512]{1,0:T(8,128)S(1)}, u32[]{:S(2)}, u32[]{:S(2)}) collective-permute-start(f32[64,512]{1,0:T(8,128)S(1)} %dynamic-slice_add_fusion.1), channel_id=1, source_target_pairs={{0,32},{16,48},{32,0},{48,16},{64,96},{80,112},{96,64},{112,80},{1... | collective-permute-start | bytes 393224 | tf_op jit(solution)/shard_map/ppermute | solution.py:96
  161.7 5.1 %collective-permute-start.34 = (f32[64,512]{1,0:T(8,128)S(1)}, f32[64,512]{1,0:T(8,128)S(1)}, u32[]{:S(2)}, u32[]{:S(2)}) collective-permute-start(f32[64,512]{1,0:T(8,128)S(1)} %add.136), channel_id=1, source_target_pairs={{0,96},{16,112},{32,64},{48,80},{64,32},{80,48},{96,0},{112,16},{1... | collective-permute-start | bytes 393224 | tf_op jit(solution)/shard_map/ppermute | solution.py:96
  (21 other events, 139.8 us)
Sparse Core Ops, SparseCore 0:
  61.2 63.5 all-gather.2

commit v13 on v10

--- a/solution.py
+++ b/solution.py
@@ -257,11 +257,12 @@
 
 
 def trail_chunk(ref, i):
-    rows = [ref[r, i, :48].astype(F32) for r in range(8)]
+    rows = [ref[r, i, :48] for r in range(8)]
     energy = ref[0, i, 48:].astype(F32)
     for r in range(1, 8):
         energy = energy + ref[r, i, 48:].astype(F32)
-    return jnp.concatenate(rows + [energy, jnp.zeros_like(energy)], axis=0).astype(BF16)
+    last = jnp.concatenate([energy, jnp.zeros_like(energy)], axis=0).astype(BF16)
+    return jnp.concatenate(rows + [last], axis=0)
 
 
 def params(mib=40):
@@ -563,9 +564,10 @@
     segment = lax.all_gather(panel, "col", axis=0, tiled=False)
     trail_other = lax.ppermute(trail_own, "row", CORE_SWAP)
     gram = sum4(gram, "col", z_pair)
+    trail_other, gram = lax.optimization_barrier((trail_other, gram))
     gram = sum4(gram, "col", x_pair)
-    trail_other, gram = lax.optimization_barrier((trail_other, gram))
     trail = trail_rows(where, trail_own, trail_other, atoms, grads, mean, order)
+    trail, gram = lax.optimization_barrier((trail, gram))
     gram = gather4(gram, "row", y_shift, y)
     trail, gram = lax.optimization_barrier((trail, gram))
     gram = jnp.concatenate(swap_gather(gram, core), axis=0)

time: 186 us -> 186 us (level)
  waiting for transfers between devices: 57.1 us -> 61.2 us
  other arithmetic: 3.65 us -> 0.56 us
    all_gather x1, waiting for transfers between devices: 12.8 us -> 17 us  [per_device(): segment = lax.all_gather(panel, 'col', axis=0, tiled=False)]
    ppermute x3, waiting for transfers between devices: 0.01 us -> 3.9 us  [gather4(): pieces = [v] + [lax.ppermute(v, axis, shift(s)) for s in (1, 2, 3)]]
    ppermute x6, waiting for transfers between devices: 20.4 us -> 16.6 us  [sum4(): v = v + lax.ppermute(v, axis, pairs(flip))]
    add x6, other arithmetic: 2.53 us -> 0.08 us  [sum4(): v = v + lax.ppermute(v, axis, pairs(flip))]
    unnamed x25 -> x27, local copies, waits for them, and re-layouts: 11.3 us -> 9.19 us
  transfers between devices with their start and end apart: 31 -> 31, of which waited for: 21 -> 22; matrix products, arithmetic and copies ran while one was open for 3% -> 2% of each run, Pallas kernels for 18% -> 18%
where the time goes in v13:
time: 186 us; the launch traced here: 185 us
  waiting for transfers between devices  61.2 us (33%)
  starting transfers between devices  50.6 us (27%)
  Pallas kernels  46 us (25%)
  between operations  14.4 us (8%)
  local copies, waits for them, and re-layouts  12.3 us (7%)
    pallas_call x1, Pallas kernels, factor_panel(): pl.pallas_call(functools.partial(factor_kernel, float(rows_total)), out_s...  20.5 us
    all_gather x1, waiting for transfers between devices, per_device(): segment = lax.all_gather(panel, 'col', axis=0, tiled=False)  17 us
    ppermute x6, waiting for transfers between devices, sum4(): v = v + lax.ppermute(v, axis, pairs(flip))  16.6 us
    all_to_all x1, starting transfers between devices, per_device(): lax.all_to_all(trail.reshape(128, SENT, 128), ('row', 'col'), 0, 0, tiled...  10.3 us
    pallas_call x1, Pallas kernels, residual(): pl.pallas_call(functools.partial(residual_kernel, float(rows_total)), out...  10.2 us
    unnamed x27, local copies, waits for them, and re-layouts  9.19 us
    ppermute x6, starting transfers between devices, shifted(): return [v] + [lax.ppermute(v, axis, shift(s)) for s in (1, 2, 3)]  8.96 us
    ppermute x6, waiting for transfers between devices, shifted(): return [v] + [lax.ppermute(v, axis, shift(s)) for s in (1, 2, 3)]  8.87 us
  transfers between devices with their start and end apart: 31, of which 22 were waited for; matrix products, arithmetic and copies ran while one was open for 2% of the time, Pallas kernels for 18%

profile of v13, /device:TPU:1, one launch (start us, length us, event | category | flops | bytes accessed | tf_op | source)
XLA Modules:
  0.0 185.1 jit_solution(10734783587823428949)
XLA Ops:
  9.6 4.6 %collective-permute-start.3 = (bf16[16,1024]{1,0:T(8,128)(2,1)S(1)}, bf16[16,1024]{1,0:T(8,128)(2,1)S(1)}, u32[]{:S(2)}, u32[]{:S(2)}) collective-permute-start(bf16[16,1024]{1,0:T(8,128)(2,1)S(1)} %constant_dynamic-slice_fusion.5), channel_id=1, source_target_pairs={{0,3},{1,0},{2,1},{3,2},{4,7},{5,4},{6,5},{7,6},{8,11},{9,8},{10,9... | collective-permute-start | bytes 98312 | tf_op jit(solution)/shard_map/ppermute | solution.py:61
  15.7 2.9 %collective-permute-done.2 = bf16[16,1024]{1,0:T(8,128)(2,1)S(1)} collective-permute-done((bf16[16,1024]{1,0:T(8,128)(2,1)S(1)}, bf16[16,1024]{1,0:T(8,128)(2,1)S(1)}, u32[]{:S(2)}, u32[]{:S(2)}) %collective-permute-start.2) | collective-permute-done | bytes 32800 | tf_op jit(solution)/shard_map/ppermute | solution.py:61
  18.6 2.5 %collective-permute-start.6 = (bf16[4,16,1024]{2,1,0:T(8,128)(2,1)S(1)}, bf16[4,16,1024]{2,1,0:T(8,128)(2,1)S(1)}, u32[]{:S(2)}, u32[]{:S(2)}) collective-permute-start(bf16[4,16,1024]{2,1,0:T(8,128)(2,1)S(1)} %get-tuple-element.71), channel_id=1, source_target_pairs={{0,12},{1,13},{2,14},{3,15},{4,0},{5,1},{6,2},{7,3},{8,4},{9,5},{1... | collective-permute-start | bytes 393224 | tf_op jit(solution)/shard_map/ppermute | solution.py:61
  23.8 2.8 %collective-permute-done.5 = bf16[4,16,1024]{2,1,0:T(8,128)(2,1)S(1)} collective-permute-done((bf16[4,16,1024]{2,1,0:T(8,128)(2,1)S(1)}, bf16[4,16,1024]{2,1,0:T(8,128)(2,1)S(1)}, u32[]{:S(2)}, u32[]{:S(2)}) %collective-permute-start.5) | collective-permute-done | bytes 131104 | tf_op jit(solution)/shard_map/ppermute | solution.py:61
  26.6 1.7 collective-permute-done.4
  28.3 4.1 %collective-permute-start.7 = (bf16[4,4,16,1024]{3,2,1,0:T(8,128)(2,1)S(1)}, bf16[4,4,16,1024]{3,2,1,0:T(8,128)(2,1)}, u32[]{:S(2)}, u32[]{:S(2)}) collective-permute-start(bf16[4,4,16,1024]{3,2,1,0:T(8,128)(2,1)S(1)} %pad_maximum_fusion.1.own), channel_id=1, source_target_pairs={{0,16},{16,0},{32,48},{48,32},{64,80},{80,64},{96,112},{112,96},{1... | collective-permute-start | bytes 1572872 | tf_op jit(solution)/shard_map/ppermute | solution.py:543
  33.3 1.9 %copy-done.3 = bf16[3,4,128,1024]{3,2,1,0:T(8,128)(2,1)S(1)} copy-done((bf16[3,4,128,1024]{3,2,1,0:T(8,128)(2,1)S(1)}, bf16[3,4,128,1024]{3,2,1,0:T(8,128)(2,1)}, u32[]{:S(2)}) %copy-start.3) | copy-done | bytes 3145752
  36.6 3.3 %shard_map.95 = (bf16[4,56,512]{2,1,0:T(8,128)(2,1)S(1)}, bf16[4,56,512]{2,1,0:T(8,128)(2,1)S(1)}, f32[1280,128]{1,0:T(8,128)S(1)}) custom-call(s32[4]{0:T(128)S(1)} %pad_add_fusion.where, bf16[4,4,16,1024]{3,2,1,0:T(8,128)(2,1)S(1)} %pad_maximum_fusion.1.own, bf16[4,4,16,1024]{3,2,1,0:T(8,128)(2,1)} %collective-permute-done.7.other, ...), custom_call_target="tpu_custom_call" | custom-call | flops 1140850688 | bytes 5242880 | tf_op jit(solution)/shard_map/pallas_call | solution.py:281
  44.1 2.7 %collective-permute-start.11 = (bf16[2,56,512]{2,1,0:T(8,128)(2,1)S(1)}, bf16[2,56,512]{2,1,0:T(8,128)(2,1)S(1)}, u32[]{:S(2)}, u32[]{:S(2)}) collective-permute-start(bf16[2,56,512]{2,1,0:T(8,128)(2,1)S(1)} %pad_maximum_fusion.6), channel_id=1, source_target_pairs={{0,64},{16,80},{32,96},{48,112},{64,0},{80,16},{96,32},{112,48},{1... | collective-permute-start | bytes 344072 | tf_op jit(solution)/shard_map/ppermute | solution.py:559
  48.7 2.3 %collective-permute-done.15 = f32[160,128]{1,0:T(8,128)S(1)} collective-permute-done((f32[160,128]{1,0:T(8,128)S(1)}, f32[160,128]{1,0:T(8,128)S(1)}, u32[]{:S(2)}, u32[]{:S(2)}) %collective-permute-start.15) | collective-permute-done | bytes 81952 | tf_op jit(solution)/shard_map/ppermute | solution.py:73
  50.9 2.6 %collective-permute-start.12 = (bf16[2,56,512]{2,1,0:T(8,128)(2,1)S(1)}, bf16[2,56,512]{2,1,0:T(8,128)(2,1)S(1)}, u32[]{:S(2)}, u32[]{:S(2)}) collective-permute-start(bf16[2,56,512]{2,1,0:T(8,128)(2,1)S(1)} %pad_maximum_fusion.7), channel_id=1, source_target_pairs={{0,96},{16,112},{32,0},{48,16},{64,32},{80,48},{96,64},{112,80},{1... | collective-permute-start | bytes 344072 | tf_op jit(solution)/shard_map/ppermute | solution.py:559
  53.9 2.5 %collective-permute-done.13 = f32[160,128]{1,0:T(8,128)S(1)} collective-permute-done((f32[160,128]{1,0:T(8,128)S(1)}, f32[160,128]{1,0:T(8,128)S(1)}, u32[]{:S(2)}, u32[]{:S(2)}) %collective-permute-start.13) | collective-permute-done | bytes 81952 | tf_op jit(solution)/shard_map/ppermute | solution.py:73
  58.9 1.7 collective-permute-start
  61.6 3.2 %collective-permute-done.16 = f32[160,128]{1,0:T(8,128)S(1)} collective-permute-done((f32[160,128]{1,0:T(8,128)S(1)}, f32[160,128]{1,0:T(8,128)S(1)}, u32[]{:S(2)}, u32[]{:S(2)}) %collective-permute-start.16) | collective-permute-done | bytes 81952 | tf_op jit(solution)/shard_map/ppermute | solution.py:96
  64.8 2.2 %collective-permute-start.17 = (f32[160,128]{1,0:T(8,128)S(1)}, f32[160,128]{1,0:T(8,128)S(1)}, u32[]{:S(2)}, u32[]{:S(2)}) collective-permute-start(f32[160,128]{1,0:T(8,128)S(1)} %add.123), channel_id=1, source_target_pairs={{0,3},{1,2},{2,1},{3,0},{4,7},{5,6},{6,5},{7,4},{8,11},{9,10},{10,... | collective-permute-start | bytes 245768 | tf_op jit(solution)/shard_map/ppermute | solution.py:96
  67.0 2.4 %collective-permute-done.17 = f32[160,128]{1,0:T(8,128)S(1)} collective-permute-done((f32[160,128]{1,0:T(8,128)S(1)}, f32[160,128]{1,0:T(8,128)S(1)}, u32[]{:S(2)}, u32[]{:S(2)}) %collective-permute-start.17) | collective-permute-done | bytes 81952 | tf_op jit(solution)/shard_map/ppermute | solution.py:96
  70.1 2.6 %collective-permute-done.18 = f32[160,128]{1,0:T(8,128)S(1)} collective-permute-done((f32[160,128]{1,0:T(8,128)S(1)}, f32[160,128]{1,0:T(8,128)S(1)}, u32[]{:S(2)}, u32[]{:S(2)}) %collective-permute-start.18) | collective-permute-done | bytes 81952 | tf_op jit(solution)/shard_map/ppermute | solution.py:96
  72.8 2.0 %collective-permute-start.19 = (f32[160,128]{1,0:T(8,128)S(1)}, f32[160,128]{1,0:T(8,128)S(1)}, u32[]{:S(2)}, u32[]{:S(2)}) collective-permute-start(f32[160,128]{1,0:T(8,128)S(1)} %add.125), channel_id=1, source_target_pairs={{0,12},{1,13},{2,14},{3,15},{4,8},{5,9},{6,10},{7,11},{8,4},{9,5},... | collective-permute-start | bytes 245768 | tf_op jit(solution)/shard_map/ppermute | solution.py:96
  74.7 1.6 copy-done.8
  76.3 7.3 %shard_map.96 = bf16[8,16,56,128]{3,2,1,0:T(8,128)(2,1)S(1)} custom-call(s32[4]{0:T(128)S(1)} %pad_add_fusion.where, bf16[16,64,1024]{2,1,0:T(8,128)(2,1)S(1)} %bitcast.30, bf16[16,64,1024]{2,1,0:T(8,128)(2,1)S(1)} %collective-permute-done.other_ref, bf16[320,1024]{1,0:T(8,128)(2,1)S(1)} %copy-done.10, bf16[768,1024]{1,0:T(8,128)(2,1)S(1)} %get-tuple-element.29.grads_ref, ...), custom_call_target="tpu_custom_call" | custom-call | flops 4563402752 | bytes 9437184 | tf_op jit(solution)/shard_map/pallas_call | solution.py:314
  84.9 2.8 %collective-permute-start.21 = (f32[160,128]{1,0:T(8,128)S(1)}, f32[160,128]{1,0:T(8,128)S(1)}, u32[]{:S(2)}, u32[]{:S(2)}) collective-permute-start(f32[160,128]{1,0:T(8,128)S(1)} %add.126), channel_id=1, source_target_pairs={{0,64},{16,80},{32,96},{48,112},{64,0},{80,16},{96,32},{112,48},{1... | collective-permute-start | bytes 245768 | tf_op jit(solution)/shard_map/ppermute | solution.py:65
  91.0 2.1 %collective-permute-done.20 = f32[160,128]{1,0:T(8,128)S(1)} collective-permute-done((f32[160,128]{1,0:T(8,128)S(1)}, f32[160,128]{1,0:T(8,128)S(1)}, u32[]{:S(2)}, u32[]{:S(2)}) %collective-permute-start.20) | collective-permute-done | bytes 81952 | tf_op jit(solution)/shard_map/ppermute | solution.py:65
  93.2 10.3 %all-to-all-start = ((bf16[128,56,128]{2,1,0:T(8,128)(2,1)}), bf16[128,56,128]{2,1,0:T(8,128)(2,1)S(1)}, u32[]{:S(2)}, u32[]{:S(2)}) async-start(bf16[128,56,128]{2,1,0:T(8,128)(2,1)} %bitcast.27), calls=%async_computation | async-start | bytes 3670016 | tf_op jit(solution)/shard_map/all_to_all | solution.py:574
  106.1 20.5 %shard_map.97 = (f32[512,512]{1,0:T(8,128)}, f32[512,512]{1,0:T(8,128)S(1)}) custom-call(f32[1280,128]{1,0:T(8,128)S(1)} %pad_maximum_fusion.gram_ref), custom_call_target="tpu_custom_call" | custom-call | flops 2684354560 | bytes 4194304 | tf_op jit(solution)/shard_map/pallas_call | solution.py:413
  126.6 17.0 %all-gather.7.cloned.1.call-done = bf16[6400,512]{1,0:T(8,128)(2,1)} async-done(((bf16[400,512]{1,0:T(8,128)(2,1)}), bf16[6400,512]{1,0:T(8,128)(2,1)}) %all-gather.7.cloned.1.call-update) | async-done | bytes 6553616 | tf_op jit(solution)/shard_map/all_gather | solution.py:564
  143.7 3.9 %all-to-all-done = bf16[128,56,128]{2,1,0:T(8,128)(2,1)S(1)} async-done(((bf16[128,56,128]{2,1,0:T(8,128)(2,1)}), bf16[128,56,128]{2,1,0:T(8,128)(2,1)S(1)}, u32[]{:S(2)}, u32[]{:S(2)}) %all-to-all-start) | async-done | bytes 1835040 | tf_op jit(solution)/shard_map/all_to_all | solution.py:574
  147.5 2.9 %copy-done.1 = bf16[6400,512]{1,0:T(8,128)(2,1)S(1)} copy-done((bf16[6400,512]{1,0:T(8,128)(2,1)S(1)}, bf16[6400,512]{1,0:T(8,128)(2,1)}, u32[]{:S(2)}) %copy-start.1) | copy-done | bytes 6553624
  150.4 1.9 %shard_map.99 = f32[128,512]{1,0:T(8,128)S(1)} custom-call(bf16[16,400,512]{2,1,0:T(8,128)(2,1)S(1)} %bitcast.22, bf16[8,16,56,128]{3,2,1,0:T(8,128)(2,1)S(1)} %bitcast.24), custom_call_target="tpu_custom_call" | custom-call | flops 1073741824 | bytes 11534336 | tf_op jit(solution)/shard_map/pallas_call | solution.py:438
  154.8 4.4 %collective-permute-done.25 = f32[64,512]{1,0:T(8,128)S(1)} collective-permute-done((f32[64,512]{1,0:T(8,128)S(1)}, f32[64,512]{1,0:T(8,128)S(1)}, u32[]{:S(2)}, u32[]{:S(2)}) %collective-permute-start.25) | collective-permute-done | bytes 131104 | tf_op jit(solution)/shard_map/ppermute | solution.py:96
  160.3 4.0 %collective-permute-done.26 = f32[64,512]{1,0:T(8,128)S(1)} collective-permute-done((f32[64,512]{1,0:T(8,128)S(1)}, f32[64,512]{1,0:T(8,128)S(1)}, u32[]{:S(2)}, u32[]{:S(2)}) %collective-permute-start.26) | collective-permute-done | bytes 131104 | tf_op jit(solution)/shard_map/ppermute | solution.py:96
  164.4 2.6 %collective-permute-start.27 = (f32[64,512]{1,0:T(8,128)S(1)}, f32[64,512]{1,0:T(8,128)S(1)}, u32[]{:S(2)}, u32[]{:S(2)}) collective-permute-start(f32[64,512]{1,0:T(8,128)S(1)} %add.134), channel_id=1, source_target_pairs={{0,16},{16,0},{32,48},{48,32},{64,80},{80,64},{96,112},{112,96},{1... | collective-permute-start | bytes 393224 | tf_op jit(solution)/shard_map/ppermute | solution.py:89
  168.1 10.2 %shard_map.100 = (f32[128,512]{1,0:T(8,128)}, f32[128,8192]{1,0:T(8,128)}) custom-call(f32[128,512]{1,0:T(8,128)S(1)} %pad_maximum_fusion.3.cross_ref, f32[512,512]{1,0:T(8,128)S(1)} %get-tuple-element.50.inverse_ref, bf16[16,400,512]{2,1,0:T(8,128)(2,1)S(1)} %bitcast.23, bf16[8,16,56,128]{3,2,1,0:T(8,128)(2,1)S(1)} %bitcast.25), custom_call_target="tpu_custom_call" | custom-call | flops 2147483648 | bytes 16777216 | tf_op jit(solution)/shard_map/pallas_call | solution.py:500
  (96 shorter events, 31.2 us)
Async XLA Ops:
  7.2 51.7 %all-gather.5.cloned.1.call-start = ((), (), s32[]{:S(2)}) async-start(), calls=%async_computation.1 | async-start | bytes 2228224 | tf_op jit(solution)/shard_map/all_gather | solution.py:539
  8.8 134.8 %all-gather.7.cloned.1.call-start = ((), (), s32[]{:S(2)}) async-start(), calls=%async_computation.2 | async-start | bytes 6963200 | tf_op jit(solution)/shard_map/all_gather | solution.py:564
  9.6 6.1 %collective-permute-start.3 = (bf16[16,1024]{1,0:T(8,128)(2,1)S(1)}, bf16[16,1024]{1,0:T(8,128)(2,1)S(1)}, u32[]{:S(2)}, u32[]{:S(2)}) collective-permute-start(bf16[16,1024]{1,0:T(8,128)(2,1)S(1)} %constant_dynamic-slice_fusion.5), channel_id=1, source_target_pairs={{0,3},{1,0},{2,1},{3,2},{4,7},{5,4},{6,5},{7,6},{8,11},{9,8},{10,9... | collective-permute-start | bytes 98312 | tf_op jit(solution)/shard_map/ppermute | solution.py:61
  14.2 4.3 %collective-permute-start.2 = (bf16[16,1024]{1,0:T(8,128)(2,1)S(1)}, bf16[16,1024]{1,0:T(8,128)(2,1)S(1)}, u32[]{:S(2)}, u32[]{:S(2)}) collective-permute-start(bf16[16,1024]{1,0:T(8,128)(2,1)S(1)} %constant_dynamic-slice_fusion.5), channel_id=1, source_target_pairs={{0,2},{1,3},{2,0},{3,1},{4,6},{5,7},{6,4},{7,5},{8,10},{9,11},{10,... | collective-permute-start | bytes 98312 | tf_op jit(solution)/shard_map/ppermute | solution.py:61
  14.2 4.3 %collective-permute-start.1 = (bf16[16,1024]{1,0:T(8,128)(2,1)S(1)}, bf16[16,1024]{1,0:T(8,128)(2,1)S(1)}, u32[]{:S(2)}, u32[]{:S(2)}) collective-permute-start(bf16[16,1024]{1,0:T(8,128)(2,1)S(1)} %constant_dynamic-slice_fusion.5), channel_id=1, source_target_pairs={{0,1},{1,2},{2,3},{3,0},{4,5},{5,6},{6,7},{7,4},{8,9},{9,10},{10,1... | collective-permute-start | bytes 98312 | tf_op jit(solution)/shard_map/ppermute | solution.py:61
  18.6 5.2 %collective-permute-start.6 = (bf16[4,16,1024]{2,1,0:T(8,128)(2,1)S(1)}, bf16[4,16,1024]{2,1,0:T(8,128)(2,1)S(1)}, u32[]{:S(2)}, u32[]{:S(2)}) collective-permute-start(bf16[4,16,1024]{2,1,0:T(8,128)(2,1)S(1)} %get-tuple-element.71), channel_id=1, source_target_pairs={{0,12},{1,13},{2,14},{3,15},{4,0},{5,1},{6,2},{7,3},{8,4},{9,5},{1... | collective-permute-start | bytes 393224 | tf_op jit(solution)/shard_map/ppermute | solution.py:61
  21.1 5.4 %collective-permute-start.5 = (bf16[4,16,1024]{2,1,0:T(8,128)(2,1)S(1)}, bf16[4,16,1024]{2,1,0:T(8,128)(2,1)S(1)}, u32[]{:S(2)}, u32[]{:S(2)}) collective-permute-start(bf16[4,16,1024]{2,1,0:T(8,128)(2,1)S(1)} %get-tuple-element.71), channel_id=1, source_target_pairs={{0,8},{1,9},{2,10},{3,11},{4,12},{5,13},{6,14},{7,15},{8,0},{9,1},... | collective-permute-start | bytes 393224 | tf_op jit(solution)/shard_map/ppermute | solution.py:61
  21.7 6.6 %collective-permute-start.4 = (bf16[4,16,1024]{2,1,0:T(8,128)(2,1)S(1)}, bf16[4,16,1024]{2,1,0:T(8,128)(2,1)S(1)}, u32[]{:S(2)}, u32[]{:S(2)}) collective-permute-start(bf16[4,16,1024]{2,1,0:T(8,128)(2,1)S(1)} %get-tuple-element.71), channel_id=1, source_target_pairs={{0,4},{1,5},{2,6},{3,7},{4,8},{5,9},{6,10},{7,11},{8,12},{9,13},{1... | collective-permute-start | bytes 393224 | tf_op jit(solution)/shard_map/ppermute | solution.py:61
  28.3 8.3 %collective-permute-start.7 = (bf16[4,4,16,1024]{3,2,1,0:T(8,128)(2,1)S(1)}, bf16[4,4,16,1024]{3,2,1,0:T(8,128)(2,1)}, u32[]{:S(2)}, u32[]{:S(2)}) collective-permute-start(bf16[4,4,16,1024]{3,2,1,0:T(8,128)(2,1)S(1)} %pad_maximum_fusion.1.own), channel_id=1, source_target_pairs={{0,16},{16,0},{32,48},{48,32},{64,80},{80,64},{96,112},{112,96},{1... | collective-permute-start | bytes 1572872 | tf_op jit(solution)/shard_map/ppermute | solution.py:543
  40.7 2.0 %collective-permute-start.9 = (f32[640,128]{1,0:T(8,128)}, f32[640,128]{1,0:T(8,128)S(1)}, u32[]{:S(2)}, u32[]{:S(2)}) collective-permute-start(f32[640,128]{1,0:T(8,128)} %constant_dynamic-slice_fusion.4), channel_id=1, source_target_pairs={{0,16},{16,0},{32,48},{48,32},{64,80},{80,64},{96,112},{112,96},{1... | collective-permute-start | bytes 983048 | tf_op jit(solution)/shard_map/ppermute | solution.py:85
  40.8 2.0 %collective-permute-start.8 = (bf16[4,56,512]{2,1,0:T(8,128)(2,1)S(1)}, bf16[4,56,512]{2,1,0:T(8,128)(2,1)S(1)}, u32[]{:S(2)}, u32[]{:S(2)}) collective-permute-start(bf16[4,56,512]{2,1,0:T(8,128)(2,1)S(1)} %get-tuple-element.33), channel_id=1, source_target_pairs={{0,16},{16,0},{32,48},{48,32},{64,80},{80,64},{96,112},{112,96},{1... | collective-permute-start | bytes 688136 | tf_op jit(solution)/shard_map/ppermute | solution.py:555
  42.7 32.0 %copy-start.10 = (bf16[320,1024]{1,0:T(8,128)(2,1)S(1)}, bf16[320,1024]{1,0:T(8,128)(2,1)}, u32[]{:S(2)}) copy-start(bf16[320,1024]{1,0:T(8,128)(2,1)} %copy-done.9) | copy-start | bytes 1966084
  42.8 13.6 %collective-permute-start.10 = (bf16[2,56,512]{2,1,0:T(8,128)(2,1)S(1)}, bf16[2,56,512]{2,1,0:T(8,128)(2,1)S(1)}, u32[]{:S(2)}, u32[]{:S(2)}) collective-permute-start(bf16[2,56,512]{2,1,0:T(8,128)(2,1)S(1)} %pad_maximum_fusion.5), channel_id=1, source_target_pairs={{0,32},{16,48},{32,64},{48,80},{64,96},{80,112},{96,0},{112,16},{1... | collective-permute-start | bytes 344072 | tf_op jit(solution)/shard_map/ppermute | solution.py:559
  44.1 12.3 %collective-permute-start.11 = (bf16[2,56,512]{2,1,0:T(8,128)(2,1)S(1)}, bf16[2,56,512]{2,1,0:T(8,128)(2,1)S(1)}, u32[]{:S(2)}, u32[]{:S(2)}) collective-permute-start(bf16[2,56,512]{2,1,0:T(8,128)(2,1)S(1)} %pad_maximum_fusion.6), channel_id=1, source_target_pairs={{0,64},{16,80},{32,96},{48,112},{64,0},{80,16},{96,32},{112,48},{1... | collective-permute-start | bytes 344072 | tf_op jit(solution)/shard_map/ppermute | solution.py:559
  46.8 4.1 %collective-permute-start.15 = (f32[160,128]{1,0:T(8,128)S(1)}, f32[160,128]{1,0:T(8,128)S(1)}, u32[]{:S(2)}, u32[]{:S(2)}) collective-permute-start(f32[160,128]{1,0:T(8,128)S(1)} %get-tuple-element.60), channel_id=1, source_target_pairs={{0,96},{16,112},{32,0},{48,16},{64,32},{80,48},{96,64},{112,80},{1... | collective-permute-start | bytes 245768 | tf_op jit(solution)/shard_map/ppermute | solution.py:73
  48.0 5.9 %collective-permute-start.14 = (f32[160,128]{1,0:T(8,128)S(1)}, f32[160,128]{1,0:T(8,128)S(1)}, u32[]{:S(2)}, u32[]{:S(2)}) collective-permute-start(f32[160,128]{1,0:T(8,128)S(1)} %get-tuple-element.61), channel_id=1, source_target_pairs={{0,64},{16,80},{32,96},{48,112},{64,0},{80,16},{96,32},{112,48},{1... | collective-permute-start | bytes 245768 | tf_op jit(solution)/shard_map/ppermute | solution.py:73
  48.1 8.3 %collective-permute-start.13 = (f32[160,128]{1,0:T(8,128)S(1)}, f32[160,128]{1,0:T(8,128)S(1)}, u32[]{:S(2)}, u32[]{:S(2)}) collective-permute-start(f32[160,128]{1,0:T(8,128)S(1)} %get-tuple-element.59), channel_id=1, source_target_pairs={{0,32},{16,48},{32,64},{48,80},{64,96},{80,112},{96,0},{112,16},{1... | collective-permute-start | bytes 245768 | tf_op jit(solution)/shard_map/ppermute | solution.py:73
  50.9 5.5 %collective-permute-start.12 = (bf16[2,56,512]{2,1,0:T(8,128)(2,1)S(1)}, bf16[2,56,512]{2,1,0:T(8,128)(2,1)S(1)}, u32[]{:S(2)}, u32[]{:S(2)}) collective-permute-start(bf16[2,56,512]{2,1,0:T(8,128)(2,1)S(1)} %pad_maximum_fusion.7), channel_id=1, source_target_pairs={{0,96},{16,112},{32,0},{48,16},{64,32},{80,48},{96,64},{112,80},{1... | collective-permute-start | bytes 344072 | tf_op jit(solution)/shard_map/ppermute | solution.py:559
  58.9 10.4 %collective-permute-start = (bf16[16,64,1024]{2,1,0:T(8,128)(2,1)}, bf16[16,64,1024]{2,1,0:T(8,128)(2,1)S(1)}, u32[]{:S(2)}, u32[]{:S(2)}) collective-permute-start(bf16[16,64,1024]{2,1,0:T(8,128)(2,1)} %bitcast.29), channel_id=1, source_target_pairs={{0,16},{16,0},{32,48},{48,32},{64,80},{80,64},{96,112},{112,96},{1... | collective-permute-start | bytes 6291464 | tf_op jit(solution)/shard_map/ppermute | solution.py:565
  60.7 4.1 %collective-permute-start.16 = (f32[160,128]{1,0:T(8,128)S(1)}, f32[160,128]{1,0:T(8,128)S(1)}, u32[]{:S(2)}, u32[]{:S(2)}) collective-permute-start(f32[160,128]{1,0:T(8,128)S(1)} %add_add_fusion), channel_id=1, source_target_pairs={{0,1},{1,0},{2,3},{3,2},{4,5},{5,4},{6,7},{7,6},{8,9},{9,8},{10,11... | collective-permute-start | bytes 245768 | tf_op jit(solution)/shard_map/ppermute | solution.py:96
  64.8 4.6 %collective-permute-start.17 = (f32[160,128]{1,0:T(8,128)S(1)}, f32[160,128]{1,0:T(8,128)S(1)}, u32[]{:S(2)}, u32[]{:S(2)}) collective-permute-start(f32[160,128]{1,0:T(8,128)S(1)} %add.123), channel_id=1, source_target_pairs={{0,3},{1,2},{2,1},{3,0},{4,7},{5,6},{6,5},{7,4},{8,11},{9,10},{10,... | collective-permute-start | bytes 245768 | tf_op jit(solution)/shard_map/ppermute | solution.py:96
  69.4 3.4 %collective-permute-start.18 = (f32[160,128]{1,0:T(8,128)S(1)}, f32[160,128]{1,0:T(8,128)S(1)}, u32[]{:S(2)}, u32[]{:S(2)}) collective-permute-start(f32[160,128]{1,0:T(8,128)S(1)} %add.124), channel_id=1, source_target_pairs={{0,4},{1,5},{2,6},{3,7},{4,0},{5,1},{6,2},{7,3},{8,12},{9,13},{10,... | collective-permute-start | bytes 245768 | tf_op jit(solution)/shard_map/ppermute | solution.py:96
  72.8 12.1 %collective-permute-start.19 = (f32[160,128]{1,0:T(8,128)S(1)}, f32[160,128]{1,0:T(8,128)S(1)}, u32[]{:S(2)}, u32[]{:S(2)}) collective-permute-start(f32[160,128]{1,0:T(8,128)S(1)} %add.125), channel_id=1, source_target_pairs={{0,12},{1,13},{2,14},{3,15},{4,8},{5,9},{6,10},{7,11},{8,4},{9,5},... | collective-permute-start | bytes 245768 | tf_op jit(solution)/shard_map/ppermute | solution.py:96
  84.9 4.9 %collective-permute-start.21 = (f32[160,128]{1,0:T(8,128)S(1)}, f32[160,128]{1,0:T(8,128)S(1)}, u32[]{:S(2)}, u32[]{:S(2)}) collective-permute-start(f32[160,128]{1,0:T(8,128)S(1)} %add.126), channel_id=1, source_target_pairs={{0,64},{16,80},{32,96},{48,112},{64,0},{80,16},{96,32},{112,48},{1... | collective-permute-start | bytes 245768 | tf_op jit(solution)/shard_map/ppermute | solution.py:65
  87.7 3.3 %collective-permute-start.22 = (f32[160,128]{1,0:T(8,128)S(1)}, f32[160,128]{1,0:T(8,128)S(1)}, u32[]{:S(2)}, u32[]{:S(2)}) collective-permute-start(f32[160,128]{1,0:T(8,128)S(1)} %add.126), channel_id=1, source_target_pairs={{0,96},{16,112},{32,0},{48,16},{64,32},{80,48},{96,64},{112,80},{1... | collective-permute-start | bytes 245768 | tf_op jit(solution)/shard_map/ppermute | solution.py:65
  88.6 4.5 %collective-permute-start.20 = (f32[160,128]{1,0:T(8,128)S(1)}, f32[160,128]{1,0:T(8,128)S(1)}, u32[]{:S(2)}, u32[]{:S(2)}) collective-permute-start(f32[160,128]{1,0:T(8,128)S(1)} %add.126), channel_id=1, source_target_pairs={{0,32},{16,48},{32,64},{48,80},{64,96},{80,112},{96,0},{112,16},{1... | collective-permute-start | bytes 245768 | tf_op jit(solution)/shard_map/ppermute | solution.py:65
  93.2 54.3 %all-to-all-start = ((bf16[128,56,128]{2,1,0:T(8,128)(2,1)}), bf16[128,56,128]{2,1,0:T(8,128)(2,1)S(1)}, u32[]{:S(2)}, u32[]{:S(2)}) async-start(bf16[128,56,128]{2,1,0:T(8,128)(2,1)} %bitcast.27), calls=%async_computation | async-start | bytes 3670016 | tf_op jit(solution)/shard_map/all_to_all | solution.py:574
  103.5 2.5 %collective-permute-start.23 = (f32[640,128]{1,0:T(8,128)S(1)}, f32[640,128]{1,0:T(8,128)S(1)}, u32[]{:S(2)}, u32[]{:S(2)}) collective-permute-start(f32[640,128]{1,0:T(8,128)S(1)} %pad_maximum_fusion.2), channel_id=1, source_target_pairs={{0,16},{16,0},{32,48},{48,32},{64,80},{80,64},{96,112},{112,96},{1... | collective-permute-start | bytes 983048 | tf_op jit(solution)/shard_map/ppermute | solution.py:89
  152.3 2.1 %collective-permute-start.24 = (f32[64,512]{1,0:T(8,128)S(1)}, f32[64,512]{1,0:T(8,128)S(1)}, u32[]{:S(2)}, u32[]{:S(2)}) collective-permute-start(f32[64,512]{1,0:T(8,128)S(1)} %constant_dynamic-slice_fusion), channel_id=1, source_target_pairs={{0,16},{16,0},{32,48},{48,32},{64,80},{80,64},{96,112},{112,96},{1... | collective-permute-start | bytes 393224 | tf_op jit(solution)/shard_map/ppermute | solution.py:85
  154.4 4.8 %collective-permute-start.25 = (f32[64,512]{1,0:T(8,128)S(1)}, f32[64,512]{1,0:T(8,128)S(1)}, u32[]{:S(2)}, u32[]{:S(2)}) collective-permute-start(f32[64,512]{1,0:T(8,128)S(1)} %dynamic-slice_add_fusion.1), channel_id=1, source_target_pairs={{0,32},{16,48},{32,0},{48,16},{64,96},{80,112},{96,64},{112,80},{1... | collective-permute-start | bytes 393224 | tf_op jit(solution)/shard_map/ppermute | solution.py:96
  159.2 5.1 %collective-permute-start.26 = (f32[64,512]{1,0:T(8,128)S(1)}, f32[64,512]{1,0:T(8,128)S(1)}, u32[]{:S(2)}, u32[]{:S(2)}) collective-permute-start(f32[64,512]{1,0:T(8,128)S(1)} %add.133), channel_id=1, source_target_pairs={{0,96},{16,112},{32,64},{48,80},{64,32},{80,48},{96,0},{112,16},{1... | collective-permute-start | bytes 393224 | tf_op jit(solution)/shard_map/ppermute | solution.py:96
  164.4 3.6 %collective-permute-start.27 = (f32[64,512]{1,0:T(8,128)S(1)}, f32[64,512]{1,0:T(8,128)S(1)}, u32[]{:S(2)}, u32[]{:S(2)}) collective-permute-start(f32[64,512]{1,0:T(8,128)S(1)} %add.134), channel_id=1, source_target_pairs={{0,16},{16,0},{32,48},{48,32},{64,80},{80,64},{96,112},{112,96},{1... | collective-permute-start | bytes 393224 | tf_op jit(solution)/shard_map/ppermute | solution.py:89
  (12 other events, 143.2 us)
Sparse Core Ops, SparseCore 0:
  10.8 48.1 all-gather.4
  61.1 82.4 all-gather.6
